TPU v7x, 128 devices: a whole 4x4x4 slice. The times are simulated.
128 devices in a mesh: row: 8 (over y, core), col: 16 (over x, z).
Axes of the slice: x: 4, y: 4, z: 4, core: 2. Of those that a mesh axis runs over, the one named last changes fastest.
Arguments:
- leaf_rhs: bfloat16 [8, 128, 2048], P('row', 'col'), may hold values from -6 to 6
- leaf_inverse: bfloat16 [8, 2048, 2048], P('row'), may hold values from -0.125 to 0.125
- interpolation: bfloat16 [8, 128, 2048], P('row'), may hold values from -0.5 to 0.5
- ranks: int32 [8], P('row'), may hold values from 32 to 128, as said below
- skeleton_rows: int32 [8, 128], P('row'), may hold values from 0 to 2047, as said below
- root_rows: int32 [8, 128], replicated, may hold values from 0 to 16383, as said below
- root_rhs: float32 [128, 16384], P('col', 'row'), may hold values from -6 to 6
- root_factor: bfloat16 [16384, 8, 2048], P('row', None, 'col')
Outputs:
- leaf_solution: float32 [8, 128, 2048], P('row', 'col')
- root_solution: float32 [128, 16384], P('col', 'row')
Inputs may be any that keep to these rules, and one draw needn't show every extreme that they name: `ranks`: some leaf has rank 128. `skeleton_rows`: distinct within each leaf. `root_rows`: all distinct over all leaves and slots.
All inputs are finite; a program needn't handle non-finite values.
Results may differ from a plain program's by a relative error of at most 0.014.
Values may be sent and summed in bfloat16 or wider, within the bound.
No kernel may reach another device: no remote copies, remote signals or barrier semaphores. Data moves between devices by JAX's collectives and lax.ppermute only.
A program may use at most 128 MiB of HBM per device.

v0:
```python
import jax
import jax.numpy as jnp
from jax import lax
from jax.sharding import PartitionSpec as P


def laid_out(tiles, dim):
    shape = list(tiles.shape[1:])
    shape[dim] *= tiles.shape[0]
    return jnp.moveaxis(tiles, 0, dim).reshape(shape)


def from_everyone(x, axis):
    length = lax.axis_size(axis)
    return lax.all_to_all(jnp.broadcast_to(x[None], (length, *x.shape)), axis, 0, 0, tiled=True)


def collect(x, axis, dim):
    return laid_out(from_everyone(x, axis), dim)


def from_root(x, axis, root):
    return lax.dynamic_index_in_dim(lax.all_gather(x, axis), root, 0, keepdims=False)


def in_blocks(x, dim, length):
    before, after = (x.shape[:dim], x.shape[dim + 1 :])
    return jnp.moveaxis(x.reshape(*before, length, -1, *after), dim, 0)


def sum_at_owner(x, axis, dim):
    length = lax.axis_size(axis)
    tiles = lax.all_to_all(in_blocks(x, dim, length), axis, 0, 0, tiled=True)
    return jnp.sum(tiles.astype(jnp.float32), axis=0)


def product_rows(left_rows, factor_rows):
    return lax.dot_general(
        left_rows, factor_rows, (((1,), (1,)), ((), ())), preferred_element_type=jnp.float32
    )


def folder(factor_block, piece):
    return product_rows(piece, factor_block)


def on_device(
    leaf_rhs, leaf_inverse, interpolation, ranks, skeleton_rows, root_rows, root_rhs, root_factor
):
    row_at = lax.axis_index("row")
    row_count = lax.axis_size("row")
    leaf_here = leaf_rhs.shape[0]
    rhs_here = leaf_rhs.shape[1]
    slot_count = skeleton_rows.shape[1]
    section = root_rhs.shape[1]
    solved = jnp.einsum("lrk,ljk->lrj", leaf_rhs, leaf_inverse, preferred_element_type=jnp.float32)
    live_slots = jnp.arange(slot_count, dtype=jnp.int32)[None, :] < ranks[:, None]
    index_table = jnp.broadcast_to(skeleton_rows[:, None, :], (leaf_here, rhs_here, slot_count))
    skeleton = jnp.where(
        live_slots[:, None, :], jnp.take_along_axis(solved, index_table, axis=2), 0.0
    )
    gathered_skel = collect(skeleton, "row", 0)
    flat_values = jnp.transpose(gathered_skel, (1, 0, 2)).reshape(rhs_here, -1)
    local_rows = root_rows.reshape(-1) - row_at * section
    inside = (local_rows >= 0) & (local_rows < section)
    target = jnp.where(inside, local_rows, section)
    assembled = root_rhs.at[:, target].add(flat_values, mode="drop")
    relaid = lax.all_to_all(root_factor, "col", split_axis=0, concat_axis=2, tiled=True)
    running = lax.all_to_all(assembled, "col", split_axis=1, concat_axis=0, tiled=True)
    for block_index in range(row_count):
        factor_block = relaid[:, block_index, :]
        arrived = from_root(running.astype(jnp.bfloat16), "row", block_index)
        update = folder(factor_block, collect(arrived, "col", 1))
        running = jnp.where(row_at > block_index, running - update, running)
    result = jnp.zeros_like(running)
    for block_index in reversed(range(row_count)):
        factor_block = relaid[:, block_index, :]
        diagonal_out = folder(factor_block, collect(running.astype(jnp.bfloat16), "col", 1))
        result = jnp.where(row_at == block_index, diagonal_out, result)
        arrived = from_root(diagonal_out.astype(jnp.bfloat16), "row", block_index)
        update = folder(factor_block, collect(arrived, "col", 1))
        running = jnp.where(row_at < block_index, running - update, running)
    root_solution = lax.all_to_all(result, "col", split_axis=0, concat_axis=1, tiled=True)
    clipped = jnp.where(inside, local_rows, 0)
    taken_all = jnp.where(inside[None, :], jnp.take(root_solution, clipped, axis=1), 0.0)
    taken_all = jnp.transpose(taken_all.reshape(rhs_here, -1, slot_count), (1, 0, 2))
    skeleton_low = sum_at_owner(taken_all.astype(jnp.bfloat16), "row", 0).astype(jnp.bfloat16)
    skeleton_solution = jnp.where(
        live_slots[:, None, :], skeleton_low, jnp.zeros_like(skeleton_low)
    )
    correction = jnp.einsum(
        "lrk,lkj->lrj", skeleton_solution, interpolation, preferred_element_type=jnp.float32
    )
    leaf_solution = solved - correction
    return (leaf_solution, root_solution)


def solution(mesh):
    in_specs = (
        P("row", "col", None),
        P("row", None, None),
        P("row", None, None),
        P("row"),
        P("row", None),
        P(),
        P("col", "row"),
        P("row", None, "col"),
    )
    out_specs = (P("row", "col", None), P("col", "row"))
    return jax.shard_map(
        on_device, mesh=mesh, in_specs=in_specs, out_specs=out_specs, check_vma=False
    )
```

profile of v0, /device:TPU:1, one launch (start us, length us, event | category | flops | bytes accessed | tf_op | source)
XLA Modules:
  0.0 715.3 jit_solution(16767967135312532196)
XLA Ops:
  33.4 13.9 %all_to_all.181 = f32[8,16,128]{2,0,1:T(8,128)S(1)} all-to-all(f32[8,16,128]{2,0,1:T(8,128)S(1)} %copy.177), channel_id=1, replica_groups=mesh['row'=8,'col'=16] {'col'}, dimensions={1} | all-to-all | bytes 131072 | tf_op jit(solution)/shard_map/all_to_all | solution.py:69
  51.9 14.8 %all_gather.88 = bf16[8,128,128]{2,1,0:T(8,128)(2,1)S(1)} all-gather(bf16[1,128,128]{2,1,0:T(8,128)(2,1)S(1)} %fusion.28), channel_id=1, replica_groups=mesh['row'=8,'col'=16] {'row'}, dimensions={0}, use_global_device_ids=true | all-gather | bytes 294912 | tf_op jit(solution)/shard_map/all_gather | solution.py:23
  66.9 36.8 %all-to-all-done.3 = bf16[2048,8,128]{2,1,0:T(8,128)(2,1)} async-done(((bf16[2048,8,128]{2,1,0:T(8,128)(2,1)}), bf16[2048,8,128]{2,1,0:T(8,128)(2,1)}, u32[]{:S(2)}, u32[]{:S(2)}) %all-to-all-start.3) | async-done | bytes 4194336 | tf_op jit(solution)/shard_map/all_to_all | solution.py:68
  120.3 18.2 %all-gather = bf16[1024,128]{1,0:T(8,128)(2,1)S(1)} all-gather(bf16[128,128]{1,0:T(8,128)(2,1)S(1)} %get-tuple-element.18), channel_id=2, replica_groups=mesh['row'=8,'col'=16] {'row'}, dimensions={0}, use_global_device_ids=true | all-gather | bytes 294912 | tf_op jit(solution)/shard_map/all_gather | solution.py:23
  143.2 10.2 %all-to-all-done.4 = bf16[16,128,128]{1,2,0:T(8,128)(2,1)S(1)} async-done(((bf16[16,128,128]{1,2,0:T(8,128)(2,1)}), bf16[16,128,128]{1,2,0:T(8,128)(2,1)S(1)}, u32[]{:S(2)}, u32[]{:S(2)}) %all-to-all-start.4) | async-done | bytes 524320 | tf_op jit(solution)/shard_map/all_to_all | solution.py:15
  154.7 14.9 %all-gather.1 = bf16[1024,128]{1,0:T(8,128)(2,1)S(1)} all-gather(bf16[128,128]{1,0:T(8,128)(2,1)S(1)} %get-tuple-element.20), channel_id=3, replica_groups=mesh['row'=8,'col'=16] {'row'}, dimensions={0}, use_global_device_ids=true | all-gather | bytes 294912 | tf_op jit(solution)/shard_map/all_gather | solution.py:23
  174.3 10.1 %all-to-all-done.5 = bf16[16,128,128]{1,2,0:T(8,128)(2,1)S(1)} async-done(((bf16[16,128,128]{1,2,0:T(8,128)(2,1)}), bf16[16,128,128]{1,2,0:T(8,128)(2,1)S(1)}, u32[]{:S(2)}, u32[]{:S(2)}) %all-to-all-start.5) | async-done | bytes 524320 | tf_op jit(solution)/shard_map/all_to_all | solution.py:15
  185.8 14.9 %all-gather.2 = bf16[1024,128]{1,0:T(8,128)(2,1)S(1)} all-gather(bf16[128,128]{1,0:T(8,128)(2,1)S(1)} %get-tuple-element.22), channel_id=4, replica_groups=mesh['row'=8,'col'=16] {'row'}, dimensions={0}, use_global_device_ids=true | all-gather | bytes 294912 | tf_op jit(solution)/shard_map/all_gather | solution.py:23
  205.4 10.1 %all-to-all-done.6 = bf16[16,128,128]{1,2,0:T(8,128)(2,1)S(1)} async-done(((bf16[16,128,128]{1,2,0:T(8,128)(2,1)}), bf16[16,128,128]{1,2,0:T(8,128)(2,1)S(1)}, u32[]{:S(2)}, u32[]{:S(2)}) %all-to-all-start.6) | async-done | bytes 524320 | tf_op jit(solution)/shard_map/all_to_all | solution.py:15
  216.9 14.9 %all-gather.3 = bf16[1024,128]{1,0:T(8,128)(2,1)S(1)} all-gather(bf16[128,128]{1,0:T(8,128)(2,1)S(1)} %get-tuple-element.24), channel_id=5, replica_groups=mesh['row'=8,'col'=16] {'row'}, dimensions={0}, use_global_device_ids=true | all-gather | bytes 294912 | tf_op jit(solution)/shard_map/all_gather | solution.py:23
  236.5 10.1 %all-to-all-done.7 = bf16[16,128,128]{1,2,0:T(8,128)(2,1)S(1)} async-done(((bf16[16,128,128]{1,2,0:T(8,128)(2,1)}), bf16[16,128,128]{1,2,0:T(8,128)(2,1)S(1)}, u32[]{:S(2)}, u32[]{:S(2)}) %all-to-all-start.7) | async-done | bytes 524320 | tf_op jit(solution)/shard_map/all_to_all | solution.py:15
  248.0 15.1 %all-gather.4 = bf16[1024,128]{1,0:T(8,128)(2,1)S(1)} all-gather(bf16[128,128]{1,0:T(8,128)(2,1)S(1)} %get-tuple-element.26), channel_id=6, replica_groups=mesh['row'=8,'col'=16] {'row'}, dimensions={0}, use_global_device_ids=true | all-gather | bytes 294912 | tf_op jit(solution)/shard_map/all_gather | solution.py:23
  279.3 14.9 %all-gather.5 = bf16[1024,128]{1,0:T(8,128)(2,1)S(1)} all-gather(bf16[128,128]{1,0:T(8,128)(2,1)S(1)} %get-tuple-element.28), channel_id=7, replica_groups=mesh['row'=8,'col'=16] {'row'}, dimensions={0}, use_global_device_ids=true | all-gather | bytes 294912 | tf_op jit(solution)/shard_map/all_gather | solution.py:23
  310.4 14.9 %all-gather.6 = bf16[1024,128]{1,0:T(8,128)(2,1)S(1)} all-gather(bf16[128,128]{1,0:T(8,128)(2,1)S(1)} %get-tuple-element.30), channel_id=8, replica_groups=mesh['row'=8,'col'=16] {'row'}, dimensions={0}, use_global_device_ids=true | all-gather | bytes 294912 | tf_op jit(solution)/shard_map/all_gather | solution.py:23
  330.0 10.1 %all-to-all-done.10 = bf16[16,128,128]{1,2,0:T(8,128)(2,1)S(1)} async-done(((bf16[16,128,128]{1,2,0:T(8,128)(2,1)}), bf16[16,128,128]{1,2,0:T(8,128)(2,1)S(1)}, u32[]{:S(2)}, u32[]{:S(2)}) %all-to-all-start.10) | async-done | bytes 524320 | tf_op jit(solution)/shard_map/all_to_all | solution.py:15
  341.8 14.1 %all_to_all.182 = bf16[16,128,128]{1,2,0:T(8,128)(2,1)S(1)} all-to-all(bf16[16,128,128]{1,2,0:T(8,128)(2,1)S(1)} %broadcast_in_dim.282), channel_id=1, replica_groups=mesh['row'=8,'col'=16] {'col'}, dimensions={0} | all-to-all | bytes 1048576 | tf_op jit(solution)/shard_map/all_to_all | solution.py:15
  357.3 15.2 %all-gather.7 = bf16[1024,128]{1,0:T(8,128)(2,1)S(1)} all-gather(bf16[128,128]{1,0:T(8,128)(2,1)S(1)} %get-tuple-element.34), channel_id=9, replica_groups=mesh['row'=8,'col'=16] {'row'}, dimensions={0}, use_global_device_ids=true | all-gather | bytes 294912 | tf_op jit(solution)/shard_map/all_gather | solution.py:23
  388.9 14.1 %all_to_all.183 = bf16[16,128,128]{1,2,0:T(8,128)(2,1)S(1)} all-to-all(bf16[16,128,128]{1,2,0:T(8,128)(2,1)S(1)} %broadcast_in_dim.285), channel_id=1, replica_groups=mesh['row'=8,'col'=16] {'col'}, dimensions={0} | all-to-all | bytes 1048576 | tf_op jit(solution)/shard_map/all_to_all | solution.py:15
  404.4 15.2 %all-gather.8 = bf16[1024,128]{1,0:T(8,128)(2,1)S(1)} all-gather(bf16[128,128]{1,0:T(8,128)(2,1)S(1)} %get-tuple-element.38), channel_id=10, replica_groups=mesh['row'=8,'col'=16] {'row'}, dimensions={0}, use_global_device_ids=true | all-gather | bytes 294912 | tf_op jit(solution)/shard_map/all_gather | solution.py:23
  436.0 14.1 %all_to_all.184 = bf16[16,128,128]{1,2,0:T(8,128)(2,1)S(1)} all-to-all(bf16[16,128,128]{1,2,0:T(8,128)(2,1)S(1)} %broadcast_in_dim.288), channel_id=1, replica_groups=mesh['row'=8,'col'=16] {'col'}, dimensions={0} | all-to-all | bytes 1048576 | tf_op jit(solution)/shard_map/all_to_all | solution.py:15
  451.6 15.2 %all-gather.9 = bf16[1024,128]{1,0:T(8,128)(2,1)S(1)} all-gather(bf16[128,128]{1,0:T(8,128)(2,1)S(1)} %get-tuple-element.42), channel_id=11, replica_groups=mesh['row'=8,'col'=16] {'row'}, dimensions={0}, use_global_device_ids=true | all-gather | bytes 294912 | tf_op jit(solution)/shard_map/all_gather | solution.py:23
  483.2 14.1 %all_to_all.185 = bf16[16,128,128]{1,2,0:T(8,128)(2,1)S(1)} all-to-all(bf16[16,128,128]{1,2,0:T(8,128)(2,1)S(1)} %broadcast_in_dim.291), channel_id=1, replica_groups=mesh['row'=8,'col'=16] {'col'}, dimensions={0} | all-to-all | bytes 1048576 | tf_op jit(solution)/shard_map/all_to_all | solution.py:15
  498.7 15.2 %all-gather.10 = bf16[1024,128]{1,0:T(8,128)(2,1)S(1)} all-gather(bf16[128,128]{1,0:T(8,128)(2,1)S(1)} %get-tuple-element.46), channel_id=12, replica_groups=mesh['row'=8,'col'=16] {'row'}, dimensions={0}, use_global_device_ids=true | all-gather | bytes 294912 | tf_op jit(solution)/shard_map/all_gather | solution.py:23
  518.6 10.1 %all-to-all-done.18 = bf16[16,128,128]{1,2,0:T(8,128)(2,1)S(1)} async-done(((bf16[16,128,128]{1,2,0:T(8,128)(2,1)}), bf16[16,128,128]{1,2,0:T(8,128)(2,1)S(1)}, u32[]{:S(2)}, u32[]{:S(2)}) %all-to-all-start.18) | async-done | bytes 524320 | tf_op jit(solution)/shard_map/all_to_all | solution.py:15
  530.3 14.1 %all_to_all.186 = bf16[16,128,128]{1,2,0:T(8,128)(2,1)S(1)} all-to-all(bf16[16,128,128]{1,2,0:T(8,128)(2,1)S(1)} %broadcast_in_dim.294), channel_id=1, replica_groups=mesh['row'=8,'col'=16] {'col'}, dimensions={0} | all-to-all | bytes 1048576 | tf_op jit(solution)/shard_map/all_to_all | solution.py:15
  545.9 15.2 %all-gather.11 = bf16[1024,128]{1,0:T(8,128)(2,1)S(1)} all-gather(bf16[128,128]{1,0:T(8,128)(2,1)S(1)} %get-tuple-element.50), channel_id=13, replica_groups=mesh['row'=8,'col'=16] {'row'}, dimensions={0}, use_global_device_ids=true | all-gather | bytes 294912 | tf_op jit(solution)/shard_map/all_gather | solution.py:23
  565.7 10.1 %all-to-all-done.20 = bf16[16,128,128]{1,2,0:T(8,128)(2,1)S(1)} async-done(((bf16[16,128,128]{1,2,0:T(8,128)(2,1)}), bf16[16,128,128]{1,2,0:T(8,128)(2,1)S(1)}, u32[]{:S(2)}, u32[]{:S(2)}) %all-to-all-start.20) | async-done | bytes 524320 | tf_op jit(solution)/shard_map/all_to_all | solution.py:15
  577.5 14.1 %all_to_all.187 = bf16[16,128,128]{1,2,0:T(8,128)(2,1)S(1)} all-to-all(bf16[16,128,128]{1,2,0:T(8,128)(2,1)S(1)} %broadcast_in_dim.297), channel_id=1, replica_groups=mesh['row'=8,'col'=16] {'col'}, dimensions={0} | all-to-all | bytes 1048576 | tf_op jit(solution)/shard_map/all_to_all | solution.py:15
  593.0 15.2 %all-gather.12 = bf16[1024,128]{1,0:T(8,128)(2,1)S(1)} all-gather(bf16[128,128]{1,0:T(8,128)(2,1)S(1)} %get-tuple-element.54), channel_id=14, replica_groups=mesh['row'=8,'col'=16] {'row'}, dimensions={0}, use_global_device_ids=true | all-gather | bytes 294912 | tf_op jit(solution)/shard_map/all_gather | solution.py:23
  612.8 10.1 %all-to-all-done.22 = bf16[16,128,128]{1,2,0:T(8,128)(2,1)S(1)} async-done(((bf16[16,128,128]{1,2,0:T(8,128)(2,1)}), bf16[16,128,128]{1,2,0:T(8,128)(2,1)S(1)}, u32[]{:S(2)}, u32[]{:S(2)}) %all-to-all-start.22) | async-done | bytes 524320 | tf_op jit(solution)/shard_map/all_to_all | solution.py:15
  624.6 14.1 %all_to_all.188 = bf16[16,128,128]{1,2,0:T(8,128)(2,1)S(1)} all-to-all(bf16[16,128,128]{1,2,0:T(8,128)(2,1)S(1)} %broadcast_in_dim.300), channel_id=1, replica_groups=mesh['row'=8,'col'=16] {'col'}, dimensions={0} | all-to-all | bytes 1048576 | tf_op jit(solution)/shard_map/all_to_all | solution.py:15
  640.1 15.2 %all-gather.13 = bf16[1024,128]{1,0:T(8,128)(2,1)S(1)} all-gather(bf16[128,128]{1,0:T(8,128)(2,1)S(1)} %get-tuple-element.58), channel_id=15, replica_groups=mesh['row'=8,'col'=16] {'row'}, dimensions={0}, use_global_device_ids=true | all-gather | bytes 294912 | tf_op jit(solution)/shard_map/all_gather | solution.py:23
  (147 shorter events, 253.2 us)
Async XLA Ops:
  0.6 713.9 %copy-start = (bf16[1,128,2048]{2,1,0:T(8,128)(2,1)S(1)}, bf16[1,128,2048]{2,1,0:T(8,128)(2,1)}, u32[]{:S(2)}) copy-start(bf16[1,128,2048]{2,1,0:T(8,128)(2,1)} %param.10) | copy-start | bytes 1572868
  2.7 5.7 copy-start.2
  8.3 13.4 %copy-start.3 = (s32[8,128]{1,0:T(8,128)S(1)}, s32[8,128]{1,0:T(8,128)}, u32[]{:S(2)}) copy-start(s32[8,128]{1,0:T(8,128)} %param.13) | copy-start | bytes 12292
  8.3 13.4 %copy-start.1 = (f32[8,2048]{1,0:T(8,128)S(1)}, f32[8,2048]{1,0:T(8,128)}, u32[]{:S(2)}) copy-start(f32[8,2048]{1,0:T(8,128)} %param.14) | copy-start | bytes 196612
  15.8 10.7 %all-to-all-start = ((f32[8,1,8,128]{3,2,1,0:T(8,128)}), f32[8,1,8,128]{3,2,1,0:T(8,128)S(1)}, u32[]{:S(2)}, u32[]{:S(2)}) async-start(f32[8,1,8,128]{3,2,1,0:T(8,128)} %broadcast_in_dim.265), calls=%async_computation | async-start | bytes 65536 | tf_op jit(solution)/shard_map/all_to_all | solution.py:15
  47.3 56.3 %all-to-all-start.3 = ((bf16[2048,8,128]{2,1,0:T(8,128)(2,1)}), bf16[2048,8,128]{2,1,0:T(8,128)(2,1)}, u32[]{:S(2)}, u32[]{:S(2)}) async-start(bf16[2048,8,128]{2,1,0:T(8,128)(2,1)} %param.15), calls=%async_computation.3 | async-start | bytes 8388608 | tf_op jit(solution)/shard_map/all_to_all | solution.py:68
  104.5 14.4 %all-to-all-start.2 = ((bf16[16,128,128]{1,2,0:T(8,128)(2,1)}), bf16[16,128,128]{1,2,0:T(8,128)(2,1)S(1)}, u32[]{:S(2)}, u32[]{:S(2)}) async-start(bf16[16,128,128]{1,2,0:T(8,128)(2,1)} %broadcast_in_dim.267), calls=%async_computation.2 | async-start | bytes 1048576 | tf_op jit(solution)/shard_map/all_to_all | solution.py:15
  139.6 13.8 %all-to-all-start.4 = ((bf16[16,128,128]{1,2,0:T(8,128)(2,1)}), bf16[16,128,128]{1,2,0:T(8,128)(2,1)S(1)}, u32[]{:S(2)}, u32[]{:S(2)}) async-start(bf16[16,128,128]{1,2,0:T(8,128)(2,1)} %broadcast_in_dim.269), calls=%async_computation.4 | async-start | bytes 1048576 | tf_op jit(solution)/shard_map/all_to_all | solution.py:15
  170.7 13.7 %all-to-all-start.5 = ((bf16[16,128,128]{1,2,0:T(8,128)(2,1)}), bf16[16,128,128]{1,2,0:T(8,128)(2,1)S(1)}, u32[]{:S(2)}, u32[]{:S(2)}) async-start(bf16[16,128,128]{1,2,0:T(8,128)(2,1)} %broadcast_in_dim.271), calls=%async_computation.5 | async-start | bytes 1048576 | tf_op jit(solution)/shard_map/all_to_all | solution.py:15
  201.8 13.7 %all-to-all-start.6 = ((bf16[16,128,128]{1,2,0:T(8,128)(2,1)}), bf16[16,128,128]{1,2,0:T(8,128)(2,1)S(1)}, u32[]{:S(2)}, u32[]{:S(2)}) async-start(bf16[16,128,128]{1,2,0:T(8,128)(2,1)} %broadcast_in_dim.273), calls=%async_computation.6 | async-start | bytes 1048576 | tf_op jit(solution)/shard_map/all_to_all | solution.py:15
  232.9 13.7 %all-to-all-start.7 = ((bf16[16,128,128]{1,2,0:T(8,128)(2,1)}), bf16[16,128,128]{1,2,0:T(8,128)(2,1)S(1)}, u32[]{:S(2)}, u32[]{:S(2)}) async-start(bf16[16,128,128]{1,2,0:T(8,128)(2,1)} %broadcast_in_dim.275), calls=%async_computation.7 | async-start | bytes 1048576 | tf_op jit(solution)/shard_map/all_to_all | solution.py:15
  264.2 13.7 %all-to-all-start.8 = ((bf16[16,128,128]{1,2,0:T(8,128)(2,1)}), bf16[16,128,128]{1,2,0:T(8,128)(2,1)S(1)}, u32[]{:S(2)}, u32[]{:S(2)}) async-start(bf16[16,128,128]{1,2,0:T(8,128)(2,1)} %broadcast_in_dim.277), calls=%async_computation.8 | async-start | bytes 1048576 | tf_op jit(solution)/shard_map/all_to_all | solution.py:15
  295.3 13.7 %all-to-all-start.9 = ((bf16[16,128,128]{1,2,0:T(8,128)(2,1)}), bf16[16,128,128]{1,2,0:T(8,128)(2,1)S(1)}, u32[]{:S(2)}, u32[]{:S(2)}) async-start(bf16[16,128,128]{1,2,0:T(8,128)(2,1)} %broadcast_in_dim.279), calls=%async_computation.9 | async-start | bytes 1048576 | tf_op jit(solution)/shard_map/all_to_all | solution.py:15
  326.4 13.7 %all-to-all-start.10 = ((bf16[16,128,128]{1,2,0:T(8,128)(2,1)}), bf16[16,128,128]{1,2,0:T(8,128)(2,1)S(1)}, u32[]{:S(2)}, u32[]{:S(2)}) async-start(bf16[16,128,128]{1,2,0:T(8,128)(2,1)} %broadcast_in_dim.281), calls=%async_computation.10 | async-start | bytes 1048576 | tf_op jit(solution)/shard_map/all_to_all | solution.py:15
  373.6 13.7 %all-to-all-start.12 = ((bf16[16,128,128]{1,2,0:T(8,128)(2,1)}), bf16[16,128,128]{1,2,0:T(8,128)(2,1)S(1)}, u32[]{:S(2)}, u32[]{:S(2)}) async-start(bf16[16,128,128]{1,2,0:T(8,128)(2,1)} %broadcast_in_dim.284), calls=%async_computation.12 | async-start | bytes 1048576 | tf_op jit(solution)/shard_map/all_to_all | solution.py:15
  420.7 13.7 %all-to-all-start.14 = ((bf16[16,128,128]{1,2,0:T(8,128)(2,1)}), bf16[16,128,128]{1,2,0:T(8,128)(2,1)S(1)}, u32[]{:S(2)}, u32[]{:S(2)}) async-start(bf16[16,128,128]{1,2,0:T(8,128)(2,1)} %broadcast_in_dim.287), calls=%async_computation.14 | async-start | bytes 1048576 | tf_op jit(solution)/shard_map/all_to_all | solution.py:15
  467.8 13.7 %all-to-all-start.16 = ((bf16[16,128,128]{1,2,0:T(8,128)(2,1)}), bf16[16,128,128]{1,2,0:T(8,128)(2,1)S(1)}, u32[]{:S(2)}, u32[]{:S(2)}) async-start(bf16[16,128,128]{1,2,0:T(8,128)(2,1)} %broadcast_in_dim.290), calls=%async_computation.16 | async-start | bytes 1048576 | tf_op jit(solution)/shard_map/all_to_all | solution.py:15
  515.0 13.7 %all-to-all-start.18 = ((bf16[16,128,128]{1,2,0:T(8,128)(2,1)}), bf16[16,128,128]{1,2,0:T(8,128)(2,1)S(1)}, u32[]{:S(2)}, u32[]{:S(2)}) async-start(bf16[16,128,128]{1,2,0:T(8,128)(2,1)} %broadcast_in_dim.293), calls=%async_computation.18 | async-start | bytes 1048576 | tf_op jit(solution)/shard_map/all_to_all | solution.py:15
  562.1 13.7 %all-to-all-start.20 = ((bf16[16,128,128]{1,2,0:T(8,128)(2,1)}), bf16[16,128,128]{1,2,0:T(8,128)(2,1)S(1)}, u32[]{:S(2)}, u32[]{:S(2)}) async-start(bf16[16,128,128]{1,2,0:T(8,128)(2,1)} %broadcast_in_dim.296), calls=%async_computation.20 | async-start | bytes 1048576 | tf_op jit(solution)/shard_map/all_to_all | solution.py:15
  609.3 13.7 %all-to-all-start.22 = ((bf16[16,128,128]{1,2,0:T(8,128)(2,1)}), bf16[16,128,128]{1,2,0:T(8,128)(2,1)S(1)}, u32[]{:S(2)}, u32[]{:S(2)}) async-start(bf16[16,128,128]{1,2,0:T(8,128)(2,1)} %broadcast_in_dim.299), calls=%async_computation.22 | async-start | bytes 1048576 | tf_op jit(solution)/shard_map/all_to_all | solution.py:15
  656.4 13.7 %all-to-all-start.24 = ((bf16[16,128,128]{1,2,0:T(8,128)(2,1)}), bf16[16,128,128]{1,2,0:T(8,128)(2,1)S(1)}, u32[]{:S(2)}, u32[]{:S(2)}) async-start(bf16[16,128,128]{1,2,0:T(8,128)(2,1)} %broadcast_in_dim.302), calls=%async_computation.24 | async-start | bytes 1048576 | tf_op jit(solution)/shard_map/all_to_all | solution.py:15
  672.6 13.5 %all-to-all-start.25 = ((bf16[16,128,128]{1,2,0:T(8,128)(2,1)}), bf16[16,128,128]{1,2,0:T(8,128)(2,1)S(1)}, u32[]{:S(2)}, u32[]{:S(2)}) async-start(bf16[16,128,128]{1,2,0:T(8,128)(2,1)} %broadcast_in_dim.303), calls=%async_computation.25 | async-start | bytes 1048576 | tf_op jit(solution)/shard_map/all_to_all | solution.py:15
  688.0 10.9 %all-to-all-start.26 = ((f32[16,8,128]{2,1,0:T(8,128)}), f32[16,8,128]{2,1,0:T(8,128)S(1)}, u32[]{:S(2)}, u32[]{:S(2)}) async-start(f32[16,8,128]{2,1,0:T(8,128)} %fusion.3), calls=%async_computation.26 | async-start | bytes 131072 | tf_op jit(solution)/shard_map/all_to_all | solution.py:83
  702.9 11.6 %all-to-all-start.27 = ((bf16[8,1,8,128]{3,2,1,0:T(8,128)(2,1)}), bf16[8,1,8,128]{3,2,1,0:T(8,128)(2,1)S(1)}, u32[]{:S(2)}, u32[]{:S(2)}) async-start(bf16[8,1,8,128]{3,2,1,0:T(8,128)(2,1)} %fusion.30), calls=%async_computation.27 | async-start | bytes 32768 | tf_op jit(solution)/shard_map/all_to_all | solution.py:33
where the time goes:
time: 719 us; the launch traced here: 715 us
  blocking collectives  342 us (48%)
  waiting for transfers between devices  205 us (29%)
  starting transfers between devices  81.6 us (11%)
  matrix products  38.9 us (5%)
  local copies, waits for them, and re-layouts  37.5 us (5%)
  other arithmetic  8.45 us (1%)
    all_gather x15, blocking collectives, from_root(): lax.all_gather(x, axis)  229 us
    all_to_all x17, waiting for transfers between devices, from_everyone(): lax.all_to_all(jnp.broadcast_to(x[None], (length, *x.shape)), axis, 0, 0,...  158 us
    all_to_all x7, blocking collectives, from_everyone(): lax.all_to_all(jnp.broadcast_to(x[None], (length, *x.shape)), axis, 0, 0,...  99 us
    all_to_all x17, starting transfers between devices, from_everyone(): lax.all_to_all(jnp.broadcast_to(x[None], (length, *x.shape)), axis, 0, 0,...  65.8 us
    all_to_all x1, waiting for transfers between devices, on_device(): lax.all_to_all(root_factor, 'col', split_axis=0, concat_axis=2, tiled=True)  36.8 us
    dot_general x23, matrix products, product_rows(): lax.dot_general(left_rows, factor_rows, (((1,), (1,)), ((), ())), preferr...  32.4 us
    broadcast_in_dim x26, local copies, waits for them, and re-layouts, from_everyone(): jnp.broadcast_to(x[None], (length, *x.shape))  16.4 us
  transfers between devices with their start and end apart: 20, of which 20 were waited for; matrix products, arithmetic and copies ran while one was open for 1% of the time, Pallas kernels for 0%

commit v1 on v0

v1 whole, which is shorter than its diff:
```python
import jax
import jax.numpy as jnp
from jax import lax
from jax.sharding import PartitionSpec as P

BF = jnp.bfloat16
F32 = jnp.float32


def dot_nt(a, b):
    return lax.dot_general(a, b, (((1,), (1,)), ((), ())), preferred_element_type=F32)


def dot_nn(a, b):
    return lax.dot_general(a, b, (((1,), (0,)), ((), ())), preferred_element_type=F32)


def exchange(x, axis):
    return lax.all_to_all(x, axis, 0, 0, tiled=True)


def split_columns(x, parts):
    rows, width = x.shape
    return jnp.transpose(x.reshape(rows, parts, width // parts), (1, 0, 2))


def on_device(
    leaf_rhs, leaf_inverse, interpolation, ranks, skeleton_rows, root_rows, root_rhs, root_factor
):
    row_at = lax.axis_index("row")
    n_row = lax.axis_size("row")
    n_col = lax.axis_size("col")
    rhs_here = leaf_rhs.shape[1]
    n_rhs = rhs_here * n_col
    slots = skeleton_rows.shape[1]
    section = root_rhs.shape[1]
    width = section // n_col
    leaf = leaf_rhs.shape[2]

    run = exchange(split_columns(root_rhs, n_col), "col").reshape(n_rhs, width)

    factor = root_factor.reshape(section, n_row * width)
    diagonal = lax.dynamic_slice_in_dim(factor, row_at * width, width, 1)
    diagonal_full = lax.all_gather(diagonal, "col", axis=1, tiled=True)
    folded = dot_nn(diagonal_full, factor).astype(BF)

    solved = dot_nt(leaf_rhs[0], leaf_inverse[0])
    live = jnp.arange(slots, dtype=jnp.int32) < ranks[0]
    chosen = jnp.where(live, skeleton_rows[0], -1)
    pick = (jnp.arange(leaf, dtype=jnp.int32)[:, None] == chosen[None, :]).astype(BF)
    skeleton = dot_nn(solved.astype(BF), pick).astype(BF)
    everyone = jnp.broadcast_to(skeleton[None], (n_row * n_col, rhs_here, slots))
    gathered = exchange(everyone, ("row", "col")).reshape(n_row, n_rhs, slots)
    gathered = jnp.transpose(gathered, (1, 0, 2)).reshape(n_rhs, n_row * slots)
    first = row_at * section + lax.axis_index("col") * width
    own_rows = first + jnp.arange(width, dtype=jnp.int32)
    place = (root_rows.reshape(-1)[:, None] == own_rows[None, :]).astype(BF)
    run = run + dot_nn(gathered, place)

    def reduce_columns(partial):
        tiles = exchange(split_columns(partial.astype(BF), n_col), "col")
        return jnp.sum(tiles.astype(F32), axis=0)

    last = n_row - 1
    low = run.astype(BF)
    known = low
    for j in range(last - 1):
        arrived = lax.ppermute(known, "row", [(j, j + 1)])
        run = run - reduce_columns(dot_nt(arrived, factor[:, : (j + 1) * width]))
        low = run.astype(BF)
        known = jnp.concatenate([arrived, low], axis=1)
    arrived = lax.ppermute(known, "row", [(last - 1, last)])
    own = dot_nt(low, diagonal)
    back = reduce_columns(own - dot_nt(arrived, folded[:, : last * width]))
    known = back.astype(BF)
    for i in reversed(range(1, last)):
        arrived = lax.ppermute(known, "row", [(i + 1, i)])
        fresh = reduce_columns(own - dot_nt(arrived, folded[:, (i + 1) * width :]))
        back = jnp.where(row_at == i, fresh, back)
        known = jnp.concatenate([fresh.astype(BF), arrived], axis=1)
    arrived = lax.ppermute(known, "row", [(1, 0)])
    partial = (own - dot_nt(arrived, folded[:, width:])).astype(BF)
    done = back.astype(BF).reshape(n_col, rhs_here, width)
    mixed = jnp.concatenate([partial.reshape(n_col, rhs_here, section), done], axis=2)
    mixed = exchange(mixed, "col")
    summed = jnp.sum(mixed[:, :, :section].astype(F32), axis=0)
    placed = jnp.transpose(mixed[:, :, section:], (1, 0, 2)).reshape(rhs_here, section)
    root_solution = jnp.where(row_at == 0, summed, placed.astype(F32))

    block_rows = row_at * section + jnp.arange(section, dtype=jnp.int32)
    take = (block_rows[:, None] == root_rows.reshape(-1)[None, :]).astype(BF)
    taken = dot_nn(root_solution.astype(BF), take).astype(BF)
    taken = exchange(split_columns(taken, n_row), "row")
    taken = jnp.sum(taken.astype(F32), axis=0)
    taken = jnp.where(live[None, :], taken, 0.0).astype(BF)
    leaf_solution = solved - dot_nn(taken, interpolation[0])
    return (leaf_solution[None], root_solution)


def solution(mesh):
    in_specs = (
        P("row", "col", None),
        P("row", None, None),
        P("row", None, None),
        P("row"),
        P("row", None),
        P(),
        P("col", "row"),
        P("row", None, "col"),
    )
    out_specs = (P("row", "col", None), P("col", "row"))
    return jax.shard_map(
        on_device, mesh=mesh, in_specs=in_specs, out_specs=out_specs, check_vma=False
    )
```

time: 719 us -> 365 us (0.51)
  blocking collectives: 342 us -> 162 us
  waiting for transfers between devices: 205 us -> 83.3 us
  starting transfers between devices: 81.6 us -> 43.8 us
  local copies, waits for them, and re-layouts: 37.5 us -> 11.3 us
  between operations: 2.03 us -> 15.5 us
    all_gather x15 -> x0, blocking collectives: 229 us -> none  [from_root(): lax.all_gather(x, axis)]
    all_to_all x20 -> x5, waiting for transfers between devices: 205 us -> 34.7 us  [exchange(): return lax.all_to_all(x, axis, 0, 0, tiled=True)]
    all_to_all x20 -> x5, starting transfers between devices: 81.6 us -> 31.6 us  [exchange(): return lax.all_to_all(x, axis, 0, 0, tiled=True)]
    all_to_all x8 -> x12, blocking collectives: 113 us -> 162 us  [exchange(): return lax.all_to_all(x, axis, 0, 0, tiled=True)]
    ppermute x0 -> x14, waiting for transfers between devices: none -> 48.6 us  [the longest x6 44.4 us: on_device(): arrived = lax.ppermute(known, 'row', [(i + 1, i)])]
    broadcast_in_dim x26 -> x1, local copies, waits for them, and re-layouts: 16.4 us -> 0.76 us  [on_device(): jnp.broadcast_to(skeleton[None], (n_row * n_col, rhs_here, slots))]
    ppermute x0 -> x14, starting transfers between devices: none -> 12.2 us  [the longest x6 5.4 us: on_device(): arrived = lax.ppermute(known, 'row', [(j, j + 1)])]
    gather x3 -> x0, local copies, waits for them, and re-layouts: 9.75 us -> none  [the longest x1 6.76 us: on_device(): jnp.take_along_axis(solved, index_table, axis=2)]
  transfers between devices with their start and end apart: 20 -> 20, of which waited for: 20 -> 8; matrix products, arithmetic and copies ran while one was open for 1% -> 10% of each run, Pallas kernels for 0% -> 0%
where the time goes in v1:
time: 365 us; the launch traced here: 363 us
  blocking collectives  162 us (44%)
  waiting for transfers between devices  83.3 us (23%)
  matrix products  44.6 us (12%)
  starting transfers between devices  43.8 us (12%)
  between operations  15.5 us (4%)
  local copies, waits for them, and re-layouts  11.3 us (3%)
    all_to_all x12, blocking collectives, exchange(): return lax.all_to_all(x, axis, 0, 0, tiled=True)  162 us
    ppermute x6, waiting for transfers between devices, on_device(): arrived = lax.ppermute(known, 'row', [(i + 1, i)])  44.4 us
    all_to_all x5, waiting for transfers between devices, exchange(): return lax.all_to_all(x, axis, 0, 0, tiled=True)  34.7 us
    all_to_all x5, starting transfers between devices, exchange(): return lax.all_to_all(x, axis, 0, 0, tiled=True)  31.6 us
    dot_general x16, matrix products, dot_nt(): lax.dot_general(a, b, (((1,), (1,)), ((), ())), preferred_element_type=F32)  28.5 us
    dot_general x5, matrix products, dot_nn(): lax.dot_general(a, b, (((1,), (0,)), ((), ())), preferred_element_type=F32)  16.1 us
  transfers between devices with their start and end apart: 20, of which 8 were waited for; matrix products, arithmetic and copies ran while one was open for 10% of the time, Pallas kernels for 0%

profile of v1, /device:TPU:1, one launch (start us, length us, event | category | flops | bytes accessed | tf_op | source)
XLA Modules:
  0.0 363.1 jit_solution(12178161248253233396)
XLA Ops:
  7.2 5.3 %copy.76 = bf16[256,8,8,128]{3,1,2,0:T(8,128)(2,1)} copy(bf16[256,8,8,128]{3,2,1,0:T(8,128)(2,1)} %bitcast.171) | data formatting | bytes 8388608
  12.6 1.9 constant_dynamic-slice_fusion
  14.5 8.4 %all-to-all-start = ((f32[16,8,128]{2,1,0:T(8,128)}), f32[16,8,128]{2,1,0:T(8,128)S(1)}, u32[]{:S(2)}, u32[]{:S(2)}) async-start(f32[16,8,128]{2,1,0:T(8,128)} %bitcast.4), calls=%async_computation | async-start | bytes 131072 | tf_op jit(solution)/shard_map/all_to_all | solution.py:19
  23.6 5.6 %fusion = f32[8,2048]{1,0:T(8,128)S(1)} fusion(bf16[1,2048,2048]{2,1,0:T(8,128)(2,1)} %param.9, bf16[1,8,2048]{2,1,0:T(8,128)(2,1)S(1)} %copy-done.4), kind=kOutput, calls=%fused_computation | convolution fusion | flops 67108864 | bytes 8486912 | tf_op jit(solution)/shard_map/dot_general | solution.py:11
  30.3 10.4 %all-to-all-start.1 = ((bf16[128,8,128]{2,1,0:T(8,128)(2,1)}), bf16[128,8,128]{2,1,0:T(8,128)(2,1)S(1)}, u32[]{:S(2)}, u32[]{:S(2)}) async-start(bf16[128,8,128]{2,1,0:T(8,128)(2,1)} %broadcast_in_dim.32), calls=%async_computation.1 | async-start | bytes 524288 | tf_op jit(solution)/shard_map/all_to_all | solution.py:19
  40.9 10.7 %all-to-all-done.1 = bf16[128,8,128]{2,1,0:T(8,128)(2,1)S(1)} async-done(((bf16[128,8,128]{2,1,0:T(8,128)(2,1)}), bf16[128,8,128]{2,1,0:T(8,128)(2,1)S(1)}, u32[]{:S(2)}, u32[]{:S(2)}) %all-to-all-start.1) | async-done | bytes 262176 | tf_op jit(solution)/shard_map/all_to_all | solution.py:19
  56.9 18.5 %all_to_all.85 = bf16[16,128,128]{2,1,0:T(8,128)(2,1)S(1)} all-to-all(bf16[16,128,128]{2,1,0:T(8,128)(2,1)S(1)} %bitcast.173), channel_id=1, replica_groups=mesh['row'=8,'col'=16] {'col'}, dimensions={0} | all-to-all | bytes 1048576 | tf_op jit(solution)/shard_map/all_to_all | solution.py:19
  80.1 17.7 %all_to_all.86 = bf16[16,128,128]{2,1,0:T(8,128)(2,1)S(1)} all-to-all(bf16[16,128,128]{2,1,0:T(8,128)(2,1)S(1)} %bitcast.174), channel_id=1, replica_groups=mesh['row'=8,'col'=16] {'col'}, dimensions={0} | all-to-all | bytes 1048576 | tf_op jit(solution)/shard_map/all_to_all | solution.py:19
  98.8 2.0 fusion.64
  101.0 16.6 %all_to_all.87 = bf16[16,128,128]{2,1,0:T(8,128)(2,1)S(1)} all-to-all(bf16[16,128,128]{2,1,0:T(8,128)(2,1)S(1)} %bitcast.175), channel_id=1, replica_groups=mesh['row'=8,'col'=16] {'col'}, dimensions={0} | all-to-all | bytes 1048576 | tf_op jit(solution)/shard_map/all_to_all | solution.py:19
  118.5 2.4 fusion.67
  121.0 12.7 %all_to_all.88 = bf16[16,128,128]{2,1,0:T(8,128)(2,1)S(1)} all-to-all(bf16[16,128,128]{2,1,0:T(8,128)(2,1)S(1)} %bitcast.176), channel_id=1, replica_groups=mesh['row'=8,'col'=16] {'col'}, dimensions={0} | all-to-all | bytes 1048576 | tf_op jit(solution)/shard_map/all_to_all | solution.py:19
  134.6 2.7 fusion.73
  137.5 12.5 %all_to_all.89 = bf16[16,128,128]{2,1,0:T(8,128)(2,1)S(1)} all-to-all(bf16[16,128,128]{2,1,0:T(8,128)(2,1)S(1)} %bitcast.177), channel_id=1, replica_groups=mesh['row'=8,'col'=16] {'col'}, dimensions={0} | all-to-all | bytes 1048576 | tf_op jit(solution)/shard_map/all_to_all | solution.py:19
  151.0 3.0 fusion.70
  154.2 12.2 %all_to_all.90 = bf16[16,128,128]{2,1,0:T(8,128)(2,1)S(1)} all-to-all(bf16[16,128,128]{2,1,0:T(8,128)(2,1)S(1)} %bitcast.178), channel_id=1, replica_groups=mesh['row'=8,'col'=16] {'col'}, dimensions={0} | all-to-all | bytes 1048576 | tf_op jit(solution)/shard_map/all_to_all | solution.py:19
  167.9 12.5 %convolution_convert_fusion = bf16[2048,1024]{1,0:T(8,128)(2,1)S(1)} fusion(bf16[2048,2048]{1,0:T(8,128)(2,1)} %all-gather.2.cloned.1.call-done, bf16[256,8,8,128]{3,2,1,0:T(8,128)(2,1)} %bitcast.172), kind=kOutput, calls=%fused_computation.7 | convolution fusion | flops 8592031744 | bytes 16777216 | tf_op jit(solution)/shard_map/dot_general | solution.py:15
  181.9 11.9 %all_to_all.91 = bf16[16,128,128]{2,1,0:T(8,128)(2,1)S(1)} all-to-all(bf16[16,128,128]{2,1,0:T(8,128)(2,1)S(1)} %bitcast.179), channel_id=1, replica_groups=mesh['row'=8,'col'=16] {'col'}, dimensions={0} | all-to-all | bytes 1048576 | tf_op jit(solution)/shard_map/all_to_all | solution.py:19
  195.0 11.9 %all_to_all.92 = bf16[16,128,128]{2,1,0:T(8,128)(2,1)S(1)} all-to-all(bf16[16,128,128]{2,1,0:T(8,128)(2,1)S(1)} %bitcast.180), channel_id=1, replica_groups=mesh['row'=8,'col'=16] {'col'}, dimensions={0} | all-to-all | bytes 1048576 | tf_op jit(solution)/shard_map/all_to_all | solution.py:19
  208.3 11.9 %all_to_all.93 = bf16[16,128,128]{2,1,0:T(8,128)(2,1)S(1)} all-to-all(bf16[16,128,128]{2,1,0:T(8,128)(2,1)S(1)} %bitcast.181), channel_id=1, replica_groups=mesh['row'=8,'col'=16] {'col'}, dimensions={0} | all-to-all | bytes 1048576 | tf_op jit(solution)/shard_map/all_to_all | solution.py:19
  221.8 11.9 %all_to_all.94 = bf16[16,128,128]{2,1,0:T(8,128)(2,1)S(1)} all-to-all(bf16[16,128,128]{2,1,0:T(8,128)(2,1)S(1)} %bitcast.182), channel_id=1, replica_groups=mesh['row'=8,'col'=16] {'col'}, dimensions={0} | all-to-all | bytes 1048576 | tf_op jit(solution)/shard_map/all_to_all | solution.py:19
  235.5 11.9 %all_to_all.95 = bf16[16,128,128]{2,1,0:T(8,128)(2,1)S(1)} all-to-all(bf16[16,128,128]{2,1,0:T(8,128)(2,1)S(1)} %bitcast.183), channel_id=1, replica_groups=mesh['row'=8,'col'=16] {'col'}, dimensions={0} | all-to-all | bytes 1048576 | tf_op jit(solution)/shard_map/all_to_all | solution.py:19
  249.4 12.6 %all_to_all.96 = bf16[16,128,128]{2,1,0:T(8,128)(2,1)S(1)} all-to-all(bf16[16,128,128]{2,1,0:T(8,128)(2,1)S(1)} %bitcast.184), channel_id=1, replica_groups=mesh['row'=8,'col'=16] {'col'}, dimensions={0} | all-to-all | bytes 1048576 | tf_op jit(solution)/shard_map/all_to_all | solution.py:19
  263.4 44.4 %collective-permute-done.12 = bf16[128,768]{1,0:T(8,128)(2,1)S(1)} collective-permute-done((bf16[128,768]{1,0:T(8,128)(2,1)S(1)}, bf16[128,768]{1,0:T(8,128)(2,1)S(1)}, u32[]{:S(2)}, u32[]{:S(2)}) %collective-permute-start.12) | collective-permute-done | bytes 196640 | tf_op jit(solution)/shard_map/ppermute | solution.py:77
  309.9 3.6 all-to-all-start.14
  313.5 8.9 %all-to-all-done.14 = bf16[16,128,128]{2,1,0:T(8,128)(2,1)S(1)} async-done(((bf16[16,128,128]{2,1,0:T(8,128)(2,1)}), bf16[16,128,128]{2,1,0:T(8,128)(2,1)S(1)}, u32[]{:S(2)}, u32[]{:S(2)}) %all-to-all-start.14) | async-done | bytes 524320 | tf_op jit(solution)/shard_map/all_to_all | solution.py:19
  324.9 3.3 fusion.52
  329.1 3.6 all-to-all-start.15
  332.7 10.4 %all-to-all-done.15 = bf16[16,8,2176]{2,1,0:T(8,128)(2,1)S(1)} async-done(((bf16[16,8,2176]{2,1,0:T(8,128)(2,1)}), bf16[16,8,2176]{2,1,0:T(8,128)(2,1)S(1)}, u32[]{:S(2)}, u32[]{:S(2)}) %all-to-all-start.15) | async-done | bytes 557088 | tf_op jit(solution)/shard_map/all_to_all | solution.py:19
  343.2 2.0 fusion.94
  345.2 5.6 %all-to-all-start.16 = ((bf16[8,8,128]{2,1,0:T(8,128)(2,1)}), bf16[8,8,128]{2,1,0:T(8,128)(2,1)S(1)}, u32[]{:S(2)}, u32[]{:S(2)}) async-start(bf16[8,8,128]{2,1,0:T(8,128)(2,1)} %fusion.94), calls=%async_computation.16 | async-start | bytes 32768 | tf_op jit(solution)/shard_map/all_to_all | solution.py:19
  350.8 4.7 %all-to-all-done.16 = bf16[8,8,128]{2,1,0:T(8,128)(2,1)S(1)} async-done(((bf16[8,8,128]{2,1,0:T(8,128)(2,1)}), bf16[8,8,128]{2,1,0:T(8,128)(2,1)S(1)}, u32[]{:S(2)}, u32[]{:S(2)}) %all-to-all-start.16) | async-done | bytes 16416 | tf_op jit(solution)/shard_map/all_to_all | solution.py:19
  (120 shorter events, 33.7 us)
Async XLA Ops:
  7.2 348.3 %copy-start = (bf16[1,128,2048]{2,1,0:T(8,128)(2,1)S(1)}, bf16[1,128,2048]{2,1,0:T(8,128)(2,1)}, u32[]{:S(2)}) copy-start(bf16[1,128,2048]{2,1,0:T(8,128)(2,1)} %param.10) | copy-start | bytes 1572868
  7.2 160.7 %all-gather.2.cloned.1.call-start = ((), (), s32[]{:S(2)}) async-start(), calls=%async_computation.17 | async-start | bytes 8912896 | tf_op jit(solution)/shard_map/all_gather | solution.py:44
  7.2 16.3 %copy-start.6 = (s32[1,128]{1,0:T(1,128)S(1)}, s32[1,128]{1,0:T(1,128)}, u32[]{:S(2)}) copy-start(s32[1,128]{1,0:T(1,128)} %param.12) | copy-start | bytes 1540
  7.2 16.3 %copy-start.4 = (bf16[1,8,2048]{2,1,0:T(8,128)(2,1)S(1)}, bf16[1,8,2048]{2,1,0:T(8,128)(2,1)}, u32[]{:S(2)}) copy-start(bf16[1,8,2048]{2,1,0:T(8,128)(2,1)} %param.8) | copy-start | bytes 98308
  14.5 15.1 %all-to-all-start = ((f32[16,8,128]{2,1,0:T(8,128)}), f32[16,8,128]{2,1,0:T(8,128)S(1)}, u32[]{:S(2)}, u32[]{:S(2)}) async-start(f32[16,8,128]{2,1,0:T(8,128)} %bitcast.4), calls=%async_computation | async-start | bytes 131072 | tf_op jit(solution)/shard_map/all_to_all | solution.py:19
  23.6 28.2 %copy-start.5 = (s32[8,128]{1,0:T(8,128)S(1)}, s32[8,128]{1,0:T(8,128)}, u32[]{:S(2)}) copy-start(s32[8,128]{1,0:T(8,128)} %param.13) | copy-start | bytes 12292
  30.3 21.3 %all-to-all-start.1 = ((bf16[128,8,128]{2,1,0:T(8,128)(2,1)}), bf16[128,8,128]{2,1,0:T(8,128)(2,1)S(1)}, u32[]{:S(2)}, u32[]{:S(2)}) async-start(bf16[128,8,128]{2,1,0:T(8,128)(2,1)} %broadcast_in_dim.32), calls=%async_computation.1 | async-start | bytes 524288 | tf_op jit(solution)/shard_map/all_to_all | solution.py:19
  52.3 3.1 collective-permute-start
  75.6 2.6 collective-permute-start.1
  98.1 0.7 collective-permute-start.2
  117.8 0.7 collective-permute-start.3
  133.9 0.7 collective-permute-start.4
  150.2 17.4 %copy-start.2 = (bf16[2048,128]{1,0:T(8,128)(2,1)S(1)}, bf16[2048,128]{1,0:T(8,128)(2,1)}, u32[]{:S(2)}) copy-start(bf16[2048,128]{1,0:T(8,128)(2,1)} %constant_dynamic-slice_fusion) | copy-start | bytes 1572868
  150.2 0.8 collective-permute-start.5
  166.7 13.7 %collective-permute-start.6 = (bf16[128,896]{0,1:T(8,128)(2,1)S(1)}, bf16[128,896]{0,1:T(8,128)(2,1)S(1)}, u32[]{:S(2)}, u32[]{:S(2)}) collective-permute-start(bf16[128,896]{0,1:T(8,128)(2,1)S(1)} %pad_maximum_fusion.1), channel_id=1, source_target_pairs={{96,112},{97,113},{98,114},{99,115},{100,116},{101,117},{102,118},... | collective-permute-start | bytes 688136 | tf_op jit(solution)/shard_map/ppermute | solution.py:72
  180.4 127.4 %copy-start.1 = (bf16[2048,1024]{1,0:T(8,128)(2,1)}, bf16[2048,1024]{1,0:T(8,128)(2,1)S(1)}, u32[]{:S(2)}) copy-start(bf16[2048,1024]{1,0:T(8,128)(2,1)S(1)} %convolution_convert_fusion) | copy-start | bytes 12582916
  193.9 0.7 collective-permute-start.7
  207.0 0.7 collective-permute-start.8
  220.4 0.7 collective-permute-start.9
  233.9 0.7 collective-permute-start.10
  247.5 0.7 collective-permute-start.11
  262.1 45.7 %collective-permute-start.12 = (bf16[128,768]{1,0:T(8,128)(2,1)S(1)}, bf16[128,768]{1,0:T(8,128)(2,1)S(1)}, u32[]{:S(2)}, u32[]{:S(2)}) collective-permute-start(bf16[128,768]{1,0:T(8,128)(2,1)S(1)} %pad_maximum_fusion.4), channel_id=1, source_target_pairs={{32,16},{33,17},{34,18},{35,19},{36,20},{37,21},{38,22},{39,23},{4... | collective-permute-start | bytes 589832 | tf_op jit(solution)/shard_map/ppermute | solution.py:77
  309.9 12.5 %all-to-all-start.14 = ((bf16[16,128,128]{2,1,0:T(8,128)(2,1)}), bf16[16,128,128]{2,1,0:T(8,128)(2,1)S(1)}, u32[]{:S(2)}, u32[]{:S(2)}) async-start(bf16[16,128,128]{2,1,0:T(8,128)(2,1)} %bitcast.137), calls=%async_computation.14 | async-start | bytes 1048576 | tf_op jit(solution)/shard_map/all_to_all | solution.py:19
  322.5 2.4 collective-permute-start.13
  329.1 14.0 %all-to-all-start.15 = ((bf16[16,8,2176]{2,1,0:T(8,128)(2,1)}), bf16[16,8,2176]{2,1,0:T(8,128)(2,1)S(1)}, u32[]{:S(2)}, u32[]{:S(2)}) async-start(bf16[16,8,2176]{2,1,0:T(8,128)(2,1)} %pad_maximum_fusion), calls=%async_computation.15 | async-start | bytes 1114112 | tf_op jit(solution)/shard_map/all_to_all | solution.py:19
  343.1 13.1 %copy-start.3 = (f32[8,2048]{1,0:T(8,128)}, f32[8,2048]{1,0:T(8,128)S(1)}, u32[]{:S(2)}) copy-start(f32[8,2048]{1,0:T(8,128)S(1)} %bitcast_select_fusion) | copy-start | bytes 196612
  345.2 10.3 %all-to-all-start.16 = ((bf16[8,8,128]{2,1,0:T(8,128)(2,1)}), bf16[8,8,128]{2,1,0:T(8,128)(2,1)S(1)}, u32[]{:S(2)}, u32[]{:S(2)}) async-start(bf16[8,8,128]{2,1,0:T(8,128)(2,1)} %fusion.94), calls=%async_computation.16 | async-start | bytes 32768 | tf_op jit(solution)/shard_map/all_to_all | solution.py:19
Sparse Core Ops, SparseCore 0:
  14.6 91.6 all-gather.1

commit v2 on v1

--- a/solution.py
+++ b/solution.py
@@ -39,16 +39,18 @@
 
     run = exchange(split_columns(root_rhs, n_col), "col").reshape(n_rhs, width)
 
+    solved = dot_nt(leaf_rhs[0], leaf_inverse[0])
+    live = jnp.arange(slots, dtype=jnp.int32) < ranks[0]
+    chosen = jnp.where(live, skeleton_rows[0], -1)
+    pick = (jnp.arange(leaf, dtype=jnp.int32)[:, None] == chosen[None, :]).astype(BF)
+    skeleton = dot_nn(solved.astype(BF), pick).astype(BF)
+
+    root_factor, skeleton = lax.optimization_barrier((root_factor, skeleton))
     factor = root_factor.reshape(section, n_row * width)
     diagonal = lax.dynamic_slice_in_dim(factor, row_at * width, width, 1)
     diagonal_full = lax.all_gather(diagonal, "col", axis=1, tiled=True)
     folded = dot_nn(diagonal_full, factor).astype(BF)
 
-    solved = dot_nt(leaf_rhs[0], leaf_inverse[0])
-    live = jnp.arange(slots, dtype=jnp.int32) < ranks[0]
-    chosen = jnp.where(live, skeleton_rows[0], -1)
-    pick = (jnp.arange(leaf, dtype=jnp.int32)[:, None] == chosen[None, :]).astype(BF)
-    skeleton = dot_nn(solved.astype(BF), pick).astype(BF)
     everyone = jnp.broadcast_to(skeleton[None], (n_row * n_col, rhs_here, slots))
     gathered = exchange(everyone, ("row", "col")).reshape(n_row, n_rhs, slots)
     gathered = jnp.transpose(gathered, (1, 0, 2)).reshape(n_rhs, n_row * slots)
@@ -61,31 +63,50 @@
         tiles = exchange(split_columns(partial.astype(BF), n_col), "col")
         return jnp.sum(tiles.astype(F32), axis=0)
 
+    def on_turn(turn, step, old, *operands):
+        return lax.cond(row_at == turn, step, lambda old, *rest: old, old, *operands)
+
     last = n_row - 1
-    low = run.astype(BF)
-    known = low
+    known = run.astype(BF)
     for j in range(last - 1):
         arrived = lax.ppermute(known, "row", [(j, j + 1)])
-        run = run - reduce_columns(dot_nt(arrived, factor[:, : (j + 1) * width]))
-        low = run.astype(BF)
-        known = jnp.concatenate([arrived, low], axis=1)
+
+        def forward(run, arrived, factor, j=j):
+            return run - reduce_columns(dot_nt(arrived, factor[:, : (j + 1) * width]))
+
+        run = on_turn(j + 1, forward, run, arrived, factor)
+        known = jnp.concatenate([arrived, run.astype(BF)], axis=1)
     arrived = lax.ppermute(known, "row", [(last - 1, last)])
-    own = dot_nt(low, diagonal)
-    back = reduce_columns(own - dot_nt(arrived, folded[:, : last * width]))
-    known = back.astype(BF)
+
+    def turn_round(run, arrived, diagonal, folded):
+        return reduce_columns(
+            dot_nt(run.astype(BF), diagonal) - dot_nt(arrived, folded[:, : last * width])
+        )
+
+    run = on_turn(last, turn_round, run, arrived, diagonal, folded)
+    known = run.astype(BF)
     for i in reversed(range(1, last)):
         arrived = lax.ppermute(known, "row", [(i + 1, i)])
-        fresh = reduce_columns(own - dot_nt(arrived, folded[:, (i + 1) * width :]))
-        back = jnp.where(row_at == i, fresh, back)
-        known = jnp.concatenate([fresh.astype(BF), arrived], axis=1)
+
+        def backward(run, arrived, diagonal, folded, i=i):
+            return reduce_columns(
+                dot_nt(run.astype(BF), diagonal) - dot_nt(arrived, folded[:, (i + 1) * width :])
+            )
+
+        run = on_turn(i, backward, run, arrived, diagonal, folded)
+        known = jnp.concatenate([run.astype(BF), arrived], axis=1)
     arrived = lax.ppermute(known, "row", [(1, 0)])
-    partial = (own - dot_nt(arrived, folded[:, width:])).astype(BF)
-    done = back.astype(BF).reshape(n_col, rhs_here, width)
-    mixed = jnp.concatenate([partial.reshape(n_col, rhs_here, section), done], axis=2)
-    mixed = exchange(mixed, "col")
-    summed = jnp.sum(mixed[:, :, :section].astype(F32), axis=0)
-    placed = jnp.transpose(mixed[:, :, section:], (1, 0, 2)).reshape(rhs_here, section)
-    root_solution = jnp.where(row_at == 0, summed, placed.astype(F32))
+
+    def gather_rhs(run, arrived, diagonal, folded):
+        done = exchange(run.astype(BF).reshape(n_col, rhs_here, width), "col")
+        return jnp.transpose(done, (1, 0, 2)).reshape(rhs_here, section).astype(F32)
+
+    def finish(run, arrived, diagonal, folded):
+        partial = dot_nt(run.astype(BF), diagonal) - dot_nt(arrived, folded[:, width:])
+        tiles = exchange(partial.astype(BF).reshape(n_col, rhs_here, section), "col")
+        return jnp.sum(tiles.astype(F32), axis=0)
+
+    root_solution = lax.cond(row_at == 0, finish, gather_rhs, run, arrived, diagonal, folded)
 
     block_rows = row_at * section + jnp.arange(section, dtype=jnp.int32)
     take = (block_rows[:, None] == root_rows.reshape(-1)[None, :]).astype(BF)

time: 365 us -> 350 us (0.959)
  waiting for transfers between devices: 83.3 us -> 223 us
  blocking collectives: 162 us -> 36.9 us
  matrix products: 44.6 us -> 27.8 us
  local copies, waits for them, and re-layouts: 11.3 us -> 6.16 us
  starting transfers between devices: 43.8 us -> 39.7 us
    ppermute x6, waiting for transfers between devices: 44.4 us -> 173 us  [on_device(): arrived = lax.ppermute(known, 'row', [(i + 1, i)])]
    all_to_all x12 -> x3, blocking collectives: 162 us -> 36.9 us  [exchange(): return lax.all_to_all(x, axis, 0, 0, tiled=True)]
    all_gather x1, waiting for transfers between devices: 0.02 us -> 21.7 us  [on_device(): diagonal_full = lax.all_gather(diagonal, 'col', axis=1, tiled=True)]
    dot_general x16 -> x4, matrix products: 28.5 us -> 10.5 us  [dot_nt(): lax.dot_general(a, b, (((1,), (1,)), ((), ())), preferred_element_type=F32)]
    all_to_all x5 -> x3, waiting for transfers between devices: 34.7 us -> 22.3 us  [exchange(): return lax.all_to_all(x, axis, 0, 0, tiled=True)]
    all_to_all x5 -> x3, starting transfers between devices: 31.6 us -> 27.5 us  [exchange(): return lax.all_to_all(x, axis, 0, 0, tiled=True)]
  transfers between devices with their start and end apart: 20 -> 18, of which waited for: 8 -> 8; matrix products, arithmetic and copies ran while one was open for 10% -> 5% of each run, Pallas kernels for 0% -> 0%
where the time goes in v2:
time: 350 us
  waiting for transfers between devices  223 us (64%)
  starting transfers between devices  39.7 us (11%)
  blocking collectives  36.9 us (11%)
  matrix products  27.8 us (8%)
  between operations  15.3 us (4%)
  local copies, waits for them, and re-layouts  6.16 us (2%)
    ppermute x6, waiting for transfers between devices, on_device(): arrived = lax.ppermute(known, 'row', [(i + 1, i)])  173 us
    all_to_all x3, blocking collectives, exchange(): return lax.all_to_all(x, axis, 0, 0, tiled=True)  36.9 us
    all_to_all x3, starting transfers between devices, exchange(): return lax.all_to_all(x, axis, 0, 0, tiled=True)  27.5 us
    all_to_all x3, waiting for transfers between devices, exchange(): return lax.all_to_all(x, axis, 0, 0, tiled=True)  22.3 us
    all_gather x1, waiting for transfers between devices, on_device(): diagonal_full = lax.all_gather(diagonal, 'col', axis=1, tiled=True)  21.7 us
    dot_general x5, matrix products, dot_nn(): lax.dot_general(a, b, (((1,), (0,)), ((), ())), preferred_element_type=F32)  17.3 us
    dot_general x4, matrix products, dot_nt(): lax.dot_general(a, b, (((1,), (1,)), ((), ())), preferred_element_type=F32)  10.5 us
  transfers between devices with their start and end apart: 18, of which 8 were waited for; matrix products, arithmetic and copies ran while one was open for 5% of the time, Pallas kernels for 0%

profile of v2, /device:TPU:1, one launch (start us, length us, event | category | flops | bytes accessed | tf_op | source)
XLA Modules:
  0.0 349.8 jit_solution(922826265448574156)
XLA Ops:
  7.9 5.8 %fusion.104 = f32[8,2048]{1,0:T(8,128)S(1)} fusion(bf16[1,2048,2048]{2,1,0:T(8,128)(2,1)} %param.37, bf16[1,8,2048]{2,1,0:T(8,128)(2,1)} %param.36), kind=kOutput, calls=%fused_computation.100 | convolution fusion | flops 67108864 | bytes 8486912 | tf_op jit(solution)/shard_map/dot_general | solution.py:11
  14.1 3.1 copy.67
  17.2 1.9 constant_dynamic-slice_fusion
  19.1 0.8 broadcast_in_dim.32
  19.8 11.5 %all-to-all-start.16 = ((bf16[128,8,128]{2,1,0:T(8,128)(2,1)}), bf16[128,8,128]{2,1,0:T(8,128)(2,1)S(1)}, u32[]{:S(2)}, u32[]{:S(2)}) async-start(bf16[128,8,128]{2,1,0:T(8,128)(2,1)} %broadcast_in_dim.32), calls=%async_computation.16 | async-start | bytes 524288 | tf_op jit(solution)/shard_map/all_to_all | solution.py:19
  31.3 11.3 %all-to-all-done.16 = bf16[128,8,128]{2,1,0:T(8,128)(2,1)S(1)} async-done(((bf16[128,8,128]{2,1,0:T(8,128)(2,1)}), bf16[128,8,128]{2,1,0:T(8,128)(2,1)S(1)}, u32[]{:S(2)}, u32[]{:S(2)}) %all-to-all-start.16) | async-done | bytes 262176 | tf_op jit(solution)/shard_map/all_to_all | solution.py:19
  42.6 4.0 %all-to-all-start.15 = ((f32[16,8,128]{2,1,0:T(8,128)}), f32[16,8,128]{2,1,0:T(8,128)S(1)}, u32[]{:S(2)}, u32[]{:S(2)}) async-start(f32[16,8,128]{2,1,0:T(8,128)} %bitcast.21), calls=%async_computation.15 | async-start | bytes 131072 | tf_op jit(solution)/shard_map/all_to_all | solution.py:19
  46.8 6.3 %all-to-all-done.15 = f32[16,8,128]{2,1,0:T(8,128)S(1)} async-done(((f32[16,8,128]{2,1,0:T(8,128)}), f32[16,8,128]{2,1,0:T(8,128)S(1)}, u32[]{:S(2)}, u32[]{:S(2)}) %all-to-all-start.15) | async-done | bytes 65568 | tf_op jit(solution)/shard_map/all_to_all | solution.py:19
  53.6 1.3 collective-permute-start
  54.9 3.2 collective-permute-done
  58.0 17.1 %conditional.14 = (f32[128,128]{1,0:T(8,128)S(1)}) conditional(s32[]{:T(128)} %convert_element_type.213, f32[128,128]{1,0:T(8,128)S(1)} %get-tuple-element.216, (bf16[2048,1024]{1,0:T(8,128)(2,1)}, bf16[128,128]{1,0:T(8,128)(2,1)S(1)}, f32[128,128]{1,0:T(8,128)S(1)}) %tuple.152), branch_computations={%region_0.1_spmd, %region_1.3_spmd} | conditional | flops 67895296 | bytes 3964936 | solution.py:67
  58.0 1.3 fusion
  59.5 15.6 %all_to_all.75 = bf16[16,128,128]{2,1,0:T(8,128)(2,1)S(1)} all-to-all(bf16[16,128,128]{2,1,0:T(8,128)(2,1)S(1)} %bitcast.181), channel_id=1, replica_groups=mesh['row'=8,'col'=16] {'col'}, dimensions={0} | all-to-all | bytes 1048576 | tf_op jit(solution)/shard_map/cond/branch_1_fun/all_to_all | solution.py:19
  75.2 1.3 collective-permute-start.1
  76.5 1.3 collective-permute-done.1
  80.1 0.7 collective-permute-start.5
  80.9 1.0 collective-permute-start.6
  81.8 21.7 %all-gather.2.cloned.1.call-done = bf16[2048,2048]{1,0:T(8,128)(2,1)} async-done(((bf16[2048,128]{1,0:T(8,128)(2,1)}), bf16[2048,2048]{1,0:T(8,128)(2,1)}) %all-gather.2.cloned.1.call-update) | async-done | bytes 8388624 | tf_op jit(solution)/shard_map/all_gather | solution.py:51
  103.6 13.8 %convolution_convert_fusion.4 = bf16[2048,1024]{1,0:T(8,128)(2,1)} fusion(bf16[2048,2048]{1,0:T(8,128)(2,1)} %all-gather.2.cloned.1.call-done, bf16[256,8,8,128]{3,2,1,0:T(8,128)(2,1)} %bitcast.179), kind=kOutput, calls=%fused_computation.107 | convolution fusion | flops 8592031744 | bytes 16777216 | tf_op jit(solution)/shard_map/dot_general | solution.py:15
  121.1 1.3 collective-permute-start.12
  122.4 173.0 %collective-permute-done.12 = bf16[128,768]{1,0:T(8,128)(2,1)S(1)} collective-permute-done((bf16[128,768]{1,0:T(8,128)(2,1)S(1)}, bf16[128,768]{1,0:T(8,128)(2,1)S(1)}, u32[]{:S(2)}, u32[]{:S(2)}) %collective-permute-start.12) | collective-permute-done | bytes 196640 | tf_op jit(solution)/shard_map/ppermute | solution.py:89
  295.4 15.5 %conditional.26 = (f32[128,128]{1,0:T(8,128)S(1)}) conditional(s32[]{:T(128)} %convert_element_type.213, f32[128,128]{1,0:T(8,128)S(1)} %get-tuple-element.232, (f32[128,128]{1,0:T(8,128)S(1)}, bf16[2048,128]{1,0:T(8,128)(2,1)S(1)}, bf16[2048,1024]{1,0:T(8,128)(2,1)}, bf16[128,768]{1,0:T(8,128)(2,1)S(1)}) %tuple.150), branch_computations={%region_36.37_spmd, %region_37.39_spmd} | conditional | flops 470810624 | bytes 9240584 | solution.py:67
  295.7 3.0 fusion.86
  298.9 11.9 %all_to_all.87 = bf16[16,128,128]{2,1,0:T(8,128)(2,1)S(1)} all-to-all(bf16[16,128,128]{2,1,0:T(8,128)(2,1)S(1)} %bitcast.193), channel_id=1, replica_groups=mesh['row'=8,'col'=16] {'col'}, dimensions={0} | all-to-all | bytes 1048576 | tf_op jit(solution)/shard_map/cond/branch_1_fun/all_to_all | solution.py:19
  310.9 1.3 collective-permute-start.13
  312.3 1.1 collective-permute-done.13
  313.3 10.1 %conditional.27 = (f32[8,2048]{1,0:T(8,128)}, bf16[8,2048]{1,0:T(8,128)(2,1)S(1)}) conditional(s32[]{:T(128)} %convert_element_type.212, f32[128,128]{1,0:T(8,128)S(1)} %get-tuple-element.233, (f32[128,128]{1,0:T(8,128)S(1)}, bf16[2048,128]{1,0:T(8,128)(2,1)S(1)}, bf16[2048,1024]{1,0:T(8,128)(2,1)}, bf16[128,896]{1,0:T(8,128)(2,1)S(1)}) %tuple.151), branch_computations={%region_39.40_spmd, %region_40.42_spmd} | conditional | flops 537935872 | bytes 8847376 | solution.py:109
  313.3 9.4 %all_to_all.88 = bf16[16,8,128]{2,1,0:T(8,128)(2,1)S(1)} all-to-all(bf16[16,8,128]{2,1,0:T(8,128)(2,1)S(1)} %convert_bitcast_fusion), channel_id=1, replica_groups=mesh['row'=8,'col'=16] {'col'}, dimensions={0} | all-to-all | bytes 65536 | tf_op jit(solution)/shard_map/cond/branch_0_fun/all_to_all | solution.py:19
  323.4 2.0 fusion.114
  325.4 12.1 %all-to-all-start.17 = ((bf16[8,8,128]{2,1,0:T(8,128)(2,1)}), bf16[8,8,128]{2,1,0:T(8,128)(2,1)S(1)}, u32[]{:S(2)}, u32[]{:S(2)}) async-start(bf16[8,8,128]{2,1,0:T(8,128)(2,1)} %fusion.114), calls=%async_computation.17 | async-start | bytes 32768 | tf_op jit(solution)/shard_map/all_to_all | solution.py:19
  337.5 4.7 %all-to-all-done.17 = bf16[8,8,128]{2,1,0:T(8,128)(2,1)S(1)} async-done(((bf16[8,8,128]{2,1,0:T(8,128)(2,1)}), bf16[8,8,128]{2,1,0:T(8,128)(2,1)S(1)}, u32[]{:S(2)}, u32[]{:S(2)}) %all-to-all-start.17) | async-done | bytes 16416 | tf_op jit(solution)/shard_map/all_to_all | solution.py:19
  342.2 0.8 fusion.110
  (82 shorter events, 8.1 us)
Async XLA Ops:
  7.2 335.0 %copy-start = (bf16[1,128,2048]{2,1,0:T(8,128)(2,1)S(1)}, bf16[1,128,2048]{2,1,0:T(8,128)(2,1)}, u32[]{:S(2)}) copy-start(bf16[1,128,2048]{2,1,0:T(8,128)(2,1)} %param.38) | copy-start | bytes 1572868
  7.2 96.4 %all-gather.2.cloned.1.call-start = ((), (), s32[]{:S(2)}) async-start(), calls=%async_computation.18 | async-start | bytes 8912896 | tf_op jit(solution)/shard_map/all_gather | solution.py:51
  7.9 5.8 %copy-start.4 = (s32[1,128]{1,0:T(1,128)S(1)}, s32[1,128]{1,0:T(1,128)}, u32[]{:S(2)}) copy-start(s32[1,128]{1,0:T(1,128)} %param.40) | copy-start | bytes 1540
  7.9 6.2 %copy-start.2 = (bf16[2048,8,128]{2,1,0:T(8,128)(2,1)S(1)}, bf16[2048,8,128]{2,1,0:T(8,128)(2,1)}, u32[]{:S(2)}) copy-start(bf16[2048,8,128]{2,1,0:T(8,128)(2,1)} %param.43) | copy-start | bytes 12582916
  14.1 39.0 %copy-start.3 = (s32[8,128]{1,0:T(8,128)S(1)}, s32[8,128]{1,0:T(8,128)}, u32[]{:S(2)}) copy-start(s32[8,128]{1,0:T(8,128)} %param.41) | copy-start | bytes 12292
  19.8 22.8 %all-to-all-start.16 = ((bf16[128,8,128]{2,1,0:T(8,128)(2,1)}), bf16[128,8,128]{2,1,0:T(8,128)(2,1)S(1)}, u32[]{:S(2)}, u32[]{:S(2)}) async-start(bf16[128,8,128]{2,1,0:T(8,128)(2,1)} %broadcast_in_dim.32), calls=%async_computation.16 | async-start | bytes 524288 | tf_op jit(solution)/shard_map/all_to_all | solution.py:19
  42.6 10.5 %all-to-all-start.15 = ((f32[16,8,128]{2,1,0:T(8,128)}), f32[16,8,128]{2,1,0:T(8,128)S(1)}, u32[]{:S(2)}, u32[]{:S(2)}) async-start(f32[16,8,128]{2,1,0:T(8,128)} %bitcast.21), calls=%async_computation.15 | async-start | bytes 131072 | tf_op jit(solution)/shard_map/all_to_all | solution.py:19
  53.6 4.5 %collective-permute-start = (bf16[128,128]{1,0:T(8,128)(2,1)S(1)}, bf16[128,128]{1,0:T(8,128)(2,1)S(1)}, u32[]{:S(2)}, u32[]{:S(2)}) collective-permute-start(bf16[128,128]{1,0:T(8,128)(2,1)S(1)} %get-tuple-element.215), channel_id=1, source_target_pairs={{0,16},{1,17},{2,18},{3,19},{4,20},{5,21},{6,22},{7,23},{8,24},{9,... | collective-permute-start | bytes 98312 | tf_op jit(solution)/shard_map/ppermute | solution.py:72
  75.2 2.6 collective-permute-start.1
  77.8 0.7 collective-permute-start.2
  78.6 0.7 collective-permute-start.3
  79.3 0.7 collective-permute-start.4
  80.1 0.7 collective-permute-start.5
  80.8 36.5 %copy-start.1 = (bf16[2048,128]{1,0:T(8,128)(2,1)S(1)}, bf16[2048,128]{1,0:T(8,128)(2,1)}, u32[]{:S(2)}) copy-start(bf16[2048,128]{1,0:T(8,128)(2,1)} %constant_dynamic-slice_fusion) | copy-start | bytes 1572868
  80.9 36.5 %collective-permute-start.6 = (bf16[128,896]{1,0:T(8,128)(2,1)S(1)}, bf16[128,896]{1,0:T(8,128)(2,1)S(1)}, u32[]{:S(2)}, u32[]{:S(2)}) collective-permute-start(bf16[128,896]{1,0:T(8,128)(2,1)S(1)} %pad_maximum_fusion), channel_id=1, source_target_pairs={{96,112},{97,113},{98,114},{99,115},{100,116},{101,117},{102,118},... | collective-permute-start | bytes 688136 | tf_op jit(solution)/shard_map/ppermute | solution.py:79
  117.4 0.7 collective-permute-start.7
  118.1 0.7 collective-permute-start.8
  118.9 0.7 collective-permute-start.9
  119.6 0.7 collective-permute-start.10
  120.3 0.7 collective-permute-start.11
  121.1 174.3 %collective-permute-start.12 = (bf16[128,768]{1,0:T(8,128)(2,1)S(1)}, bf16[128,768]{1,0:T(8,128)(2,1)S(1)}, u32[]{:S(2)}, u32[]{:S(2)}) collective-permute-start(bf16[128,768]{1,0:T(8,128)(2,1)S(1)} %pad_maximum_fusion.3), channel_id=1, source_target_pairs={{32,16},{33,17},{34,18},{35,19},{36,20},{37,21},{38,22},{39,23},{4... | collective-permute-start | bytes 589832 | tf_op jit(solution)/shard_map/ppermute | solution.py:89
  310.9 2.4 collective-permute-start.13
  325.4 16.7 %all-to-all-start.17 = ((bf16[8,8,128]{2,1,0:T(8,128)(2,1)}), bf16[8,8,128]{2,1,0:T(8,128)(2,1)S(1)}, u32[]{:S(2)}, u32[]{:S(2)}) async-start(bf16[8,8,128]{2,1,0:T(8,128)(2,1)} %fusion.114), calls=%async_computation.17 | async-start | bytes 32768 | tf_op jit(solution)/shard_map/all_to_all | solution.py:19
Sparse Core Ops, SparseCore 0:
  19.2 84.3 all-gather.1

commit v3 on v2

--- a/solution.py
+++ b/solution.py
@@ -34,8 +34,12 @@
     n_rhs = rhs_here * n_col
     slots = skeleton_rows.shape[1]
     section = root_rhs.shape[1]
+    half = section // 2
     width = section // n_col
     leaf = leaf_rhs.shape[2]
+    even = row_at % 2 == 0
+    up = [(r, r + 1) for r in range(0, n_row, 2)]
+    down = [(r + 1, r) for r in range(0, n_row, 2)]
 
     run = exchange(split_columns(root_rhs, n_col), "col").reshape(n_rhs, width)
 
@@ -45,12 +49,15 @@
     pick = (jnp.arange(leaf, dtype=jnp.int32)[:, None] == chosen[None, :]).astype(BF)
     skeleton = dot_nn(solved.astype(BF), pick).astype(BF)
 
-    root_factor, skeleton = lax.optimization_barrier((root_factor, skeleton))
-    factor = root_factor.reshape(section, n_row * width)
-    diagonal = lax.dynamic_slice_in_dim(factor, row_at * width, width, 1)
-    diagonal_full = lax.all_gather(diagonal, "col", axis=1, tiled=True)
-    folded = dot_nn(diagonal_full, factor).astype(BF)
-
+    diagonal = lax.dynamic_index_in_dim(root_factor, row_at, 1, keepdims=False)
+    above = lax.dynamic_index_in_dim(root_factor, row_at | 1, 1, keepdims=False)
+    lower = lax.ppermute(above[half:], "row", up)
+    above = jnp.where(even, above[:half], lower)
+    whole = lax.all_gather(
+        jnp.concatenate([diagonal, above], axis=0), "col", axis=1, tiled=True
+    )
+
+    skeleton, run, root_factor = lax.optimization_barrier((skeleton, run, root_factor))
     everyone = jnp.broadcast_to(skeleton[None], (n_row * n_col, rhs_here, slots))
     gathered = exchange(everyone, ("row", "col")).reshape(n_row, n_rhs, slots)
     gathered = jnp.transpose(gathered, (1, 0, 2)).reshape(n_rhs, n_row * slots)
@@ -59,14 +66,17 @@
     place = (root_rows.reshape(-1)[:, None] == own_rows[None, :]).astype(BF)
     run = run + dot_nn(gathered, place)
 
+    factor = root_factor.reshape(section, n_row * width)
+
+    last = n_row - 1
+
     def reduce_columns(partial):
         tiles = exchange(split_columns(partial.astype(BF), n_col), "col")
         return jnp.sum(tiles.astype(F32), axis=0)
 
     def on_turn(turn, step, old, *operands):
-        return lax.cond(row_at == turn, step, lambda old, *rest: old, old, *operands)
-
-    last = n_row - 1
+        return lax.cond(turn, step, lambda old, *rest: old, old, *operands)
+
     known = run.astype(BF)
     for j in range(last - 1):
         arrived = lax.ppermute(known, "row", [(j, j + 1)])
@@ -74,39 +84,100 @@
         def forward(run, arrived, factor, j=j):
             return run - reduce_columns(dot_nt(arrived, factor[:, : (j + 1) * width]))
 
-        run = on_turn(j + 1, forward, run, arrived, factor)
+        run = on_turn(row_at == j + 1, forward, run, arrived, factor)
         known = jnp.concatenate([arrived, run.astype(BF)], axis=1)
+        if j == last - 4:
+            held, _ = lax.optimization_barrier((factor, known))
+            folded = dot_nn(whole[:section], held).astype(BF)
+
+    def merge_pair(folded, whole, factor):
+        odd_part = lax.ppermute(factor, "row", down[:-1])
+        odd_part = jnp.where(even, odd_part, factor)
+        through = dot_nn(whole[section:], odd_part).astype(BF)
+        through = jnp.concatenate([through, lax.ppermute(through, "row", down[:-1])], axis=0)
+
+        def merge_even(folded, whole, through):
+            passed = dot_nn(whole[:section], through)
+            later = jnp.arange(n_row * width, dtype=jnp.int32) // width > row_at + 1
+            return jnp.where(later[None, :], folded.astype(F32) - passed, passed).astype(BF)
+
+        return lax.cond(
+            even, merge_even, lambda folded, *rest: folded, folded, whole, through
+        )
+
+    held, _ = lax.optimization_barrier((whole, known))
+    own_block = jnp.arange(n_row * width, dtype=jnp.int32) // width == row_at
+    merged = lax.cond(
+        row_at < last - 1,
+        merge_pair,
+        lambda folded, *rest: jnp.zeros_like(folded),
+        folded,
+        held,
+        jnp.where(own_block[None, :], factor, folded),
+    )
     arrived = lax.ppermute(known, "row", [(last - 1, last)])
-
-    def turn_round(run, arrived, diagonal, folded):
+    arrived, merged = lax.optimization_barrier((arrived, merged))
+
+    def solve_last(run, arrived, diagonal, folded):
         return reduce_columns(
             dot_nt(run.astype(BF), diagonal) - dot_nt(arrived, folded[:, : last * width])
         )
 
-    run = on_turn(last, turn_round, run, arrived, diagonal, folded)
-    known = run.astype(BF)
-    for i in reversed(range(1, last)):
-        arrived = lax.ppermute(known, "row", [(i + 1, i)])
-
-        def backward(run, arrived, diagonal, folded, i=i):
-            return reduce_columns(
-                dot_nt(run.astype(BF), diagonal) - dot_nt(arrived, folded[:, (i + 1) * width :])
-            )
-
-        run = on_turn(i, backward, run, arrived, diagonal, folded)
-        known = jnp.concatenate([run.astype(BF), arrived], axis=1)
-    arrived = lax.ppermute(known, "row", [(1, 0)])
-
-    def gather_rhs(run, arrived, diagonal, folded):
-        done = exchange(run.astype(BF).reshape(n_col, rhs_here, width), "col")
+    run = on_turn(row_at == last, solve_last, run, arrived, diagonal, folded)
+    low = run.astype(BF)
+    arrived = lax.ppermute(low, "row", [(last, last - 1)])
+
+    def solve_next(run, arrived, diagonal, folded):
+        return reduce_columns(
+            dot_nt(run.astype(BF), diagonal) - dot_nt(arrived, folded[:, last * width :])
+        )
+
+    run = on_turn(row_at == last - 1, solve_next, run, arrived, diagonal, folded)
+    low = run.astype(BF)
+
+    other = lax.ppermute(low, "row", down)
+    block = lax.dynamic_slice_in_dim(merged, (row_at | 1) * width, width, 1)
+    known = jnp.concatenate([low, arrived], axis=1)
+    known = (
+        lax.ppermute(known, "row", [(last - 1, last - 3)])
+        + lax.ppermute(known, "row", [(last - 1, last - 2)])
+    )
+
+    def partial_sum(low, other, known, diagonal, block, merged, start):
+        own = dot_nt(low, diagonal) - dot_nt(known, merged[:, start:])
+        return own - jnp.where(even, dot_nt(other, block), 0.0)
+
+    for pair in (2, 1):
+        start = (2 * pair + 2) * width
+
+        def backward(run, low, other, known, diagonal, block, merged, start=start):
+            return reduce_columns(partial_sum(low, other, known, diagonal, block, merged, start))
+
+        run = on_turn(
+            row_at // 2 == pair, backward, run, low, other, known, diagonal, block, merged
+        )
+        low = run.astype(BF)
+        same = [(2 * pair, 2 * pair - 2), (2 * pair + 1, 2 * pair - 1)]
+        cross = [(2 * pair, 2 * pair - 1), (2 * pair + 1, 2 * pair - 2)]
+        same = lax.ppermute(jnp.concatenate([low, known], axis=1), "row", same)
+        cross = lax.ppermute(low, "row", cross)
+        same, older = same[:, :width], same[:, width:]
+        known = jnp.concatenate(
+            [jnp.where(even, same, cross), jnp.where(even, cross, same), older], axis=1
+        )
+
+    def gather_rhs(low, other, known, diagonal, block, merged):
+        done = exchange(low.reshape(n_col, rhs_here, width), "col")
         return jnp.transpose(done, (1, 0, 2)).reshape(rhs_here, section).astype(F32)
 
-    def finish(run, arrived, diagonal, folded):
-        partial = dot_nt(run.astype(BF), diagonal) - dot_nt(arrived, folded[:, width:])
+    def finish(low, other, known, diagonal, block, merged):
+        partial = partial_sum(low, other, known, diagonal, block, merged, 2 * width)
         tiles = exchange(partial.astype(BF).reshape(n_col, rhs_here, section), "col")
         return jnp.sum(tiles.astype(F32), axis=0)
 
-    root_solution = lax.cond(row_at == 0, finish, gather_rhs, run, arrived, diagonal, folded)
+    root_solution = lax.cond(
+        row_at < 2, finish, gather_rhs, low, other, known, diagonal, block, merged
+    )
 
     block_rows = row_at * section + jnp.arange(section, dtype=jnp.int32)
     take = (block_rows[:, None] == root_rows.reshape(-1)[None, :]).astype(BF)

time: 350 us -> 327 us (0.934)
  waiting for transfers between devices: 223 us -> 155 us
  starting transfers between devices: 39.7 us -> 58.5 us
  local copies, waits for them, and re-layouts: 6.16 us -> 19 us
  other arithmetic: 1.12 us -> 12.2 us
  matrix products: 27.8 us -> 35.7 us
  blocking collectives: 36.9 us -> 29 us
    ppermute x7 -> x11, waiting for transfers between devices: 174 us -> 101 us  [the longest x2 89.8 us: on_device(): same = lax.ppermute(jnp.concatenate([low, known], axis=1), 'row', same)]
    ppermute x7 -> x11, starting transfers between devices: 5.93 us -> 27.2 us  [the longest x1 12.1 us: on_device(): other = lax.ppermute(low, 'row', down)]
    all_gather x1, waiting for transfers between devices: 21.7 us -> 34.7 us  [on_device(): lax.all_gather(jnp.concatenate([diagonal, above], axis=0), 'col', axis=1,...]
    all_to_all x3 -> x2, blocking collectives: 36.9 us -> 29 us  [exchange(): return lax.all_to_all(x, axis, 0, 0, tiled=True)]
    dot_general x5 -> x6, matrix products: 17.3 us -> 24.3 us  [dot_nn(): lax.dot_general(a, b, (((1,), (0,)), ((), ())), preferred_element_type=F32)]
    concatenate x6 -> x7, other arithmetic: 0.1 us -> 5.79 us  [the longest x1 4.02 us: merge_pair(): jnp.concatenate([through, lax.ppermute(through, 'row', down[:-1])], axis=0)]
    cond x0 -> x2, local copies, waits for them, and re-layouts: none -> 5.35 us
    all_to_all x3, waiting for transfers between devices: 22.3 us -> 17.7 us  [exchange(): return lax.all_to_all(x, axis, 0, 0, tiled=True)]
  transfers between devices with their start and end apart: 18 -> 22, of which waited for: 8 -> 8; matrix products, arithmetic and copies ran while one was open for 5% -> 16% of each run, Pallas kernels for 0% -> 0%
where the time goes in v3:
time: 327 us; the launch traced here: 325 us
  waiting for transfers between devices  155 us (47%)
  starting transfers between devices  58.5 us (18%)
  matrix products  35.7 us (11%)
  blocking collectives  29 us (9%)
  local copies, waits for them, and re-layouts  19 us (6%)
  between operations  15.4 us (5%)
  other arithmetic  12.2 us (4%)
    ppermute x2, waiting for transfers between devices, on_device(): same = lax.ppermute(jnp.concatenate([low, known], axis=1), 'row', same)  89.8 us
    all_gather x1, waiting for transfers between devices, on_device(): lax.all_gather(jnp.concatenate([diagonal, above], axis=0), 'col', axis=1,...  34.7 us
    all_to_all x2, blocking collectives, exchange(): return lax.all_to_all(x, axis, 0, 0, tiled=True)  29 us
    all_to_all x3, starting transfers between devices, exchange(): return lax.all_to_all(x, axis, 0, 0, tiled=True)  24.7 us
    dot_general x6, matrix products, dot_nn(): lax.dot_general(a, b, (((1,), (0,)), ((), ())), preferred_element_type=F32)  24.3 us
    all_to_all x3, waiting for transfers between devices, exchange(): return lax.all_to_all(x, axis, 0, 0, tiled=True)  17.7 us
    ppermute x1, starting transfers between devices, on_device(): other = lax.ppermute(low, 'row', down)  12.1 us
    dot_general x5, matrix products, dot_nt(): lax.dot_general(a, b, (((1,), (1,)), ((), ())), preferred_element_type=F32)  11.4 us
  transfers between devices with their start and end apart: 22, of which 8 were waited for; matrix products, arithmetic and copies ran while one was open for 16% of the time, Pallas kernels for 0%

profile of v3, /device:TPU:1, one launch (start us, length us, event | category | flops | bytes accessed | tf_op | source)
XLA Modules:
  0.0 325.5 jit_solution(8509636988806078810)
XLA Ops:
  7.2 3.4 %constant_dynamic-slice_fusion = (bf16[1024,1,128]{2,1,0:T(2,128)(2,1)S(1)}, bf16[1024,1,128]{2,1,0:T(2,128)(2,1)S(1)}) fusion(bf16[2048,8,128]{2,1,0:T(8,128)(2,1)} %param.41, s32[]{:T(128)S(6)} %select_n.115, s32[]{:T(128)S(6)} %add.70), kind=kLoop, calls=%fused_computation.144 | loop fusion | bytes 1048584 | tf_op jit(solution)/shard_map/slice | solution.py:55
  12.0 2.8 constant_dynamic-slice_fusion.3
  15.9 8.4 %all-to-all-start.12 = ((f32[16,8,128]{2,1,0:T(8,128)}), f32[16,8,128]{2,1,0:T(8,128)S(1)}, u32[]{:S(2)}, u32[]{:S(2)}) async-start(f32[16,8,128]{2,1,0:T(8,128)} %bitcast.20), calls=%async_computation.12 | async-start | bytes 131072 | tf_op jit(solution)/shard_map/all_to_all | solution.py:19
  25.0 5.6 %fusion.82 = f32[8,2048]{1,0:T(8,128)S(1)} fusion(bf16[1,2048,2048]{2,1,0:T(8,128)(2,1)} %param.35, bf16[1,8,2048]{2,1,0:T(8,128)(2,1)S(1)} %copy-done.1), kind=kOutput, calls=%fused_computation.96 | convolution fusion | flops 67108864 | bytes 8486912 | tf_op jit(solution)/shard_map/dot_general | solution.py:11
  31.7 10.9 %all-to-all-start.13 = ((bf16[128,8,128]{2,1,0:T(8,128)(2,1)}), bf16[128,8,128]{2,1,0:T(8,128)(2,1)S(1)}, u32[]{:S(2)}, u32[]{:S(2)}) async-start(bf16[128,8,128]{2,1,0:T(8,128)(2,1)} %broadcast_in_dim.64), calls=%async_computation.13 | async-start | bytes 524288 | tf_op jit(solution)/shard_map/all_to_all | solution.py:19
  42.7 13.0 %all-to-all-done.13 = bf16[128,8,128]{2,1,0:T(8,128)(2,1)S(1)} async-done(((bf16[128,8,128]{2,1,0:T(8,128)(2,1)}), bf16[128,8,128]{2,1,0:T(8,128)(2,1)S(1)}, u32[]{:S(2)}, u32[]{:S(2)}) %all-to-all-start.13) | async-done | bytes 262176 | tf_op jit(solution)/shard_map/all_to_all | solution.py:19
  57.7 5.2 %copy.70 = bf16[256,8,8,128]{3,1,2,0:T(8,128)(2,1)} copy(bf16[256,8,8,128]{3,2,1,0:T(8,128)(2,1)} %bitcast.175) | data formatting | bytes 8388608
  62.9 16.9 %conditional.13 = (f32[128,128]{1,0:T(8,128)S(1)}) conditional(s32[]{:T(128)} %convert_element_type.197, f32[128,128]{1,0:T(8,128)S(1)} %get-tuple-element.281, (bf16[2048,1024]{1,0:T(8,128)(2,1)}, bf16[128,128]{1,0:T(8,128)(2,1)S(1)}, f32[128,128]{1,0:T(8,128)S(1)}) %tuple.151), branch_computations={%region_0.1_spmd, %region_1.3_spmd} | conditional | flops 67895296 | bytes 3964936 | solution.py:78
  64.4 15.3 %all_to_all.63 = bf16[16,128,128]{2,1,0:T(8,128)(2,1)S(1)} all-to-all(bf16[16,128,128]{2,1,0:T(8,128)(2,1)S(1)} %bitcast.176), channel_id=1, replica_groups=mesh['row'=8,'col'=16] {'col'}, dimensions={0} | all-to-all | bytes 1048576 | tf_op jit(solution)/shard_map/cond/branch_1_fun/all_to_all | solution.py:19
  85.6 1.4 collective-permute-start.9
  87.0 34.7 %all-gather.2.cloned.1.call-done = bf16[3072,2048]{1,0:T(8,128)(2,1)} async-done(((bf16[3072,128]{1,0:T(8,128)(2,1)}), bf16[3072,2048]{1,0:T(8,128)(2,1)}) %all-gather.2.cloned.1.call-update) | async-done | bytes 12582928 | tf_op jit(solution)/shard_map/all_gather | solution.py:56
  121.7 13.8 %fusion.88 = bf16[2048,1024]{1,0:T(8,128)(2,1)} fusion(bf16[2048,1024]{1,0:T(8,128)(2,1)} %bitcast.167, bf16[3072,2048]{1,0:T(8,128)(2,1)} %all-gather.2.cloned.1.call-done), kind=kOutput, calls=%fused_computation.103 | convolution fusion | flops 8592031744 | bytes 16777216 | tf_op jit(solution)/shard_map/dot_general | solution.py:15
  135.5 36.4 %conditional.19 = (bf16[2048,1024]{1,0:T(8,128)(2,1)}) conditional(s32[]{:T(128)} %convert_element_type.208, () %tuple.109, (pred[]{:T(512)}, s32[1,1024]{1,0:T(1,128)S(1)}, s32[]{:T(128)}, bf16[2048,1024]{1,0:T(8,128)(2,1)}, bf16[2048,1024]{1,0:T(8,128)(2,1)}, /*index=5*/bf16[3072,2048]{1,0:T(8,128)(2,1)}) %tuple.157), branch_computations={%region_18.19_spmd, %region_19.22_spmd} | conditional | flops 12906940416 | bytes 81797776 | solution.py:110
  135.5 3.9 %broadcast_select_fusion = bf16[2048,1024]{1,0:T(8,128)(2,1)S(1)} fusion(bf16[2048,1024]{1,0:T(8,128)(2,1)} %get-tuple-element.220, bf16[2048,1024]{1,0:T(8,128)(2,1)} %get-tuple-element.216, pred[1024]{0:T(1024)(128)(4,1)S(1)} %compare_reduce_fusion), kind=kLoop, calls=%fused_computation.89 | loop fusion | flops 2097152 | bytes 12583936 | tf_op jit(solution)/shard_map/jit(_where)/select_n | solution.py:116
  139.4 4.2 %collective-permute-start = (bf16[2048,1024]{1,0:T(8,128)(2,1)S(1)}, bf16[2048,1024]{1,0:T(8,128)(2,1)S(1)}, u32[]{:S(2)}, u32[]{:S(2)}) collective-permute-start(bf16[2048,1024]{1,0:T(8,128)(2,1)S(1)} %broadcast_select_fusion), channel_id=1, source_target_pairs={{16,0},{48,32},{80,64},{17,1},{49,33},{81,65},{18,2},{50,34},{82,6... | collective-permute-start | bytes 12582920 | tf_op jit(solution)/shard_map/cond/branch_1_fun/ppermute | solution.py:94
  143.7 6.5 %collective-permute-done = bf16[2048,1024]{1,0:T(8,128)(2,1)S(1)} collective-permute-done((bf16[2048,1024]{1,0:T(8,128)(2,1)S(1)}, bf16[2048,1024]{1,0:T(8,128)(2,1)S(1)}, u32[]{:S(2)}, u32[]{:S(2)}) %collective-permute-start) | collective-permute-done | bytes 4194336 | tf_op jit(solution)/shard_map/cond/branch_1_fun/ppermute | solution.py:94
  150.2 6.9 %convert_bitcast_fusion = bf16[1024,1024]{1,0:T(8,128)(2,1)S(1)} fusion(bf16[2048,1024]{1,0:T(8,128)(2,1)S(1)} %collective-permute-done, bf16[2048,1024]{1,0:T(8,128)(2,1)S(1)} %broadcast_select_fusion, pred[]{:T(512)} %get-tuple-element.215, bf16[3072,2048]{1,0:T(8,128)(2,1)} %get-tuple-element.218), kind=kOutput, calls=%fused_computation.91 | convolution fusion | flops 4298113024 | bytes 14680576 | tf_op jit(solution)/shard_map/cond/branch_1_fun/dot_general | solution.py:15
  157.1 3.7 %collective-permute-start.1 = (bf16[1024,1024]{1,0:T(8,128)(2,1)S(1)}, bf16[1024,1024]{1,0:T(8,128)(2,1)}, u32[]{:S(2)}, u32[]{:S(2)}) collective-permute-start(bf16[1024,1024]{1,0:T(8,128)(2,1)S(1)} %convert_bitcast_fusion), channel_id=1, source_target_pairs={{16,0},{48,32},{80,64},{17,1},{49,33},{81,65},{18,2},{50,34},{82,6... | collective-permute-start | bytes 6291464 | tf_op jit(solution)/shard_map/cond/branch_1_fun/ppermute | solution.py:97
  160.8 2.5 collective-permute-done.1
  163.3 4.0 %pad_maximum_fusion = bf16[2048,1024]{1,0:T(8,128)(2,1)} fusion(bf16[1024,1024]{1,0:T(8,128)(2,1)} %collective-permute-done.1, bf16[1024,1024]{1,0:T(8,128)(2,1)S(1)} %convert_bitcast_fusion), kind=kLoop, calls=%fused_computation.85 | loop fusion | flops 8388608 | bytes 8388608 | tf_op jit(solution)/shard_map/cond/branch_1_fun/concatenate | solution.py:97
  167.3 4.6 %conditional = (bf16[2048,1024]{1,0:T(8,128)(2,1)}) conditional(s32[]{:T(128)} %convert_element_type.144, bf16[2048,1024]{1,0:T(8,128)(2,1)} %get-tuple-element.216, (s32[]{:T(128)}, bf16[2048,1024]{1,0:T(8,128)(2,1)}, bf16[3072,2048]{1,0:T(8,128)(2,1)}, bf16[2048,1024]{1,0:T(8,128)(2,1)}) %tuple.77), branch_computations={%region_20.20_spmd, %region_21.21_spmd} | conditional | flops 8598332416 | bytes 20973592 | solution.py:104
  167.3 4.6 %copy.73 = bf16[2048,1024]{1,0:T(8,128)(2,1)} copy(bf16[2048,1024]{1,0:T(8,128)(2,1)} %param.13) | data formatting | bytes 8388608 | tf_op jit(solution)/shard_map/cond/branch_1_fun/cond
  174.0 12.1 %collective-permute-start.13 = (bf16[128,128]{1,0:T(8,128)(2,1)S(1)}, bf16[128,128]{1,0:T(8,128)(2,1)S(1)}, u32[]{:S(2)}, u32[]{:S(2)}) collective-permute-start(bf16[128,128]{1,0:T(8,128)(2,1)S(1)} %convert_element_type.210), channel_id=1, source_target_pairs={{16,0},{48,32},{80,64},{112,96},{17,1},{49,33},{81,65},{113,97},{1... | collective-permute-start | bytes 98312 | tf_op jit(solution)/shard_map/ppermute | solution.py:138
  188.8 1.4 conditional.23
  193.6 89.8 %collective-permute-done.16 = bf16[128,640]{1,0:T(8,128)(2,1)S(1)} collective-permute-done((bf16[128,640]{1,0:T(8,128)(2,1)S(1)}, bf16[128,640]{1,0:T(8,128)(2,1)S(1)}, u32[]{:S(2)}, u32[]{:S(2)}) %collective-permute-start.16) | collective-permute-done | bytes 163872 | tf_op jit(solution)/shard_map/ppermute | solution.py:162
  283.4 2.6 collective-permute-done.17
  286.0 19.8 %conditional.24 = (f32[8,2048]{1,0:T(8,128)}, bf16[8,2048]{1,0:T(8,128)(2,1)S(1)}) conditional(s32[]{:T(128)} %convert_element_type.188, bf16[128,128]{1,0:T(8,128)(2,1)S(1)} %get-tuple-element.270, (bf16[128,128]{1,0:T(8,128)(2,1)}, bf16[2048,128]{1,0:T(8,128)(2,1)S(1)}, bf16[2048,1024]{1,0:T(8,128)(2,1)}, bf16[128,768]{1,0:T(8,128)(2,1)S(1)}, ...), branch_computations={%region_34.35_spmd, %region_35.37_spmd} | conditional | flops 538443776 | bytes 10911761 | solution.py:178
  287.1 3.0 fusion.67
  290.5 13.8 %all_to_all.74 = bf16[16,8,2048]{2,1,0:T(8,128)(2,1)S(1)} all-to-all(bf16[16,8,2048]{2,1,0:T(8,128)(2,1)S(1)} %fusion.71), channel_id=1, replica_groups=mesh['row'=8,'col'=16] {'col'}, dimensions={0} | all-to-all | bytes 1048576 | tf_op jit(solution)/shard_map/cond/branch_1_fun/all_to_all | solution.py:19
  305.8 2.0 fusion.95
  307.8 5.3 %all-to-all-start.14 = ((bf16[8,8,128]{2,1,0:T(8,128)(2,1)}), bf16[8,8,128]{2,1,0:T(8,128)(2,1)S(1)}, u32[]{:S(2)}, u32[]{:S(2)}) async-start(bf16[8,8,128]{2,1,0:T(8,128)(2,1)} %fusion.95), calls=%async_computation.14 | async-start | bytes 32768 | tf_op jit(solution)/shard_map/all_to_all | solution.py:19
  313.1 4.7 %all-to-all-done.14 = bf16[8,8,128]{2,1,0:T(8,128)(2,1)S(1)} async-done(((bf16[8,8,128]{2,1,0:T(8,128)(2,1)}), bf16[8,8,128]{2,1,0:T(8,128)(2,1)S(1)}, u32[]{:S(2)}, u32[]{:S(2)}) %all-to-all-start.14) | async-done | bytes 16416 | tf_op jit(solution)/shard_map/all_to_all | solution.py:19
  (99 shorter events, 25.8 us)
Async XLA Ops:
  7.2 310.6 %copy-start = (bf16[1,128,2048]{2,1,0:T(8,128)(2,1)S(1)}, bf16[1,128,2048]{2,1,0:T(8,128)(2,1)}, u32[]{:S(2)}) copy-start(bf16[1,128,2048]{2,1,0:T(8,128)(2,1)} %param.36) | copy-start | bytes 1572868
  7.2 114.6 %all-gather.2.cloned.1.call-start = ((), (), s32[]{:S(2)}) async-start(), calls=%async_computation.15 | async-start | bytes 13369344 | tf_op jit(solution)/shard_map/all_gather | solution.py:56
  10.6 14.4 %copy-start.3 = (s32[1,128]{1,0:T(1,128)S(1)}, s32[1,128]{1,0:T(1,128)}, u32[]{:S(2)}) copy-start(s32[1,128]{1,0:T(1,128)} %param.38) | copy-start | bytes 1540
  10.6 14.4 %copy-start.1 = (bf16[1,8,2048]{2,1,0:T(8,128)(2,1)S(1)}, bf16[1,8,2048]{2,1,0:T(8,128)(2,1)}, u32[]{:S(2)}) copy-start(bf16[1,8,2048]{2,1,0:T(8,128)(2,1)} %param.34) | copy-start | bytes 98308
  10.7 4.2 %collective-permute-start.8 = (bf16[1024,128]{1,0:T(8,128)(2,1)S(1)}, bf16[1024,128]{1,0:T(8,128)(2,1)S(1)}, u32[]{:S(2)}, u32[]{:S(2)}) collective-permute-start(bf16[1024,128]{1,0:T(8,128)(2,1)S(1)} %bitcast.187), channel_id=1, source_target_pairs={{0,16},{32,48},{64,80},{96,112},{1,17},{33,49},{65,81},{97,113},{2... | collective-permute-start | bytes 786440 | tf_op jit(solution)/shard_map/ppermute | solution.py:54
  15.9 15.1 %all-to-all-start.12 = ((f32[16,8,128]{2,1,0:T(8,128)}), f32[16,8,128]{2,1,0:T(8,128)S(1)}, u32[]{:S(2)}, u32[]{:S(2)}) async-start(f32[16,8,128]{2,1,0:T(8,128)} %bitcast.20), calls=%async_computation.12 | async-start | bytes 131072 | tf_op jit(solution)/shard_map/all_to_all | solution.py:19
  25.0 30.9 %copy-start.2 = (s32[8,128]{1,0:T(8,128)S(1)}, s32[8,128]{1,0:T(8,128)}, u32[]{:S(2)}) copy-start(s32[8,128]{1,0:T(8,128)} %param.39) | copy-start | bytes 12292
  31.7 24.0 %all-to-all-start.13 = ((bf16[128,8,128]{2,1,0:T(8,128)(2,1)}), bf16[128,8,128]{2,1,0:T(8,128)(2,1)S(1)}, u32[]{:S(2)}, u32[]{:S(2)}) async-start(bf16[128,8,128]{2,1,0:T(8,128)(2,1)} %broadcast_in_dim.64), calls=%async_computation.13 | async-start | bytes 524288 | tf_op jit(solution)/shard_map/all_to_all | solution.py:19
  56.4 6.5 %collective-permute-start.2 = (bf16[128,128]{1,0:T(8,128)(2,1)S(1)}, bf16[128,128]{1,0:T(8,128)(2,1)S(1)}, u32[]{:S(2)}, u32[]{:S(2)}) collective-permute-start(bf16[128,128]{1,0:T(8,128)(2,1)S(1)} %get-tuple-element.280), channel_id=1, source_target_pairs={{0,16},{1,17},{2,18},{3,19},{4,20},{5,21},{6,22},{7,23},{8,24},{9,... | collective-permute-start | bytes 98312 | tf_op jit(solution)/shard_map/ppermute | solution.py:82
  79.8 2.6 collective-permute-start.3
  82.4 0.7 collective-permute-start.4
  83.2 0.7 collective-permute-start.5
  83.9 0.7 collective-permute-start.6
  84.7 0.7 collective-permute-start.7
  85.6 86.3 %collective-permute-start.9 = (bf16[128,896]{1,0:T(8,128)(2,1)S(1)}, bf16[128,896]{1,0:T(8,128)(2,1)}, u32[]{:S(2)}, u32[]{:S(2)}) collective-permute-start(bf16[128,896]{1,0:T(8,128)(2,1)S(1)} %pad_maximum_fusion.2), channel_id=1, source_target_pairs={{96,112},{97,113},{98,114},{99,115},{100,116},{101,117},{102,118},... | collective-permute-start | bytes 688136 | tf_op jit(solution)/shard_map/ppermute | solution.py:118
  139.4 10.7 %collective-permute-start = (bf16[2048,1024]{1,0:T(8,128)(2,1)S(1)}, bf16[2048,1024]{1,0:T(8,128)(2,1)S(1)}, u32[]{:S(2)}, u32[]{:S(2)}) collective-permute-start(bf16[2048,1024]{1,0:T(8,128)(2,1)S(1)} %broadcast_select_fusion), channel_id=1, source_target_pairs={{16,0},{48,32},{80,64},{17,1},{49,33},{81,65},{18,2},{50,34},{82,6... | collective-permute-start | bytes 12582920 | tf_op jit(solution)/shard_map/cond/branch_1_fun/ppermute | solution.py:94
  157.1 6.2 %collective-permute-start.1 = (bf16[1024,1024]{1,0:T(8,128)(2,1)S(1)}, bf16[1024,1024]{1,0:T(8,128)(2,1)}, u32[]{:S(2)}, u32[]{:S(2)}) collective-permute-start(bf16[1024,1024]{1,0:T(8,128)(2,1)S(1)} %convert_bitcast_fusion), channel_id=1, source_target_pairs={{16,0},{48,32},{80,64},{17,1},{49,33},{81,65},{18,2},{50,34},{82,6... | collective-permute-start | bytes 6291464 | tf_op jit(solution)/shard_map/cond/branch_1_fun/ppermute | solution.py:97
  171.9 0.7 collective-permute-start.10
  172.7 14.6 %collective-permute-start.11 = (bf16[128,256]{1,0:T(8,128)(2,1)S(1)}, bf16[128,256]{1,0:T(8,128)(2,1)S(1)}, u32[]{:S(2)}, u32[]{:S(2)}) collective-permute-start(bf16[128,256]{1,0:T(8,128)(2,1)S(1)} %pad_maximum_fusion.12), channel_id=1, source_target_pairs={{96,64},{97,65},{98,66},{99,67},{100,68},{101,69},{102,70},{103,71... | collective-permute-start | bytes 196616 | tf_op jit(solution)/shard_map/ppermute | solution.py:142
  173.4 13.9 %collective-permute-start.12 = (bf16[128,256]{1,0:T(8,128)(2,1)S(1)}, bf16[128,256]{1,0:T(8,128)(2,1)S(1)}, u32[]{:S(2)}, u32[]{:S(2)}) collective-permute-start(bf16[128,256]{1,0:T(8,128)(2,1)S(1)} %pad_maximum_fusion.12), channel_id=1, source_target_pairs={{96,80},{97,81},{98,82},{99,83},{100,84},{101,85},{102,86},{103,87... | collective-permute-start | bytes 196616 | tf_op jit(solution)/shard_map/ppermute | solution.py:143
  174.0 13.3 %collective-permute-start.13 = (bf16[128,128]{1,0:T(8,128)(2,1)S(1)}, bf16[128,128]{1,0:T(8,128)(2,1)S(1)}, u32[]{:S(2)}, u32[]{:S(2)}) collective-permute-start(bf16[128,128]{1,0:T(8,128)(2,1)S(1)} %convert_element_type.210), channel_id=1, source_target_pairs={{16,0},{48,32},{80,64},{112,96},{17,1},{49,33},{81,65},{113,97},{1... | collective-permute-start | bytes 98312 | tf_op jit(solution)/shard_map/ppermute | solution.py:138
  187.3 1.4 collective-permute-start.14
  188.0 0.7 collective-permute-start.15
  191.0 92.5 %collective-permute-start.16 = (bf16[128,640]{1,0:T(8,128)(2,1)S(1)}, bf16[128,640]{1,0:T(8,128)(2,1)S(1)}, u32[]{:S(2)}, u32[]{:S(2)}) collective-permute-start(bf16[128,640]{1,0:T(8,128)(2,1)S(1)} %pad_maximum_fusion.6), channel_id=1, source_target_pairs={{32,0},{48,16},{33,1},{49,17},{34,2},{50,18},{35,3},{51,19},{36,4}... | collective-permute-start | bytes 491528 | tf_op jit(solution)/shard_map/ppermute | solution.py:162
  192.3 93.7 %collective-permute-start.17 = (bf16[128,128]{1,0:T(8,128)(2,1)}, bf16[128,128]{1,0:T(8,128)(2,1)S(1)}, u32[]{:S(2)}, u32[]{:S(2)}) collective-permute-start(bf16[128,128]{1,0:T(8,128)(2,1)} %get-tuple-element.271), channel_id=1, source_target_pairs={{32,16},{48,0},{33,17},{49,1},{34,18},{50,2},{35,19},{51,3},{36,20... | collective-permute-start | bytes 98312 | tf_op jit(solution)/shard_map/ppermute | solution.py:163
  307.8 10.0 %all-to-all-start.14 = ((bf16[8,8,128]{2,1,0:T(8,128)(2,1)}), bf16[8,8,128]{2,1,0:T(8,128)(2,1)S(1)}, u32[]{:S(2)}, u32[]{:S(2)}) async-start(bf16[8,8,128]{2,1,0:T(8,128)(2,1)} %fusion.95), calls=%async_computation.14 | async-start | bytes 32768 | tf_op jit(solution)/shard_map/all_to_all | solution.py:19
Sparse Core Ops, SparseCore 0:
  16.0 105.7 all-gather.1

commit v4 on v3

--- a/solution.py
+++ b/solution.py
@@ -1,7 +1,10 @@
 import jax
 import jax.numpy as jnp
 from jax import lax
+from jax.experimental import pallas as pl
+from jax.experimental.pallas import tpu as pltpu
 from jax.sharding import PartitionSpec as P
+
 
 BF = jnp.bfloat16
 F32 = jnp.float32
@@ -22,6 +25,66 @@
 def split_columns(x, parts):
     rows, width = x.shape
     return jnp.transpose(x.reshape(rows, parts, width // parts), (1, 0, 2))
+
+
+def fold_kernel(at_ref, left_ref, right_ref, own_ref, out_ref):
+    step = pl.program_id(0)
+    first, own = at_ref[0], at_ref[1]
+
+    @pl.when(step >= first)
+    def _():
+        total = jnp.dot(left_ref[...], right_ref[...], preferred_element_type=F32)
+        width = out_ref.shape[1] // 2
+        for part in range(2):
+            here = slice(part * width, (part + 1) * width)
+            kept = (2 * step + part == own).astype(F32)
+            out_ref[:, here] = jnp.where(
+                kept > 0.5, own_ref[:, here], total[:, here].astype(out_ref.dtype)
+            )
+
+
+def merge_kernel(at_ref, left_ref, high_ref, low_ref, folded_ref, out_ref):
+    step = pl.program_id(0)
+    first, own = at_ref[0], at_ref[1]
+
+    @pl.when(step >= first)
+    def _():
+        half = high_ref.shape[0]
+        total = jnp.dot(left_ref[:, :half], high_ref[...], preferred_element_type=F32)
+        total += jnp.dot(left_ref[:, half:], low_ref[...], preferred_element_type=F32)
+        width = out_ref.shape[1] // 2
+        for part in range(2):
+            here = slice(part * width, (part + 1) * width)
+            later = (2 * step + part > own + 1).astype(F32)
+            out_ref[:, here] = (
+                jnp.where(later > 0.5, folded_ref[:, here].astype(F32) - total[:, here], total[:, here])
+            ).astype(out_ref.dtype)
+
+
+def chunked(kernel, at, left, rows, left_block, rights, out_columns, chunk):
+    def column(step, at):
+        return (0, jnp.maximum(step, at[0]))
+
+    grid_spec = pltpu.PrefetchScalarGridSpec(
+        num_scalar_prefetch=1,
+        grid=(out_columns // chunk,),
+        in_specs=[pl.BlockSpec((rows, left.shape[1]), lambda step, at: (left_block, 0))]
+        + [pl.BlockSpec((x.shape[0], chunk), column) for x in rights],
+        out_specs=pl.BlockSpec((rows, chunk), column),
+    )
+    return pl.pallas_call(
+        kernel,
+        grid_spec=grid_spec,
+        out_shape=jax.ShapeDtypeStruct((rows, out_columns), BF),
+    )(at, left, *rights)
+
+
+def through_kernel(at_ref, left_ref, right_ref, out_ref):
+    @pl.when(pl.program_id(0) >= at_ref[0])
+    def _():
+        out_ref[...] = jnp.dot(
+            left_ref[...], right_ref[...], preferred_element_type=F32
+        ).astype(out_ref.dtype)
 
 
 def on_device(
@@ -41,8 +104,6 @@
     up = [(r, r + 1) for r in range(0, n_row, 2)]
     down = [(r + 1, r) for r in range(0, n_row, 2)]
 
-    run = exchange(split_columns(root_rhs, n_col), "col").reshape(n_rhs, width)
-
     solved = dot_nt(leaf_rhs[0], leaf_inverse[0])
     live = jnp.arange(slots, dtype=jnp.int32) < ranks[0]
     chosen = jnp.where(live, skeleton_rows[0], -1)
@@ -53,18 +114,16 @@
     above = lax.dynamic_index_in_dim(root_factor, row_at | 1, 1, keepdims=False)
     lower = lax.ppermute(above[half:], "row", up)
     above = jnp.where(even, above[:half], lower)
-    whole = lax.all_gather(
-        jnp.concatenate([diagonal, above], axis=0), "col", axis=1, tiled=True
-    )
-
-    skeleton, run, root_factor = lax.optimization_barrier((skeleton, run, root_factor))
-    everyone = jnp.broadcast_to(skeleton[None], (n_row * n_col, rhs_here, slots))
-    gathered = exchange(everyone, ("row", "col")).reshape(n_row, n_rhs, slots)
-    gathered = jnp.transpose(gathered, (1, 0, 2)).reshape(n_rhs, n_row * slots)
-    first = row_at * section + lax.axis_index("col") * width
-    own_rows = first + jnp.arange(width, dtype=jnp.int32)
-    place = (root_rows.reshape(-1)[:, None] == own_rows[None, :]).astype(BF)
-    run = run + dot_nn(gathered, place)
+    held = jnp.concatenate([diagonal, above], axis=0)
+    whole = lax.all_gather(held, "col", axis=1, tiled=True)
+
+    spread = exchange(jnp.broadcast_to(skeleton[None], (n_row, rhs_here, slots)), "row")
+    spread = jnp.transpose(spread, (1, 0, 2)).reshape(rhs_here, n_row * slots)
+    block_rows = row_at * section + jnp.arange(section, dtype=jnp.int32)
+    place = (root_rows.reshape(-1)[:, None] == block_rows[None, :]).astype(BF)
+    run = split_columns(root_rhs + dot_nn(spread, place), n_col)
+    run = exchange(run, "col")
+    run = run.reshape(n_rhs, width)
 
     factor = root_factor.reshape(section, n_row * width)
 
@@ -88,32 +147,46 @@
         known = jnp.concatenate([arrived, run.astype(BF)], axis=1)
         if j == last - 4:
             held, _ = lax.optimization_barrier((factor, known))
-            folded = dot_nn(whole[:section], held).astype(BF)
-
-    def merge_pair(folded, whole, factor):
-        odd_part = lax.ppermute(factor, "row", down[:-1])
-        odd_part = jnp.where(even, odd_part, factor)
-        through = dot_nn(whole[section:], odd_part).astype(BF)
-        through = jnp.concatenate([through, lax.ppermute(through, "row", down[:-1])], axis=0)
-
-        def merge_even(folded, whole, through):
-            passed = dot_nn(whole[:section], through)
-            later = jnp.arange(n_row * width, dtype=jnp.int32) // width > row_at + 1
-            return jnp.where(later[None, :], folded.astype(F32) - passed, passed).astype(BF)
+            first = jnp.where(row_at == last, 0, row_at // 2)
+            at = jnp.stack([first, row_at]).astype(jnp.int32)
+            folded = chunked(
+                fold_kernel, at, whole, section, 0, (held, held), n_row * width, 2 * width
+            )
+
+    def merge_pair(at, whole, folded):
+        odd_part = lax.ppermute(folded, "row", down[:-1])
+
+        def pass_through(odd_part, _=None):
+            return chunked(
+                through_kernel, at, whole, half, 2, (odd_part,), n_row * width, 2 * width
+            )
+
+        through = lax.cond(even, pass_through, lambda _, own: pass_through(own), odd_part, folded)
+        low_half = lax.ppermute(through, "row", down[:-1])
+
+        def merge_even(at, whole, through, low_half, folded):
+            rights = (through, low_half, folded)
+            return chunked(merge_kernel, at, whole, section, 0, rights, n_row * width, 2 * width)
 
         return lax.cond(
-            even, merge_even, lambda folded, *rest: folded, folded, whole, through
+            even,
+            merge_even,
+            lambda at, whole, through, low_half, folded: folded,
+            at,
+            whole,
+            through,
+            low_half,
+            folded,
         )
 
     held, _ = lax.optimization_barrier((whole, known))
-    own_block = jnp.arange(n_row * width, dtype=jnp.int32) // width == row_at
     merged = lax.cond(
         row_at < last - 1,
         merge_pair,
-        lambda folded, *rest: jnp.zeros_like(folded),
+        lambda at, whole, folded: jnp.zeros_like(folded),
+        at,
+        held,
         folded,
-        held,
-        jnp.where(own_block[None, :], factor, folded),
     )
     arrived = lax.ppermute(known, "row", [(last - 1, last)])
     arrived, merged = lax.optimization_barrier((arrived, merged))
@@ -179,7 +252,6 @@
         row_at < 2, finish, gather_rhs, low, other, known, diagonal, block, merged
     )
 
-    block_rows = row_at * section + jnp.arange(section, dtype=jnp.int32)
     take = (block_rows[:, None] == root_rows.reshape(-1)[None, :]).astype(BF)
     taken = dot_nn(root_solution.astype(BF), take).astype(BF)
     taken = exchange(split_columns(taken, n_row), "row")
@@ -201,6 +273,7 @@
         P("row", None, "col"),
     )
     out_specs = (P("row", "col", None), P("col", "row"))
+
     return jax.shard_map(
         on_device, mesh=mesh, in_specs=in_specs, out_specs=out_specs, check_vma=False
     )

time: 327 us -> 316 us (0.966)
  Pallas kernels: 0 us -> 23.7 us
  matrix products: 35.7 us -> 15.9 us
  blocking collectives: 29 us -> 43.9 us
  waiting for transfers between devices: 155 us -> 144 us
  starting transfers between devices: 58.5 us -> 48.5 us
  other arithmetic: 12.2 us -> 4.43 us
    pallas_call x0 -> x2, Pallas kernels: none -> 23.7 us  [chunked(): pl.pallas_call(kernel, grid_spec=grid_spec, out_shape=jax.ShapeDtypeStruc...]
    dot_general x6 -> x4, matrix products: 24.3 us -> 4.54 us  [dot_nn(): lax.dot_general(a, b, (((1,), (0,)), ((), ())), preferred_element_type=F32)]
    all_to_all x2 -> x3, blocking collectives: 29 us -> 43.9 us  [exchange(): return lax.all_to_all(x, axis, 0, 0, tiled=True)]
    all_to_all x3 -> x2, starting transfers between devices: 24.7 us -> 11.7 us  [exchange(): return lax.all_to_all(x, axis, 0, 0, tiled=True)]
    all_to_all x3 -> x2, waiting for transfers between devices: 17.7 us -> 9.31 us  [exchange(): return lax.all_to_all(x, axis, 0, 0, tiled=True)]
    ppermute x2, waiting for transfers between devices: 89.8 us -> 84.4 us  [on_device(): same = lax.ppermute(jnp.concatenate([low, known], axis=1), 'row', same)]
    concatenate x2 -> x1, other arithmetic: 4.95 us -> 1 us  [on_device(): held = jnp.concatenate([diagonal, above], axis=0)]
    select_n x1 -> x0, other arithmetic: 3.9 us -> none  [on_device(): jnp.where(own_block[None, :], factor, folded)]
  transfers between devices with their start and end apart: 22 -> 21, of which waited for: 8 -> 8; matrix products, arithmetic and copies ran while one was open for 16% -> 7% of each run, Pallas kernels for 0% -> 8%
where the time goes in v4:
time: 316 us; the launch traced here: 315 us
  waiting for transfers between devices  144 us (46%)
  starting transfers between devices  48.5 us (15%)
  blocking collectives  43.9 us (14%)
  Pallas kernels  23.7 us (8%)
  local copies, waits for them, and re-layouts  18.7 us (6%)
  matrix products  15.9 us (5%)
  between operations  15.3 us (5%)
  other arithmetic  4.43 us (1%)
    ppermute x2, waiting for transfers between devices, on_device(): same = lax.ppermute(jnp.concatenate([low, known], axis=1), 'row', same)  84.4 us
    all_to_all x3, blocking collectives, exchange(): return lax.all_to_all(x, axis, 0, 0, tiled=True)  43.9 us
    all_gather x1, waiting for transfers between devices, on_device(): whole = lax.all_gather(held, 'col', axis=1, tiled=True)  38.6 us
    pallas_call x2, Pallas kernels, chunked(): pl.pallas_call(kernel, grid_spec=grid_spec, out_shape=jax.ShapeDtypeStruc...  23.7 us
    ppermute x1, starting transfers between devices, on_device(): other = lax.ppermute(low, 'row', down)  13.4 us
    all_to_all x2, starting transfers between devices, exchange(): return lax.all_to_all(x, axis, 0, 0, tiled=True)  11.7 us
    dot_general x5, matrix products, dot_nt(): lax.dot_general(a, b, (((1,), (1,)), ((), ())), preferred_element_type=F32)  11.4 us
    all_to_all x2, waiting for transfers between devices, exchange(): return lax.all_to_all(x, axis, 0, 0, tiled=True)  9.31 us
  transfers between devices with their start and end apart: 21, of which 8 were waited for; matrix products, arithmetic and copies ran while one was open for 7% of the time, Pallas kernels for 8%

profile of v4, /device:TPU:1, one launch (start us, length us, event | category | flops | bytes accessed | tf_op | source)
XLA Modules:
  0.0 314.6 jit_solution(723830940317915736)
XLA Ops:
  7.2 3.4 %constant_dynamic-slice_fusion = (bf16[1024,1,128]{2,1,0:T(2,128)(2,1)S(1)}, bf16[1024,1,128]{2,1,0:T(2,128)(2,1)S(1)}) fusion(bf16[2048,8,128]{2,1,0:T(8,128)(2,1)} %param.43, s32[]{:T(128)S(6)} %select_n.90, s32[]{:T(128)S(6)} %add.44), kind=kLoop, calls=%fused_computation.123 | loop fusion | bytes 1048584 | tf_op jit(solution)/shard_map/slice | solution.py:116
  12.0 2.8 constant_dynamic-slice_fusion.3
  16.6 5.7 %fusion.63 = f32[8,2048]{1,0:T(8,128)S(1)} fusion(bf16[1,2048,2048]{2,1,0:T(8,128)(2,1)} %param.37, bf16[1,8,2048]{2,1,0:T(8,128)(2,1)S(1)} %copy-done.1), kind=kOutput, calls=%fused_computation.73 | convolution fusion | flops 67108864 | bytes 8486912 | tf_op jit(solution)/shard_map/dot_general | solution.py:14
  23.3 6.4 %all-to-all-start.12 = ((bf16[8,8,128]{2,1,0:T(8,128)(2,1)}), bf16[8,8,128]{2,1,0:T(8,128)(2,1)S(1)}, u32[]{:S(2)}, u32[]{:S(2)}) async-start(bf16[8,8,128]{2,1,0:T(8,128)(2,1)} %broadcast_in_dim.42), calls=%async_computation.12 | async-start | bytes 32768 | tf_op jit(solution)/shard_map/all_to_all | solution.py:22
  29.7 4.6 %all-to-all-done.12 = bf16[8,8,128]{2,1,0:T(8,128)(2,1)S(1)} async-done(((bf16[8,8,128]{2,1,0:T(8,128)(2,1)}), bf16[8,8,128]{2,1,0:T(8,128)(2,1)S(1)}, u32[]{:S(2)}, u32[]{:S(2)}) %all-to-all-start.12) | async-done | bytes 16416 | tf_op jit(solution)/shard_map/all_to_all | solution.py:22
  34.3 1.4 fusion.77
  35.7 14.3 %all_to_all.75 = f32[16,8,128]{2,1,0:T(8,128)S(1)} all-to-all(f32[16,8,128]{2,1,0:T(8,128)S(1)} %fusion.77), channel_id=1, replica_groups=mesh['row'=8,'col'=16] {'col'}, dimensions={0} | all-to-all | bytes 131072 | tf_op jit(solution)/shard_map/all_to_all | solution.py:22
  51.3 5.2 %copy.66 = bf16[256,8,8,128]{3,1,2,0:T(8,128)(2,1)} copy(bf16[256,8,8,128]{3,2,1,0:T(8,128)(2,1)} %bitcast.177) | data formatting | bytes 8388608
  56.5 17.4 %conditional.14 = (f32[128,128]{1,0:T(8,128)S(1)}) conditional(s32[]{:T(128)} %convert_element_type.180, f32[128,128]{1,0:T(8,128)S(1)} %bitcast.169, (bf16[2048,1024]{1,0:T(8,128)(2,1)}, bf16[128,128]{1,0:T(8,128)(2,1)S(1)}, f32[128,128]{1,0:T(8,128)S(1)}) %tuple.161), branch_computations={%region_0.1_spmd, %region_1.3_spmd} | conditional | flops 67895296 | bytes 3964936 | solution.py:137
  58.0 15.9 %all_to_all.63 = bf16[16,128,128]{2,1,0:T(8,128)(2,1)S(1)} all-to-all(bf16[16,128,128]{2,1,0:T(8,128)(2,1)S(1)} %bitcast.178), channel_id=1, replica_groups=mesh['row'=8,'col'=16] {'col'}, dimensions={0} | all-to-all | bytes 1048576 | tf_op jit(solution)/shard_map/cond/branch_1_fun/all_to_all | solution.py:22
  79.8 1.4 collective-permute-start.9
  81.2 38.6 %all-gather.2.cloned.1.call-done.left_ref = bf16[3072,2048]{1,0:T(8,128)(2,1)} async-done(((bf16[3072,128]{1,0:T(8,128)(2,1)}), bf16[3072,2048]{1,0:T(8,128)(2,1)}) %all-gather.2.cloned.1.call-update) | async-done | bytes 12582928 | tf_op jit(solution)/shard_map/all_gather | solution.py:118
  119.8 15.2 %shard_map.95 = bf16[2048,1024]{1,0:T(8,128)(2,1)} custom-call(s32[2]{0:T(128)S(1)} %pad_add_fusion.at_ref, bf16[3072,2048]{1,0:T(8,128)(2,1)} %all-gather.2.cloned.1.call-done.left_ref, bf16[2048,1024]{1,0:T(8,128)(2,1)} %bitcast.167, bf16[2048,1024]{1,0:T(8,128)(2,1)} %bitcast.168), custom_call_target="tpu_custom_call" | custom-call | tf_op jit(solution)/shard_map/pallas_call | solution.py:75
  135.0 30.3 %conditional.20 = (bf16[2048,1024]{1,0:T(8,128)(2,1)}) conditional(s32[]{:T(128)} %convert_element_type.190, () %tuple.112, (pred[]{:T(512)}, bf16[2048,1024]{1,0:T(8,128)(2,1)}, s32[2]{0:T(128)S(1)}, bf16[3072,2048]{1,0:T(8,128)(2,1)}) %tuple.114), branch_computations={%region_18.19_spmd, %region_19.24_spmd} | conditional | flops 1 | bytes 33554620 | solution.py:183
  135.0 5.9 %collective-permute-start = (bf16[2048,1024]{1,0:T(8,128)(2,1)}, bf16[2048,1024]{1,0:T(8,128)(2,1)}, u32[]{:S(2)}, u32[]{:S(2)}) collective-permute-start(bf16[2048,1024]{1,0:T(8,128)(2,1)} %get-tuple-element.208), channel_id=1, source_target_pairs={{16,0},{48,32},{80,64},{17,1},{49,33},{81,65},{18,2},{50,34},{82,6... | collective-permute-start | bytes 12582920 | tf_op jit(solution)/shard_map/cond/branch_1_fun/ppermute | solution.py:157
  140.9 5.2 %collective-permute-done = bf16[2048,1024]{1,0:T(8,128)(2,1)} collective-permute-done((bf16[2048,1024]{1,0:T(8,128)(2,1)}, bf16[2048,1024]{1,0:T(8,128)(2,1)}, u32[]{:S(2)}, u32[]{:S(2)}) %collective-permute-start) | collective-permute-done | bytes 4194336 | tf_op jit(solution)/shard_map/cond/branch_1_fun/ppermute | solution.py:157
  146.1 8.5 %conditional = (bf16[1024,1024]{1,0:T(8,128)(2,1)S(1)}) conditional(s32[]{:T(128)} %convert_element_type.130, (s32[2]{0:T(128)S(1)}, bf16[3072,2048]{1,0:T(8,128)(2,1)}, bf16[2048,1024]{1,0:T(8,128)(2,1)}) %tuple.80, (s32[2]{0:T(128)S(1)}, bf16[3072,2048]{1,0:T(8,128)(2,1)}, bf16[2048,1024]{1,0:T(8,128)(2,1)}) %tuple.81), branch_computations={%region_20.20_spmd, %region_21.21_spmd} | conditional | bytes 8 | solution.py:164
  146.1 8.5 %branch_0_fun.1 = bf16[1024,1024]{1,0:T(8,128)(2,1)S(1)} custom-call(s32[2]{0:T(128)S(1)} %get-tuple-element.196.at_ref, bf16[3072,2048]{1,0:T(8,128)(2,1)} %get-tuple-element.197.left_ref, bf16[2048,1024]{1,0:T(8,128)(2,1)} %get-tuple-element.198.right_ref), custom_call_target="tpu_custom_call" | custom-call | tf_op jit(solution)/shard_map/cond/branch_1_fun/cond/branch_0_fun/pallas_call | solution.py:75
  154.5 3.6 %collective-permute-start.1 = (bf16[1024,1024]{1,0:T(8,128)(2,1)S(1)}, bf16[1024,1024]{1,0:T(8,128)(2,1)}, u32[]{:S(2)}, u32[]{:S(2)}) collective-permute-start(bf16[1024,1024]{1,0:T(8,128)(2,1)S(1)} %get-tuple-element.272), channel_id=1, source_target_pairs={{16,0},{48,32},{80,64},{17,1},{49,33},{81,65},{18,2},{50,34},{82,6... | collective-permute-start | bytes 6291464 | tf_op jit(solution)/shard_map/cond/branch_1_fun/ppermute | solution.py:165
  158.2 2.6 collective-permute-done.1
  160.7 4.6 %conditional.1 = (bf16[2048,1024]{1,0:T(8,128)(2,1)}) conditional(s32[]{:T(128)} %convert_element_type.130, bf16[2048,1024]{1,0:T(8,128)(2,1)} %get-tuple-element.208, (s32[2]{0:T(128)S(1)}, bf16[3072,2048]{1,0:T(8,128)(2,1)}, bf16[1024,1024]{1,0:T(8,128)(2,1)S(1)}, bf16[1024,1024]{1,0:T(8,128)(2,1)}, bf16[2048,1024]{1,0:T(8,128)(2,1)}) %tuple.82), branch_computations={%region_22.22_spmd, %region_23.23_spmd} | conditional | bytes 8388616 | solution.py:171
  160.7 4.6 %copy.71 = bf16[2048,1024]{1,0:T(8,128)(2,1)} copy(bf16[2048,1024]{1,0:T(8,128)(2,1)} %param.15) | data formatting | bytes 8388608 | tf_op jit(solution)/shard_map/cond/branch_1_fun/cond
  167.4 13.4 %collective-permute-start.13 = (bf16[128,128]{1,0:T(8,128)(2,1)S(1)}, bf16[128,128]{1,0:T(8,128)(2,1)S(1)}, u32[]{:S(2)}, u32[]{:S(2)}) collective-permute-start(bf16[128,128]{1,0:T(8,128)(2,1)S(1)} %convert_element_type.192), channel_id=1, source_target_pairs={{16,0},{48,32},{80,64},{112,96},{17,1},{49,33},{81,65},{113,97},{1... | collective-permute-start | bytes 98312 | tf_op jit(solution)/shard_map/ppermute | solution.py:211
  183.4 1.4 conditional.24
  188.2 84.4 %collective-permute-done.16 = bf16[128,640]{1,0:T(8,128)(2,1)S(1)} collective-permute-done((bf16[128,640]{1,0:T(8,128)(2,1)S(1)}, bf16[128,640]{1,0:T(8,128)(2,1)S(1)}, u32[]{:S(2)}, u32[]{:S(2)}) %collective-permute-start.16) | collective-permute-done | bytes 163872 | tf_op jit(solution)/shard_map/ppermute | solution.py:235
  272.6 2.6 collective-permute-done.17
  275.2 19.8 %conditional.25 = (f32[8,2048]{1,0:T(8,128)}, bf16[8,2048]{1,0:T(8,128)(2,1)S(1)}) conditional(s32[]{:T(128)} %convert_element_type.171, bf16[128,128]{1,0:T(8,128)(2,1)S(1)} %get-tuple-element.254, (bf16[128,128]{1,0:T(8,128)(2,1)}, bf16[2048,128]{1,0:T(8,128)(2,1)S(1)}, bf16[2048,1024]{1,0:T(8,128)(2,1)}, bf16[128,768]{1,0:T(8,128)(2,1)S(1)}, ...), branch_computations={%region_36.37_spmd, %region_37.39_spmd} | conditional | flops 538443776 | bytes 10911761 | solution.py:251
  276.3 3.0 fusion.58
  279.6 13.8 %all_to_all.74 = bf16[16,8,2048]{2,1,0:T(8,128)(2,1)S(1)} all-to-all(bf16[16,8,2048]{2,1,0:T(8,128)(2,1)S(1)} %fusion.62), channel_id=1, replica_groups=mesh['row'=8,'col'=16] {'col'}, dimensions={0} | all-to-all | bytes 1048576 | tf_op jit(solution)/shard_map/cond/branch_1_fun/all_to_all | solution.py:22
  295.0 2.0 fusion.83
  297.0 5.3 %all-to-all-start.14 = ((bf16[8,8,128]{2,1,0:T(8,128)(2,1)}), bf16[8,8,128]{2,1,0:T(8,128)(2,1)S(1)}, u32[]{:S(2)}, u32[]{:S(2)}) async-start(bf16[8,8,128]{2,1,0:T(8,128)(2,1)} %fusion.83), calls=%async_computation.14 | async-start | bytes 32768 | tf_op jit(solution)/shard_map/all_to_all | solution.py:22
  302.3 4.7 %all-to-all-done.14 = bf16[8,8,128]{2,1,0:T(8,128)(2,1)S(1)} async-done(((bf16[8,8,128]{2,1,0:T(8,128)(2,1)}), bf16[8,8,128]{2,1,0:T(8,128)(2,1)S(1)}, u32[]{:S(2)}, u32[]{:S(2)}) %all-to-all-start.14) | async-done | bytes 16416 | tf_op jit(solution)/shard_map/all_to_all | solution.py:22
  (97 shorter events, 25.1 us)
Async XLA Ops:
  7.2 299.8 %copy-start = (bf16[1,128,2048]{2,1,0:T(8,128)(2,1)S(1)}, bf16[1,128,2048]{2,1,0:T(8,128)(2,1)}, u32[]{:S(2)}) copy-start(bf16[1,128,2048]{2,1,0:T(8,128)(2,1)} %param.38) | copy-start | bytes 1572868
  7.2 112.6 %all-gather.2.cloned.1.call-start = ((), (), s32[]{:S(2)}) async-start(), calls=%async_computation.15 | async-start | bytes 13369344 | tf_op jit(solution)/shard_map/all_gather | solution.py:118
  10.6 6.0 %copy-start.4 = (s32[1,128]{1,0:T(1,128)S(1)}, s32[1,128]{1,0:T(1,128)}, u32[]{:S(2)}) copy-start(s32[1,128]{1,0:T(1,128)} %param.40) | copy-start | bytes 1540
  10.6 6.0 %copy-start.1 = (bf16[1,8,2048]{2,1,0:T(8,128)(2,1)S(1)}, bf16[1,8,2048]{2,1,0:T(8,128)(2,1)}, u32[]{:S(2)}) copy-start(bf16[1,8,2048]{2,1,0:T(8,128)(2,1)} %param.36) | copy-start | bytes 98308
  10.7 4.2 %collective-permute-start.8 = (bf16[1024,128]{1,0:T(8,128)(2,1)S(1)}, bf16[1024,128]{1,0:T(8,128)(2,1)S(1)}, u32[]{:S(2)}, u32[]{:S(2)}) collective-permute-start(bf16[1024,128]{1,0:T(8,128)(2,1)S(1)} %bitcast.188), channel_id=1, source_target_pairs={{0,16},{32,48},{64,80},{96,112},{1,17},{33,49},{65,81},{97,113},{2... | collective-permute-start | bytes 786440 | tf_op jit(solution)/shard_map/ppermute | solution.py:115
  16.6 17.7 %copy-start.2 = (f32[8,2048]{1,0:T(8,128)S(1)}, f32[8,2048]{1,0:T(8,128)}, u32[]{:S(2)}) copy-start(f32[8,2048]{1,0:T(8,128)} %param.42) | copy-start | bytes 196612
  16.6 17.7 %copy-start.3 = (s32[8,128]{1,0:T(8,128)S(1)}, s32[8,128]{1,0:T(8,128)}, u32[]{:S(2)}) copy-start(s32[8,128]{1,0:T(8,128)} %param.41) | copy-start | bytes 12292
  23.3 11.1 %all-to-all-start.12 = ((bf16[8,8,128]{2,1,0:T(8,128)(2,1)}), bf16[8,8,128]{2,1,0:T(8,128)(2,1)S(1)}, u32[]{:S(2)}, u32[]{:S(2)}) async-start(bf16[8,8,128]{2,1,0:T(8,128)(2,1)} %broadcast_in_dim.42), calls=%async_computation.12 | async-start | bytes 32768 | tf_op jit(solution)/shard_map/all_to_all | solution.py:22
  50.0 6.5 %collective-permute-start.2 = (bf16[128,128]{1,0:T(8,128)(2,1)S(1)}, bf16[128,128]{1,0:T(8,128)(2,1)S(1)}, u32[]{:S(2)}, u32[]{:S(2)}) collective-permute-start(bf16[128,128]{1,0:T(8,128)(2,1)S(1)} %bitcast_convert_fusion), channel_id=1, source_target_pairs={{0,16},{1,17},{2,18},{3,19},{4,20},{5,21},{6,22},{7,23},{8,24},{9,... | collective-permute-start | bytes 98312 | tf_op jit(solution)/shard_map/ppermute | solution.py:141
  74.0 2.6 collective-permute-start.3
  76.6 0.7 collective-permute-start.4
  77.4 0.7 collective-permute-start.5
  78.1 0.7 collective-permute-start.6
  78.9 0.7 collective-permute-start.7
  79.8 85.5 %collective-permute-start.9 = (bf16[128,896]{1,0:T(8,128)(2,1)S(1)}, bf16[128,896]{1,0:T(8,128)(2,1)}, u32[]{:S(2)}, u32[]{:S(2)}) collective-permute-start(bf16[128,896]{1,0:T(8,128)(2,1)S(1)} %pad_maximum_fusion.1), channel_id=1, source_target_pairs={{96,112},{97,113},{98,114},{99,115},{100,116},{101,117},{102,118},... | collective-permute-start | bytes 688136 | tf_op jit(solution)/shard_map/ppermute | solution.py:191
  135.0 11.0 %collective-permute-start = (bf16[2048,1024]{1,0:T(8,128)(2,1)}, bf16[2048,1024]{1,0:T(8,128)(2,1)}, u32[]{:S(2)}, u32[]{:S(2)}) collective-permute-start(bf16[2048,1024]{1,0:T(8,128)(2,1)} %get-tuple-element.208), channel_id=1, source_target_pairs={{16,0},{48,32},{80,64},{17,1},{49,33},{81,65},{18,2},{50,34},{82,6... | collective-permute-start | bytes 12582920 | tf_op jit(solution)/shard_map/cond/branch_1_fun/ppermute | solution.py:157
  154.5 6.2 %collective-permute-start.1 = (bf16[1024,1024]{1,0:T(8,128)(2,1)S(1)}, bf16[1024,1024]{1,0:T(8,128)(2,1)}, u32[]{:S(2)}, u32[]{:S(2)}) collective-permute-start(bf16[1024,1024]{1,0:T(8,128)(2,1)S(1)} %get-tuple-element.272), channel_id=1, source_target_pairs={{16,0},{48,32},{80,64},{17,1},{49,33},{81,65},{18,2},{50,34},{82,6... | collective-permute-start | bytes 6291464 | tf_op jit(solution)/shard_map/cond/branch_1_fun/ppermute | solution.py:165
  165.3 0.7 collective-permute-start.10
  166.0 15.8 %collective-permute-start.11 = (bf16[128,256]{1,0:T(8,128)(2,1)S(1)}, bf16[128,256]{1,0:T(8,128)(2,1)S(1)}, u32[]{:S(2)}, u32[]{:S(2)}) collective-permute-start(bf16[128,256]{1,0:T(8,128)(2,1)S(1)} %pad_maximum_fusion.11), channel_id=1, source_target_pairs={{96,64},{97,65},{98,66},{99,67},{100,68},{101,69},{102,70},{103,71... | collective-permute-start | bytes 196616 | tf_op jit(solution)/shard_map/ppermute | solution.py:215
  166.7 15.2 %collective-permute-start.12 = (bf16[128,256]{1,0:T(8,128)(2,1)S(1)}, bf16[128,256]{1,0:T(8,128)(2,1)S(1)}, u32[]{:S(2)}, u32[]{:S(2)}) collective-permute-start(bf16[128,256]{1,0:T(8,128)(2,1)S(1)} %pad_maximum_fusion.11), channel_id=1, source_target_pairs={{96,80},{97,81},{98,82},{99,83},{100,84},{101,85},{102,86},{103,87... | collective-permute-start | bytes 196616 | tf_op jit(solution)/shard_map/ppermute | solution.py:216
  167.4 14.5 %collective-permute-start.13 = (bf16[128,128]{1,0:T(8,128)(2,1)S(1)}, bf16[128,128]{1,0:T(8,128)(2,1)S(1)}, u32[]{:S(2)}, u32[]{:S(2)}) collective-permute-start(bf16[128,128]{1,0:T(8,128)(2,1)S(1)} %convert_element_type.192), channel_id=1, source_target_pairs={{16,0},{48,32},{80,64},{112,96},{17,1},{49,33},{81,65},{113,97},{1... | collective-permute-start | bytes 98312 | tf_op jit(solution)/shard_map/ppermute | solution.py:211
  182.0 1.4 collective-permute-start.14
  182.7 0.7 collective-permute-start.15
  185.6 87.0 %collective-permute-start.16 = (bf16[128,640]{1,0:T(8,128)(2,1)S(1)}, bf16[128,640]{1,0:T(8,128)(2,1)S(1)}, u32[]{:S(2)}, u32[]{:S(2)}) collective-permute-start(bf16[128,640]{1,0:T(8,128)(2,1)S(1)} %pad_maximum_fusion.5), channel_id=1, source_target_pairs={{32,0},{48,16},{33,1},{49,17},{34,2},{50,18},{35,3},{51,19},{36,4}... | collective-permute-start | bytes 491528 | tf_op jit(solution)/shard_map/ppermute | solution.py:235
  186.9 88.3 %collective-permute-start.17 = (bf16[128,128]{1,0:T(8,128)(2,1)}, bf16[128,128]{1,0:T(8,128)(2,1)S(1)}, u32[]{:S(2)}, u32[]{:S(2)}) collective-permute-start(bf16[128,128]{1,0:T(8,128)(2,1)} %get-tuple-element.255), channel_id=1, source_target_pairs={{32,16},{48,0},{33,17},{49,1},{34,18},{50,2},{35,19},{51,3},{36,20... | collective-permute-start | bytes 98312 | tf_op jit(solution)/shard_map/ppermute | solution.py:236
  297.0 10.0 %all-to-all-start.14 = ((bf16[8,8,128]{2,1,0:T(8,128)(2,1)}), bf16[8,8,128]{2,1,0:T(8,128)(2,1)S(1)}, u32[]{:S(2)}, u32[]{:S(2)}) async-start(bf16[8,8,128]{2,1,0:T(8,128)(2,1)} %fusion.83), calls=%async_computation.14 | async-start | bytes 32768 | tf_op jit(solution)/shard_map/all_to_all | solution.py:22
Sparse Core Ops, SparseCore 0:
  16.1 103.7 all-gather.1

commit v5 on v4

v5 whole, which is shorter than its diff:
```python
import jax
import jax.numpy as jnp
from jax import lax
from jax.experimental import pallas as pl
from jax.experimental.pallas import tpu as pltpu
from jax.sharding import PartitionSpec as P


BF = jnp.bfloat16
F32 = jnp.float32


def dot_nt(a, b):
    return lax.dot_general(a, b, (((1,), (1,)), ((), ())), preferred_element_type=F32)


def dot_nn(a, b):
    return lax.dot_general(a, b, (((1,), (0,)), ((), ())), preferred_element_type=F32)


def exchange(x, axis):
    return lax.all_to_all(x, axis, 0, 0, tiled=True)


def split_columns(x, parts):
    rows, width = x.shape
    return jnp.transpose(x.reshape(rows, parts, width // parts), (1, 0, 2))


def fold_kernel(at_ref, right_ref, left_ref, out_ref):
    step = pl.program_id(0)
    first, own = at_ref[0], at_ref[1]

    @pl.when(step >= first)
    def _():
        total = jnp.dot(left_ref[...], right_ref[...], preferred_element_type=F32)
        width = out_ref.shape[0] // 2
        for part in range(2):
            here = slice(part * width, (part + 1) * width)
            kept = (2 * step + part == own).astype(F32)
            out_ref[here, :] = jnp.where(
                kept > 0.5, left_ref[here, :], total[here, :].astype(out_ref.dtype)
            )


def through_kernel(at_ref, right_ref, left_ref, out_ref):
    @pl.when(pl.program_id(0) >= at_ref[0])
    def _():
        out_ref[...] = jnp.dot(
            left_ref[...], right_ref[...], preferred_element_type=F32
        ).astype(out_ref.dtype)


def merge_kernel(at_ref, right_ref, high_ref, low_ref, folded_ref, out_ref):
    step = pl.program_id(0)
    first, own = at_ref[0], at_ref[1]

    @pl.when(step >= first)
    def _():
        half = high_ref.shape[1]
        total = jnp.dot(high_ref[...], right_ref[:half, :], preferred_element_type=F32)
        total += jnp.dot(low_ref[...], right_ref[half:, :], preferred_element_type=F32)
        width = out_ref.shape[0] // 2
        for part in range(2):
            here = slice(part * width, (part + 1) * width)
            block = 2 * step + part
            kept = (block != own + 1).astype(F32)
            passed = (block != own).astype(F32)
            old = jnp.where(kept > 0.5, folded_ref[here, :].astype(F32), 0.0)
            new = jnp.where(passed > 0.5, total[here, :], 0.0)
            new = jnp.where(kept > 0.5, -new, new)
            out_ref[here, :] = (old + new).astype(out_ref.dtype)


def chunked(kernel, at, right, columns, right_block, lefts, chunk):
    def row(step, at):
        return (jnp.maximum(step, at[0]), 0)

    rows = lefts[0].shape[0]
    grid_spec = pltpu.PrefetchScalarGridSpec(
        num_scalar_prefetch=1,
        grid=(rows // chunk,),
        in_specs=[pl.BlockSpec((right.shape[0], columns), lambda step, at: (0, right_block))]
        + [pl.BlockSpec((chunk, x.shape[1]), row) for x in lefts],
        out_specs=pl.BlockSpec((chunk, columns), row),
    )
    return pl.pallas_call(
        kernel,
        grid_spec=grid_spec,
        out_shape=jax.ShapeDtypeStruct((rows, columns), BF),
    )(at, right, *lefts)


def on_device(
    leaf_rhs, leaf_inverse, interpolation, ranks, skeleton_rows, root_rows, root_rhs, root_factor
):
    row_at = lax.axis_index("row")
    n_row = lax.axis_size("row")
    n_col = lax.axis_size("col")
    rhs_here = leaf_rhs.shape[1]
    n_rhs = rhs_here * n_col
    slots = skeleton_rows.shape[1]
    section = root_rhs.shape[1]
    half = section // 2
    width = section // n_col
    leaf = leaf_rhs.shape[2]
    even = row_at % 2 == 0
    up = [(r, r + 1) for r in range(0, n_row, 2)]
    down = [(r + 1, r) for r in range(0, n_row, 2)]

    solved = dot_nt(leaf_rhs[0], leaf_inverse[0])
    live = jnp.arange(slots, dtype=jnp.int32) < ranks[0]
    chosen = jnp.where(live, skeleton_rows[0], -1)
    pick = (jnp.arange(leaf, dtype=jnp.int32)[:, None] == chosen[None, :]).astype(BF)
    skeleton = dot_nn(solved.astype(BF), pick).astype(BF)

    factor = jnp.transpose(root_factor, (1, 2, 0)).reshape(n_row * width, section)
    diagonal = lax.dynamic_slice_in_dim(factor, row_at * width, width, 0)
    above = lax.dynamic_slice_in_dim(factor, (row_at | 1) * width, width, 0)

    lower = lax.ppermute(above[:, half:], "row", up)
    held = jnp.concatenate([diagonal, jnp.where(even, above[:, :half], lower)], axis=1)
    whole = lax.all_gather(held, "col", axis=0, tiled=True)

    spread = exchange(jnp.broadcast_to(skeleton[None], (n_row, rhs_here, slots)), "row")
    spread = jnp.transpose(spread, (1, 0, 2)).reshape(rhs_here, n_row * slots)
    block_rows = row_at * section + jnp.arange(section, dtype=jnp.int32)
    place = (root_rows.reshape(-1)[:, None] == block_rows[None, :]).astype(BF)
    run = split_columns(root_rhs + dot_nn(spread, place), n_col)
    run = exchange(run, "col")
    run = run.reshape(n_rhs, width)

    last = n_row - 1

    def reduce_columns(partial):
        tiles = exchange(split_columns(partial.astype(BF), n_col), "col")
        return jnp.sum(tiles.astype(F32), axis=0)

    def on_turn(turn, step, old, *operands):
        return lax.cond(turn, step, lambda old, *rest: old, old, *operands)

    known = run.astype(BF)
    for j in range(last - 1):
        arrived = lax.ppermute(known, "row", [(j, j + 1)])

        def forward(run, arrived, factor, j=j):
            return run - reduce_columns(dot_nn(arrived, factor[: (j + 1) * width]))

        run = on_turn(row_at == j + 1, forward, run, arrived, factor)
        known = jnp.concatenate([arrived, run.astype(BF)], axis=1)
        if j == last - 4:
            held, _ = lax.optimization_barrier((factor, known))
            first = jnp.where(row_at == last, 0, row_at // 2)
            at = jnp.stack([first, row_at]).astype(jnp.int32)
            folded = chunked(fold_kernel, at, whole, section, 0, (held,), 2 * width)

    def merge_pair(at, whole, folded):
        odd_part = lax.ppermute(folded, "row", down[:-1])

        def pass_through(odd_part, _=None):
            return chunked(through_kernel, at, whole, half, 2, (odd_part,), 2 * width)

        through = lax.cond(even, pass_through, lambda _, own: pass_through(own), odd_part, folded)
        low_half = lax.ppermute(through, "row", down[:-1])

        def merge_even(at, whole, through, low_half, folded):
            lefts = (through, low_half, folded)
            return chunked(merge_kernel, at, whole, section, 0, lefts, 2 * width)

        return lax.cond(
            even,
            merge_even,
            lambda at, whole, through, low_half, folded: folded,
            at,
            whole,
            through,
            low_half,
            folded,
        )

    held, _ = lax.optimization_barrier((whole, known))
    merged = lax.cond(
        row_at < last - 1,
        merge_pair,
        lambda at, whole, folded: jnp.zeros_like(folded),
        at,
        held,
        folded,
    )
    arrived = lax.ppermute(known, "row", [(last - 1, last)])
    arrived, merged = lax.optimization_barrier((arrived, merged))

    def solve_last(run, arrived, folded):
        return reduce_columns(
            dot_nn(jnp.concatenate([-arrived, run.astype(BF)], axis=1), folded)
        )

    run = on_turn(row_at == last, solve_last, run, arrived, folded)
    arrived = lax.ppermute(run.astype(BF), "row", [(last, last - 1)])

    def solve_next(run, arrived, folded):
        return reduce_columns(
            dot_nn(
                jnp.concatenate([run.astype(BF), -arrived], axis=1), folded[(last - 1) * width :]
            )
        )

    run = on_turn(row_at == last - 1, solve_next, run, arrived, folded)
    low = run.astype(BF)

    other = lax.ppermute(low, "row", down)
    zero = jnp.zeros_like(low)
    held = jnp.where(even, jnp.concatenate([low, -other], 1), jnp.concatenate([zero, low], 1))
    known = jnp.concatenate([low, arrived], axis=1)
    known = (
        lax.ppermute(known, "row", [(last - 1, last - 3)])
        + lax.ppermute(known, "row", [(last - 1, last - 2)])
    )

    def partial_sum(held, known, merged, pair):
        return dot_nn(jnp.concatenate([held, -known], axis=1), merged[2 * pair * width :])

    for pair in (2, 1):

        def backward(run, held, known, merged, pair=pair):
            return reduce_columns(partial_sum(held, known, merged, pair))

        run = on_turn(row_at // 2 == pair, backward, run, held, known, merged)
        low = run.astype(BF)
        same = [(2 * pair, 2 * pair - 2), (2 * pair + 1, 2 * pair - 1)]
        cross = [(2 * pair, 2 * pair - 1), (2 * pair + 1, 2 * pair - 2)]
        same = lax.ppermute(jnp.concatenate([low, known], axis=1), "row", same)
        cross = lax.ppermute(low, "row", cross)
        same, older = same[:, :width], same[:, width:]
        known = jnp.concatenate(
            [jnp.where(even, same, cross), jnp.where(even, cross, same), older], axis=1
        )

    def gather_rhs(low, held, known, merged):
        done = exchange(low.reshape(n_col, rhs_here, width), "col")
        return jnp.transpose(done, (1, 0, 2)).reshape(rhs_here, section).astype(F32)

    def finish(low, held, known, merged):
        partial = partial_sum(held, known, merged, 0)
        tiles = exchange(partial.astype(BF).reshape(n_col, rhs_here, section), "col")
        return jnp.sum(tiles.astype(F32), axis=0)

    root_solution = lax.cond(row_at < 2, finish, gather_rhs, low, held, known, merged)

    take = (block_rows[:, None] == root_rows.reshape(-1)[None, :]).astype(BF)
    taken = dot_nn(root_solution.astype(BF), take).astype(BF)
    taken = exchange(split_columns(taken, n_row), "row")
    taken = jnp.sum(taken.astype(F32), axis=0)
    taken = jnp.where(live[None, :], taken, 0.0).astype(BF)
    leaf_solution = solved - dot_nn(taken, interpolation[0])
    return (leaf_solution[None], root_solution)


def solution(mesh):
    in_specs = (
        P("row", "col", None),
        P("row", None, None),
        P("row", None, None),
        P("row"),
        P("row", None),
        P(),
        P("col", "row"),
        P("row", None, "col"),
    )
    out_specs = (P("row", "col", None), P("col", "row"))

    return jax.shard_map(
        on_device, mesh=mesh, in_specs=in_specs, out_specs=out_specs, check_vma=False
    )
```

time: 316 us -> 313 us (level)
  waiting for transfers between devices: 144 us -> 150 us
  starting transfers between devices: 48.5 us -> 44.8 us
  local copies, waits for them, and re-layouts: 18.7 us -> 15.1 us
    transpose x0 -> x1, local copies, waits for them, and re-layouts: none -> 6.73 us  [on_device(): jnp.transpose(root_factor, (1, 2, 0)).reshape(n_row * width, section)]
    dot_general x5 -> x1, matrix products: 11.4 us -> 5.67 us  [dot_nt(): lax.dot_general(a, b, (((1,), (1,)), ((), ())), preferred_element_type=F32)]
    unnamed x13 -> x10, local copies, waits for them, and re-layouts: 5.36 us -> 0.03 us
    ppermute x2, waiting for transfers between devices: 84.4 us -> 88.7 us  [on_device(): same = lax.ppermute(jnp.concatenate([low, known], axis=1), 'row', same)]
    dot_general x4 -> x6, matrix products: 4.54 us -> 8.79 us  [dot_nn(): lax.dot_general(a, b, (((1,), (0,)), ((), ())), preferred_element_type=F32)]
  transfers between devices with their start and end apart: 21 -> 21, of which waited for: 8 -> 11; matrix products, arithmetic and copies ran while one was open for 7% -> 5% of each run, Pallas kernels for 8% -> 7%
where the time goes in v5:
time: 313 us; the launch traced here: 311 us
  waiting for transfers between devices  150 us (48%)
  starting transfers between devices  44.8 us (14%)
  blocking collectives  43.3 us (14%)
  Pallas kernels  22.8 us (7%)
  between operations  15.3 us (5%)
  local copies, waits for them, and re-layouts  15.1 us (5%)
  matrix products  14.5 us (5%)
  other arithmetic  5.47 us (2%)
    ppermute x2, waiting for transfers between devices, on_device(): same = lax.ppermute(jnp.concatenate([low, known], axis=1), 'row', same)  88.7 us
    all_to_all x3, blocking collectives, exchange(): return lax.all_to_all(x, axis, 0, 0, tiled=True)  43.3 us
    all_gather x1, waiting for transfers between devices, on_device(): whole = lax.all_gather(held, 'col', axis=0, tiled=True)  35.5 us
    pallas_call x2, Pallas kernels, chunked(): pl.pallas_call(kernel, grid_spec=grid_spec, out_shape=jax.ShapeDtypeStruc...  22.8 us
    ppermute x1, starting transfers between devices, on_device(): other = lax.ppermute(low, 'row', down)  12.7 us
    all_to_all x2, starting transfers between devices, exchange(): return lax.all_to_all(x, axis, 0, 0, tiled=True)  10.5 us
    all_to_all x2, waiting for transfers between devices, exchange(): return lax.all_to_all(x, axis, 0, 0, tiled=True)  9.31 us
    dot_general x6, matrix products, dot_nn(): lax.dot_general(a, b, (((1,), (0,)), ((), ())), preferred_element_type=F32)  8.79 us
  transfers between devices with their start and end apart: 21, of which 11 were waited for; matrix products, arithmetic and copies ran while one was open for 5% of the time, Pallas kernels for 7%

profile of v5, /device:TPU:1, one launch (start us, length us, event | category | flops | bytes accessed | tf_op | source)
XLA Modules:
  0.0 311.4 jit_solution(15762839703880681275)
XLA Ops:
  7.2 6.7 %copy.21 = bf16[8,128,2048]{2,1,0:T(8,128)(2,1)} copy(bf16[8,128,2048]{1,0,2:T(8,128)(2,1)} %bitcast.144) | data formatting | bytes 8388608 | tf_op jit(solution)/shard_map/transpose | solution.py:117
  21.4 5.7 %fusion.64 = f32[8,2048]{1,0:T(8,128)S(1)} fusion(bf16[1,2048,2048]{2,1,0:T(8,128)(2,1)} %param.37, bf16[1,8,2048]{2,1,0:T(8,128)(2,1)S(1)} %copy-done.1), kind=kOutput, calls=%fused_computation.74 | convolution fusion | flops 67108864 | bytes 8486912 | tf_op jit(solution)/shard_map/dot_general | solution.py:14
  28.0 5.2 %all-to-all-start.12 = ((bf16[8,8,128]{2,1,0:T(8,128)(2,1)}), bf16[8,8,128]{2,1,0:T(8,128)(2,1)S(1)}, u32[]{:S(2)}, u32[]{:S(2)}) async-start(bf16[8,8,128]{2,1,0:T(8,128)(2,1)} %broadcast_in_dim.33), calls=%async_computation.12 | async-start | bytes 32768 | tf_op jit(solution)/shard_map/all_to_all | solution.py:22
  33.2 4.6 %all-to-all-done.12 = bf16[8,8,128]{2,1,0:T(8,128)(2,1)S(1)} async-done(((bf16[8,8,128]{2,1,0:T(8,128)(2,1)}), bf16[8,8,128]{2,1,0:T(8,128)(2,1)S(1)}, u32[]{:S(2)}, u32[]{:S(2)}) %all-to-all-start.12) | async-done | bytes 16416 | tf_op jit(solution)/shard_map/all_to_all | solution.py:22
  37.8 1.4 fusion.78
  39.2 14.0 %all_to_all.75 = f32[16,8,128]{2,1,0:T(8,128)S(1)} all-to-all(f32[16,8,128]{2,1,0:T(8,128)S(1)} %fusion.78), channel_id=1, replica_groups=mesh['row'=8,'col'=16] {'col'}, dimensions={0} | all-to-all | bytes 131072 | tf_op jit(solution)/shard_map/all_to_all | solution.py:22
  54.5 2.7 collective-permute-done.2
  57.2 17.1 %conditional.14 = (f32[128,128]{1,0:T(8,128)S(1)}) conditional(s32[]{:T(128)} %convert_element_type.180, f32[128,128]{1,0:T(8,128)S(1)} %bitcast.142, (bf16[1024,2048]{1,0:T(8,128)(2,1)}, bf16[128,128]{1,0:T(8,128)(2,1)S(1)}, f32[128,128]{1,0:T(8,128)S(1)}) %tuple.161), branch_computations={%region_0.1_spmd, %region_1.3_spmd} | conditional | flops 67895296 | bytes 3964936 | solution.py:140
  57.3 1.3 fusion
  58.7 15.5 %all_to_all.63 = bf16[16,128,128]{2,1,0:T(8,128)(2,1)S(1)} all-to-all(bf16[16,128,128]{2,1,0:T(8,128)(2,1)S(1)} %bitcast.145), channel_id=1, replica_groups=mesh['row'=8,'col'=16] {'col'}, dimensions={0} | all-to-all | bytes 1048576 | tf_op jit(solution)/shard_map/cond/branch_1_fun/all_to_all | solution.py:22
  75.7 1.3 collective-permute-done.3
  81.0 35.5 %all-gather.2.cloned.1.call-done.right_ref = bf16[2048,3072]{1,0:T(8,128)(2,1)} async-done(((bf16[128,3072]{1,0:T(8,128)(2,1)}), bf16[2048,3072]{1,0:T(8,128)(2,1)}) %all-gather.2.cloned.1.call-update) | async-done | bytes 12582928 | tf_op jit(solution)/shard_map/all_gather | solution.py:123
  116.5 14.7 %shard_map.95 = bf16[1024,2048]{1,0:T(8,128)(2,1)} custom-call(s32[2]{0:T(128)S(1)} %pad_add_fusion.at_ref, bf16[2048,3072]{1,0:T(8,128)(2,1)} %all-gather.2.cloned.1.call-done.right_ref, bf16[1024,2048]{1,0:T(8,128)(2,1)} %bitcast.141), custom_call_target="tpu_custom_call" | custom-call | tf_op jit(solution)/shard_map/pallas_call | solution.py:87
  131.2 28.9 %conditional.20 = (bf16[1024,2048]{1,0:T(8,128)(2,1)}) conditional(s32[]{:T(128)} %convert_element_type.190, () %tuple.111, (pred[]{:T(512)}, bf16[1024,2048]{1,0:T(8,128)(2,1)}, s32[2]{0:T(128)S(1)}, bf16[2048,3072]{1,0:T(8,128)(2,1)}) %tuple.114), branch_computations={%region_18.19_spmd, %region_19.24_spmd} | conditional | flops 1 | bytes 33554620 | solution.py:182
  131.2 4.7 %collective-permute-start = (bf16[1024,2048]{1,0:T(8,128)(2,1)}, bf16[1024,2048]{1,0:T(8,128)(2,1)}, u32[]{:S(2)}, u32[]{:S(2)}) collective-permute-start(bf16[1024,2048]{1,0:T(8,128)(2,1)} %get-tuple-element.180), channel_id=1, source_target_pairs={{16,0},{48,32},{80,64},{17,1},{49,33},{81,65},{18,2},{50,34},{82,6... | collective-permute-start | bytes 12582920 | tf_op jit(solution)/shard_map/cond/branch_1_fun/ppermute | solution.py:158
  135.9 5.2 %collective-permute-done = bf16[1024,2048]{1,0:T(8,128)(2,1)} collective-permute-done((bf16[1024,2048]{1,0:T(8,128)(2,1)}, bf16[1024,2048]{1,0:T(8,128)(2,1)}, u32[]{:S(2)}, u32[]{:S(2)}) %collective-permute-start) | collective-permute-done | bytes 4194336 | tf_op jit(solution)/shard_map/cond/branch_1_fun/ppermute | solution.py:158
  141.0 8.2 %conditional = (bf16[1024,1024]{1,0:T(8,128)(2,1)S(1)}) conditional(s32[]{:T(128)} %convert_element_type.130, (s32[2]{0:T(128)S(1)}, bf16[2048,3072]{1,0:T(8,128)(2,1)}, bf16[1024,2048]{1,0:T(8,128)(2,1)}) %tuple.80, (s32[2]{0:T(128)S(1)}, bf16[2048,3072]{1,0:T(8,128)(2,1)}, bf16[1024,2048]{1,0:T(8,128)(2,1)}) %tuple.81), branch_computations={%region_20.20_spmd, %region_21.21_spmd} | conditional | bytes 8 | solution.py:163
  141.0 8.1 %branch_0_fun.1 = bf16[1024,1024]{1,0:T(8,128)(2,1)S(1)} custom-call(s32[2]{0:T(128)S(1)} %get-tuple-element.168.at_ref, bf16[2048,3072]{1,0:T(8,128)(2,1)} %get-tuple-element.169.right_ref, bf16[1024,2048]{1,0:T(8,128)(2,1)} %get-tuple-element.170.left_ref), custom_call_target="tpu_custom_call" | custom-call | tf_op jit(solution)/shard_map/cond/branch_1_fun/cond/branch_0_fun/pallas_call | solution.py:87
  149.2 3.6 %collective-permute-start.1 = (bf16[1024,1024]{1,0:T(8,128)(2,1)S(1)}, bf16[1024,1024]{1,0:T(8,128)(2,1)}, u32[]{:S(2)}, u32[]{:S(2)}) collective-permute-start(bf16[1024,1024]{1,0:T(8,128)(2,1)S(1)} %get-tuple-element.230), channel_id=1, source_target_pairs={{16,0},{48,32},{80,64},{17,1},{49,33},{81,65},{18,2},{50,34},{82,6... | collective-permute-start | bytes 6291464 | tf_op jit(solution)/shard_map/cond/branch_1_fun/ppermute | solution.py:164
  152.8 2.6 collective-permute-done.1
  155.4 4.7 %conditional.1 = (bf16[1024,2048]{1,0:T(8,128)(2,1)}) conditional(s32[]{:T(128)} %convert_element_type.130, bf16[1024,2048]{1,0:T(8,128)(2,1)} %get-tuple-element.180, (s32[2]{0:T(128)S(1)}, bf16[2048,3072]{1,0:T(8,128)(2,1)}, bf16[1024,1024]{1,0:T(8,128)(2,1)S(1)}, bf16[1024,1024]{1,0:T(8,128)(2,1)}, bf16[1024,2048]{1,0:T(8,128)(2,1)}) %tuple.82), branch_computations={%region_22.22_spmd, %region_23.23_spmd} | conditional | bytes 8388616 | solution.py:170
  155.4 4.7 %copy.54 = bf16[1024,2048]{1,0:T(8,128)(2,1)} copy(bf16[1024,2048]{1,0:T(8,128)(2,1)} %param.15) | data formatting | bytes 8388608 | tf_op jit(solution)/shard_map/cond/branch_1_fun/cond
  160.8 12.7 %collective-permute-start.13 = (bf16[128,128]{1,0:T(8,128)(2,1)S(1)}, bf16[128,128]{1,0:T(8,128)(2,1)S(1)}, u32[]{:S(2)}, u32[]{:S(2)}) collective-permute-start(bf16[128,128]{1,0:T(8,128)(2,1)S(1)} %convert_element_type.192), channel_id=1, source_target_pairs={{16,0},{48,32},{80,64},{112,96},{17,1},{49,33},{81,65},{113,97},{1... | collective-permute-start | bytes 98312 | tf_op jit(solution)/shard_map/ppermute | solution.py:211
  177.2 1.4 conditional.24
  182.0 88.7 %collective-permute-done.16 = bf16[128,640]{1,0:T(8,128)(2,1)S(1)} collective-permute-done((bf16[128,640]{1,0:T(8,128)(2,1)S(1)}, bf16[128,640]{1,0:T(8,128)(2,1)S(1)}, u32[]{:S(2)}, u32[]{:S(2)}) %collective-permute-start.16) | collective-permute-done | bytes 163872 | tf_op jit(solution)/shard_map/ppermute | solution.py:232
  270.8 2.6 collective-permute-done.17
  273.4 18.3 %conditional.25 = (f32[8,2048]{1,0:T(8,128)}, bf16[8,2048]{1,0:T(8,128)(2,1)S(1)}) conditional(s32[]{:T(128)} %convert_element_type.171, bf16[128,128]{1,0:T(8,128)(2,1)S(1)} %get-tuple-element.212, (bf16[128,768]{1,0:T(8,128)(2,1)S(1)}, bf16[128,256]{1,0:T(8,128)(2,1)S(1)}, bf16[1024,2048]{1,0:T(8,128)(2,1)}) %tuple.120), branch_computations={%region_36.37_spmd, %region_37.39_spmd} | conditional | flops 538279936 | bytes 7110672 | solution.py:248
  273.5 2.9 fusion.59
  276.4 13.8 %all_to_all.74 = bf16[16,8,2048]{2,1,0:T(8,128)(2,1)S(1)} all-to-all(bf16[16,8,2048]{2,1,0:T(8,128)(2,1)S(1)} %fusion.59), channel_id=1, replica_groups=mesh['row'=8,'col'=16] {'col'}, dimensions={0} | all-to-all | bytes 1048576 | tf_op jit(solution)/shard_map/cond/branch_1_fun/all_to_all | solution.py:22
  291.7 2.0 fusion.84
  293.7 5.3 %all-to-all-start.14 = ((bf16[8,8,128]{2,1,0:T(8,128)(2,1)}), bf16[8,8,128]{2,1,0:T(8,128)(2,1)S(1)}, u32[]{:S(2)}, u32[]{:S(2)}) async-start(bf16[8,8,128]{2,1,0:T(8,128)(2,1)} %fusion.84), calls=%async_computation.14 | async-start | bytes 32768 | tf_op jit(solution)/shard_map/all_to_all | solution.py:22
  299.0 4.7 %all-to-all-done.14 = bf16[8,8,128]{2,1,0:T(8,128)(2,1)S(1)} async-done(((bf16[8,8,128]{2,1,0:T(8,128)(2,1)}), bf16[8,8,128]{2,1,0:T(8,128)(2,1)S(1)}, u32[]{:S(2)}, u32[]{:S(2)}) %all-to-all-start.14) | async-done | bytes 16416 | tf_op jit(solution)/shard_map/all_to_all | solution.py:22
  (94 shorter events, 25.8 us)
Async XLA Ops:
  7.2 296.6 %copy-start = (bf16[1,128,2048]{2,1,0:T(8,128)(2,1)S(1)}, bf16[1,128,2048]{2,1,0:T(8,128)(2,1)}, u32[]{:S(2)}) copy-start(bf16[1,128,2048]{2,1,0:T(8,128)(2,1)} %param.38) | copy-start | bytes 1572868
  7.2 109.3 %all-gather.2.cloned.1.call-start = ((), (), s32[]{:S(2)}) async-start(), calls=%async_computation.15 | async-start | bytes 13369344 | tf_op jit(solution)/shard_map/all_gather | solution.py:123
  14.0 7.4 %copy-start.4 = (s32[1,128]{1,0:T(1,128)S(1)}, s32[1,128]{1,0:T(1,128)}, u32[]{:S(2)}) copy-start(s32[1,128]{1,0:T(1,128)} %param.40) | copy-start | bytes 1540
  14.0 7.4 %copy-start.1 = (bf16[1,8,2048]{2,1,0:T(8,128)(2,1)S(1)}, bf16[1,8,2048]{2,1,0:T(8,128)(2,1)}, u32[]{:S(2)}) copy-start(bf16[1,8,2048]{2,1,0:T(8,128)(2,1)} %param.36) | copy-start | bytes 98308
  15.0 3.7 %collective-permute-start.9 = (bf16[128,1024]{1,0:T(8,128)(2,1)S(1)}, bf16[128,1024]{1,0:T(8,128)(2,1)S(1)}, u32[]{:S(2)}, u32[]{:S(2)}) collective-permute-start(bf16[128,1024]{1,0:T(8,128)(2,1)S(1)} %dynamic-slice.1), channel_id=1, source_target_pairs={{0,16},{32,48},{64,80},{96,112},{1,17},{33,49},{65,81},{97,113},{2... | collective-permute-start | bytes 786440 | tf_op jit(solution)/shard_map/ppermute | solution.py:121
  21.4 16.5 %copy-start.2 = (f32[8,2048]{1,0:T(8,128)S(1)}, f32[8,2048]{1,0:T(8,128)}, u32[]{:S(2)}) copy-start(f32[8,2048]{1,0:T(8,128)} %param.42) | copy-start | bytes 196612
  21.4 16.4 %copy-start.3 = (s32[8,128]{1,0:T(8,128)S(1)}, s32[8,128]{1,0:T(8,128)}, u32[]{:S(2)}) copy-start(s32[8,128]{1,0:T(8,128)} %param.41) | copy-start | bytes 12292
  28.0 9.8 %all-to-all-start.12 = ((bf16[8,8,128]{2,1,0:T(8,128)(2,1)}), bf16[8,8,128]{2,1,0:T(8,128)(2,1)S(1)}, u32[]{:S(2)}, u32[]{:S(2)}) async-start(bf16[8,8,128]{2,1,0:T(8,128)(2,1)} %broadcast_in_dim.33), calls=%async_computation.12 | async-start | bytes 32768 | tf_op jit(solution)/shard_map/all_to_all | solution.py:22
  53.2 4.0 %collective-permute-start.2 = (bf16[128,128]{1,0:T(8,128)(2,1)S(1)}, bf16[128,128]{1,0:T(8,128)(2,1)S(1)}, u32[]{:S(2)}, u32[]{:S(2)}) collective-permute-start(bf16[128,128]{1,0:T(8,128)(2,1)S(1)} %bitcast_convert_fusion), channel_id=1, source_target_pairs={{0,16},{1,17},{2,18},{3,19},{4,20},{5,21},{6,22},{7,23},{8,24},{9,... | collective-permute-start | bytes 98312 | tf_op jit(solution)/shard_map/ppermute | solution.py:144
  74.4 2.6 collective-permute-start.3
  77.0 0.7 collective-permute-start.4
  77.8 0.7 collective-permute-start.5
  78.5 0.7 collective-permute-start.6
  79.3 0.7 collective-permute-start.7
  80.0 80.1 %collective-permute-start.8 = (bf16[128,896]{1,0:T(8,128)(2,1)S(1)}, bf16[128,896]{1,0:T(8,128)(2,1)S(1)}, u32[]{:S(2)}, u32[]{:S(2)}) collective-permute-start(bf16[128,896]{1,0:T(8,128)(2,1)S(1)} %pad_maximum_fusion.1), channel_id=1, source_target_pairs={{96,112},{97,113},{98,114},{99,115},{100,116},{101,117},{102,118},... | collective-permute-start | bytes 688136 | tf_op jit(solution)/shard_map/ppermute | solution.py:190
  131.2 9.9 %collective-permute-start = (bf16[1024,2048]{1,0:T(8,128)(2,1)}, bf16[1024,2048]{1,0:T(8,128)(2,1)}, u32[]{:S(2)}, u32[]{:S(2)}) collective-permute-start(bf16[1024,2048]{1,0:T(8,128)(2,1)} %get-tuple-element.180), channel_id=1, source_target_pairs={{16,0},{48,32},{80,64},{17,1},{49,33},{81,65},{18,2},{50,34},{82,6... | collective-permute-start | bytes 12582920 | tf_op jit(solution)/shard_map/cond/branch_1_fun/ppermute | solution.py:158
  149.2 6.2 %collective-permute-start.1 = (bf16[1024,1024]{1,0:T(8,128)(2,1)S(1)}, bf16[1024,1024]{1,0:T(8,128)(2,1)}, u32[]{:S(2)}, u32[]{:S(2)}) collective-permute-start(bf16[1024,1024]{1,0:T(8,128)(2,1)S(1)} %get-tuple-element.230), channel_id=1, source_target_pairs={{16,0},{48,32},{80,64},{17,1},{49,33},{81,65},{18,2},{50,34},{82,6... | collective-permute-start | bytes 6291464 | tf_op jit(solution)/shard_map/cond/branch_1_fun/ppermute | solution.py:164
  160.1 0.7 collective-permute-start.10
  160.8 13.5 %collective-permute-start.13 = (bf16[128,128]{1,0:T(8,128)(2,1)S(1)}, bf16[128,128]{1,0:T(8,128)(2,1)S(1)}, u32[]{:S(2)}, u32[]{:S(2)}) collective-permute-start(bf16[128,128]{1,0:T(8,128)(2,1)S(1)} %convert_element_type.192), channel_id=1, source_target_pairs={{16,0},{48,32},{80,64},{112,96},{17,1},{49,33},{81,65},{113,97},{1... | collective-permute-start | bytes 98312 | tf_op jit(solution)/shard_map/ppermute | solution.py:211
  174.4 1.4 collective-permute-start.11
  175.0 0.7 collective-permute-start.12
  175.8 1.4 collective-permute-start.14
  176.5 0.7 collective-permute-start.15
  179.4 91.3 %collective-permute-start.16 = (bf16[128,640]{1,0:T(8,128)(2,1)S(1)}, bf16[128,640]{1,0:T(8,128)(2,1)S(1)}, u32[]{:S(2)}, u32[]{:S(2)}) collective-permute-start(bf16[128,640]{1,0:T(8,128)(2,1)S(1)} %pad_maximum_fusion.5), channel_id=1, source_target_pairs={{32,0},{48,16},{33,1},{49,17},{34,2},{50,18},{35,3},{51,19},{36,4}... | collective-permute-start | bytes 491528 | tf_op jit(solution)/shard_map/ppermute | solution.py:232
  180.7 92.6 %collective-permute-start.17 = (bf16[128,128]{1,0:T(8,128)(2,1)}, bf16[128,128]{1,0:T(8,128)(2,1)S(1)}, u32[]{:S(2)}, u32[]{:S(2)}) collective-permute-start(bf16[128,128]{1,0:T(8,128)(2,1)} %get-tuple-element.213), channel_id=1, source_target_pairs={{32,16},{48,0},{33,17},{49,1},{34,18},{50,2},{35,19},{51,3},{36,20... | collective-permute-start | bytes 98312 | tf_op jit(solution)/shard_map/ppermute | solution.py:233
  293.7 10.0 %all-to-all-start.14 = ((bf16[8,8,128]{2,1,0:T(8,128)(2,1)}), bf16[8,8,128]{2,1,0:T(8,128)(2,1)S(1)}, u32[]{:S(2)}, u32[]{:S(2)}) async-start(bf16[8,8,128]{2,1,0:T(8,128)(2,1)} %fusion.84), calls=%async_computation.14 | async-start | bytes 32768 | tf_op jit(solution)/shard_map/all_to_all | solution.py:22
Sparse Core Ops, SparseCore 0:
  20.8 95.6 all-gather.1

commit v6 on v5

--- a/solution.py
+++ b/solution.py
@@ -115,9 +115,9 @@
     skeleton = dot_nn(solved.astype(BF), pick).astype(BF)
 
     factor = jnp.transpose(root_factor, (1, 2, 0)).reshape(n_row * width, section)
+
     diagonal = lax.dynamic_slice_in_dim(factor, row_at * width, width, 0)
     above = lax.dynamic_slice_in_dim(factor, (row_at | 1) * width, width, 0)
-
     lower = lax.ppermute(above[:, half:], "row", up)
     held = jnp.concatenate([diagonal, jnp.where(even, above[:, :half], lower)], axis=1)
     whole = lax.all_gather(held, "col", axis=0, tiled=True)
@@ -132,21 +132,21 @@
 
     last = n_row - 1
 
-    def reduce_columns(partial):
-        tiles = exchange(split_columns(partial.astype(BF), n_col), "col")
-        return jnp.sum(tiles.astype(F32), axis=0)
-
-    def on_turn(turn, step, old, *operands):
-        return lax.cond(turn, step, lambda old, *rest: old, old, *operands)
+    def tiles_of(partial):
+        return split_columns(partial.astype(BF), n_col)
+
+    def take_turn(turn, run, partial, sign=0):
+        def reduce_columns(run, tiles):
+            total = jnp.sum(exchange(tiles, "col").astype(F32), axis=0)
+            return run - total if sign else total
+
+        return lax.cond(turn, reduce_columns, lambda run, tiles: run, run, tiles_of(partial))
 
     known = run.astype(BF)
     for j in range(last - 1):
         arrived = lax.ppermute(known, "row", [(j, j + 1)])
-
-        def forward(run, arrived, factor, j=j):
-            return run - reduce_columns(dot_nn(arrived, factor[: (j + 1) * width]))
-
-        run = on_turn(row_at == j + 1, forward, run, arrived, factor)
+        partial = dot_nn(arrived, factor[: (j + 1) * width])
+        run = take_turn(row_at == j + 1, run, partial, -1)
         known = jnp.concatenate([arrived, run.astype(BF)], axis=1)
         if j == last - 4:
             held, _ = lax.optimization_barrier((factor, known))
@@ -178,6 +178,11 @@
             folded,
         )
 
+    arrived = lax.ppermute(known, "row", [(last - 1, last)])
+    low = run.astype(BF)
+    other = lax.ppermute(low, "row", down[:-1])
+    zero = jnp.zeros_like(low)
+    held_rhs = jnp.where(even, jnp.concatenate([low, -other], 1), jnp.concatenate([zero, low], 1))
     held, _ = lax.optimization_barrier((whole, known))
     merged = lax.cond(
         row_at < last - 1,
@@ -187,65 +192,48 @@
         held,
         folded,
     )
-    arrived = lax.ppermute(known, "row", [(last - 1, last)])
     arrived, merged = lax.optimization_barrier((arrived, merged))
 
-    def solve_last(run, arrived, folded):
-        return reduce_columns(
-            dot_nn(jnp.concatenate([-arrived, run.astype(BF)], axis=1), folded)
-        )
-
-    run = on_turn(row_at == last, solve_last, run, arrived, folded)
-    arrived = lax.ppermute(run.astype(BF), "row", [(last, last - 1)])
-
-    def solve_next(run, arrived, folded):
-        return reduce_columns(
-            dot_nn(
-                jnp.concatenate([run.astype(BF), -arrived], axis=1), folded[(last - 1) * width :]
-            )
-        )
-
-    run = on_turn(row_at == last - 1, solve_next, run, arrived, folded)
-    low = run.astype(BF)
-
-    other = lax.ppermute(low, "row", down)
-    zero = jnp.zeros_like(low)
-    held = jnp.where(even, jnp.concatenate([low, -other], 1), jnp.concatenate([zero, low], 1))
-    known = jnp.concatenate([low, arrived], axis=1)
-    known = (
-        lax.ppermute(known, "row", [(last - 1, last - 3)])
-        + lax.ppermute(known, "row", [(last - 1, last - 2)])
-    )
-
-    def partial_sum(held, known, merged, pair):
-        return dot_nn(jnp.concatenate([held, -known], axis=1), merged[2 * pair * width :])
+    partial = dot_nn(jnp.concatenate([-arrived, low], axis=1), folded)
+    run = take_turn(row_at == last, run, partial)
+    seventh = run.astype(BF)
+    arrived = lax.ppermute(seventh, "row", [(last, last - 1)])
+    early = lax.ppermute(seventh, "row", [(last, last - 2)])
+    early += lax.ppermute(seventh, "row", [(last, last - 3)])
+    partial = dot_nn(jnp.concatenate([low, -arrived], axis=1), folded[(last - 1) * width :])
+    run = take_turn(row_at == last - 1, run, partial)
+    sixth = run.astype(BF)
+    arrived = lax.ppermute(sixth, "row", [(last - 1, last - 3)])
+    arrived += lax.ppermute(sixth, "row", [(last - 1, last - 2)])
+    known = jnp.concatenate([arrived, early], axis=1)
+
+    def partial_sum(known, pair):
+        return dot_nn(jnp.concatenate([held_rhs, -known], axis=1), merged[2 * pair * width :])
 
     for pair in (2, 1):
-
-        def backward(run, held, known, merged, pair=pair):
-            return reduce_columns(partial_sum(held, known, merged, pair))
-
-        run = on_turn(row_at // 2 == pair, backward, run, held, known, merged)
+        run = take_turn(row_at // 2 == pair, run, partial_sum(known, pair))
         low = run.astype(BF)
         same = [(2 * pair, 2 * pair - 2), (2 * pair + 1, 2 * pair - 1)]
         cross = [(2 * pair, 2 * pair - 1), (2 * pair + 1, 2 * pair - 2)]
-        same = lax.ppermute(jnp.concatenate([low, known], axis=1), "row", same)
-        cross = lax.ppermute(low, "row", cross)
-        same, older = same[:, :width], same[:, width:]
+        straight = lax.ppermute(low, "row", same)
+        crossed = lax.ppermute(low, "row", cross)
+        older = lax.ppermute(known, "row", same)
         known = jnp.concatenate(
-            [jnp.where(even, same, cross), jnp.where(even, cross, same), older], axis=1
+            [jnp.where(even, straight, crossed), jnp.where(even, crossed, straight), older], axis=1
         )
 
-    def gather_rhs(low, held, known, merged):
-        done = exchange(low.reshape(n_col, rhs_here, width), "col")
-        return jnp.transpose(done, (1, 0, 2)).reshape(rhs_here, section).astype(F32)
-
-    def finish(low, held, known, merged):
-        partial = partial_sum(held, known, merged, 0)
-        tiles = exchange(partial.astype(BF).reshape(n_col, rhs_here, section), "col")
-        return jnp.sum(tiles.astype(F32), axis=0)
-
-    root_solution = lax.cond(row_at < 2, finish, gather_rhs, low, held, known, merged)
+    def gather_rhs(run, partial):
+        done = exchange(run.astype(BF).reshape(n_col, rhs_here, width), "col")
+        done = jnp.transpose(done, (1, 0, 2)).reshape(rhs_here, section).astype(F32)
+        return lax.optimization_barrier(done)
+
+    def finish(run, partial):
+        tiles = exchange(partial.reshape(n_col, rhs_here, section), "col")
+        return lax.optimization_barrier(jnp.sum(tiles.astype(F32), axis=0))
+
+    root_solution = lax.cond(
+        row_at < 2, finish, gather_rhs, run, partial_sum(known, 0).astype(BF)
+    )
 
     take = (block_rows[:, None] == root_rows.reshape(-1)[None, :]).astype(BF)
     taken = dot_nn(root_solution.astype(BF), take).astype(BF)

time: 313 us -> 308 us (0.984)
  waiting for transfers between devices: 150 us -> 129 us
  matrix products: 14.5 us -> 27.8 us
  local copies, waits for them, and re-layouts: 15.1 us -> 26.8 us
  starting transfers between devices: 44.8 us -> 38.7 us
    all_gather x1, waiting for transfers between devices: 35.5 us -> 19.2 us  [on_device(): whole = lax.all_gather(held, 'col', axis=0, tiled=True)]
    dot_general x6 -> x15, matrix products: 8.79 us -> 22.2 us  [dot_nn(): lax.dot_general(a, b, (((1,), (0,)), ((), ())), preferred_element_type=F32)]
    slice x2 -> x5, local copies, waits for them, and re-layouts: 0.02 us -> 10.6 us  [on_device(): partial = dot_nn(arrived, factor[:(j + 1) * width])]
    ppermute x8 -> x12, starting transfers between devices: 18.6 us -> 10.6 us  [the longest x2 1.96 us: on_device(): older = lax.ppermute(known, 'row', same)]
    unnamed x10 -> x12, local copies, waits for them, and re-layouts: 0.03 us -> 7.6 us
    transpose x1 -> x0, local copies, waits for them, and re-layouts: 6.73 us -> none  [on_device(): jnp.transpose(root_factor, (1, 2, 0)).reshape(n_row * width, section)]
    ppermute x8 -> x12, waiting for transfers between devices: 92.2 us -> 88.3 us  [the longest x2 83.4 us: on_device(): straight = lax.ppermute(low, 'row', same)]
  transfers between devices with their start and end apart: 21 -> 25, of which waited for: 11 -> 9; matrix products, arithmetic and copies ran while one was open for 5% -> 12% of each run, Pallas kernels for 7% -> 7%
where the time goes in v6:
time: 308 us; the launch traced here: 306 us
  waiting for transfers between devices  129 us (42%)
  blocking collectives  41.8 us (14%)
  starting transfers between devices  38.7 us (13%)
  matrix products  27.8 us (9%)
  local copies, waits for them, and re-layouts  26.8 us (9%)
  Pallas kernels  22.8 us (7%)
  between operations  15.6 us (5%)
  other arithmetic  3.9 us (1%)
    ppermute x2, waiting for transfers between devices, on_device(): straight = lax.ppermute(low, 'row', same)  83.4 us
    all_to_all x3, blocking collectives, exchange(): return lax.all_to_all(x, axis, 0, 0, tiled=True)  41.8 us
    pallas_call x2, Pallas kernels, chunked(): pl.pallas_call(kernel, grid_spec=grid_spec, out_shape=jax.ShapeDtypeStruc...  22.8 us
    dot_general x15, matrix products, dot_nn(): lax.dot_general(a, b, (((1,), (0,)), ((), ())), preferred_element_type=F32)  22.2 us
    all_gather x1, waiting for transfers between devices, on_device(): whole = lax.all_gather(held, 'col', axis=0, tiled=True)  19.2 us
    all_to_all x2, starting transfers between devices, exchange(): return lax.all_to_all(x, axis, 0, 0, tiled=True)  12.5 us
    slice x5, local copies, waits for them, and re-layouts, on_device(): partial = dot_nn(arrived, factor[:(j + 1) * width])  10.6 us
    all_to_all x2, waiting for transfers between devices, exchange(): return lax.all_to_all(x, axis, 0, 0, tiled=True)  9.31 us
  transfers between devices with their start and end apart: 25, of which 9 were waited for; matrix products, arithmetic and copies ran while one was open for 12% of the time, Pallas kernels for 7%

profile of v6, /device:TPU:1, one launch (start us, length us, event | category | flops | bytes accessed | tf_op | source)
XLA Modules:
  0.0 306.1 jit_solution(471167047331186274)
XLA Ops:
  7.2 6.7 %copy.21 = bf16[2048,8,128]{0,2,1:T(8,128)(2,1)} copy(bf16[2048,8,128]{2,1,0:T(8,128)(2,1)} %param.43) | data formatting | bytes 8388608 | tf_op args[7]
  21.3 5.7 %fusion = f32[8,2048]{1,0:T(8,128)S(1)} fusion(bf16[1,2048,2048]{2,1,0:T(8,128)(2,1)} %param.37, bf16[1,8,2048]{2,1,0:T(8,128)(2,1)S(1)} %copy-done.1), kind=kOutput, calls=%fused_computation.13 | convolution fusion | flops 67108864 | bytes 8486912 | tf_op jit(solution)/shard_map/dot_general | solution.py:14
  27.9 5.2 %all-to-all-start.12 = ((bf16[8,8,128]{2,1,0:T(8,128)(2,1)}), bf16[8,8,128]{2,1,0:T(8,128)(2,1)S(1)}, u32[]{:S(2)}, u32[]{:S(2)}) async-start(bf16[8,8,128]{2,1,0:T(8,128)(2,1)} %broadcast_in_dim.33), calls=%async_computation.12 | async-start | bytes 32768 | tf_op jit(solution)/shard_map/all_to_all | solution.py:22
  33.1 4.6 %all-to-all-done.12 = bf16[8,8,128]{2,1,0:T(8,128)(2,1)S(1)} async-done(((bf16[8,8,128]{2,1,0:T(8,128)(2,1)}), bf16[8,8,128]{2,1,0:T(8,128)(2,1)S(1)}, u32[]{:S(2)}, u32[]{:S(2)}) %all-to-all-start.12) | async-done | bytes 16416 | tf_op jit(solution)/shard_map/all_to_all | solution.py:22
  39.2 14.0 %all_to_all.75 = f32[16,8,128]{2,1,0:T(8,128)S(1)} all-to-all(f32[16,8,128]{2,1,0:T(8,128)S(1)} %fusion.34), channel_id=1, replica_groups=mesh['row'=8,'col'=16] {'col'}, dimensions={0} | all-to-all | bytes 131072 | tf_op jit(solution)/shard_map/all_to_all | solution.py:22
  54.4 2.7 collective-permute-done.2
  58.7 15.6 %conditional.19 = (f32[128,128]{1,0:T(8,128)S(1)}) conditional(s32[]{:T(128)} %convert_element_type.189, f32[128,128]{1,0:T(8,128)S(1)} %bitcast.155, (bf16[16,128,128]{2,1,0:T(8,128)(2,1)S(1)}, f32[128,128]{1,0:T(8,128)S(1)}) %tuple.163), branch_computations={%region_0.1_spmd, %region_1.3_spmd} | conditional | flops 524288 | bytes 1835016 | solution.py:143
  58.7 15.5 %all_to_all.63 = bf16[16,128,128]{2,1,0:T(8,128)(2,1)S(1)} all-to-all(bf16[16,128,128]{2,1,0:T(8,128)(2,1)S(1)} %get-tuple-element.120), channel_id=1, replica_groups=mesh['row'=8,'col'=16] {'col'}, dimensions={0} | all-to-all | bytes 1048576 | tf_op jit(solution)/shard_map/cond/branch_1_fun/all_to_all | solution.py:22
  88.1 4.1 %slice.73 = bf16[6,128,2048]{2,1,0:T(8,128)(2,1)} slice(bf16[8,128,2048]{2,1,0:T(8,128)(2,1)} %bitcast.153), slice={[0:6], [0:128], [0:2048]} | slice | bytes 6291456 | tf_op jit(solution)/shard_map/slice | solution.py:148
  92.2 2.6 fusion.24
  97.3 19.2 %all-gather.2.cloned.1.call-done.right_ref = bf16[2048,3072]{1,0:T(8,128)(2,1)} async-done(((bf16[128,3072]{1,0:T(8,128)(2,1)}), bf16[2048,3072]{1,0:T(8,128)(2,1)}) %all-gather.2.cloned.1.call-update) | async-done | bytes 12582928 | tf_op jit(solution)/shard_map/all_gather | solution.py:123
  116.4 14.7 %shard_map.95 = bf16[1024,2048]{1,0:T(8,128)(2,1)} custom-call(s32[2]{0:T(128)S(1)} %pad_add_fusion.at_ref, bf16[2048,3072]{1,0:T(8,128)(2,1)} %all-gather.2.cloned.1.call-done.right_ref, bf16[1024,2048]{1,0:T(8,128)(2,1)} %bitcast.154), custom_call_target="tpu_custom_call" | custom-call | tf_op jit(solution)/shard_map/pallas_call | solution.py:87
  131.1 28.9 %conditional.25 = (bf16[1024,2048]{1,0:T(8,128)(2,1)}) conditional(s32[]{:T(128)} %convert_element_type.205, () %tuple.113, (pred[]{:T(512)}, bf16[1024,2048]{1,0:T(8,128)(2,1)}, s32[2]{0:T(128)S(1)}, bf16[2048,3072]{1,0:T(8,128)(2,1)}) %tuple.116), branch_computations={%region_18.19_spmd, %region_19.24_spmd} | conditional | flops 1 | bytes 33554620 | solution.py:187
  131.1 4.7 %collective-permute-start = (bf16[1024,2048]{1,0:T(8,128)(2,1)}, bf16[1024,2048]{1,0:T(8,128)(2,1)}, u32[]{:S(2)}, u32[]{:S(2)}) collective-permute-start(bf16[1024,2048]{1,0:T(8,128)(2,1)} %get-tuple-element.143), channel_id=1, source_target_pairs={{16,0},{48,32},{80,64},{17,1},{49,33},{81,65},{18,2},{50,34},{82,6... | collective-permute-start | bytes 12582920 | tf_op jit(solution)/shard_map/cond/branch_1_fun/ppermute | solution.py:158
  135.8 5.2 %collective-permute-done = bf16[1024,2048]{1,0:T(8,128)(2,1)} collective-permute-done((bf16[1024,2048]{1,0:T(8,128)(2,1)}, bf16[1024,2048]{1,0:T(8,128)(2,1)}, u32[]{:S(2)}, u32[]{:S(2)}) %collective-permute-start) | collective-permute-done | bytes 4194336 | tf_op jit(solution)/shard_map/cond/branch_1_fun/ppermute | solution.py:158
  141.0 8.2 %conditional.2 = (bf16[1024,1024]{1,0:T(8,128)(2,1)S(1)}) conditional(s32[]{:T(128)} %convert_element_type.131, (s32[2]{0:T(128)S(1)}, bf16[2048,3072]{1,0:T(8,128)(2,1)}, bf16[1024,2048]{1,0:T(8,128)(2,1)}) %tuple.89, (s32[2]{0:T(128)S(1)}, bf16[2048,3072]{1,0:T(8,128)(2,1)}, bf16[1024,2048]{1,0:T(8,128)(2,1)}) %tuple.90), branch_computations={%region_20.20_spmd, %region_21.21_spmd} | conditional | bytes 8 | solution.py:163
  141.0 8.1 %branch_0_fun.1 = bf16[1024,1024]{1,0:T(8,128)(2,1)S(1)} custom-call(s32[2]{0:T(128)S(1)} %get-tuple-element.131.at_ref, bf16[2048,3072]{1,0:T(8,128)(2,1)} %get-tuple-element.132.right_ref, bf16[1024,2048]{1,0:T(8,128)(2,1)} %get-tuple-element.133.left_ref), custom_call_target="tpu_custom_call" | custom-call | tf_op jit(solution)/shard_map/cond/branch_1_fun/cond/branch_0_fun/pallas_call | solution.py:87
  149.1 3.6 %collective-permute-start.1 = (bf16[1024,1024]{1,0:T(8,128)(2,1)S(1)}, bf16[1024,1024]{1,0:T(8,128)(2,1)}, u32[]{:S(2)}, u32[]{:S(2)}) collective-permute-start(bf16[1024,1024]{1,0:T(8,128)(2,1)S(1)} %get-tuple-element.184), channel_id=1, source_target_pairs={{16,0},{48,32},{80,64},{17,1},{49,33},{81,65},{18,2},{50,34},{82,6... | collective-permute-start | bytes 6291464 | tf_op jit(solution)/shard_map/cond/branch_1_fun/ppermute | solution.py:164
  152.8 2.6 collective-permute-done.1
  155.3 4.7 %conditional.6 = (bf16[1024,2048]{1,0:T(8,128)(2,1)}) conditional(s32[]{:T(128)} %convert_element_type.131, bf16[1024,2048]{1,0:T(8,128)(2,1)} %get-tuple-element.143, (s32[2]{0:T(128)S(1)}, bf16[2048,3072]{1,0:T(8,128)(2,1)}, bf16[1024,1024]{1,0:T(8,128)(2,1)S(1)}, bf16[1024,1024]{1,0:T(8,128)(2,1)}, bf16[1024,2048]{1,0:T(8,128)(2,1)}) %tuple.91), branch_computations={%region_22.22_spmd, %region_23.23_spmd} | conditional | bytes 8388616 | solution.py:170
  155.3 4.7 %copy.64 = bf16[1024,2048]{1,0:T(8,128)(2,1)} copy(bf16[1024,2048]{1,0:T(8,128)(2,1)} %param.15) | data formatting | bytes 8388608 | tf_op jit(solution)/shard_map/cond/branch_1_fun/cond
  160.1 3.0 fusion.25
  168.5 2.0 fusion.26
  172.8 2.5 fusion.29
  179.4 83.4 %collective-permute-done.19 = bf16[128,128]{1,0:T(8,128)(2,1)S(1)} collective-permute-done((bf16[128,128]{1,0:T(8,128)(2,1)S(1)}, bf16[128,128]{1,0:T(8,128)(2,1)S(1)}, u32[]{:S(2)}, u32[]{:S(2)}) %collective-permute-start.19) | collective-permute-done | bytes 32800 | tf_op jit(solution)/shard_map/ppermute | solution.py:218
  262.8 4.8 %collective-permute-done.20 = bf16[128,128]{1,0:T(8,128)(2,1)S(1)} collective-permute-done((bf16[128,128]{1,0:T(8,128)(2,1)S(1)}, bf16[128,128]{1,0:T(8,128)(2,1)S(1)}, u32[]{:S(2)}, u32[]{:S(2)}) %collective-permute-start.20) | collective-permute-done | bytes 32800 | tf_op jit(solution)/shard_map/ppermute | solution.py:219
  267.7 2.9 convolution_convert_fusion
  270.6 13.8 %conditional.31 = (f32[8,2048]{1,0:T(8,128)}, f32[8,2048]{1,0:T(8,128)S(1)}) conditional(s32[]{:T(128)} %convert_element_type.180, f32[128,128]{1,0:T(8,128)S(1)} %get-tuple-element.196, bf16[128,2048]{1,0:T(8,128)(2,1)S(1)} %convolution_convert_fusion), branch_computations={%region_36.37_spmd, %region_37.39_spmd} | conditional | flops 507904 | bytes 1769488
  270.6 12.3 %all_to_all.74 = bf16[16,8,2048]{2,1,0:T(8,128)(2,1)S(1)} all-to-all(bf16[16,8,2048]{2,1,0:T(8,128)(2,1)S(1)} %bitcast.162), channel_id=1, replica_groups=mesh['row'=8,'col'=16] {'col'}, dimensions={0} | all-to-all | bytes 1048576 | tf_op jit(solution)/shard_map/cond/branch_1_fun/all_to_all | solution.py:22
  284.4 2.0 fusion.40
  286.4 7.3 %all-to-all-start.14 = ((bf16[8,8,128]{2,1,0:T(8,128)(2,1)}), bf16[8,8,128]{2,1,0:T(8,128)(2,1)S(1)}, u32[]{:S(2)}, u32[]{:S(2)}) async-start(bf16[8,8,128]{2,1,0:T(8,128)(2,1)} %fusion.40), calls=%async_computation.14 | async-start | bytes 32768 | tf_op jit(solution)/shard_map/all_to_all | solution.py:22
  293.8 4.7 %all-to-all-done.14 = bf16[8,8,128]{2,1,0:T(8,128)(2,1)S(1)} async-done(((bf16[8,8,128]{2,1,0:T(8,128)(2,1)}), bf16[8,8,128]{2,1,0:T(8,128)(2,1)S(1)}, u32[]{:S(2)}, u32[]{:S(2)}) %all-to-all-start.14) | async-done | bytes 16416 | tf_op jit(solution)/shard_map/all_to_all | solution.py:22
  (123 shorter events, 41.7 us)
Async XLA Ops:
  7.2 291.3 %copy-start = (bf16[1,128,2048]{2,1,0:T(8,128)(2,1)S(1)}, bf16[1,128,2048]{2,1,0:T(8,128)(2,1)}, u32[]{:S(2)}) copy-start(bf16[1,128,2048]{2,1,0:T(8,128)(2,1)} %param.38) | copy-start | bytes 1572868
  7.2 109.3 %all-gather.2.cloned.1.call-start = ((), (), s32[]{:S(2)}) async-start(), calls=%async_computation.15 | async-start | bytes 13369344 | tf_op jit(solution)/shard_map/all_gather | solution.py:123
  14.0 7.3 %copy-start.4 = (s32[1,128]{1,0:T(1,128)S(1)}, s32[1,128]{1,0:T(1,128)}, u32[]{:S(2)}) copy-start(s32[1,128]{1,0:T(1,128)} %param.40) | copy-start | bytes 1540
  14.0 7.3 %copy-start.1 = (bf16[1,8,2048]{2,1,0:T(8,128)(2,1)S(1)}, bf16[1,8,2048]{2,1,0:T(8,128)(2,1)}, u32[]{:S(2)}) copy-start(bf16[1,8,2048]{2,1,0:T(8,128)(2,1)} %param.36) | copy-start | bytes 98308
  14.9 3.7 %collective-permute-start.9 = (bf16[128,1024]{1,0:T(8,128)(2,1)S(1)}, bf16[128,1024]{1,0:T(8,128)(2,1)S(1)}, u32[]{:S(2)}, u32[]{:S(2)}) collective-permute-start(bf16[128,1024]{1,0:T(8,128)(2,1)S(1)} %dynamic-slice.1), channel_id=1, source_target_pairs={{0,16},{32,48},{64,80},{96,112},{1,17},{33,49},{65,81},{97,113},{2... | collective-permute-start | bytes 786440 | tf_op jit(solution)/shard_map/ppermute | solution.py:121
  21.3 16.5 %copy-start.2 = (f32[8,2048]{1,0:T(8,128)S(1)}, f32[8,2048]{1,0:T(8,128)}, u32[]{:S(2)}) copy-start(f32[8,2048]{1,0:T(8,128)} %param.42) | copy-start | bytes 196612
  21.3 16.4 %copy-start.3 = (s32[8,128]{1,0:T(8,128)S(1)}, s32[8,128]{1,0:T(8,128)}, u32[]{:S(2)}) copy-start(s32[8,128]{1,0:T(8,128)} %param.41) | copy-start | bytes 12292
  27.9 9.8 %all-to-all-start.12 = ((bf16[8,8,128]{2,1,0:T(8,128)(2,1)}), bf16[8,8,128]{2,1,0:T(8,128)(2,1)S(1)}, u32[]{:S(2)}, u32[]{:S(2)}) async-start(bf16[8,8,128]{2,1,0:T(8,128)(2,1)} %broadcast_in_dim.33), calls=%async_computation.12 | async-start | bytes 32768 | tf_op jit(solution)/shard_map/all_to_all | solution.py:22
  53.1 4.0 %collective-permute-start.2 = (bf16[128,128]{1,0:T(8,128)(2,1)S(1)}, bf16[128,128]{1,0:T(8,128)(2,1)S(1)}, u32[]{:S(2)}, u32[]{:S(2)}) collective-permute-start(bf16[128,128]{1,0:T(8,128)(2,1)S(1)} %bitcast_convert_fusion), channel_id=1, source_target_pairs={{0,16},{1,17},{2,18},{3,19},{4,20},{5,21},{6,22},{7,23},{8,24},{9,... | collective-permute-start | bytes 98312 | tf_op jit(solution)/shard_map/ppermute | solution.py:147
  74.3 2.6 collective-permute-start.3
  77.5 2.2 collective-permute-start.4
  80.3 2.4 collective-permute-start.5
  84.1 2.6 collective-permute-start.6
  87.5 4.7 %collective-permute-start.7 = (bf16[128,768]{1,0:T(8,128)(2,1)S(1)}, bf16[128,768]{1,0:T(8,128)(2,1)S(1)}, u32[]{:S(2)}, u32[]{:S(2)}) collective-permute-start(bf16[128,768]{1,0:T(8,128)(2,1)S(1)} %pad_maximum_fusion.2), channel_id=1, source_target_pairs={{80,96},{81,97},{82,98},{83,99},{84,100},{85,101},{86,102},{87,103... | collective-permute-start | bytes 589832 | tf_op jit(solution)/shard_map/ppermute | solution.py:147
  95.0 65.0 %collective-permute-start.8 = (bf16[128,896]{1,0:T(8,128)(2,1)S(1)}, bf16[128,896]{1,0:T(8,128)(2,1)S(1)}, u32[]{:S(2)}, u32[]{:S(2)}) collective-permute-start(bf16[128,896]{1,0:T(8,128)(2,1)S(1)} %pad_maximum_fusion.1), channel_id=1, source_target_pairs={{96,112},{97,113},{98,114},{99,115},{100,116},{101,117},{102,118},... | collective-permute-start | bytes 688136 | tf_op jit(solution)/shard_map/ppermute | solution.py:181
  95.8 68.1 %collective-permute-start.11 = (bf16[128,128]{1,0:T(8,128)(2,1)S(1)}, bf16[128,128]{1,0:T(8,128)(2,1)S(1)}, u32[]{:S(2)}, u32[]{:S(2)}) collective-permute-start(bf16[128,128]{1,0:T(8,128)(2,1)S(1)} %convert_element_type.204), channel_id=1, source_target_pairs={{16,0},{48,32},{80,64},{17,1},{49,33},{81,65},{18,2},{50,34},{82,6... | collective-permute-start | bytes 98312 | tf_op jit(solution)/shard_map/ppermute | solution.py:183
  131.1 9.9 %collective-permute-start = (bf16[1024,2048]{1,0:T(8,128)(2,1)}, bf16[1024,2048]{1,0:T(8,128)(2,1)}, u32[]{:S(2)}, u32[]{:S(2)}) collective-permute-start(bf16[1024,2048]{1,0:T(8,128)(2,1)} %get-tuple-element.143), channel_id=1, source_target_pairs={{16,0},{48,32},{80,64},{17,1},{49,33},{81,65},{18,2},{50,34},{82,6... | collective-permute-start | bytes 12582920 | tf_op jit(solution)/shard_map/cond/branch_1_fun/ppermute | solution.py:158
  149.1 6.2 %collective-permute-start.1 = (bf16[1024,1024]{1,0:T(8,128)(2,1)S(1)}, bf16[1024,1024]{1,0:T(8,128)(2,1)}, u32[]{:S(2)}, u32[]{:S(2)}) collective-permute-start(bf16[1024,1024]{1,0:T(8,128)(2,1)S(1)} %get-tuple-element.184), channel_id=1, source_target_pairs={{16,0},{48,32},{80,64},{17,1},{49,33},{81,65},{18,2},{50,34},{82,6... | collective-permute-start | bytes 6291464 | tf_op jit(solution)/shard_map/cond/branch_1_fun/ppermute | solution.py:164
  163.2 2.1 collective-permute-start.10
  163.9 4.5 %collective-permute-start.14 = (bf16[128,128]{1,0:T(8,128)(2,1)S(1)}, bf16[128,128]{1,0:T(8,128)(2,1)S(1)}, u32[]{:S(2)}, u32[]{:S(2)}) collective-permute-start(bf16[128,128]{1,0:T(8,128)(2,1)S(1)} %convert_element_type.207), channel_id=1, source_target_pairs={{112,80},{113,81},{114,82},{115,83},{116,84},{117,85},{118,86},{11... | collective-permute-start | bytes 98312 | tf_op jit(solution)/shard_map/ppermute | solution.py:201
  164.6 3.8 %collective-permute-start.15 = (bf16[128,128]{1,0:T(8,128)(2,1)S(1)}, bf16[128,128]{1,0:T(8,128)(2,1)S(1)}, u32[]{:S(2)}, u32[]{:S(2)}) collective-permute-start(bf16[128,128]{1,0:T(8,128)(2,1)S(1)} %convert_element_type.207), channel_id=1, source_target_pairs={{112,64},{113,65},{114,66},{115,67},{116,68},{117,69},{118,70},{11... | collective-permute-start | bytes 98312 | tf_op jit(solution)/shard_map/ppermute | solution.py:202
  167.0 1.4 collective-permute-start.12
  167.7 0.8 collective-permute-start.13
  170.7 2.0 collective-permute-start.16
  171.4 1.4 collective-permute-start.17
  172.0 0.7 collective-permute-start.18
  175.4 87.3 %collective-permute-start.19 = (bf16[128,128]{1,0:T(8,128)(2,1)S(1)}, bf16[128,128]{1,0:T(8,128)(2,1)S(1)}, u32[]{:S(2)}, u32[]{:S(2)}) collective-permute-start(bf16[128,128]{1,0:T(8,128)(2,1)S(1)} %convert_element_type.213), channel_id=1, source_target_pairs={{32,0},{48,16},{33,1},{49,17},{34,2},{50,18},{35,3},{51,19},{36,4}... | collective-permute-start | bytes 98312 | tf_op jit(solution)/shard_map/ppermute | solution.py:218
  176.7 90.9 %collective-permute-start.20 = (bf16[128,128]{1,0:T(8,128)(2,1)S(1)}, bf16[128,128]{1,0:T(8,128)(2,1)S(1)}, u32[]{:S(2)}, u32[]{:S(2)}) collective-permute-start(bf16[128,128]{1,0:T(8,128)(2,1)S(1)} %convert_element_type.213), channel_id=1, source_target_pairs={{32,16},{48,0},{33,17},{49,1},{34,18},{50,2},{35,19},{51,3},{36,20... | collective-permute-start | bytes 98312 | tf_op jit(solution)/shard_map/ppermute | solution.py:219
  178.1 89.6 %collective-permute-start.21 = (bf16[128,512]{1,0:T(8,128)(2,1)S(1)}, bf16[128,512]{1,0:T(8,128)(2,1)S(1)}, u32[]{:S(2)}, u32[]{:S(2)}) collective-permute-start(bf16[128,512]{1,0:T(8,128)(2,1)S(1)} %get-tuple-element.164), channel_id=1, source_target_pairs={{32,0},{48,16},{33,1},{49,17},{34,2},{50,18},{35,3},{51,19},{36,4}... | collective-permute-start | bytes 393224 | tf_op jit(solution)/shard_map/ppermute | solution.py:220
  286.4 12.0 %all-to-all-start.14 = ((bf16[8,8,128]{2,1,0:T(8,128)(2,1)}), bf16[8,8,128]{2,1,0:T(8,128)(2,1)S(1)}, u32[]{:S(2)}, u32[]{:S(2)}) async-start(bf16[8,8,128]{2,1,0:T(8,128)(2,1)} %fusion.40), calls=%async_computation.14 | async-start | bytes 32768 | tf_op jit(solution)/shard_map/all_to_all | solution.py:22
Sparse Core Ops, SparseCore 0:
  20.8 95.6 all-gather.1

commit v7 on v6

--- a/solution.py
+++ b/solution.py
@@ -1,3 +1,5 @@
+import functools
+
 import jax
 import jax.numpy as jnp
 from jax import lax
@@ -89,6 +91,31 @@
         grid_spec=grid_spec,
         out_shape=jax.ShapeDtypeStruct((rows, columns), BF),
     )(at, right, *lefts)
+
+
+def late_kernel(sign, x_ref, weight_ref, sums_ref, out_ref):
+    total = jnp.dot(x_ref[...], weight_ref[...], preferred_element_type=F32)
+    total = sums_ref[...] + total if sign > 0 else sums_ref[...] - total
+    width = out_ref.shape[2]
+    for tile in range(out_ref.shape[0]):
+        out_ref[tile] = total[:, tile * width : (tile + 1) * width].astype(out_ref.dtype)
+
+
+def late_part(x, weights, block, sums, width, sign, chunks=2):
+    rows, depth = x.shape
+    columns = weights.shape[1] // chunks
+    tiles = weights.shape[1] // width
+    return pl.pallas_call(
+        functools.partial(late_kernel, sign),
+        grid=(chunks,),
+        in_specs=[
+            pl.BlockSpec((rows, depth), lambda step: (0, 0)),
+            pl.BlockSpec((depth, columns), lambda step: (block, step)),
+            pl.BlockSpec((rows, columns), lambda step: (0, step)),
+        ],
+        out_specs=pl.BlockSpec((tiles // chunks, rows, width), lambda step: (step, 0, 0)),
+        out_shape=jax.ShapeDtypeStruct((tiles, rows, width), BF),
+    )(x, weights, sums)
 
 
 def on_device(
@@ -135,21 +162,43 @@
     def tiles_of(partial):
         return split_columns(partial.astype(BF), n_col)
 
-    def take_turn(turn, run, partial, sign=0):
+    def take_turn(turn, run, tiles, sign=0):
         def reduce_columns(run, tiles):
             total = jnp.sum(exchange(tiles, "col").astype(F32), axis=0)
             return run - total if sign else total
 
-        return lax.cond(turn, reduce_columns, lambda run, tiles: run, run, tiles_of(partial))
-
-    known = run.astype(BF)
+        return lax.cond(turn, reduce_columns, lambda run, tiles: run, run, tiles)
+
+    def early_part(turn, part, *operands):
+        return lax.cond(
+            turn, part, lambda *rest: jnp.zeros((n_rhs, section), F32), *operands
+        )
+
+    def blocks(weights, first, count):
+        return weights[first * width : (first + count) * width]
+
+    low = run.astype(BF)
+    before, sums = None, None
     for j in range(last - 1):
-        arrived = lax.ppermute(known, "row", [(j, j + 1)])
-        partial = dot_nn(arrived, factor[: (j + 1) * width])
-        run = take_turn(row_at == j + 1, run, partial, -1)
-        known = jnp.concatenate([arrived, run.astype(BF)], axis=1)
+        arrived = lax.ppermute(low, "row", [(j, j + 1)])
+        known = low if before is None else jnp.concatenate([before, low], axis=1)
+        known = lax.ppermute(known, "row", [(j, j + 2)])
+        late, early = sums, None
+        if j < last - 2:
+            early = early_part(
+                row_at == j + 2, lambda x, w, j=j: dot_nn(x, blocks(w, 0, j + 1)), known, factor
+            )
+            arrived, early = lax.optimization_barrier((arrived, early))
+        if late is None:
+            tiles = tiles_of(dot_nn(arrived, blocks(factor, j, 1)))
+        else:
+            tiles = late_part(arrived, factor, j, late, width, 1)
+        run = take_turn(row_at == j + 1, run, tiles, -1)
+        low = run.astype(BF)
+        before = arrived if j == 0 else jnp.concatenate([older, arrived], axis=1)
+        older, sums = known, early
         if j == last - 4:
-            held, _ = lax.optimization_barrier((factor, known))
+            held, _ = lax.optimization_barrier((factor, low))
             first = jnp.where(row_at == last, 0, row_at // 2)
             at = jnp.stack([first, row_at]).astype(jnp.int32)
             folded = chunked(fold_kernel, at, whole, section, 0, (held,), 2 * width)
@@ -178,12 +227,11 @@
             folded,
         )
 
-    arrived = lax.ppermute(known, "row", [(last - 1, last)])
-    low = run.astype(BF)
+    arrived = lax.ppermute(low, "row", [(last - 1, last)])
     other = lax.ppermute(low, "row", down[:-1])
     zero = jnp.zeros_like(low)
     held_rhs = jnp.where(even, jnp.concatenate([low, -other], 1), jnp.concatenate([zero, low], 1))
-    held, _ = lax.optimization_barrier((whole, known))
+    held, _ = lax.optimization_barrier((whole, low))
     merged = lax.cond(
         row_at < last - 1,
         merge_pair,
@@ -192,35 +240,80 @@
         held,
         folded,
     )
-    arrived, merged = lax.optimization_barrier((arrived, merged))
-
-    partial = dot_nn(jnp.concatenate([-arrived, low], axis=1), folded)
-    run = take_turn(row_at == last, run, partial)
-    seventh = run.astype(BF)
-    arrived = lax.ppermute(seventh, "row", [(last, last - 1)])
-    early = lax.ppermute(seventh, "row", [(last, last - 2)])
-    early += lax.ppermute(seventh, "row", [(last, last - 3)])
-    partial = dot_nn(jnp.concatenate([low, -arrived], axis=1), folded[(last - 1) * width :])
-    run = take_turn(row_at == last - 1, run, partial)
+    sums = early_part(
+        row_at == last,
+        lambda low, known, w: dot_nn(low, blocks(w, last, 1)) - dot_nn(known, blocks(w, 0, last - 1)),
+        low,
+        known,
+        folded,
+    )
+    later = early_part(
+        row_at == last - 1, lambda low, w: dot_nn(low, blocks(w, last - 1, 1)), low, folded
+    )
+    arrived, merged, sums, later = lax.optimization_barrier((arrived, merged, sums, later))
+    run = take_turn(row_at == last, run, late_part(arrived, folded, last - 1, sums, width, -1))
+    final = run.astype(BF)
+    seventh = lax.ppermute(final, "row", [(last, last - 1)])
+    final, seventh = lax.optimization_barrier((final, seventh))
+    ahead = lax.ppermute(final, "row", [(last, last - 2)])
+    ahead += lax.ppermute(final, "row", [(last, last - 3)])
+    run = take_turn(row_at == last - 1, run, late_part(seventh, folded, last, later, width, -1))
     sixth = run.astype(BF)
+    sums = early_part(
+        row_at // 2 == 2,
+        lambda held, x, w: dot_nn(held, blocks(w, 4, 2)) - dot_nn(x, blocks(w, 7, 1)),
+        held_rhs,
+        ahead,
+        merged,
+    )
     arrived = lax.ppermute(sixth, "row", [(last - 1, last - 3)])
     arrived += lax.ppermute(sixth, "row", [(last - 1, last - 2)])
-    known = jnp.concatenate([arrived, early], axis=1)
-
-    def partial_sum(known, pair):
-        return dot_nn(jnp.concatenate([held_rhs, -known], axis=1), merged[2 * pair * width :])
-
-    for pair in (2, 1):
-        run = take_turn(row_at // 2 == pair, run, partial_sum(known, pair))
-        low = run.astype(BF)
-        same = [(2 * pair, 2 * pair - 2), (2 * pair + 1, 2 * pair - 1)]
-        cross = [(2 * pair, 2 * pair - 1), (2 * pair + 1, 2 * pair - 2)]
-        straight = lax.ppermute(low, "row", same)
-        crossed = lax.ppermute(low, "row", cross)
-        older = lax.ppermute(known, "row", same)
-        known = jnp.concatenate(
-            [jnp.where(even, straight, crossed), jnp.where(even, crossed, straight), older], axis=1
+    arrived, sums = lax.optimization_barrier((arrived, sums))
+
+    run = take_turn(row_at // 2 == 2, run, late_part(arrived, merged, 6, sums, width, -1))
+
+    sixth, _ = lax.optimization_barrier((sixth, arrived))
+    both = jnp.where(
+        even,
+        jnp.concatenate([sixth, seventh], axis=1),
+        jnp.concatenate([lax.ppermute(sixth, "row", [(last - 1, last)]), final], axis=1),
+    )
+    far = lax.ppermute(both, "row", [(6, 2), (7, 3)])
+    farther = lax.ppermute(both, "row", [(6, 0), (7, 1)])
+
+    def pair_sums(pair, held, x, w):
+        return dot_nn(held, blocks(w, 2 * pair, 2)) - dot_nn(x, w[(2 * pair + 4) * width :])
+
+    def next_pair(low, pair):
+        straight = lax.ppermute(low, "row", [(2 * pair, 2 * pair - 2), (2 * pair + 1, 2 * pair - 1)])
+        crossed = lax.ppermute(low, "row", [(2 * pair, 2 * pair - 1), (2 * pair + 1, 2 * pair - 2)])
+        return jnp.concatenate(
+            [jnp.where(even, straight, crossed), jnp.where(even, crossed, straight)], axis=1
         )
+
+    sums = early_part(
+        row_at // 2 == 1, lambda *rest: pair_sums(1, *rest), held_rhs, far, merged
+    )
+    low = run.astype(BF)
+    arrived = next_pair(low, 2)
+    arrived, sums = lax.optimization_barrier((arrived, sums))
+    low, _ = lax.optimization_barrier((low, arrived))
+    swapped = lax.ppermute(low, "row", [(4, 5), (5, 4)])
+    both = jnp.where(
+        even, jnp.concatenate([low, swapped], axis=1), jnp.concatenate([swapped, low], axis=1)
+    )
+    both = lax.ppermute(both, "row", [(4, 0), (5, 1)])
+    run = take_turn(row_at // 2 == 1, run, late_part(arrived, merged, 2, sums, width, -1))
+    sums = early_part(
+        row_at < 2,
+        lambda *rest: pair_sums(0, *rest),
+        held_rhs,
+        jnp.concatenate([both, farther], axis=1),
+        merged,
+    )
+    arrived = next_pair(run.astype(BF), 1)
+    arrived, sums = lax.optimization_barrier((arrived, sums))
+    partial = sums - dot_nn(arrived, blocks(merged, 2, 2))
 
     def gather_rhs(run, partial):
         done = exchange(run.astype(BF).reshape(n_col, rhs_here, width), "col")
@@ -232,7 +325,7 @@
         return lax.optimization_barrier(jnp.sum(tiles.astype(F32), axis=0))
 
     root_solution = lax.cond(
-        row_at < 2, finish, gather_rhs, run, partial_sum(known, 0).astype(BF)
+        row_at < 2, finish, gather_rhs, run, partial.astype(BF)
     )
 
     take = (block_rows[:, None] == root_rows.reshape(-1)[None, :]).astype(BF)

time: 308 us -> 322 us (1.045)
  Pallas kernels: 22.8 us -> 35.8 us
  matrix products: 27.8 us -> 16.8 us
  starting transfers between devices: 38.7 us -> 44.6 us
  local copies, waits for them, and re-layouts: 26.8 us -> 21.3 us
  waiting for transfers between devices: 129 us -> 134 us
  other arithmetic: 3.9 us -> 8.19 us
    pallas_call x0 -> x9, Pallas kernels: none -> 12.9 us  [late_part(): pl.pallas_call(functools.partial(late_kernel, sign), grid=(chunks,), in_s...]
    dot_general x15 -> x8, matrix products: 22.2 us -> 11.2 us  [dot_nn(): lax.dot_general(a, b, (((1,), (0,)), ((), ())), preferred_element_type=F32)]
    ppermute x16 -> x25, waiting for transfers between devices: 91 us -> 102 us  [the longest x2 94.7 us: next_pair(): lax.ppermute(low, 'row', [(2 * pair, 2 * pair - 2), (2 * pair + 1, 2 * pa...]
    slice x5 -> x0, local copies, waits for them, and re-layouts: 10.6 us -> none  [on_device(): partial = dot_nn(arrived, factor[:(j + 1) * width])]
    ppermute x16 -> x25, starting transfers between devices: 13.8 us -> 21 us  [the longest x6 5.24 us: on_device(): arrived = lax.ppermute(low, 'row', [(j, j + 1)])]
    unnamed x12 -> x32, local copies, waits for them, and re-layouts: 7.6 us -> 12.8 us
    all_gather x1, waiting for transfers between devices: 19.2 us -> 14 us  [on_device(): whole = lax.all_gather(held, 'col', axis=0, tiled=True)]
  transfers between devices with their start and end apart: 25 -> 34, of which waited for: 9 -> 10; matrix products, arithmetic and copies ran while one was open for 12% -> 7% of each run, Pallas kernels for 7% -> 11%
where the time goes in v7:
time: 322 us; the launch traced here: 320 us
  waiting for transfers between devices  134 us (42%)
  starting transfers between devices  44.6 us (14%)
  blocking collectives  42.5 us (13%)
  Pallas kernels  35.8 us (11%)
  local copies, waits for them, and re-layouts  21.3 us (7%)
  matrix products  16.8 us (5%)
  between operations  15.7 us (5%)
  other arithmetic  8.19 us (3%)
    ppermute x2, waiting for transfers between devices, next_pair(): lax.ppermute(low, 'row', [(2 * pair, 2 * pair - 2), (2 * pair + 1, 2 * pa...  94.7 us
    all_to_all x3, blocking collectives, exchange(): return lax.all_to_all(x, axis, 0, 0, tiled=True)  42.5 us
    pallas_call x2, Pallas kernels, chunked(): pl.pallas_call(kernel, grid_spec=grid_spec, out_shape=jax.ShapeDtypeStruc...  22.8 us
    all_gather x1, waiting for transfers between devices, on_device(): whole = lax.all_gather(held, 'col', axis=0, tiled=True)  14 us
    pallas_call x9, Pallas kernels, late_part(): pl.pallas_call(functools.partial(late_kernel, sign), grid=(chunks,), in_s...  12.9 us
    unnamed x32, local copies, waits for them, and re-layouts  12.8 us
    dot_general x8, matrix products, dot_nn(): lax.dot_general(a, b, (((1,), (0,)), ((), ())), preferred_element_type=F32)  11.2 us
    all_to_all x2, starting transfers between devices, exchange(): return lax.all_to_all(x, axis, 0, 0, tiled=True)  10.7 us
  transfers between devices with their start and end apart: 34, of which 10 were waited for; matrix products, arithmetic and copies ran while one was open for 7% of the time, Pallas kernels for 11%

profile of v7, /device:TPU:1, one launch (start us, length us, event | category | flops | bytes accessed | tf_op | source)
XLA Modules:
  0.0 319.8 jit_solution(11244203705843954543)
XLA Ops:
  7.2 6.7 %copy.12 = bf16[2048,8,128]{0,2,1:T(8,128)(2,1)} copy(bf16[2048,8,128]{2,1,0:T(8,128)(2,1)} %param.63) | data formatting | bytes 8388608 | tf_op args[7]
  21.3 5.7 %fusion.29 = f32[8,2048]{1,0:T(8,128)S(1)} fusion(bf16[1,2048,2048]{2,1,0:T(8,128)(2,1)} %param.57, bf16[1,8,2048]{2,1,0:T(8,128)(2,1)S(1)} %copy-done.9), kind=kOutput, calls=%fused_computation.43 | convolution fusion | flops 67108864 | bytes 8486912 | tf_op jit(solution)/shard_map/dot_general | solution.py:16
  27.9 5.2 %all-to-all-start.12 = ((bf16[8,8,128]{2,1,0:T(8,128)(2,1)}), bf16[8,8,128]{2,1,0:T(8,128)(2,1)S(1)}, u32[]{:S(2)}, u32[]{:S(2)}) async-start(bf16[8,8,128]{2,1,0:T(8,128)(2,1)} %broadcast_in_dim.33), calls=%async_computation.12 | async-start | bytes 32768 | tf_op jit(solution)/shard_map/all_to_all | solution.py:24
  33.1 4.6 %all-to-all-done.12 = bf16[8,8,128]{2,1,0:T(8,128)(2,1)S(1)} async-done(((bf16[8,8,128]{2,1,0:T(8,128)(2,1)}), bf16[8,8,128]{2,1,0:T(8,128)(2,1)S(1)}, u32[]{:S(2)}, u32[]{:S(2)}) %all-to-all-start.12) | async-done | bytes 16416 | tf_op jit(solution)/shard_map/all_to_all | solution.py:24
  39.2 14.0 %all_to_all.75 = f32[16,8,128]{2,1,0:T(8,128)S(1)} all-to-all(f32[16,8,128]{2,1,0:T(8,128)S(1)} %fusion.45), channel_id=1, replica_groups=mesh['row'=8,'col'=16] {'col'}, dimensions={0} | all-to-all | bytes 131072 | tf_op jit(solution)/shard_map/all_to_all | solution.py:24
  55.2 4.4 %collective-permute-done.2 = bf16[128,128]{1,0:T(8,128)(2,1)S(1)} collective-permute-done((bf16[128,128]{1,0:T(8,128)(2,1)S(1)}, bf16[128,128]{1,0:T(8,128)(2,1)S(1)}, u32[]{:S(2)}, u32[]{:S(2)}) %collective-permute-start.2) | collective-permute-done | bytes 32800 | tf_op jit(solution)/shard_map/ppermute | solution.py:183
  61.3 15.5 %conditional.30 = (f32[128,128]{1,0:T(8,128)S(1)}) conditional(s32[]{:T(128)} %convert_element_type.171, f32[128,128]{1,0:T(8,128)S(1)} %bitcast.85, (bf16[16,128,128]{2,1,0:T(8,128)(2,1)S(1)}, f32[128,128]{1,0:T(8,128)S(1)}) %tuple.288), branch_computations={%region_2.3_spmd, %region_3.5_spmd} | conditional | flops 524288 | bytes 1835016 | solution.py:170
  61.3 15.4 %all_to_all.63 = bf16[16,128,128]{2,1,0:T(8,128)(2,1)S(1)} all-to-all(bf16[16,128,128]{2,1,0:T(8,128)(2,1)S(1)} %get-tuple-element.203), channel_id=1, replica_groups=mesh['row'=8,'col'=16] {'col'}, dimensions={0} | all-to-all | bytes 1048576 | tf_op jit(solution)/shard_map/cond/branch_1_fun/all_to_all | solution.py:24
  100.5 1.9 collective-permute-start.19
  102.4 14.0 %all-gather.2.cloned.1.call-done.right_ref = bf16[2048,3072]{1,0:T(8,128)(2,1)} async-done(((bf16[128,3072]{1,0:T(8,128)(2,1)}), bf16[2048,3072]{1,0:T(8,128)(2,1)}) %all-gather.2.cloned.1.call-update) | async-done | bytes 12582928 | tf_op jit(solution)/shard_map/all_gather | solution.py:150
  116.4 14.7 %shard_map.100.weight_ref = bf16[1024,2048]{1,0:T(8,128)(2,1)} custom-call(s32[2]{0:T(128)S(1)} %pad_add_fusion.at_ref, bf16[2048,3072]{1,0:T(8,128)(2,1)} %all-gather.2.cloned.1.call-done.right_ref, bf16[1024,2048]{1,0:T(8,128)(2,1)} %bitcast.84), custom_call_target="tpu_custom_call" | custom-call | tf_op jit(solution)/shard_map/pallas_call | solution.py:89
  132.2 29.0 %conditional.40 = (bf16[1024,2048]{1,0:T(8,128)(2,1)}) conditional(s32[]{:T(128)} %convert_element_type.182, () %tuple.199, (pred[]{:T(512)}, bf16[1024,2048]{1,0:T(8,128)(2,1)}, s32[2]{0:T(128)S(1)}, bf16[2048,3072]{1,0:T(8,128)(2,1)}) %tuple.202), branch_computations={%region_28.29_spmd, %region_29.34_spmd} | conditional | flops 1 | bytes 33554620 | solution.py:235
  132.2 4.7 %collective-permute-start = (bf16[1024,2048]{1,0:T(8,128)(2,1)}, bf16[1024,2048]{1,0:T(8,128)(2,1)}, u32[]{:S(2)}, u32[]{:S(2)}) collective-permute-start(bf16[1024,2048]{1,0:T(8,128)(2,1)} %get-tuple-element.234), channel_id=1, source_target_pairs={{16,0},{48,32},{80,64},{17,1},{49,33},{81,65},{18,2},{50,34},{82,6... | collective-permute-start | bytes 12582920 | tf_op jit(solution)/shard_map/cond/branch_1_fun/ppermute | solution.py:207
  137.0 5.1 %collective-permute-done = bf16[1024,2048]{1,0:T(8,128)(2,1)} collective-permute-done((bf16[1024,2048]{1,0:T(8,128)(2,1)}, bf16[1024,2048]{1,0:T(8,128)(2,1)}, u32[]{:S(2)}, u32[]{:S(2)}) %collective-permute-start) | collective-permute-done | bytes 4194336 | tf_op jit(solution)/shard_map/cond/branch_1_fun/ppermute | solution.py:207
  142.1 8.2 %conditional.2 = (bf16[1024,1024]{1,0:T(8,128)(2,1)S(1)}) conditional(s32[]{:T(128)} %convert_element_type.122, (s32[2]{0:T(128)S(1)}, bf16[2048,3072]{1,0:T(8,128)(2,1)}, bf16[1024,2048]{1,0:T(8,128)(2,1)}) %tuple.129, (s32[2]{0:T(128)S(1)}, bf16[2048,3072]{1,0:T(8,128)(2,1)}, bf16[1024,2048]{1,0:T(8,128)(2,1)}) %tuple.130), branch_computations={%region_30.30_spmd, %region_31.31_spmd} | conditional | bytes 8 | solution.py:212
  142.1 8.1 %branch_0_fun.1 = bf16[1024,1024]{1,0:T(8,128)(2,1)S(1)} custom-call(s32[2]{0:T(128)S(1)} %get-tuple-element.222.at_ref, bf16[2048,3072]{1,0:T(8,128)(2,1)} %get-tuple-element.223.right_ref, bf16[1024,2048]{1,0:T(8,128)(2,1)} %get-tuple-element.224.left_ref), custom_call_target="tpu_custom_call" | custom-call | tf_op jit(solution)/shard_map/cond/branch_1_fun/cond/branch_0_fun/pallas_call | solution.py:89
  150.2 3.6 %collective-permute-start.1 = (bf16[1024,1024]{1,0:T(8,128)(2,1)S(1)}, bf16[1024,1024]{1,0:T(8,128)(2,1)}, u32[]{:S(2)}, u32[]{:S(2)}) collective-permute-start(bf16[1024,1024]{1,0:T(8,128)(2,1)S(1)} %get-tuple-element.330), channel_id=1, source_target_pairs={{16,0},{48,32},{80,64},{17,1},{49,33},{81,65},{18,2},{50,34},{82,6... | collective-permute-start | bytes 6291464 | tf_op jit(solution)/shard_map/cond/branch_1_fun/ppermute | solution.py:213
  153.9 2.5 collective-permute-done.1
  156.4 4.8 %conditional.6 = (bf16[1024,2048]{1,0:T(8,128)(2,1)}) conditional(s32[]{:T(128)} %convert_element_type.122, bf16[1024,2048]{1,0:T(8,128)(2,1)} %get-tuple-element.234, (s32[2]{0:T(128)S(1)}, bf16[2048,3072]{1,0:T(8,128)(2,1)}, bf16[1024,1024]{1,0:T(8,128)(2,1)S(1)}, bf16[1024,1024]{1,0:T(8,128)(2,1)}, bf16[1024,2048]{1,0:T(8,128)(2,1)}) %tuple.131), branch_computations={%region_32.32_spmd, %region_33.33_spmd} | conditional | bytes 8388616 | solution.py:219
  156.4 4.8 %copy.19 = bf16[1024,2048]{1,0:T(8,128)(2,1)} copy(bf16[1024,2048]{1,0:T(8,128)(2,1)} %param.25) | data formatting | bytes 8388608 | tf_op jit(solution)/shard_map/cond/branch_1_fun/cond
  177.4 1.6 shard_map.104
  183.0 94.7 %collective-permute-done.26 = bf16[128,128]{1,0:T(8,128)(2,1)S(1)} collective-permute-done((bf16[128,128]{1,0:T(8,128)(2,1)S(1)}, bf16[128,128]{1,0:T(8,128)(2,1)S(1)}, u32[]{:S(2)}, u32[]{:S(2)}) %collective-permute-start.26) | collective-permute-done | bytes 32800 | tf_op jit(solution)/shard_map/ppermute | solution.py:288
  277.7 2.0 collective-permute-done.27
  279.7 3.9 %conditional.49 = (f32[128,2048]{1,0:T(8,128)S(1)}) conditional(s32[]{:T(128)} %convert_element_type.162, () %tuple.216, (bf16[1024,2048]{1,0:T(8,128)(2,1)}, bf16[128,256]{1,0:T(8,128)(2,1)S(1)}, bf16[128,512]{1,0:T(8,128)(2,1)S(1)}) %tuple.218), branch_computations={%region_54.55_spmd, %region_55.56_spmd} | conditional | flops 402915328 | bytes 6488072 | solution.py:173
  280.0 1.5 fusion.27
  281.5 2.1 convolution_subtract_fusion.2
  283.6 1.5 fusion.39
  285.1 14.8 %conditional.51 = (f32[8,2048]{1,0:T(8,128)}, f32[8,2048]{1,0:T(8,128)S(1)}) conditional(s32[]{:T(128)} %convert_element_type.162, f32[128,128]{1,0:T(8,128)S(1)} %get-tuple-element.351, bf16[128,2048]{1,0:T(8,128)(2,1)S(1)} %fusion.39), branch_computations={%region_56.57_spmd, %region_57.59_spmd} | conditional | flops 507904 | bytes 1769488
  285.2 13.2 %all_to_all.74 = bf16[16,8,2048]{2,1,0:T(8,128)(2,1)S(1)} all-to-all(bf16[16,8,2048]{2,1,0:T(8,128)(2,1)S(1)} %bitcast.88), channel_id=1, replica_groups=mesh['row'=8,'col'=16] {'col'}, dimensions={0} | all-to-all | bytes 1048576 | tf_op jit(solution)/shard_map/cond/branch_1_fun/all_to_all | solution.py:24
  299.9 2.0 fusion.51
  301.9 5.5 %all-to-all-start.14 = ((bf16[8,8,128]{2,1,0:T(8,128)(2,1)}), bf16[8,8,128]{2,1,0:T(8,128)(2,1)S(1)}, u32[]{:S(2)}, u32[]{:S(2)}) async-start(bf16[8,8,128]{2,1,0:T(8,128)(2,1)} %fusion.51), calls=%async_computation.14 | async-start | bytes 32768 | tf_op jit(solution)/shard_map/all_to_all | solution.py:24
  307.5 4.7 %all-to-all-done.14 = bf16[8,8,128]{2,1,0:T(8,128)(2,1)S(1)} async-done(((bf16[8,8,128]{2,1,0:T(8,128)(2,1)}), bf16[8,8,128]{2,1,0:T(8,128)(2,1)S(1)}, u32[]{:S(2)}, u32[]{:S(2)}) %all-to-all-start.14) | async-done | bytes 16416 | tf_op jit(solution)/shard_map/all_to_all | solution.py:24
  (166 shorter events, 60.3 us)
Async XLA Ops:
  7.2 109.3 %all-gather.2.cloned.1.call-start = ((), (), s32[]{:S(2)}) async-start(), calls=%async_computation.15 | async-start | bytes 13369344 | tf_op jit(solution)/shard_map/all_gather | solution.py:150
  14.9 3.7 %collective-permute-start.14 = (bf16[128,1024]{1,0:T(8,128)(2,1)S(1)}, bf16[128,1024]{1,0:T(8,128)(2,1)S(1)}, u32[]{:S(2)}, u32[]{:S(2)}) collective-permute-start(bf16[128,1024]{1,0:T(8,128)(2,1)S(1)} %dynamic-slice.1), channel_id=1, source_target_pairs={{0,16},{32,48},{64,80},{96,112},{1,17},{33,49},{65,81},{97,113},{2... | collective-permute-start | bytes 786440 | tf_op jit(solution)/shard_map/ppermute | solution.py:148
  27.9 9.8 %all-to-all-start.12 = ((bf16[8,8,128]{2,1,0:T(8,128)(2,1)}), bf16[8,8,128]{2,1,0:T(8,128)(2,1)S(1)}, u32[]{:S(2)}, u32[]{:S(2)}) async-start(bf16[8,8,128]{2,1,0:T(8,128)(2,1)} %broadcast_in_dim.33), calls=%async_computation.12 | async-start | bytes 32768 | tf_op jit(solution)/shard_map/all_to_all | solution.py:24
  53.1 2.0 collective-permute-start.3
  53.8 5.9 %collective-permute-start.2 = (bf16[128,128]{1,0:T(8,128)(2,1)S(1)}, bf16[128,128]{1,0:T(8,128)(2,1)S(1)}, u32[]{:S(2)}, u32[]{:S(2)}) collective-permute-start(bf16[128,128]{1,0:T(8,128)(2,1)S(1)} %bitcast_convert_fusion), channel_id=1, source_target_pairs={{0,16},{1,17},{2,18},{3,19},{4,20},{5,21},{6,22},{7,23},{8,24},{9,... | collective-permute-start | bytes 98312 | tf_op jit(solution)/shard_map/ppermute | solution.py:183
  76.8 2.6 collective-permute-start.5
  78.1 2.3 collective-permute-start.4
  83.3 1.4 collective-permute-start.7
  83.9 0.8 collective-permute-start.6
  87.6 1.4 collective-permute-start.9
  88.3 0.8 collective-permute-start.8
  92.0 1.4 collective-permute-start.11
  92.6 0.8 collective-permute-start.10
  96.3 64.9 %collective-permute-start.15 = (bf16[128,768]{1,0:T(8,128)(2,1)S(1)}, bf16[128,768]{1,0:T(8,128)(2,1)S(1)}, u32[]{:S(2)}, u32[]{:S(2)}) collective-permute-start(bf16[128,768]{1,0:T(8,128)(2,1)S(1)} %pad_maximum_fusion.1), channel_id=1, source_target_pairs={{80,112},{81,113},{82,114},{83,115},{84,116},{85,117},{86,118},{87... | collective-permute-start | bytes 589832 | tf_op jit(solution)/shard_map/ppermute | solution.py:185
  99.8 61.6 %collective-permute-start.13 = (bf16[128,128]{1,0:T(8,128)(2,1)S(1)}, bf16[128,128]{1,0:T(8,128)(2,1)S(1)}, u32[]{:S(2)}, u32[]{:S(2)}) collective-permute-start(bf16[128,128]{1,0:T(8,128)(2,1)S(1)} %convert_element_type.181), channel_id=1, source_target_pairs={{96,112},{97,113},{98,114},{99,115},{100,116},{101,117},{102,118},... | collective-permute-start | bytes 98312 | tf_op jit(solution)/shard_map/ppermute | solution.py:230
  100.5 63.6 %collective-permute-start.19 = (bf16[128,128]{1,0:T(8,128)(2,1)S(1)}, bf16[128,128]{1,0:T(8,128)(2,1)}, u32[]{:S(2)}, u32[]{:S(2)}) collective-permute-start(bf16[128,128]{1,0:T(8,128)(2,1)S(1)} %convert_element_type.181), channel_id=1, source_target_pairs={{16,0},{48,32},{80,64},{17,1},{49,33},{81,65},{18,2},{50,34},{82,6... | collective-permute-start | bytes 98312 | tf_op jit(solution)/shard_map/ppermute | solution.py:231
  132.2 9.9 %collective-permute-start = (bf16[1024,2048]{1,0:T(8,128)(2,1)}, bf16[1024,2048]{1,0:T(8,128)(2,1)}, u32[]{:S(2)}, u32[]{:S(2)}) collective-permute-start(bf16[1024,2048]{1,0:T(8,128)(2,1)} %get-tuple-element.234), channel_id=1, source_target_pairs={{16,0},{48,32},{80,64},{17,1},{49,33},{81,65},{18,2},{50,34},{82,6... | collective-permute-start | bytes 12582920 | tf_op jit(solution)/shard_map/cond/branch_1_fun/ppermute | solution.py:207
  150.2 6.2 %collective-permute-start.1 = (bf16[1024,1024]{1,0:T(8,128)(2,1)S(1)}, bf16[1024,1024]{1,0:T(8,128)(2,1)}, u32[]{:S(2)}, u32[]{:S(2)}) collective-permute-start(bf16[1024,1024]{1,0:T(8,128)(2,1)S(1)} %get-tuple-element.330), channel_id=1, source_target_pairs={{16,0},{48,32},{80,64},{17,1},{49,33},{81,65},{18,2},{50,34},{82,6... | collective-permute-start | bytes 6291464 | tf_op jit(solution)/shard_map/cond/branch_1_fun/ppermute | solution.py:213
  163.4 1.5 collective-permute-start.16
  166.9 2.9 collective-permute-start.17
  167.6 2.2 collective-permute-start.18
  168.3 1.4 collective-permute-start.20
  170.5 3.5 %collective-permute-start.24 = (bf16[128,128]{1,0:T(8,128)(2,1)S(1)}, bf16[128,128]{1,0:T(8,128)(2,1)S(1)}, u32[]{:S(2)}, u32[]{:S(2)}) collective-permute-start(bf16[128,128]{1,0:T(8,128)(2,1)S(1)} %convert_element_type.184), channel_id=1, source_target_pairs={{96,112},{97,113},{98,114},{99,115},{100,116},{101,117},{102,118},... | collective-permute-start | bytes 98312 | tf_op jit(solution)/shard_map/ppermute | solution.py:279
  172.6 2.1 collective-permute-start.22
  173.3 1.4 collective-permute-start.23
  174.0 1.4 collective-permute-start.25
  175.5 6.2 %collective-permute-start.28 = (bf16[128,128]{1,0:T(8,128)(2,1)S(1)}, bf16[128,128]{1,0:T(8,128)(2,1)S(1)}, u32[]{:S(2)}, u32[]{:S(2)}) collective-permute-start(bf16[128,128]{1,0:T(8,128)(2,1)S(1)} %convert_element_type.185), channel_id=1, source_target_pairs={{64,80},{80,64},{65,81},{81,65},{66,82},{82,66},{67,83},{83,67},{6... | collective-permute-start | bytes 98312 | tf_op jit(solution)/shard_map/ppermute | solution.py:301
  176.1 103.6 %collective-permute-start.30 = (bf16[128,256]{1,0:T(8,128)(2,1)S(1)}, bf16[128,256]{1,0:T(8,128)(2,1)S(1)}, u32[]{:S(2)}, u32[]{:S(2)}) collective-permute-start(bf16[128,256]{1,0:T(8,128)(2,1)S(1)} %maximum_select_fusion.1), channel_id=1, source_target_pairs={{96,0},{112,16},{97,1},{113,17},{98,2},{114,18},{99,3},{115,19},{1... | collective-permute-start | bytes 196616 | tf_op jit(solution)/shard_map/ppermute | solution.py:282
  179.0 98.6 %collective-permute-start.26 = (bf16[128,128]{1,0:T(8,128)(2,1)S(1)}, bf16[128,128]{1,0:T(8,128)(2,1)S(1)}, u32[]{:S(2)}, u32[]{:S(2)}) collective-permute-start(bf16[128,128]{1,0:T(8,128)(2,1)S(1)} %convert_element_type.186), channel_id=1, source_target_pairs={{32,0},{48,16},{33,1},{49,17},{34,2},{50,18},{35,3},{51,19},{36,4}... | collective-permute-start | bytes 98312 | tf_op jit(solution)/shard_map/ppermute | solution.py:288
  180.3 99.3 %collective-permute-start.27 = (bf16[128,128]{1,0:T(8,128)(2,1)S(1)}, bf16[128,128]{1,0:T(8,128)(2,1)S(1)}, u32[]{:S(2)}, u32[]{:S(2)}) collective-permute-start(bf16[128,128]{1,0:T(8,128)(2,1)S(1)} %convert_element_type.186), channel_id=1, source_target_pairs={{32,16},{48,0},{33,17},{49,1},{34,18},{50,2},{35,19},{51,3},{36,20... | collective-permute-start | bytes 98312 | tf_op jit(solution)/shard_map/ppermute | solution.py:289
  181.7 98.0 %collective-permute-start.29 = (bf16[128,256]{1,0:T(8,128)(2,1)S(1)}, bf16[128,256]{1,0:T(8,128)(2,1)S(1)}, u32[]{:S(2)}, u32[]{:S(2)}) collective-permute-start(bf16[128,256]{1,0:T(8,128)(2,1)S(1)} %maximum_select_fusion.2), channel_id=1, source_target_pairs={{64,0},{80,16},{65,1},{81,17},{66,2},{82,18},{67,3},{83,19},{68,4}... | collective-permute-start | bytes 196616 | tf_op jit(solution)/shard_map/ppermute | solution.py:305
  301.9 10.2 %all-to-all-start.14 = ((bf16[8,8,128]{2,1,0:T(8,128)(2,1)}), bf16[8,8,128]{2,1,0:T(8,128)(2,1)S(1)}, u32[]{:S(2)}, u32[]{:S(2)}) async-start(bf16[8,8,128]{2,1,0:T(8,128)(2,1)} %fusion.51), calls=%async_computation.14 | async-start | bytes 32768 | tf_op jit(solution)/shard_map/all_to_all | solution.py:24
  (17 other events, 367.6 us)
Sparse Core Ops, SparseCore 0:
  20.7 95.6 all-gather.1

commit v8 on v6

--- a/solution.py
+++ b/solution.py
@@ -142,11 +142,21 @@
 
         return lax.cond(turn, reduce_columns, lambda run, tiles: run, run, tiles_of(partial))
 
+    def take_whole_turn(turn, run, sign, *operands):
+        def reduce_columns(run, x, weights):
+            total = jnp.sum(exchange(tiles_of(dot_nn(x, weights)), "col").astype(F32), axis=0)
+            return run - total if sign else total
+
+        return lax.cond(turn, reduce_columns, lambda run, *rest: run, run, *operands)
+
     known = run.astype(BF)
     for j in range(last - 1):
         arrived = lax.ppermute(known, "row", [(j, j + 1)])
-        partial = dot_nn(arrived, factor[: (j + 1) * width])
-        run = take_turn(row_at == j + 1, run, partial, -1)
+        if j < last - 2:
+            partial = dot_nn(arrived, factor[: (j + 1) * width])
+            run = take_turn(row_at == j + 1, run, partial, -1)
+        else:
+            run = take_whole_turn(row_at == j + 1, run, -1, arrived, factor[: (j + 1) * width])
         known = jnp.concatenate([arrived, run.astype(BF)], axis=1)
         if j == last - 4:
             held, _ = lax.optimization_barrier((factor, known))
@@ -194,18 +204,33 @@
     )
     arrived, merged = lax.optimization_barrier((arrived, merged))
 
-    partial = dot_nn(jnp.concatenate([-arrived, low], axis=1), folded)
-    run = take_turn(row_at == last, run, partial)
+    run = take_whole_turn(
+        row_at == last, run, 0, jnp.concatenate([-arrived, low], axis=1), folded
+    )
     seventh = run.astype(BF)
     arrived = lax.ppermute(seventh, "row", [(last, last - 1)])
     early = lax.ppermute(seventh, "row", [(last, last - 2)])
     early += lax.ppermute(seventh, "row", [(last, last - 3)])
-    partial = dot_nn(jnp.concatenate([low, -arrived], axis=1), folded[(last - 1) * width :])
-    run = take_turn(row_at == last - 1, run, partial)
+    run = take_whole_turn(
+        row_at == last - 1,
+        run,
+        0,
+        jnp.concatenate([low, -arrived], axis=1),
+        folded[(last - 1) * width :],
+    )
     sixth = run.astype(BF)
-    arrived = lax.ppermute(sixth, "row", [(last - 1, last - 3)])
-    arrived += lax.ppermute(sixth, "row", [(last - 1, last - 2)])
-    known = jnp.concatenate([arrived, early], axis=1)
+    newest = lax.ppermute(sixth, "row", [(last - 1, last - 3)])
+    newest += lax.ppermute(sixth, "row", [(last - 1, last - 2)])
+    known = jnp.concatenate([newest, early], axis=1)
+
+    swapped = lax.ppermute(sixth, "row", [(last - 1, last)])
+    both = jnp.where(
+        even,
+        jnp.concatenate([sixth, arrived], axis=1),
+        jnp.concatenate([swapped, seventh], axis=1),
+    )
+    far = lax.ppermute(both, "row", [(6, 2), (7, 3)])
+    farther = lax.ppermute(both, "row", [(6, 0), (7, 1)])
 
     def partial_sum(known, pair):
         return dot_nn(jnp.concatenate([held_rhs, -known], axis=1), merged[2 * pair * width :])
@@ -217,10 +242,17 @@
         cross = [(2 * pair, 2 * pair - 1), (2 * pair + 1, 2 * pair - 2)]
         straight = lax.ppermute(low, "row", same)
         crossed = lax.ppermute(low, "row", cross)
-        older = lax.ppermute(known, "row", same)
-        known = jnp.concatenate(
-            [jnp.where(even, straight, crossed), jnp.where(even, crossed, straight), older], axis=1
-        )
+        newest = [jnp.where(even, straight, crossed), jnp.where(even, crossed, straight)]
+        known = jnp.concatenate(newest + [far], axis=1)
+        if pair == 2:
+            swapped = lax.ppermute(low, "row", [(4, 5), (5, 4)])
+            both = jnp.where(
+                even,
+                jnp.concatenate([low, swapped], axis=1),
+                jnp.concatenate([swapped, low], axis=1),
+            )
+            both = lax.ppermute(both, "row", [(4, 0), (5, 1)])
+            far = jnp.concatenate([both, farther], axis=1)
 
     def gather_rhs(run, partial):
         done = exchange(run.astype(BF).reshape(n_col, rhs_here, width), "col")

time: 308 us -> 303 us (0.984)
  matrix products: 27.8 us -> 20.8 us
  waiting for transfers between devices: 129 us -> 134 us
  local copies, waits for them, and re-layouts: 26.8 us -> 22.4 us
    dot_general x15 -> x12, matrix products: 22.2 us -> 15.1 us  [dot_nn(): lax.dot_general(a, b, (((1,), (0,)), ((), ())), preferred_element_type=F32)]
    all_gather x1, waiting for transfers between devices: 19.2 us -> 26 us  [on_device(): whole = lax.all_gather(held, 'col', axis=0, tiled=True)]
    slice x5 -> x4, local copies, waits for them, and re-layouts: 10.6 us -> 6.5 us  [on_device(): partial = dot_nn(arrived, factor[:(j + 1) * width])]
  transfers between devices with their start and end apart: 25 -> 28, of which waited for: 9 -> 9; matrix products, arithmetic and copies ran while one was open for 12% -> 10% of each run, Pallas kernels for 7% -> 8%
where the time goes in v8:
time: 303 us; the launch traced here: 301 us
  waiting for transfers between devices  134 us (44%)
  blocking collectives  43.1 us (14%)
  starting transfers between devices  39.1 us (13%)
  Pallas kernels  22.8 us (8%)
  local copies, waits for them, and re-layouts  22.4 us (7%)
  matrix products  20.8 us (7%)
  between operations  15.6 us (5%)
  other arithmetic  4.02 us (1%)
    ppermute x2, waiting for transfers between devices, on_device(): straight = lax.ppermute(low, 'row', same)  82.7 us
    all_to_all x3, blocking collectives, exchange(): return lax.all_to_all(x, axis, 0, 0, tiled=True)  43.1 us
    all_gather x1, waiting for transfers between devices, on_device(): whole = lax.all_gather(held, 'col', axis=0, tiled=True)  26 us
    pallas_call x2, Pallas kernels, chunked(): pl.pallas_call(kernel, grid_spec=grid_spec, out_shape=jax.ShapeDtypeStruc...  22.8 us
    dot_general x12, matrix products, dot_nn(): lax.dot_general(a, b, (((1,), (0,)), ((), ())), preferred_element_type=F32)  15.1 us
    all_to_all x2, starting transfers between devices, exchange(): return lax.all_to_all(x, axis, 0, 0, tiled=True)  10.3 us
    all_to_all x2, waiting for transfers between devices, exchange(): return lax.all_to_all(x, axis, 0, 0, tiled=True)  9.31 us
    unnamed x12, local copies, waits for them, and re-layouts  7.59 us
  transfers between devices with their start and end apart: 28, of which 9 were waited for; matrix products, arithmetic and copies ran while one was open for 10% of the time, Pallas kernels for 8%

profile of v8, /device:TPU:1, one launch (start us, length us, event | category | flops | bytes accessed | tf_op | source)
XLA Modules:
  0.0 301.5 jit_solution(2300946155380029622)
XLA Ops:
  7.2 6.7 %copy.21 = bf16[2048,8,128]{0,2,1:T(8,128)(2,1)} copy(bf16[2048,8,128]{2,1,0:T(8,128)(2,1)} %param.43) | data formatting | bytes 8388608 | tf_op args[7]
  21.4 5.7 %fusion.4 = f32[8,2048]{1,0:T(8,128)S(1)} fusion(bf16[1,2048,2048]{2,1,0:T(8,128)(2,1)} %param.37, bf16[1,8,2048]{2,1,0:T(8,128)(2,1)S(1)} %copy-done.1), kind=kOutput, calls=%fused_computation.23 | convolution fusion | flops 67108864 | bytes 8486912 | tf_op jit(solution)/shard_map/dot_general | solution.py:14
  28.0 5.2 %all-to-all-start.12 = ((bf16[8,8,128]{2,1,0:T(8,128)(2,1)}), bf16[8,8,128]{2,1,0:T(8,128)(2,1)S(1)}, u32[]{:S(2)}, u32[]{:S(2)}) async-start(bf16[8,8,128]{2,1,0:T(8,128)(2,1)} %broadcast_in_dim.33), calls=%async_computation.12 | async-start | bytes 32768 | tf_op jit(solution)/shard_map/all_to_all | solution.py:22
  33.2 4.6 %all-to-all-done.12 = bf16[8,8,128]{2,1,0:T(8,128)(2,1)S(1)} async-done(((bf16[8,8,128]{2,1,0:T(8,128)(2,1)}), bf16[8,8,128]{2,1,0:T(8,128)(2,1)S(1)}, u32[]{:S(2)}, u32[]{:S(2)}) %all-to-all-start.12) | async-done | bytes 16416 | tf_op jit(solution)/shard_map/all_to_all | solution.py:22
  39.2 14.0 %all_to_all.75 = f32[16,8,128]{2,1,0:T(8,128)S(1)} all-to-all(f32[16,8,128]{2,1,0:T(8,128)S(1)} %fusion.35), channel_id=1, replica_groups=mesh['row'=8,'col'=16] {'col'}, dimensions={0} | all-to-all | bytes 131072 | tf_op jit(solution)/shard_map/all_to_all | solution.py:22
  54.5 2.7 collective-permute-done.2
  58.7 15.6 %conditional.19 = (f32[128,128]{1,0:T(8,128)S(1)}) conditional(s32[]{:T(128)} %convert_element_type.189, f32[128,128]{1,0:T(8,128)S(1)} %bitcast.157, (bf16[16,128,128]{2,1,0:T(8,128)(2,1)S(1)}, f32[128,128]{1,0:T(8,128)S(1)}) %tuple.165), branch_computations={%region_0.1_spmd, %region_1.3_spmd} | conditional | flops 524288 | bytes 1835016 | solution.py:143
  58.7 15.5 %all_to_all.63 = bf16[16,128,128]{2,1,0:T(8,128)(2,1)S(1)} all-to-all(bf16[16,128,128]{2,1,0:T(8,128)(2,1)S(1)} %get-tuple-element.128), channel_id=1, replica_groups=mesh['row'=8,'col'=16] {'col'}, dimensions={0} | all-to-all | bytes 1048576 | tf_op jit(solution)/shard_map/cond/branch_1_fun/all_to_all | solution.py:22
  78.2 1.5 slice.73
  81.1 1.7 slice.74
  84.8 1.9 slice.75
  90.5 26.0 %all-gather.2.cloned.1.call-done.right_ref = bf16[2048,3072]{1,0:T(8,128)(2,1)} async-done(((bf16[128,3072]{1,0:T(8,128)(2,1)}), bf16[2048,3072]{1,0:T(8,128)(2,1)}) %all-gather.2.cloned.1.call-update) | async-done | bytes 12582928 | tf_op jit(solution)/shard_map/all_gather | solution.py:123
  116.5 14.7 %shard_map.95 = bf16[1024,2048]{1,0:T(8,128)(2,1)} custom-call(s32[2]{0:T(128)S(1)} %pad_add_fusion.at_ref, bf16[2048,3072]{1,0:T(8,128)(2,1)} %all-gather.2.cloned.1.call-done.right_ref, bf16[1024,2048]{1,0:T(8,128)(2,1)} %bitcast.156), custom_call_target="tpu_custom_call" | custom-call | tf_op jit(solution)/shard_map/pallas_call | solution.py:87
  131.2 28.9 %conditional.25 = (bf16[1024,2048]{1,0:T(8,128)(2,1)}) conditional(s32[]{:T(128)} %convert_element_type.204, () %tuple.113, (pred[]{:T(512)}, bf16[1024,2048]{1,0:T(8,128)(2,1)}, s32[2]{0:T(128)S(1)}, bf16[2048,3072]{1,0:T(8,128)(2,1)}) %tuple.116), branch_computations={%region_18.19_spmd, %region_19.24_spmd} | conditional | flops 1 | bytes 33554620 | solution.py:197
  131.2 4.7 %collective-permute-start = (bf16[1024,2048]{1,0:T(8,128)(2,1)}, bf16[1024,2048]{1,0:T(8,128)(2,1)}, u32[]{:S(2)}, u32[]{:S(2)}) collective-permute-start(bf16[1024,2048]{1,0:T(8,128)(2,1)} %get-tuple-element.152), channel_id=1, source_target_pairs={{16,0},{48,32},{80,64},{17,1},{49,33},{81,65},{18,2},{50,34},{82,6... | collective-permute-start | bytes 12582920 | tf_op jit(solution)/shard_map/cond/branch_1_fun/ppermute | solution.py:168
  135.9 5.2 %collective-permute-done = bf16[1024,2048]{1,0:T(8,128)(2,1)} collective-permute-done((bf16[1024,2048]{1,0:T(8,128)(2,1)}, bf16[1024,2048]{1,0:T(8,128)(2,1)}, u32[]{:S(2)}, u32[]{:S(2)}) %collective-permute-start) | collective-permute-done | bytes 4194336 | tf_op jit(solution)/shard_map/cond/branch_1_fun/ppermute | solution.py:168
  141.1 8.2 %conditional.2 = (bf16[1024,1024]{1,0:T(8,128)(2,1)S(1)}) conditional(s32[]{:T(128)} %convert_element_type.132, (s32[2]{0:T(128)S(1)}, bf16[2048,3072]{1,0:T(8,128)(2,1)}, bf16[1024,2048]{1,0:T(8,128)(2,1)}) %tuple.87, (s32[2]{0:T(128)S(1)}, bf16[2048,3072]{1,0:T(8,128)(2,1)}, bf16[1024,2048]{1,0:T(8,128)(2,1)}) %tuple.88), branch_computations={%region_20.20_spmd, %region_21.21_spmd} | conditional | bytes 8 | solution.py:173
  141.1 8.1 %branch_0_fun.1 = bf16[1024,1024]{1,0:T(8,128)(2,1)S(1)} custom-call(s32[2]{0:T(128)S(1)} %get-tuple-element.140.at_ref, bf16[2048,3072]{1,0:T(8,128)(2,1)} %get-tuple-element.141.right_ref, bf16[1024,2048]{1,0:T(8,128)(2,1)} %get-tuple-element.142.left_ref), custom_call_target="tpu_custom_call" | custom-call | tf_op jit(solution)/shard_map/cond/branch_1_fun/cond/branch_0_fun/pallas_call | solution.py:87
  149.2 3.6 %collective-permute-start.1 = (bf16[1024,1024]{1,0:T(8,128)(2,1)S(1)}, bf16[1024,1024]{1,0:T(8,128)(2,1)}, u32[]{:S(2)}, u32[]{:S(2)}) collective-permute-start(bf16[1024,1024]{1,0:T(8,128)(2,1)S(1)} %get-tuple-element.198), channel_id=1, source_target_pairs={{16,0},{48,32},{80,64},{17,1},{49,33},{81,65},{18,2},{50,34},{82,6... | collective-permute-start | bytes 6291464 | tf_op jit(solution)/shard_map/cond/branch_1_fun/ppermute | solution.py:174
  152.9 2.5 collective-permute-done.1
  155.4 4.7 %conditional.6 = (bf16[1024,2048]{1,0:T(8,128)(2,1)}) conditional(s32[]{:T(128)} %convert_element_type.132, bf16[1024,2048]{1,0:T(8,128)(2,1)} %get-tuple-element.152, (s32[2]{0:T(128)S(1)}, bf16[2048,3072]{1,0:T(8,128)(2,1)}, bf16[1024,1024]{1,0:T(8,128)(2,1)S(1)}, bf16[1024,1024]{1,0:T(8,128)(2,1)}, bf16[1024,2048]{1,0:T(8,128)(2,1)}) %tuple.89), branch_computations={%region_22.22_spmd, %region_23.23_spmd} | conditional | bytes 8388616 | solution.py:180
  155.4 4.7 %copy.61 = bf16[1024,2048]{1,0:T(8,128)(2,1)} copy(bf16[1024,2048]{1,0:T(8,128)(2,1)} %param.15) | data formatting | bytes 8388608 | tf_op jit(solution)/shard_map/cond/branch_1_fun/cond
  164.5 2.0 fusion.28
  170.8 2.5 fusion.31
  177.4 82.7 %collective-permute-done.20 = bf16[128,128]{1,0:T(8,128)(2,1)S(1)} collective-permute-done((bf16[128,128]{1,0:T(8,128)(2,1)S(1)}, bf16[128,128]{1,0:T(8,128)(2,1)S(1)}, u32[]{:S(2)}, u32[]{:S(2)}) %collective-permute-start.20) | collective-permute-done | bytes 32800 | tf_op jit(solution)/shard_map/ppermute | solution.py:243
  260.1 3.8 %collective-permute-done.21 = bf16[128,128]{1,0:T(8,128)(2,1)S(1)} collective-permute-done((bf16[128,128]{1,0:T(8,128)(2,1)S(1)}, bf16[128,128]{1,0:T(8,128)(2,1)S(1)}, u32[]{:S(2)}, u32[]{:S(2)}) %collective-permute-start.21) | collective-permute-done | bytes 32800 | tf_op jit(solution)/shard_map/ppermute | solution.py:244
  263.9 2.9 convolution_convert_fusion.3
  266.9 15.2 %conditional.31 = (f32[8,2048]{1,0:T(8,128)}, f32[8,2048]{1,0:T(8,128)S(1)}) conditional(s32[]{:T(128)} %convert_element_type.180, f32[128,128]{1,0:T(8,128)S(1)} %get-tuple-element.210, bf16[128,2048]{1,0:T(8,128)(2,1)S(1)} %convolution_convert_fusion.3), branch_computations={%region_36.37_spmd, %region_37.39_spmd} | conditional | flops 507904 | bytes 1769488
  266.9 13.6 %all_to_all.74 = bf16[16,8,2048]{2,1,0:T(8,128)(2,1)S(1)} all-to-all(bf16[16,8,2048]{2,1,0:T(8,128)(2,1)S(1)} %bitcast.164), channel_id=1, replica_groups=mesh['row'=8,'col'=16] {'col'}, dimensions={0} | all-to-all | bytes 1048576 | tf_op jit(solution)/shard_map/cond/branch_1_fun/all_to_all | solution.py:22
  282.0 2.0 fusion.41
  284.0 5.1 %all-to-all-start.14 = ((bf16[8,8,128]{2,1,0:T(8,128)(2,1)}), bf16[8,8,128]{2,1,0:T(8,128)(2,1)S(1)}, u32[]{:S(2)}, u32[]{:S(2)}) async-start(bf16[8,8,128]{2,1,0:T(8,128)(2,1)} %fusion.41), calls=%async_computation.14 | async-start | bytes 32768 | tf_op jit(solution)/shard_map/all_to_all | solution.py:22
  289.1 4.7 %all-to-all-done.14 = bf16[8,8,128]{2,1,0:T(8,128)(2,1)S(1)} async-done(((bf16[8,8,128]{2,1,0:T(8,128)(2,1)}), bf16[8,8,128]{2,1,0:T(8,128)(2,1)S(1)}, u32[]{:S(2)}, u32[]{:S(2)}) %all-to-all-start.14) | async-done | bytes 16416 | tf_op jit(solution)/shard_map/all_to_all | solution.py:22
  (125 shorter events, 37.4 us)
Async XLA Ops:
  7.2 286.7 %copy-start = (bf16[1,128,2048]{2,1,0:T(8,128)(2,1)S(1)}, bf16[1,128,2048]{2,1,0:T(8,128)(2,1)}, u32[]{:S(2)}) copy-start(bf16[1,128,2048]{2,1,0:T(8,128)(2,1)} %param.38) | copy-start | bytes 1572868
  7.2 109.3 %all-gather.2.cloned.1.call-start = ((), (), s32[]{:S(2)}) async-start(), calls=%async_computation.15 | async-start | bytes 13369344 | tf_op jit(solution)/shard_map/all_gather | solution.py:123
  14.0 7.4 %copy-start.1 = (bf16[1,8,2048]{2,1,0:T(8,128)(2,1)S(1)}, bf16[1,8,2048]{2,1,0:T(8,128)(2,1)}, u32[]{:S(2)}) copy-start(bf16[1,8,2048]{2,1,0:T(8,128)(2,1)} %param.36) | copy-start | bytes 98308
  14.9 3.7 %collective-permute-start.9 = (bf16[128,1024]{1,0:T(8,128)(2,1)S(1)}, bf16[128,1024]{1,0:T(8,128)(2,1)S(1)}, u32[]{:S(2)}, u32[]{:S(2)}) collective-permute-start(bf16[128,1024]{1,0:T(8,128)(2,1)S(1)} %dynamic-slice.1), channel_id=1, source_target_pairs={{0,16},{32,48},{64,80},{96,112},{1,17},{33,49},{65,81},{97,113},{2... | collective-permute-start | bytes 786440 | tf_op jit(solution)/shard_map/ppermute | solution.py:121
  21.4 16.5 %copy-start.2 = (f32[8,2048]{1,0:T(8,128)S(1)}, f32[8,2048]{1,0:T(8,128)}, u32[]{:S(2)}) copy-start(f32[8,2048]{1,0:T(8,128)} %param.42) | copy-start | bytes 196612
  21.4 16.4 %copy-start.3 = (s32[8,128]{1,0:T(8,128)S(1)}, s32[8,128]{1,0:T(8,128)}, u32[]{:S(2)}) copy-start(s32[8,128]{1,0:T(8,128)} %param.41) | copy-start | bytes 12292
  28.0 9.8 %all-to-all-start.12 = ((bf16[8,8,128]{2,1,0:T(8,128)(2,1)}), bf16[8,8,128]{2,1,0:T(8,128)(2,1)S(1)}, u32[]{:S(2)}, u32[]{:S(2)}) async-start(bf16[8,8,128]{2,1,0:T(8,128)(2,1)} %broadcast_in_dim.33), calls=%async_computation.12 | async-start | bytes 32768 | tf_op jit(solution)/shard_map/all_to_all | solution.py:22
  53.2 4.0 %collective-permute-start.2 = (bf16[128,128]{1,0:T(8,128)(2,1)S(1)}, bf16[128,128]{1,0:T(8,128)(2,1)S(1)}, u32[]{:S(2)}, u32[]{:S(2)}) collective-permute-start(bf16[128,128]{1,0:T(8,128)(2,1)S(1)} %bitcast_convert_fusion), channel_id=1, source_target_pairs={{0,16},{1,17},{2,18},{3,19},{4,20},{5,21},{6,22},{7,23},{8,24},{9,... | collective-permute-start | bytes 98312 | tf_op jit(solution)/shard_map/ppermute | solution.py:154
  74.4 2.6 collective-permute-start.3
  77.5 2.2 collective-permute-start.4
  80.4 2.4 collective-permute-start.5
  84.1 2.6 collective-permute-start.6
  87.5 0.7 collective-permute-start.7
  88.3 71.9 %collective-permute-start.8 = (bf16[128,896]{1,0:T(8,128)(2,1)S(1)}, bf16[128,896]{1,0:T(8,128)(2,1)S(1)}, u32[]{:S(2)}, u32[]{:S(2)}) collective-permute-start(bf16[128,896]{1,0:T(8,128)(2,1)S(1)} %pad_maximum_fusion.2), channel_id=1, source_target_pairs={{96,112},{97,113},{98,114},{99,115},{100,116},{101,117},{102,118},... | collective-permute-start | bytes 688136 | tf_op jit(solution)/shard_map/ppermute | solution.py:191
  89.1 71.9 %collective-permute-start.11 = (bf16[128,128]{1,0:T(8,128)(2,1)S(1)}, bf16[128,128]{1,0:T(8,128)(2,1)S(1)}, u32[]{:S(2)}, u32[]{:S(2)}) collective-permute-start(bf16[128,128]{1,0:T(8,128)(2,1)S(1)} %convert_element_type.203), channel_id=1, source_target_pairs={{16,0},{48,32},{80,64},{17,1},{49,33},{81,65},{18,2},{50,34},{82,6... | collective-permute-start | bytes 98312 | tf_op jit(solution)/shard_map/ppermute | solution.py:193
  131.2 9.9 %collective-permute-start = (bf16[1024,2048]{1,0:T(8,128)(2,1)}, bf16[1024,2048]{1,0:T(8,128)(2,1)}, u32[]{:S(2)}, u32[]{:S(2)}) collective-permute-start(bf16[1024,2048]{1,0:T(8,128)(2,1)} %get-tuple-element.152), channel_id=1, source_target_pairs={{16,0},{48,32},{80,64},{17,1},{49,33},{81,65},{18,2},{50,34},{82,6... | collective-permute-start | bytes 12582920 | tf_op jit(solution)/shard_map/cond/branch_1_fun/ppermute | solution.py:168
  149.2 6.2 %collective-permute-start.1 = (bf16[1024,1024]{1,0:T(8,128)(2,1)S(1)}, bf16[1024,1024]{1,0:T(8,128)(2,1)}, u32[]{:S(2)}, u32[]{:S(2)}) collective-permute-start(bf16[1024,1024]{1,0:T(8,128)(2,1)S(1)} %get-tuple-element.198), channel_id=1, source_target_pairs={{16,0},{48,32},{80,64},{17,1},{49,33},{81,65},{18,2},{50,34},{82,6... | collective-permute-start | bytes 6291464 | tf_op jit(solution)/shard_map/cond/branch_1_fun/ppermute | solution.py:174
  160.2 2.0 collective-permute-start.10
  160.9 3.5 %collective-permute-start.14 = (bf16[128,128]{1,0:T(8,128)(2,1)S(1)}, bf16[128,128]{1,0:T(8,128)(2,1)S(1)}, u32[]{:S(2)}, u32[]{:S(2)}) collective-permute-start(bf16[128,128]{1,0:T(8,128)(2,1)S(1)} %convert_element_type.205), channel_id=1, source_target_pairs={{112,80},{113,81},{114,82},{115,83},{116,84},{117,85},{118,86},{11... | collective-permute-start | bytes 98312 | tf_op jit(solution)/shard_map/ppermute | solution.py:212
  161.6 2.8 collective-permute-start.15
  162.4 2.1 collective-permute-start.12
  163.0 1.4 collective-permute-start.13
  163.7 5.0 %collective-permute-start.18 = (bf16[128,128]{1,0:T(8,128)(2,1)S(1)}, bf16[128,128]{1,0:T(8,128)(2,1)S(1)}, u32[]{:S(2)}, u32[]{:S(2)}) collective-permute-start(bf16[128,128]{1,0:T(8,128)(2,1)S(1)} %convert_element_type.206), channel_id=1, source_target_pairs={{96,112},{97,113},{98,114},{99,115},{100,116},{101,117},{102,118},... | collective-permute-start | bytes 98312 | tf_op jit(solution)/shard_map/ppermute | solution.py:226
  166.7 4.0 %collective-permute-start.16 = (bf16[128,128]{1,0:T(8,128)(2,1)S(1)}, bf16[128,128]{1,0:T(8,128)(2,1)S(1)}, u32[]{:S(2)}, u32[]{:S(2)}) collective-permute-start(bf16[128,128]{1,0:T(8,128)(2,1)S(1)} %convert_element_type.208), channel_id=1, source_target_pairs={{64,32},{80,48},{65,33},{81,49},{66,34},{82,50},{67,35},{83,51},{6... | collective-permute-start | bytes 98312 | tf_op jit(solution)/shard_map/ppermute | solution.py:243
  167.4 3.4 %collective-permute-start.17 = (bf16[128,128]{1,0:T(8,128)(2,1)S(1)}, bf16[128,128]{1,0:T(8,128)(2,1)S(1)}, u32[]{:S(2)}, u32[]{:S(2)}) collective-permute-start(bf16[128,128]{1,0:T(8,128)(2,1)S(1)} %convert_element_type.208), channel_id=1, source_target_pairs={{64,48},{80,32},{65,49},{81,33},{66,50},{82,34},{67,51},{83,35},{6... | collective-permute-start | bytes 98312 | tf_op jit(solution)/shard_map/ppermute | solution.py:244
  168.1 8.0 %collective-permute-start.22 = (bf16[128,128]{1,0:T(8,128)(2,1)S(1)}, bf16[128,128]{1,0:T(8,128)(2,1)S(1)}, u32[]{:S(2)}, u32[]{:S(2)}) collective-permute-start(bf16[128,128]{1,0:T(8,128)(2,1)S(1)} %convert_element_type.208), channel_id=1, source_target_pairs={{64,80},{80,64},{65,81},{81,65},{66,82},{82,66},{67,83},{83,67},{6... | collective-permute-start | bytes 98312 | tf_op jit(solution)/shard_map/ppermute | solution.py:248
  168.8 2.0 collective-permute-start.19
  169.4 94.4 %collective-permute-start.24 = (bf16[128,256]{1,0:T(8,128)(2,1)S(1)}, bf16[128,256]{1,0:T(8,128)(2,1)S(1)}, u32[]{:S(2)}, u32[]{:S(2)}) collective-permute-start(bf16[128,256]{1,0:T(8,128)(2,1)S(1)} %maximum_select_fusion), channel_id=1, source_target_pairs={{96,0},{112,16},{97,1},{113,17},{98,2},{114,18},{99,3},{115,19},{1... | collective-permute-start | bytes 196616 | tf_op jit(solution)/shard_map/ppermute | solution.py:233
  173.5 86.6 %collective-permute-start.20 = (bf16[128,128]{1,0:T(8,128)(2,1)S(1)}, bf16[128,128]{1,0:T(8,128)(2,1)S(1)}, u32[]{:S(2)}, u32[]{:S(2)}) collective-permute-start(bf16[128,128]{1,0:T(8,128)(2,1)S(1)} %convert_element_type.210), channel_id=1, source_target_pairs={{32,0},{48,16},{33,1},{49,17},{34,2},{50,18},{35,3},{51,19},{36,4}... | collective-permute-start | bytes 98312 | tf_op jit(solution)/shard_map/ppermute | solution.py:243
  174.8 89.1 %collective-permute-start.21 = (bf16[128,128]{1,0:T(8,128)(2,1)S(1)}, bf16[128,128]{1,0:T(8,128)(2,1)S(1)}, u32[]{:S(2)}, u32[]{:S(2)}) collective-permute-start(bf16[128,128]{1,0:T(8,128)(2,1)S(1)} %convert_element_type.210), channel_id=1, source_target_pairs={{32,16},{48,0},{33,17},{49,1},{34,18},{50,2},{35,19},{51,3},{36,20... | collective-permute-start | bytes 98312 | tf_op jit(solution)/shard_map/ppermute | solution.py:244
  176.1 87.8 %collective-permute-start.23 = (bf16[128,256]{1,0:T(8,128)(2,1)S(1)}, bf16[128,256]{1,0:T(8,128)(2,1)S(1)}, u32[]{:S(2)}, u32[]{:S(2)}) collective-permute-start(bf16[128,256]{1,0:T(8,128)(2,1)S(1)} %maximum_select_fusion.1), channel_id=1, source_target_pairs={{64,0},{80,16},{65,1},{81,17},{66,2},{82,18},{67,3},{83,19},{68,4}... | collective-permute-start | bytes 196616 | tf_op jit(solution)/shard_map/ppermute | solution.py:254
  284.0 9.8 %all-to-all-start.14 = ((bf16[8,8,128]{2,1,0:T(8,128)(2,1)}), bf16[8,8,128]{2,1,0:T(8,128)(2,1)S(1)}, u32[]{:S(2)}, u32[]{:S(2)}) async-start(bf16[8,8,128]{2,1,0:T(8,128)(2,1)} %fusion.41), calls=%async_computation.14 | async-start | bytes 32768 | tf_op jit(solution)/shard_map/all_to_all | solution.py:22
  (1 other events, 7.4 us)
Sparse Core Ops, SparseCore 0:
  20.8 95.6 all-gather.1

commit v9 on v8

--- a/solution.py
+++ b/solution.py
@@ -27,11 +27,20 @@
     return jnp.transpose(x.reshape(rows, parts, width // parts), (1, 0, 2))
 
 
-def fold_kernel(at_ref, right_ref, left_ref, out_ref):
+def fold_kernel(at_ref, right_ref, left_ref, passed_low_ref, passed_high_ref, out_ref):
     step = pl.program_id(0)
-    first, own = at_ref[0], at_ref[1]
-
-    @pl.when(step >= first)
+    first, own, last = at_ref[0], at_ref[1], at_ref[2]
+
+    @pl.when((step >= first) & (own == last) & (step < pl.num_programs(0) - 1))
+    def _():
+        half = passed_low_ref.shape[1]
+        low = left_ref[:, :half].astype(F32) - passed_low_ref[...].astype(F32)
+        high = left_ref[:, half:].astype(F32) - passed_high_ref[...].astype(F32)
+        total = jnp.dot(low.astype(BF), right_ref[:half, :], preferred_element_type=F32)
+        total += jnp.dot(high.astype(BF), right_ref[half:, :], preferred_element_type=F32)
+        out_ref[...] = total.astype(out_ref.dtype)
+
+    @pl.when((step >= first) & ((own != last) | (step == pl.num_programs(0) - 1)))
     def _():
         total = jnp.dot(left_ref[...], right_ref[...], preferred_element_type=F32)
         width = out_ref.shape[0] // 2
@@ -72,17 +81,18 @@
             out_ref[here, :] = (old + new).astype(out_ref.dtype)
 
 
-def chunked(kernel, at, right, columns, right_block, lefts, chunk):
-    def row(step, at):
-        return (jnp.maximum(step, at[0]), 0)
-
-    rows = lefts[0].shape[0]
+def chunked(kernel, at, right, columns, right_block, lefts, chunk, rows=None):
+    rows = lefts[0].shape[0] if rows is None else rows
+
+    def row_map(count):
+        return lambda step, at: (jnp.minimum(jnp.maximum(step, at[0]), count - 1), 0)
+
     grid_spec = pltpu.PrefetchScalarGridSpec(
         num_scalar_prefetch=1,
         grid=(rows // chunk,),
         in_specs=[pl.BlockSpec((right.shape[0], columns), lambda step, at: (0, right_block))]
-        + [pl.BlockSpec((chunk, x.shape[1]), row) for x in lefts],
-        out_specs=pl.BlockSpec((chunk, columns), row),
+        + [pl.BlockSpec((chunk, x.shape[1]), row_map(x.shape[0] // chunk)) for x in lefts],
+        out_specs=pl.BlockSpec((chunk, columns), row_map(rows // chunk)),
     )
     return pl.pallas_call(
         kernel,
@@ -117,9 +127,13 @@
     factor = jnp.transpose(root_factor, (1, 2, 0)).reshape(n_row * width, section)
 
     diagonal = lax.dynamic_slice_in_dim(factor, row_at * width, width, 0)
-    above = lax.dynamic_slice_in_dim(factor, (row_at | 1) * width, width, 0)
-    lower = lax.ppermute(above[:, half:], "row", up)
-    held = jnp.concatenate([diagonal, jnp.where(even, above[:, :half], lower)], axis=1)
+    pick_block = jnp.where(row_at == n_row - 1, n_row - 2, row_at | 1)
+    above = lax.dynamic_slice_in_dim(factor, pick_block * width, width, 0)
+    kept = jnp.where(even, above[:, :half], above[:, half:])
+    sent = jnp.where(even, above[:, half:], above[:, :half])
+    sent = lax.ppermute(sent, "row", up[:-1] + down[-1:])
+    giver = (row_at < n_row - 2) == even
+    held = jnp.concatenate([diagonal, jnp.where(giver, kept, sent)], axis=1)
     whole = lax.all_gather(held, "col", axis=0, tiled=True)
 
     spread = exchange(jnp.broadcast_to(skeleton[None], (n_row, rhs_here, slots)), "row")
@@ -149,20 +163,57 @@
 
         return lax.cond(turn, reduce_columns, lambda run, *rest: run, run, *operands)
 
-    known = run.astype(BF)
-    for j in range(last - 1):
+    low = run.astype(BF)
+    known = low
+    for j in range(last - 2):
         arrived = lax.ppermute(known, "row", [(j, j + 1)])
-        if j < last - 2:
-            partial = dot_nn(arrived, factor[: (j + 1) * width])
-            run = take_turn(row_at == j + 1, run, partial, -1)
-        else:
-            run = take_whole_turn(row_at == j + 1, run, -1, arrived, factor[: (j + 1) * width])
-        known = jnp.concatenate([arrived, run.astype(BF)], axis=1)
-        if j == last - 4:
-            held, _ = lax.optimization_barrier((factor, known))
-            first = jnp.where(row_at == last, 0, row_at // 2)
-            at = jnp.stack([first, row_at]).astype(jnp.int32)
-            folded = chunked(fold_kernel, at, whole, section, 0, (held,), 2 * width)
+        if j == last - 3:
+            ahead = lax.ppermute(known, "row", [(j, j + 2)])
+        partial = dot_nn(arrived, factor[: (j + 1) * width])
+        run = take_turn(row_at == j + 1, run, partial, -1)
+        low = run.astype(BF)
+        known = jnp.concatenate([arrived, low], axis=1)
+        if j == 1:
+            partner = lax.ppermute(factor, "row", [(last - 1, last)])
+            partner_low = lax.ppermute(low, "row", [(last - 1, last)])
+    newest = lax.ppermute(low, "row", [(last - 2, last - 1)])
+    newest_last = lax.ppermute(low, "row", [(last - 2, last)])
+    ahead_last = lax.ppermute(ahead, "row", [(last - 1, last)])
+
+    def pass_on(whole, factor, partner):
+        def product(left):
+            return chunked(
+                through_kernel,
+                jnp.zeros((3,), jnp.int32),
+                whole,
+                half,
+                2,
+                (left,),
+                2 * width,
+                (last - 1) * width,
+            )
+
+        mine = lax.cond(even, lambda a, b: product(a), lambda a, b: product(b), factor, partner)
+        return lax.ppermute(mine, "row", [(last - 1, last)]), mine
+
+    def pass_nothing(whole, factor, partner):
+        nothing = jnp.zeros(((last - 1) * width, half), BF)
+        return nothing, nothing
+
+    passed_low, passed_high = lax.cond(
+        row_at >= last - 1, pass_on, pass_nothing, whole, factor, partner
+    )
+    known = jnp.concatenate([ahead, newest], axis=1)
+    forward = low
+    run = take_whole_turn(
+        row_at == last - 1, run, -1, known, factor[: (last - 1) * width]
+    )
+
+    first = jnp.where(row_at == last, 0, row_at // 2)
+    at = jnp.stack([first, row_at, jnp.full_like(row_at, last)]).astype(jnp.int32)
+    folded = chunked(
+        fold_kernel, at, whole, section, 0, (factor, passed_low, passed_high), 2 * width
+    )
 
     def merge_pair(at, whole, folded):
         odd_part = lax.ppermute(folded, "row", down[:-1])
@@ -188,26 +239,21 @@
             folded,
         )
 
-    arrived = lax.ppermute(known, "row", [(last - 1, last)])
+    other = lax.ppermute(forward, "row", down[:-1])
+    zero = jnp.zeros_like(forward)
+    held_rhs = jnp.where(
+        even,
+        jnp.concatenate([forward, -other], axis=1),
+        jnp.concatenate([zero, forward], axis=1),
+    )
+    merged = lax.cond(
+        row_at < last - 1, merge_pair, lambda at, whole, folded: folded, at, whole, folded
+    )
+
+    x = jnp.concatenate([-ahead_last, -newest_last, -partner_low, forward], axis=1)
+    run = take_whole_turn(row_at == last, run, 0, x, merged)
     low = run.astype(BF)
-    other = lax.ppermute(low, "row", down[:-1])
-    zero = jnp.zeros_like(low)
-    held_rhs = jnp.where(even, jnp.concatenate([low, -other], 1), jnp.concatenate([zero, low], 1))
-    held, _ = lax.optimization_barrier((whole, known))
-    merged = lax.cond(
-        row_at < last - 1,
-        merge_pair,
-        lambda at, whole, folded: jnp.zeros_like(folded),
-        at,
-        held,
-        folded,
-    )
-    arrived, merged = lax.optimization_barrier((arrived, merged))
-
-    run = take_whole_turn(
-        row_at == last, run, 0, jnp.concatenate([-arrived, low], axis=1), folded
-    )
-    seventh = run.astype(BF)
+    seventh = low
     arrived = lax.ppermute(seventh, "row", [(last, last - 1)])
     early = lax.ppermute(seventh, "row", [(last, last - 2)])
     early += lax.ppermute(seventh, "row", [(last, last - 3)])
@@ -216,7 +262,7 @@
         run,
         0,
         jnp.concatenate([low, -arrived], axis=1),
-        folded[(last - 1) * width :],
+        merged[(last - 1) * width :],
     )
     sixth = run.astype(BF)
     newest = lax.ppermute(sixth, "row", [(last - 1, last - 3)])

time: 303 us -> 329 us (1.086)
  waiting for transfers between devices: 134 us -> 153 us
  starting transfers between devices: 39.1 us -> 46.1 us
    ppermute x2, waiting for transfers between devices: 82.7 us -> 110 us  [on_device(): straight = lax.ppermute(low, 'row', same)]
    all_gather x1, waiting for transfers between devices: 26 us -> 17.7 us  [on_device(): whole = lax.all_gather(held, 'col', axis=0, tiled=True)]
    ppermute x3 -> x8, starting transfers between devices: 3.43 us -> 9.21 us  [the longest x1 2.64 us: on_device(): partner = lax.ppermute(factor, 'row', [(last - 1, last)])]
    cond x1 -> x0, local copies, waits for them, and re-layouts: 4.73 us -> none
  transfers between devices with their start and end apart: 28 -> 32, of which waited for: 9 -> 9; matrix products, arithmetic and copies ran while one was open for 10% -> 9% of each run, Pallas kernels for 8% -> 7%
where the time goes in v9:
time: 329 us; the launch traced here: 328 us
  waiting for transfers between devices  153 us (47%)
  starting transfers between devices  46.1 us (14%)
  blocking collectives  43 us (13%)
  Pallas kernels  23.4 us (7%)
  matrix products  20.8 us (6%)
  local copies, waits for them, and re-layouts  19.5 us (6%)
  between operations  15.6 us (5%)
  other arithmetic  6.17 us (2%)
    ppermute x2, waiting for transfers between devices, on_device(): straight = lax.ppermute(low, 'row', same)  110 us
    all_to_all x3, blocking collectives, exchange(): return lax.all_to_all(x, axis, 0, 0, tiled=True)  43 us
    pallas_call x2, Pallas kernels, chunked(): pl.pallas_call(kernel, grid_spec=grid_spec, out_shape=jax.ShapeDtypeStruc...  23.4 us
    all_gather x1, waiting for transfers between devices, on_device(): whole = lax.all_gather(held, 'col', axis=0, tiled=True)  17.7 us
    dot_general x12, matrix products, dot_nn(): lax.dot_general(a, b, (((1,), (0,)), ((), ())), preferred_element_type=F32)  15.1 us
    all_to_all x2, starting transfers between devices, exchange(): return lax.all_to_all(x, axis, 0, 0, tiled=True)  12 us
    all_to_all x2, waiting for transfers between devices, exchange(): return lax.all_to_all(x, axis, 0, 0, tiled=True)  9.38 us
    unnamed x12, local copies, waits for them, and re-layouts  7.67 us
  transfers between devices with their start and end apart: 32, of which 9 were waited for; matrix products, arithmetic and copies ran while one was open for 9% of the time, Pallas kernels for 7%

profile of v9, /device:TPU:1, one launch (start us, length us, event | category | flops | bytes accessed | tf_op | source)
XLA Modules:
  0.0 327.7 jit_solution(3457541870402301628)
XLA Ops:
  7.2 6.8 %copy.21 = bf16[2048,8,128]{0,2,1:T(8,128)(2,1)} copy(bf16[2048,8,128]{2,1,0:T(8,128)(2,1)} %param.47) | data formatting | bytes 8388608 | tf_op args[7]
  21.0 2.6 collective-permute-start.14
  24.4 5.7 %fusion.4 = f32[8,2048]{1,0:T(8,128)S(1)} fusion(bf16[1,2048,2048]{2,1,0:T(8,128)(2,1)} %param.41, bf16[1,8,2048]{2,1,0:T(8,128)(2,1)S(1)} %copy-done.1), kind=kOutput, calls=%fused_computation.23 | convolution fusion | flops 67108864 | bytes 8486912 | tf_op jit(solution)/shard_map/dot_general | solution.py:14
  31.0 6.9 %all-to-all-start.12 = ((bf16[8,8,128]{2,1,0:T(8,128)(2,1)}), bf16[8,8,128]{2,1,0:T(8,128)(2,1)S(1)}, u32[]{:S(2)}, u32[]{:S(2)}) async-start(bf16[8,8,128]{2,1,0:T(8,128)(2,1)} %broadcast_in_dim.33), calls=%async_computation.12 | async-start | bytes 32768 | tf_op jit(solution)/shard_map/all_to_all | solution.py:22
  37.9 4.7 %all-to-all-done.12 = bf16[8,8,128]{2,1,0:T(8,128)(2,1)S(1)} async-done(((bf16[8,8,128]{2,1,0:T(8,128)(2,1)}), bf16[8,8,128]{2,1,0:T(8,128)(2,1)S(1)}, u32[]{:S(2)}, u32[]{:S(2)}) %all-to-all-start.12) | async-done | bytes 16416 | tf_op jit(solution)/shard_map/all_to_all | solution.py:22
  44.0 13.9 %all_to_all.75 = f32[16,8,128]{2,1,0:T(8,128)S(1)} all-to-all(f32[16,8,128]{2,1,0:T(8,128)S(1)} %fusion.35), channel_id=1, replica_groups=mesh['row'=8,'col'=16] {'col'}, dimensions={0} | all-to-all | bytes 131072 | tf_op jit(solution)/shard_map/all_to_all | solution.py:22
  59.2 2.7 collective-permute-done.3
  63.4 15.6 %conditional.21 = (f32[128,128]{1,0:T(8,128)S(1)}) conditional(s32[]{:T(128)} %convert_element_type.191, f32[128,128]{1,0:T(8,128)S(1)} %bitcast.159, (bf16[16,128,128]{2,1,0:T(8,128)(2,1)S(1)}, f32[128,128]{1,0:T(8,128)S(1)}) %tuple.178), branch_computations={%region_0.1_spmd, %region_1.3_spmd} | conditional | flops 524288 | bytes 1835016 | solution.py:157
  63.4 15.5 %all_to_all.63 = bf16[16,128,128]{2,1,0:T(8,128)(2,1)S(1)} all-to-all(bf16[16,128,128]{2,1,0:T(8,128)(2,1)S(1)} %get-tuple-element.148), channel_id=1, replica_groups=mesh['row'=8,'col'=16] {'col'}, dimensions={0} | all-to-all | bytes 1048576 | tf_op jit(solution)/shard_map/cond/branch_1_fun/all_to_all | solution.py:22
  82.9 1.6 slice.75
  85.8 1.7 slice.76
  89.5 1.9 slice.77
  98.8 17.7 %all-gather.2.cloned.1.call-done.right_ref = bf16[2048,3072]{1,0:T(8,128)(2,1)} async-done(((bf16[128,3072]{1,0:T(8,128)(2,1)}), bf16[2048,3072]{1,0:T(8,128)(2,1)}) %all-gather.2.cloned.1.call-update) | async-done | bytes 12582928 | tf_op jit(solution)/shard_map/all_gather | solution.py:137
  116.5 2.7 conditional.27
  119.2 15.3 %shard_map.95 = bf16[1024,2048]{1,0:T(8,128)(2,1)} custom-call(s32[3]{0:T(128)S(1)} %pad_add_fusion.at_ref, bf16[2048,3072]{1,0:T(8,128)(2,1)} %all-gather.2.cloned.1.call-done.right_ref, bf16[1024,2048]{1,0:T(8,128)(2,1)} %bitcast.158, bf16[768,1024]{1,0:T(8,128)(2,1)} %get-tuple-element.193.passed_low_ref, bf16[768,1024]{1,0:T(8,128)(2,1)} %get-tuple-element.194.passed_high_ref), custom_call_target="tpu_custom_call" | custom-call | tf_op jit(solution)/shard_map/pallas_call | solution.py:97
  134.5 24.2 %conditional.28 = (bf16[1024,2048]{1,0:T(8,128)(2,1)}) conditional(s32[]{:T(128)} %convert_element_type.205, bf16[1024,2048]{1,0:T(8,128)(2,1)} %shard_map.95, (pred[]{:T(512)}, bf16[1024,2048]{1,0:T(8,128)(2,1)}, s32[3]{0:T(128)S(1)}, bf16[2048,3072]{1,0:T(8,128)(2,1)}) %tuple.126), branch_computations={%region_22.23_spmd, %region_23.28_spmd} | conditional | flops 1 | bytes 33554620 | solution.py:249
  134.5 4.7 %collective-permute-start.1 = (bf16[1024,2048]{1,0:T(8,128)(2,1)}, bf16[1024,2048]{1,0:T(8,128)(2,1)}, u32[]{:S(2)}, u32[]{:S(2)}) collective-permute-start(bf16[1024,2048]{1,0:T(8,128)(2,1)} %get-tuple-element.180), channel_id=1, source_target_pairs={{16,0},{48,32},{80,64},{17,1},{49,33},{81,65},{18,2},{50,34},{82,6... | collective-permute-start | bytes 12582920 | tf_op jit(solution)/shard_map/cond/branch_1_fun/ppermute | solution.py:219
  139.1 5.2 %collective-permute-done.1 = bf16[1024,2048]{1,0:T(8,128)(2,1)} collective-permute-done((bf16[1024,2048]{1,0:T(8,128)(2,1)}, bf16[1024,2048]{1,0:T(8,128)(2,1)}, u32[]{:S(2)}, u32[]{:S(2)}) %collective-permute-start.1) | collective-permute-done | bytes 4194336 | tf_op jit(solution)/shard_map/cond/branch_1_fun/ppermute | solution.py:219
  144.3 8.2 %conditional.6 = (bf16[1024,1024]{1,0:T(8,128)(2,1)S(1)}) conditional(s32[]{:T(128)} %convert_element_type.134, (s32[3]{0:T(128)S(1)}, bf16[2048,3072]{1,0:T(8,128)(2,1)}, bf16[1024,2048]{1,0:T(8,128)(2,1)}) %tuple.100, (s32[3]{0:T(128)S(1)}, bf16[2048,3072]{1,0:T(8,128)(2,1)}, bf16[1024,2048]{1,0:T(8,128)(2,1)}) %tuple.101), branch_computations={%region_24.24_spmd, %region_25.25_spmd} | conditional | bytes 8 | solution.py:224
  144.3 8.1 %branch_0_fun.3 = bf16[1024,1024]{1,0:T(8,128)(2,1)S(1)} custom-call(s32[3]{0:T(128)S(1)} %get-tuple-element.168.at_ref, bf16[2048,3072]{1,0:T(8,128)(2,1)} %get-tuple-element.169.right_ref, bf16[1024,2048]{1,0:T(8,128)(2,1)} %get-tuple-element.170.left_ref), custom_call_target="tpu_custom_call" | custom-call | tf_op jit(solution)/shard_map/cond/branch_1_fun/cond/branch_0_fun/pallas_call | solution.py:97
  152.5 3.7 %collective-permute-start.2 = (bf16[1024,1024]{1,0:T(8,128)(2,1)S(1)}, bf16[1024,1024]{1,0:T(8,128)(2,1)}, u32[]{:S(2)}, u32[]{:S(2)}) collective-permute-start(bf16[1024,1024]{1,0:T(8,128)(2,1)S(1)} %get-tuple-element.225), channel_id=1, source_target_pairs={{16,0},{48,32},{80,64},{17,1},{49,33},{81,65},{18,2},{50,34},{82,6... | collective-permute-start | bytes 6291464 | tf_op jit(solution)/shard_map/cond/branch_1_fun/ppermute | solution.py:225
  156.1 2.5 collective-permute-done.2
  162.9 2.0 fusion.28
  169.3 2.5 fusion.31
  176.1 110.2 %collective-permute-done.25 = bf16[128,128]{1,0:T(8,128)(2,1)S(1)} collective-permute-done((bf16[128,128]{1,0:T(8,128)(2,1)S(1)}, bf16[128,128]{1,0:T(8,128)(2,1)S(1)}, u32[]{:S(2)}, u32[]{:S(2)}) %collective-permute-start.25) | collective-permute-done | bytes 32800 | tf_op jit(solution)/shard_map/ppermute | solution.py:289
  286.2 3.8 %collective-permute-done.26 = bf16[128,128]{1,0:T(8,128)(2,1)S(1)} collective-permute-done((bf16[128,128]{1,0:T(8,128)(2,1)S(1)}, bf16[128,128]{1,0:T(8,128)(2,1)S(1)}, u32[]{:S(2)}, u32[]{:S(2)}) %collective-permute-start.26) | collective-permute-done | bytes 32800 | tf_op jit(solution)/shard_map/ppermute | solution.py:290
  290.1 2.9 convolution_convert_fusion.3
  293.0 15.2 %conditional.34 = (f32[8,2048]{1,0:T(8,128)}, f32[8,2048]{1,0:T(8,128)S(1)}) conditional(s32[]{:T(128)} %convert_element_type.182, f32[128,128]{1,0:T(8,128)S(1)} %get-tuple-element.237, bf16[128,2048]{1,0:T(8,128)(2,1)S(1)} %convolution_convert_fusion.3), branch_computations={%region_40.41_spmd, %region_41.43_spmd} | conditional | flops 507904 | bytes 1769488
  293.1 13.6 %all_to_all.74 = bf16[16,8,2048]{2,1,0:T(8,128)(2,1)S(1)} all-to-all(bf16[16,8,2048]{2,1,0:T(8,128)(2,1)S(1)} %bitcast.166), channel_id=1, replica_groups=mesh['row'=8,'col'=16] {'col'}, dimensions={0} | all-to-all | bytes 1048576 | tf_op jit(solution)/shard_map/cond/branch_1_fun/all_to_all | solution.py:22
  308.2 2.0 fusion.41
  310.2 5.1 %all-to-all-start.14 = ((bf16[8,8,128]{2,1,0:T(8,128)(2,1)}), bf16[8,8,128]{2,1,0:T(8,128)(2,1)S(1)}, u32[]{:S(2)}, u32[]{:S(2)}) async-start(bf16[8,8,128]{2,1,0:T(8,128)(2,1)} %fusion.41), calls=%async_computation.14 | async-start | bytes 32768 | tf_op jit(solution)/shard_map/all_to_all | solution.py:22
  315.3 4.7 %all-to-all-done.14 = bf16[8,8,128]{2,1,0:T(8,128)(2,1)S(1)} async-done(((bf16[8,8,128]{2,1,0:T(8,128)(2,1)}), bf16[8,8,128]{2,1,0:T(8,128)(2,1)S(1)}, u32[]{:S(2)}, u32[]{:S(2)}) %all-to-all-start.14) | async-done | bytes 16416 | tf_op jit(solution)/shard_map/all_to_all | solution.py:22
  (136 shorter events, 43.9 us)
Async XLA Ops:
  7.2 109.3 %all-gather.2.cloned.1.call-start = ((), (), s32[]{:S(2)}) async-start(), calls=%async_computation.15 | async-start | bytes 13369344 | tf_op jit(solution)/shard_map/all_gather | solution.py:137
  15.2 3.7 %collective-permute-start.13 = (bf16[128,1024]{1,0:T(8,128)(2,1)S(1)}, bf16[128,1024]{1,0:T(8,128)(2,1)S(1)}, u32[]{:S(2)}, u32[]{:S(2)}) collective-permute-start(bf16[128,1024]{1,0:T(8,128)(2,1)S(1)} %broadcast_select_fusion), channel_id=1, source_target_pairs={{0,16},{32,48},{64,80},{112,96},{1,17},{33,49},{65,81},{113,97},{2... | collective-permute-start | bytes 786440 | tf_op jit(solution)/shard_map/ppermute | solution.py:134
  21.0 77.8 %collective-permute-start.14 = (bf16[1024,2048]{1,0:T(8,128)(2,1)}, bf16[1024,2048]{1,0:T(8,128)(2,1)}, u32[]{:S(2)}, u32[]{:S(2)}) collective-permute-start(bf16[1024,2048]{1,0:T(8,128)(2,1)} %bitcast.150), channel_id=1, source_target_pairs={{96,112},{97,113},{98,114},{99,115},{100,116},{101,117},{102,118},... | collective-permute-start | bytes 12582920 | tf_op jit(solution)/shard_map/ppermute | solution.py:177
  31.0 11.6 %all-to-all-start.12 = ((bf16[8,8,128]{2,1,0:T(8,128)(2,1)}), bf16[8,8,128]{2,1,0:T(8,128)(2,1)S(1)}, u32[]{:S(2)}, u32[]{:S(2)}) async-start(bf16[8,8,128]{2,1,0:T(8,128)(2,1)} %broadcast_in_dim.33), calls=%async_computation.12 | async-start | bytes 32768 | tf_op jit(solution)/shard_map/all_to_all | solution.py:22
  57.9 4.0 %collective-permute-start.3 = (bf16[128,128]{1,0:T(8,128)(2,1)S(1)}, bf16[128,128]{1,0:T(8,128)(2,1)S(1)}, u32[]{:S(2)}, u32[]{:S(2)}) collective-permute-start(bf16[128,128]{1,0:T(8,128)(2,1)S(1)} %bitcast_convert_fusion), channel_id=1, source_target_pairs={{0,16},{1,17},{2,18},{3,19},{4,20},{5,21},{6,22},{7,23},{8,24},{9,... | collective-permute-start | bytes 98312 | tf_op jit(solution)/shard_map/ppermute | solution.py:169
  79.1 2.6 collective-permute-start.4
  82.2 2.3 collective-permute-start.5
  85.1 2.4 collective-permute-start.6
  88.9 4.6 %collective-permute-start.7 = (bf16[128,640]{1,0:T(8,128)(2,1)}, bf16[128,640]{1,0:T(8,128)(2,1)S(1)}, u32[]{:S(2)}, u32[]{:S(2)}) collective-permute-start(bf16[128,640]{1,0:T(8,128)(2,1)} %pad_maximum_fusion.3), channel_id=1, source_target_pairs={{64,80},{65,81},{66,82},{67,83},{68,84},{69,85},{70,86},{71,87},{7... | collective-permute-start | bytes 491528 | tf_op jit(solution)/shard_map/ppermute | solution.py:169
  91.5 4.2 %collective-permute-start.12 = (bf16[128,128]{1,0:T(8,128)(2,1)S(1)}, bf16[128,128]{1,0:T(8,128)(2,1)S(1)}, u32[]{:S(2)}, u32[]{:S(2)}) collective-permute-start(bf16[128,128]{1,0:T(8,128)(2,1)S(1)} %convert_element_type.198), channel_id=1, source_target_pairs={{96,112},{97,113},{98,114},{99,115},{100,116},{101,117},{102,118},... | collective-permute-start | bytes 98312 | tf_op jit(solution)/shard_map/ppermute | solution.py:178
  92.2 2.8 collective-permute-start.8
  94.3 3.4 %collective-permute-start.9 = (bf16[128,128]{1,0:T(8,128)(2,1)S(1)}, bf16[128,128]{1,0:T(8,128)(2,1)S(1)}, u32[]{:S(2)}, u32[]{:S(2)}) collective-permute-start(bf16[128,128]{1,0:T(8,128)(2,1)S(1)} %convert_element_type.204), channel_id=1, source_target_pairs={{80,96},{81,97},{82,98},{83,99},{84,100},{85,101},{86,102},{87,103... | collective-permute-start | bytes 98312 | tf_op jit(solution)/shard_map/ppermute | solution.py:179
  94.9 3.7 %collective-permute-start.10 = (bf16[128,640]{1,0:T(8,128)(2,1)}, bf16[128,640]{1,0:T(8,128)(2,1)S(1)}, u32[]{:S(2)}, u32[]{:S(2)}) collective-permute-start(bf16[128,640]{1,0:T(8,128)(2,1)} %collective-permute-done.8), channel_id=1, source_target_pairs={{96,112},{97,113},{98,114},{99,115},{100,116},{101,117},{102,118},... | collective-permute-start | bytes 491528 | tf_op jit(solution)/shard_map/ppermute | solution.py:181
  95.7 2.9 collective-permute-start.11
  96.4 63.0 %collective-permute-start.16 = (bf16[128,128]{1,0:T(8,128)(2,1)S(1)}, bf16[128,128]{1,0:T(8,128)(2,1)S(1)}, u32[]{:S(2)}, u32[]{:S(2)}) collective-permute-start(bf16[128,128]{1,0:T(8,128)(2,1)S(1)} %convert_element_type.204), channel_id=1, source_target_pairs={{16,0},{48,32},{80,64},{17,1},{49,33},{81,65},{18,2},{50,34},{82,6... | collective-permute-start | bytes 98312 | tf_op jit(solution)/shard_map/ppermute | solution.py:242
  134.5 9.8 %collective-permute-start.1 = (bf16[1024,2048]{1,0:T(8,128)(2,1)}, bf16[1024,2048]{1,0:T(8,128)(2,1)}, u32[]{:S(2)}, u32[]{:S(2)}) collective-permute-start(bf16[1024,2048]{1,0:T(8,128)(2,1)} %get-tuple-element.180), channel_id=1, source_target_pairs={{16,0},{48,32},{80,64},{17,1},{49,33},{81,65},{18,2},{50,34},{82,6... | collective-permute-start | bytes 12582920 | tf_op jit(solution)/shard_map/cond/branch_1_fun/ppermute | solution.py:219
  152.5 6.2 %collective-permute-start.2 = (bf16[1024,1024]{1,0:T(8,128)(2,1)S(1)}, bf16[1024,1024]{1,0:T(8,128)(2,1)}, u32[]{:S(2)}, u32[]{:S(2)}) collective-permute-start(bf16[1024,1024]{1,0:T(8,128)(2,1)S(1)} %get-tuple-element.225), channel_id=1, source_target_pairs={{16,0},{48,32},{80,64},{17,1},{49,33},{81,65},{18,2},{50,34},{82,6... | collective-permute-start | bytes 6291464 | tf_op jit(solution)/shard_map/cond/branch_1_fun/ppermute | solution.py:225
  158.7 2.1 collective-permute-start.15
  159.4 3.5 %collective-permute-start.19 = (bf16[128,128]{1,0:T(8,128)(2,1)S(1)}, bf16[128,128]{1,0:T(8,128)(2,1)S(1)}, u32[]{:S(2)}, u32[]{:S(2)}) collective-permute-start(bf16[128,128]{1,0:T(8,128)(2,1)S(1)} %convert_element_type.207), channel_id=1, source_target_pairs={{112,80},{113,81},{114,82},{115,83},{116,84},{117,85},{118,86},{11... | collective-permute-start | bytes 98312 | tf_op jit(solution)/shard_map/ppermute | solution.py:258
  160.0 2.8 collective-permute-start.20
  160.8 2.1 collective-permute-start.17
  161.5 1.4 collective-permute-start.18
  162.2 4.3 %collective-permute-start.23 = (bf16[128,128]{1,0:T(8,128)(2,1)S(1)}, bf16[128,128]{1,0:T(8,128)(2,1)S(1)}, u32[]{:S(2)}, u32[]{:S(2)}) collective-permute-start(bf16[128,128]{1,0:T(8,128)(2,1)S(1)} %convert_element_type.208), channel_id=1, source_target_pairs={{96,112},{97,113},{98,114},{99,115},{100,116},{101,117},{102,118},... | collective-permute-start | bytes 98312 | tf_op jit(solution)/shard_map/ppermute | solution.py:272
  165.2 4.0 %collective-permute-start.21 = (bf16[128,128]{1,0:T(8,128)(2,1)S(1)}, bf16[128,128]{1,0:T(8,128)(2,1)S(1)}, u32[]{:S(2)}, u32[]{:S(2)}) collective-permute-start(bf16[128,128]{1,0:T(8,128)(2,1)S(1)} %convert_element_type.210), channel_id=1, source_target_pairs={{64,32},{80,48},{65,33},{81,49},{66,34},{82,50},{67,35},{83,51},{6... | collective-permute-start | bytes 98312 | tf_op jit(solution)/shard_map/ppermute | solution.py:289
  165.8 3.4 %collective-permute-start.22 = (bf16[128,128]{1,0:T(8,128)(2,1)S(1)}, bf16[128,128]{1,0:T(8,128)(2,1)S(1)}, u32[]{:S(2)}, u32[]{:S(2)}) collective-permute-start(bf16[128,128]{1,0:T(8,128)(2,1)S(1)} %convert_element_type.210), channel_id=1, source_target_pairs={{64,48},{80,32},{65,49},{81,33},{66,50},{82,34},{67,51},{83,35},{6... | collective-permute-start | bytes 98312 | tf_op jit(solution)/shard_map/ppermute | solution.py:290
  166.5 2.7 collective-permute-start.24
  167.2 122.8 %collective-permute-start.29 = (bf16[128,256]{1,0:T(8,128)(2,1)S(1)}, bf16[128,256]{1,0:T(8,128)(2,1)S(1)}, u32[]{:S(2)}, u32[]{:S(2)}) collective-permute-start(bf16[128,256]{1,0:T(8,128)(2,1)S(1)} %maximum_select_fusion.1), channel_id=1, source_target_pairs={{96,0},{112,16},{97,1},{113,17},{98,2},{114,18},{99,3},{115,19},{1... | collective-permute-start | bytes 196616 | tf_op jit(solution)/shard_map/ppermute | solution.py:279
  168.5 6.0 %collective-permute-start.27 = (bf16[128,128]{1,0:T(8,128)(2,1)S(1)}, bf16[128,128]{1,0:T(8,128)(2,1)S(1)}, u32[]{:S(2)}, u32[]{:S(2)}) collective-permute-start(bf16[128,128]{1,0:T(8,128)(2,1)S(1)} %convert_element_type.210), channel_id=1, source_target_pairs={{64,80},{80,64},{65,81},{81,65},{66,82},{82,66},{67,83},{83,67},{6... | collective-permute-start | bytes 98312 | tf_op jit(solution)/shard_map/ppermute | solution.py:294
  171.9 114.3 %collective-permute-start.25 = (bf16[128,128]{1,0:T(8,128)(2,1)S(1)}, bf16[128,128]{1,0:T(8,128)(2,1)S(1)}, u32[]{:S(2)}, u32[]{:S(2)}) collective-permute-start(bf16[128,128]{1,0:T(8,128)(2,1)S(1)} %convert_element_type.212), channel_id=1, source_target_pairs={{32,0},{48,16},{33,1},{49,17},{34,2},{50,18},{35,3},{51,19},{36,4}... | collective-permute-start | bytes 98312 | tf_op jit(solution)/shard_map/ppermute | solution.py:289
  173.2 116.8 %collective-permute-start.26 = (bf16[128,128]{1,0:T(8,128)(2,1)S(1)}, bf16[128,128]{1,0:T(8,128)(2,1)S(1)}, u32[]{:S(2)}, u32[]{:S(2)}) collective-permute-start(bf16[128,128]{1,0:T(8,128)(2,1)S(1)} %convert_element_type.212), channel_id=1, source_target_pairs={{32,16},{48,0},{33,17},{49,1},{34,18},{50,2},{35,19},{51,3},{36,20... | collective-permute-start | bytes 98312 | tf_op jit(solution)/shard_map/ppermute | solution.py:290
  174.6 115.5 %collective-permute-start.28 = (bf16[128,256]{1,0:T(8,128)(2,1)S(1)}, bf16[128,256]{1,0:T(8,128)(2,1)S(1)}, u32[]{:S(2)}, u32[]{:S(2)}) collective-permute-start(bf16[128,256]{1,0:T(8,128)(2,1)S(1)} %maximum_select_fusion.2), channel_id=1, source_target_pairs={{64,0},{80,16},{65,1},{81,17},{66,2},{82,18},{67,3},{83,19},{68,4}... | collective-permute-start | bytes 196616 | tf_op jit(solution)/shard_map/ppermute | solution.py:300
  310.2 9.8 %all-to-all-start.14 = ((bf16[8,8,128]{2,1,0:T(8,128)(2,1)}), bf16[8,8,128]{2,1,0:T(8,128)(2,1)S(1)}, u32[]{:S(2)}, u32[]{:S(2)}) async-start(bf16[8,8,128]{2,1,0:T(8,128)(2,1)} %fusion.41), calls=%async_computation.14 | async-start | bytes 32768 | tf_op jit(solution)/shard_map/all_to_all | solution.py:22
  (5 other events, 369.9 us)
Sparse Core Ops, SparseCore 0:
  21.1 95.3 all-gather.1

commit v10 on v9

--- a/solution.py
+++ b/solution.py
@@ -81,7 +81,7 @@
             out_ref[here, :] = (old + new).astype(out_ref.dtype)
 
 
-def chunked(kernel, at, right, columns, right_block, lefts, chunk, rows=None):
+def chunked(kernel, at, right, columns, right_block, lefts, chunk, rows=None, aliases=None):
     rows = lefts[0].shape[0] if rows is None else rows
 
     def row_map(count):
@@ -98,6 +98,7 @@
         kernel,
         grid_spec=grid_spec,
         out_shape=jax.ShapeDtypeStruct((rows, columns), BF),
+        input_output_aliases=aliases or {},
     )(at, right, *lefts)
 
 
@@ -226,7 +227,10 @@
 
         def merge_even(at, whole, through, low_half, folded):
             lefts = (through, low_half, folded)
-            return chunked(merge_kernel, at, whole, section, 0, lefts, 2 * width)
+            aliases = {4: 0}
+            return chunked(
+                merge_kernel, at, whole, section, 0, lefts, 2 * width, aliases=aliases
+            )
 
         return lax.cond(
             even,

time: 329 us -> 329 us (level)
  no operation moved by 1% of the time
where the time goes in v10:
time: 329 us; the launch traced here: 328 us
  waiting for transfers between devices  153 us (47%)
  starting transfers between devices  46.1 us (14%)
  blocking collectives  43 us (13%)
  Pallas kernels  23.4 us (7%)
  matrix products  20.8 us (6%)
  local copies, waits for them, and re-layouts  19.5 us (6%)
  between operations  15.6 us (5%)
  other arithmetic  6.17 us (2%)
    ppermute x2, waiting for transfers between devices, on_device(): straight = lax.ppermute(low, 'row', same)  110 us
    all_to_all x3, blocking collectives, exchange(): return lax.all_to_all(x, axis, 0, 0, tiled=True)  43 us
    pallas_call x2, Pallas kernels, chunked(): pl.pallas_call(kernel, grid_spec=grid_spec, out_shape=jax.ShapeDtypeStruc...  23.4 us
    all_gather x1, waiting for transfers between devices, on_device(): whole = lax.all_gather(held, 'col', axis=0, tiled=True)  17.7 us
    dot_general x12, matrix products, dot_nn(): lax.dot_general(a, b, (((1,), (0,)), ((), ())), preferred_element_type=F32)  15.1 us
    all_to_all x2, starting transfers between devices, exchange(): return lax.all_to_all(x, axis, 0, 0, tiled=True)  12 us
    all_to_all x2, waiting for transfers between devices, exchange(): return lax.all_to_all(x, axis, 0, 0, tiled=True)  9.38 us
    unnamed x12, local copies, waits for them, and re-layouts  7.67 us
  transfers between devices with their start and end apart: 32, of which 9 were waited for; matrix products, arithmetic and copies ran while one was open for 9% of the time, Pallas kernels for 7%

profile of v10, /device:TPU:1, one launch (start us, length us, event | category | flops | bytes accessed | tf_op | source)
XLA Modules:
  0.0 327.7 jit_solution(12645080814802364259)
XLA Ops:
  7.2 6.8 %copy.22 = bf16[2048,8,128]{0,2,1:T(8,128)(2,1)} copy(bf16[2048,8,128]{2,1,0:T(8,128)(2,1)} %param.47) | data formatting | bytes 8388608 | tf_op args[7]
  21.0 2.6 collective-permute-start.14
  24.4 5.7 %fusion.4 = f32[8,2048]{1,0:T(8,128)S(1)} fusion(bf16[1,2048,2048]{2,1,0:T(8,128)(2,1)} %param.41, bf16[1,8,2048]{2,1,0:T(8,128)(2,1)S(1)} %copy-done.1), kind=kOutput, calls=%fused_computation.23 | convolution fusion | flops 67108864 | bytes 8486912 | tf_op jit(solution)/shard_map/dot_general | solution.py:14
  31.0 6.9 %all-to-all-start.12 = ((bf16[8,8,128]{2,1,0:T(8,128)(2,1)}), bf16[8,8,128]{2,1,0:T(8,128)(2,1)S(1)}, u32[]{:S(2)}, u32[]{:S(2)}) async-start(bf16[8,8,128]{2,1,0:T(8,128)(2,1)} %broadcast_in_dim.33), calls=%async_computation.12 | async-start | bytes 32768 | tf_op jit(solution)/shard_map/all_to_all | solution.py:22
  37.9 4.7 %all-to-all-done.12 = bf16[8,8,128]{2,1,0:T(8,128)(2,1)S(1)} async-done(((bf16[8,8,128]{2,1,0:T(8,128)(2,1)}), bf16[8,8,128]{2,1,0:T(8,128)(2,1)S(1)}, u32[]{:S(2)}, u32[]{:S(2)}) %all-to-all-start.12) | async-done | bytes 16416 | tf_op jit(solution)/shard_map/all_to_all | solution.py:22
  44.0 13.9 %all_to_all.75 = f32[16,8,128]{2,1,0:T(8,128)S(1)} all-to-all(f32[16,8,128]{2,1,0:T(8,128)S(1)} %fusion.35), channel_id=1, replica_groups=mesh['row'=8,'col'=16] {'col'}, dimensions={0} | all-to-all | bytes 131072 | tf_op jit(solution)/shard_map/all_to_all | solution.py:22
  59.2 2.7 collective-permute-done.3
  63.4 15.6 %conditional.21 = (f32[128,128]{1,0:T(8,128)S(1)}) conditional(s32[]{:T(128)} %convert_element_type.191, f32[128,128]{1,0:T(8,128)S(1)} %bitcast.159, (bf16[16,128,128]{2,1,0:T(8,128)(2,1)S(1)}, f32[128,128]{1,0:T(8,128)S(1)}) %tuple.178), branch_computations={%region_0.1_spmd, %region_1.3_spmd} | conditional | flops 524288 | bytes 1835016 | solution.py:158
  63.4 15.5 %all_to_all.63 = bf16[16,128,128]{2,1,0:T(8,128)(2,1)S(1)} all-to-all(bf16[16,128,128]{2,1,0:T(8,128)(2,1)S(1)} %get-tuple-element.148), channel_id=1, replica_groups=mesh['row'=8,'col'=16] {'col'}, dimensions={0} | all-to-all | bytes 1048576 | tf_op jit(solution)/shard_map/cond/branch_1_fun/all_to_all | solution.py:22
  82.9 1.6 slice.75
  85.8 1.7 slice.76
  89.5 1.9 slice.77
  98.8 17.7 %all-gather.2.cloned.1.call-done.right_ref = bf16[2048,3072]{1,0:T(8,128)(2,1)} async-done(((bf16[128,3072]{1,0:T(8,128)(2,1)}), bf16[2048,3072]{1,0:T(8,128)(2,1)}) %all-gather.2.cloned.1.call-update) | async-done | bytes 12582928 | tf_op jit(solution)/shard_map/all_gather | solution.py:138
  116.5 2.7 conditional.27
  119.2 15.3 %shard_map.95 = bf16[1024,2048]{1,0:T(8,128)(2,1)} custom-call(s32[3]{0:T(128)S(1)} %pad_add_fusion.at_ref, bf16[2048,3072]{1,0:T(8,128)(2,1)} %all-gather.2.cloned.1.call-done.right_ref, bf16[1024,2048]{1,0:T(8,128)(2,1)} %bitcast.158, bf16[768,1024]{1,0:T(8,128)(2,1)} %get-tuple-element.193.passed_low_ref, bf16[768,1024]{1,0:T(8,128)(2,1)} %get-tuple-element.194.passed_high_ref), custom_call_target="tpu_custom_call" | custom-call | tf_op jit(solution)/shard_map/pallas_call | solution.py:97
  134.5 24.2 %conditional.28 = (bf16[1024,2048]{1,0:T(8,128)(2,1)}) conditional(s32[]{:T(128)} %convert_element_type.205, bf16[1024,2048]{1,0:T(8,128)(2,1)} %shard_map.95, (pred[]{:T(512)}, bf16[1024,2048]{1,0:T(8,128)(2,1)}, s32[3]{0:T(128)S(1)}, bf16[2048,3072]{1,0:T(8,128)(2,1)}) %tuple.126), branch_computations={%region_22.23_spmd, %region_23.28_spmd} | conditional | flops 1 | bytes 25166012 | solution.py:253
  134.5 4.7 %collective-permute-start.1 = (bf16[1024,2048]{1,0:T(8,128)(2,1)}, bf16[1024,2048]{1,0:T(8,128)(2,1)}, u32[]{:S(2)}, u32[]{:S(2)}) collective-permute-start(bf16[1024,2048]{1,0:T(8,128)(2,1)} %get-tuple-element.180), channel_id=1, source_target_pairs={{16,0},{48,32},{80,64},{17,1},{49,33},{81,65},{18,2},{50,34},{82,6... | collective-permute-start | bytes 12582920 | tf_op jit(solution)/shard_map/cond/branch_1_fun/ppermute | solution.py:220
  139.1 5.2 %collective-permute-done.1 = bf16[1024,2048]{1,0:T(8,128)(2,1)} collective-permute-done((bf16[1024,2048]{1,0:T(8,128)(2,1)}, bf16[1024,2048]{1,0:T(8,128)(2,1)}, u32[]{:S(2)}, u32[]{:S(2)}) %collective-permute-start.1) | collective-permute-done | bytes 4194336 | tf_op jit(solution)/shard_map/cond/branch_1_fun/ppermute | solution.py:220
  144.3 8.2 %conditional.6 = (bf16[1024,1024]{1,0:T(8,128)(2,1)S(1)}) conditional(s32[]{:T(128)} %convert_element_type.134, (s32[3]{0:T(128)S(1)}, bf16[2048,3072]{1,0:T(8,128)(2,1)}, bf16[1024,2048]{1,0:T(8,128)(2,1)}) %tuple.100, (s32[3]{0:T(128)S(1)}, bf16[2048,3072]{1,0:T(8,128)(2,1)}, bf16[1024,2048]{1,0:T(8,128)(2,1)}) %tuple.101), branch_computations={%region_24.24_spmd, %region_25.25_spmd} | conditional | bytes 8 | solution.py:225
  144.3 8.1 %branch_0_fun.3 = bf16[1024,1024]{1,0:T(8,128)(2,1)S(1)} custom-call(s32[3]{0:T(128)S(1)} %get-tuple-element.168.at_ref, bf16[2048,3072]{1,0:T(8,128)(2,1)} %get-tuple-element.169.right_ref, bf16[1024,2048]{1,0:T(8,128)(2,1)} %get-tuple-element.170.left_ref), custom_call_target="tpu_custom_call" | custom-call | tf_op jit(solution)/shard_map/cond/branch_1_fun/cond/branch_0_fun/pallas_call | solution.py:97
  152.5 3.6 %collective-permute-start.2 = (bf16[1024,1024]{1,0:T(8,128)(2,1)S(1)}, bf16[1024,1024]{1,0:T(8,128)(2,1)}, u32[]{:S(2)}, u32[]{:S(2)}) collective-permute-start(bf16[1024,1024]{1,0:T(8,128)(2,1)S(1)} %get-tuple-element.225), channel_id=1, source_target_pairs={{16,0},{48,32},{80,64},{17,1},{49,33},{81,65},{18,2},{50,34},{82,6... | collective-permute-start | bytes 6291464 | tf_op jit(solution)/shard_map/cond/branch_1_fun/ppermute | solution.py:226
  156.1 2.6 collective-permute-done.2
  162.9 2.0 fusion.28
  169.3 2.5 fusion.31
  176.1 110.2 %collective-permute-done.25 = bf16[128,128]{1,0:T(8,128)(2,1)S(1)} collective-permute-done((bf16[128,128]{1,0:T(8,128)(2,1)S(1)}, bf16[128,128]{1,0:T(8,128)(2,1)S(1)}, u32[]{:S(2)}, u32[]{:S(2)}) %collective-permute-start.25) | collective-permute-done | bytes 32800 | tf_op jit(solution)/shard_map/ppermute | solution.py:293
  286.2 3.8 %collective-permute-done.26 = bf16[128,128]{1,0:T(8,128)(2,1)S(1)} collective-permute-done((bf16[128,128]{1,0:T(8,128)(2,1)S(1)}, bf16[128,128]{1,0:T(8,128)(2,1)S(1)}, u32[]{:S(2)}, u32[]{:S(2)}) %collective-permute-start.26) | collective-permute-done | bytes 32800 | tf_op jit(solution)/shard_map/ppermute | solution.py:294
  290.1 2.9 convolution_convert_fusion.3
  293.0 15.2 %conditional.34 = (f32[8,2048]{1,0:T(8,128)}, f32[8,2048]{1,0:T(8,128)S(1)}) conditional(s32[]{:T(128)} %convert_element_type.182, f32[128,128]{1,0:T(8,128)S(1)} %get-tuple-element.237, bf16[128,2048]{1,0:T(8,128)(2,1)S(1)} %convolution_convert_fusion.3), branch_computations={%region_40.41_spmd, %region_41.43_spmd} | conditional | flops 507904 | bytes 1769488
  293.1 13.6 %all_to_all.74 = bf16[16,8,2048]{2,1,0:T(8,128)(2,1)S(1)} all-to-all(bf16[16,8,2048]{2,1,0:T(8,128)(2,1)S(1)} %bitcast.166), channel_id=1, replica_groups=mesh['row'=8,'col'=16] {'col'}, dimensions={0} | all-to-all | bytes 1048576 | tf_op jit(solution)/shard_map/cond/branch_1_fun/all_to_all | solution.py:22
  308.2 2.0 fusion.41
  310.2 5.1 %all-to-all-start.14 = ((bf16[8,8,128]{2,1,0:T(8,128)(2,1)}), bf16[8,8,128]{2,1,0:T(8,128)(2,1)S(1)}, u32[]{:S(2)}, u32[]{:S(2)}) async-start(bf16[8,8,128]{2,1,0:T(8,128)(2,1)} %fusion.41), calls=%async_computation.14 | async-start | bytes 32768 | tf_op jit(solution)/shard_map/all_to_all | solution.py:22
  315.3 4.7 %all-to-all-done.14 = bf16[8,8,128]{2,1,0:T(8,128)(2,1)S(1)} async-done(((bf16[8,8,128]{2,1,0:T(8,128)(2,1)}), bf16[8,8,128]{2,1,0:T(8,128)(2,1)S(1)}, u32[]{:S(2)}, u32[]{:S(2)}) %all-to-all-start.14) | async-done | bytes 16416 | tf_op jit(solution)/shard_map/all_to_all | solution.py:22
  (136 shorter events, 43.9 us)
Async XLA Ops:
  7.2 109.3 %all-gather.2.cloned.1.call-start = ((), (), s32[]{:S(2)}) async-start(), calls=%async_computation.15 | async-start | bytes 13369344 | tf_op jit(solution)/shard_map/all_gather | solution.py:138
  15.2 3.7 %collective-permute-start.13 = (bf16[128,1024]{1,0:T(8,128)(2,1)S(1)}, bf16[128,1024]{1,0:T(8,128)(2,1)S(1)}, u32[]{:S(2)}, u32[]{:S(2)}) collective-permute-start(bf16[128,1024]{1,0:T(8,128)(2,1)S(1)} %broadcast_select_fusion), channel_id=1, source_target_pairs={{0,16},{32,48},{64,80},{112,96},{1,17},{33,49},{65,81},{113,97},{2... | collective-permute-start | bytes 786440 | tf_op jit(solution)/shard_map/ppermute | solution.py:135
  21.0 77.8 %collective-permute-start.14 = (bf16[1024,2048]{1,0:T(8,128)(2,1)}, bf16[1024,2048]{1,0:T(8,128)(2,1)}, u32[]{:S(2)}, u32[]{:S(2)}) collective-permute-start(bf16[1024,2048]{1,0:T(8,128)(2,1)} %bitcast.150), channel_id=1, source_target_pairs={{96,112},{97,113},{98,114},{99,115},{100,116},{101,117},{102,118},... | collective-permute-start | bytes 12582920 | tf_op jit(solution)/shard_map/ppermute | solution.py:178
  31.0 11.6 %all-to-all-start.12 = ((bf16[8,8,128]{2,1,0:T(8,128)(2,1)}), bf16[8,8,128]{2,1,0:T(8,128)(2,1)S(1)}, u32[]{:S(2)}, u32[]{:S(2)}) async-start(bf16[8,8,128]{2,1,0:T(8,128)(2,1)} %broadcast_in_dim.33), calls=%async_computation.12 | async-start | bytes 32768 | tf_op jit(solution)/shard_map/all_to_all | solution.py:22
  57.9 4.0 %collective-permute-start.3 = (bf16[128,128]{1,0:T(8,128)(2,1)S(1)}, bf16[128,128]{1,0:T(8,128)(2,1)S(1)}, u32[]{:S(2)}, u32[]{:S(2)}) collective-permute-start(bf16[128,128]{1,0:T(8,128)(2,1)S(1)} %bitcast_convert_fusion), channel_id=1, source_target_pairs={{0,16},{1,17},{2,18},{3,19},{4,20},{5,21},{6,22},{7,23},{8,24},{9,... | collective-permute-start | bytes 98312 | tf_op jit(solution)/shard_map/ppermute | solution.py:170
  79.1 2.6 collective-permute-start.4
  82.2 2.3 collective-permute-start.5
  85.1 2.4 collective-permute-start.6
  88.9 4.6 %collective-permute-start.7 = (bf16[128,640]{1,0:T(8,128)(2,1)}, bf16[128,640]{1,0:T(8,128)(2,1)S(1)}, u32[]{:S(2)}, u32[]{:S(2)}) collective-permute-start(bf16[128,640]{1,0:T(8,128)(2,1)} %pad_maximum_fusion.3), channel_id=1, source_target_pairs={{64,80},{65,81},{66,82},{67,83},{68,84},{69,85},{70,86},{71,87},{7... | collective-permute-start | bytes 491528 | tf_op jit(solution)/shard_map/ppermute | solution.py:170
  91.5 4.2 %collective-permute-start.12 = (bf16[128,128]{1,0:T(8,128)(2,1)S(1)}, bf16[128,128]{1,0:T(8,128)(2,1)S(1)}, u32[]{:S(2)}, u32[]{:S(2)}) collective-permute-start(bf16[128,128]{1,0:T(8,128)(2,1)S(1)} %convert_element_type.198), channel_id=1, source_target_pairs={{96,112},{97,113},{98,114},{99,115},{100,116},{101,117},{102,118},... | collective-permute-start | bytes 98312 | tf_op jit(solution)/shard_map/ppermute | solution.py:179
  92.2 2.8 collective-permute-start.8
  94.3 3.4 %collective-permute-start.9 = (bf16[128,128]{1,0:T(8,128)(2,1)S(1)}, bf16[128,128]{1,0:T(8,128)(2,1)S(1)}, u32[]{:S(2)}, u32[]{:S(2)}) collective-permute-start(bf16[128,128]{1,0:T(8,128)(2,1)S(1)} %convert_element_type.204), channel_id=1, source_target_pairs={{80,96},{81,97},{82,98},{83,99},{84,100},{85,101},{86,102},{87,103... | collective-permute-start | bytes 98312 | tf_op jit(solution)/shard_map/ppermute | solution.py:180
  94.9 3.7 %collective-permute-start.10 = (bf16[128,640]{1,0:T(8,128)(2,1)}, bf16[128,640]{1,0:T(8,128)(2,1)S(1)}, u32[]{:S(2)}, u32[]{:S(2)}) collective-permute-start(bf16[128,640]{1,0:T(8,128)(2,1)} %collective-permute-done.8), channel_id=1, source_target_pairs={{96,112},{97,113},{98,114},{99,115},{100,116},{101,117},{102,118},... | collective-permute-start | bytes 491528 | tf_op jit(solution)/shard_map/ppermute | solution.py:182
  95.7 2.9 collective-permute-start.11
  96.4 63.0 %collective-permute-start.16 = (bf16[128,128]{1,0:T(8,128)(2,1)S(1)}, bf16[128,128]{1,0:T(8,128)(2,1)S(1)}, u32[]{:S(2)}, u32[]{:S(2)}) collective-permute-start(bf16[128,128]{1,0:T(8,128)(2,1)S(1)} %convert_element_type.204), channel_id=1, source_target_pairs={{16,0},{48,32},{80,64},{17,1},{49,33},{81,65},{18,2},{50,34},{82,6... | collective-permute-start | bytes 98312 | tf_op jit(solution)/shard_map/ppermute | solution.py:246
  134.5 9.8 %collective-permute-start.1 = (bf16[1024,2048]{1,0:T(8,128)(2,1)}, bf16[1024,2048]{1,0:T(8,128)(2,1)}, u32[]{:S(2)}, u32[]{:S(2)}) collective-permute-start(bf16[1024,2048]{1,0:T(8,128)(2,1)} %get-tuple-element.180), channel_id=1, source_target_pairs={{16,0},{48,32},{80,64},{17,1},{49,33},{81,65},{18,2},{50,34},{82,6... | collective-permute-start | bytes 12582920 | tf_op jit(solution)/shard_map/cond/branch_1_fun/ppermute | solution.py:220
  152.5 6.2 %collective-permute-start.2 = (bf16[1024,1024]{1,0:T(8,128)(2,1)S(1)}, bf16[1024,1024]{1,0:T(8,128)(2,1)}, u32[]{:S(2)}, u32[]{:S(2)}) collective-permute-start(bf16[1024,1024]{1,0:T(8,128)(2,1)S(1)} %get-tuple-element.225), channel_id=1, source_target_pairs={{16,0},{48,32},{80,64},{17,1},{49,33},{81,65},{18,2},{50,34},{82,6... | collective-permute-start | bytes 6291464 | tf_op jit(solution)/shard_map/cond/branch_1_fun/ppermute | solution.py:226
  158.7 2.1 collective-permute-start.15
  159.4 3.5 %collective-permute-start.19 = (bf16[128,128]{1,0:T(8,128)(2,1)S(1)}, bf16[128,128]{1,0:T(8,128)(2,1)S(1)}, u32[]{:S(2)}, u32[]{:S(2)}) collective-permute-start(bf16[128,128]{1,0:T(8,128)(2,1)S(1)} %convert_element_type.207), channel_id=1, source_target_pairs={{112,80},{113,81},{114,82},{115,83},{116,84},{117,85},{118,86},{11... | collective-permute-start | bytes 98312 | tf_op jit(solution)/shard_map/ppermute | solution.py:262
  160.0 2.8 collective-permute-start.20
  160.8 2.1 collective-permute-start.17
  161.5 1.4 collective-permute-start.18
  162.2 4.3 %collective-permute-start.23 = (bf16[128,128]{1,0:T(8,128)(2,1)S(1)}, bf16[128,128]{1,0:T(8,128)(2,1)S(1)}, u32[]{:S(2)}, u32[]{:S(2)}) collective-permute-start(bf16[128,128]{1,0:T(8,128)(2,1)S(1)} %convert_element_type.208), channel_id=1, source_target_pairs={{96,112},{97,113},{98,114},{99,115},{100,116},{101,117},{102,118},... | collective-permute-start | bytes 98312 | tf_op jit(solution)/shard_map/ppermute | solution.py:276
  165.2 4.0 %collective-permute-start.21 = (bf16[128,128]{1,0:T(8,128)(2,1)S(1)}, bf16[128,128]{1,0:T(8,128)(2,1)S(1)}, u32[]{:S(2)}, u32[]{:S(2)}) collective-permute-start(bf16[128,128]{1,0:T(8,128)(2,1)S(1)} %convert_element_type.210), channel_id=1, source_target_pairs={{64,32},{80,48},{65,33},{81,49},{66,34},{82,50},{67,35},{83,51},{6... | collective-permute-start | bytes 98312 | tf_op jit(solution)/shard_map/ppermute | solution.py:293
  165.8 3.4 %collective-permute-start.22 = (bf16[128,128]{1,0:T(8,128)(2,1)S(1)}, bf16[128,128]{1,0:T(8,128)(2,1)S(1)}, u32[]{:S(2)}, u32[]{:S(2)}) collective-permute-start(bf16[128,128]{1,0:T(8,128)(2,1)S(1)} %convert_element_type.210), channel_id=1, source_target_pairs={{64,48},{80,32},{65,49},{81,33},{66,50},{82,34},{67,51},{83,35},{6... | collective-permute-start | bytes 98312 | tf_op jit(solution)/shard_map/ppermute | solution.py:294
  166.5 2.7 collective-permute-start.24
  167.2 122.8 %collective-permute-start.29 = (bf16[128,256]{1,0:T(8,128)(2,1)S(1)}, bf16[128,256]{1,0:T(8,128)(2,1)S(1)}, u32[]{:S(2)}, u32[]{:S(2)}) collective-permute-start(bf16[128,256]{1,0:T(8,128)(2,1)S(1)} %maximum_select_fusion.1), channel_id=1, source_target_pairs={{96,0},{112,16},{97,1},{113,17},{98,2},{114,18},{99,3},{115,19},{1... | collective-permute-start | bytes 196616 | tf_op jit(solution)/shard_map/ppermute | solution.py:283
  168.5 6.0 %collective-permute-start.27 = (bf16[128,128]{1,0:T(8,128)(2,1)S(1)}, bf16[128,128]{1,0:T(8,128)(2,1)S(1)}, u32[]{:S(2)}, u32[]{:S(2)}) collective-permute-start(bf16[128,128]{1,0:T(8,128)(2,1)S(1)} %convert_element_type.210), channel_id=1, source_target_pairs={{64,80},{80,64},{65,81},{81,65},{66,82},{82,66},{67,83},{83,67},{6... | collective-permute-start | bytes 98312 | tf_op jit(solution)/shard_map/ppermute | solution.py:298
  171.9 114.3 %collective-permute-start.25 = (bf16[128,128]{1,0:T(8,128)(2,1)S(1)}, bf16[128,128]{1,0:T(8,128)(2,1)S(1)}, u32[]{:S(2)}, u32[]{:S(2)}) collective-permute-start(bf16[128,128]{1,0:T(8,128)(2,1)S(1)} %convert_element_type.212), channel_id=1, source_target_pairs={{32,0},{48,16},{33,1},{49,17},{34,2},{50,18},{35,3},{51,19},{36,4}... | collective-permute-start | bytes 98312 | tf_op jit(solution)/shard_map/ppermute | solution.py:293
  173.2 116.8 %collective-permute-start.26 = (bf16[128,128]{1,0:T(8,128)(2,1)S(1)}, bf16[128,128]{1,0:T(8,128)(2,1)S(1)}, u32[]{:S(2)}, u32[]{:S(2)}) collective-permute-start(bf16[128,128]{1,0:T(8,128)(2,1)S(1)} %convert_element_type.212), channel_id=1, source_target_pairs={{32,16},{48,0},{33,17},{49,1},{34,18},{50,2},{35,19},{51,3},{36,20... | collective-permute-start | bytes 98312 | tf_op jit(solution)/shard_map/ppermute | solution.py:294
  174.6 115.5 %collective-permute-start.28 = (bf16[128,256]{1,0:T(8,128)(2,1)S(1)}, bf16[128,256]{1,0:T(8,128)(2,1)S(1)}, u32[]{:S(2)}, u32[]{:S(2)}) collective-permute-start(bf16[128,256]{1,0:T(8,128)(2,1)S(1)} %maximum_select_fusion.2), channel_id=1, source_target_pairs={{64,0},{80,16},{65,1},{81,17},{66,2},{82,18},{67,3},{83,19},{68,4}... | collective-permute-start | bytes 196616 | tf_op jit(solution)/shard_map/ppermute | solution.py:304
  310.2 9.8 %all-to-all-start.14 = ((bf16[8,8,128]{2,1,0:T(8,128)(2,1)}), bf16[8,8,128]{2,1,0:T(8,128)(2,1)S(1)}, u32[]{:S(2)}, u32[]{:S(2)}) async-start(bf16[8,8,128]{2,1,0:T(8,128)(2,1)} %fusion.41), calls=%async_computation.14 | async-start | bytes 32768 | tf_op jit(solution)/shard_map/all_to_all | solution.py:22
  (5 other events, 369.9 us)
Sparse Core Ops, SparseCore 0:
  21.1 95.3 all-gather.1

commit v11 on v10

--- a/solution.py
+++ b/solution.py
@@ -28,10 +28,12 @@
 
 
 def fold_kernel(at_ref, right_ref, left_ref, passed_low_ref, passed_high_ref, out_ref):
-    step = pl.program_id(0)
+    part_of, step = pl.program_id(0), pl.program_id(1)
     first, own, last = at_ref[0], at_ref[1], at_ref[2]
-
-    @pl.when((step >= first) & (own == last) & (step < pl.num_programs(0) - 1))
+    final = pl.num_programs(1) - 1
+    columns = out_ref.shape[1]
+
+    @pl.when((step >= first) & (own == last) & (step < final))
     def _():
         half = passed_low_ref.shape[1]
         low = left_ref[:, :half].astype(F32) - passed_low_ref[...].astype(F32)
@@ -40,20 +42,19 @@
         total += jnp.dot(high.astype(BF), right_ref[half:, :], preferred_element_type=F32)
         out_ref[...] = total.astype(out_ref.dtype)
 
-    @pl.when((step >= first) & ((own != last) | (step == pl.num_programs(0) - 1)))
+    @pl.when((step >= first) & ((own != last) | (step == final)))
     def _():
         total = jnp.dot(left_ref[...], right_ref[...], preferred_element_type=F32)
         width = out_ref.shape[0] // 2
         for part in range(2):
             here = slice(part * width, (part + 1) * width)
             kept = (2 * step + part == own).astype(F32)
-            out_ref[here, :] = jnp.where(
-                kept > 0.5, left_ref[here, :], total[here, :].astype(out_ref.dtype)
-            )
+            old = left_ref[here, pl.ds(pl.multiple_of(part_of * columns, columns), columns)]
+            out_ref[here, :] = jnp.where(kept > 0.5, old, total[here, :].astype(out_ref.dtype))
 
 
 def through_kernel(at_ref, right_ref, left_ref, out_ref):
-    @pl.when(pl.program_id(0) >= at_ref[0])
+    @pl.when(pl.program_id(1) >= at_ref[0])
     def _():
         out_ref[...] = jnp.dot(
             left_ref[...], right_ref[...], preferred_element_type=F32
@@ -61,7 +62,7 @@
 
 
 def merge_kernel(at_ref, right_ref, high_ref, low_ref, folded_ref, out_ref):
-    step = pl.program_id(0)
+    step = pl.program_id(1)
     first, own = at_ref[0], at_ref[1]
 
     @pl.when(step >= first)
@@ -83,16 +84,34 @@
 
 def chunked(kernel, at, right, columns, right_block, lefts, chunk, rows=None, aliases=None):
     rows = lefts[0].shape[0] if rows is None else rows
-
-    def row_map(count):
-        return lambda step, at: (jnp.minimum(jnp.maximum(step, at[0]), count - 1), 0)
+    part = columns // 2
+
+    def left_spec(index, x):
+        count = x.shape[0] // chunk
+
+        def whole(side, step, at):
+            return (jnp.minimum(jnp.maximum(step, at[0]), count - 1), 0)
+
+        def halves(side, step, at):
+            return (jnp.minimum(jnp.maximum(step, at[0]), count - 1), side)
+
+        if aliases and index + 2 in aliases:
+            return pl.BlockSpec((chunk, part), halves)
+        return pl.BlockSpec((chunk, x.shape[1]), whole)
+
+    def out_map(side, step, at):
+        return (jnp.minimum(jnp.maximum(step, at[0]), rows // chunk - 1), side)
 
     grid_spec = pltpu.PrefetchScalarGridSpec(
         num_scalar_prefetch=1,
-        grid=(rows // chunk,),
-        in_specs=[pl.BlockSpec((right.shape[0], columns), lambda step, at: (0, right_block))]
-        + [pl.BlockSpec((chunk, x.shape[1]), row_map(x.shape[0] // chunk)) for x in lefts],
-        out_specs=pl.BlockSpec((chunk, columns), row_map(rows // chunk)),
+        grid=(2, rows // chunk),
+        in_specs=[
+            pl.BlockSpec(
+                (right.shape[0], part), lambda side, step, at: (0, 2 * right_block + side)
+            )
+        ]
+        + [left_spec(index, x) for index, x in enumerate(lefts)],
+        out_specs=pl.BlockSpec((chunk, part), out_map),
     )
     return pl.pallas_call(
         kernel,
@@ -157,12 +176,17 @@
 
         return lax.cond(turn, reduce_columns, lambda run, tiles: run, run, tiles_of(partial))
 
-    def take_whole_turn(turn, run, sign, *operands):
-        def reduce_columns(run, x, weights):
-            total = jnp.sum(exchange(tiles_of(dot_nn(x, weights)), "col").astype(F32), axis=0)
-            return run - total if sign else total
-
-        return lax.cond(turn, reduce_columns, lambda run, *rest: run, run, *operands)
+    def reduce_product(x, weights):
+        return jnp.sum(exchange(tiles_of(dot_nn(x, weights)), "col").astype(F32), axis=0)
+
+    def take_whole_turn(turn, run, *operands):
+        return lax.cond(
+            turn,
+            lambda run, x, weights: reduce_product(x, weights),
+            lambda run, *rest: run,
+            run,
+            *operands,
+        )
 
     low = run.astype(BF)
     known = low
@@ -198,16 +222,27 @@
         return lax.ppermute(mine, "row", [(last - 1, last)]), mine
 
     def pass_nothing(whole, factor, partner):
-        nothing = jnp.zeros(((last - 1) * width, half), BF)
-        return nothing, nothing
+        shape = jax.ShapeDtypeStruct(((last - 1) * width, half), BF)
+        anywhere = pl.BlockSpec(memory_space=pl.ANY)
+        return pl.pallas_call(
+            lambda low_ref, high_ref: None,
+            out_shape=(shape, shape),
+            out_specs=(anywhere, anywhere),
+        )()
 
     passed_low, passed_high = lax.cond(
         row_at >= last - 1, pass_on, pass_nothing, whole, factor, partner
     )
-    known = jnp.concatenate([ahead, newest], axis=1)
     forward = low
-    run = take_whole_turn(
-        row_at == last - 1, run, -1, known, factor[: (last - 1) * width]
+    run = lax.cond(
+        row_at == last - 1,
+        lambda run, ahead, newest, factor: run
+        - reduce_product(jnp.concatenate([ahead, newest], axis=1), factor[: (last - 1) * width]),
+        lambda run, *rest: run,
+        run,
+        ahead,
+        newest,
+        factor,
     )
 
     first = jnp.where(row_at == last, 0, row_at // 2)
@@ -255,7 +290,7 @@
     )
 
     x = jnp.concatenate([-ahead_last, -newest_last, -partner_low, forward], axis=1)
-    run = take_whole_turn(row_at == last, run, 0, x, merged)
+    run = take_whole_turn(row_at == last, run, x, merged)
     low = run.astype(BF)
     seventh = low
     arrived = lax.ppermute(seventh, "row", [(last, last - 1)])
@@ -264,7 +299,6 @@
     run = take_whole_turn(
         row_at == last - 1,
         run,
-        0,
         jnp.concatenate([low, -arrived], axis=1),
         merged[(last - 1) * width :],
     )

time: 329 us -> 334 us (1.015)
  Pallas kernels: 23.4 us -> 27.8 us
    pallas_call x2, Pallas kernels: 23.4 us -> 27.8 us  [chunked(): pl.pallas_call(kernel, grid_spec=grid_spec, out_shape=jax.ShapeDtypeStruc...]
    ppermute x2, waiting for transfers between devices: 110 us -> 114 us  [on_device(): straight = lax.ppermute(low, 'row', same)]
  transfers between devices with their start and end apart: 32 -> 32, of which waited for: 9 -> 9; matrix products, arithmetic and copies ran while one was open for 9% -> 8% of each run, Pallas kernels for 7% -> 8%
where the time goes in v11:
time: 334 us; the launch traced here: 333 us
  waiting for transfers between devices  156 us (47%)
  starting transfers between devices  46.5 us (14%)
  blocking collectives  43 us (13%)
  Pallas kernels  27.8 us (8%)
  matrix products  20.8 us (6%)
  local copies, waits for them, and re-layouts  16.8 us (5%)
  between operations  15.6 us (5%)
  other arithmetic  6.11 us (2%)
    ppermute x2, waiting for transfers between devices, on_device(): straight = lax.ppermute(low, 'row', same)  114 us
    all_to_all x3, blocking collectives, exchange(): return lax.all_to_all(x, axis, 0, 0, tiled=True)  43 us
    pallas_call x2, Pallas kernels, chunked(): pl.pallas_call(kernel, grid_spec=grid_spec, out_shape=jax.ShapeDtypeStruc...  27.8 us
    all_gather x1, waiting for transfers between devices, on_device(): whole = lax.all_gather(held, 'col', axis=0, tiled=True)  17 us
    dot_general x12, matrix products, dot_nn(): lax.dot_general(a, b, (((1,), (0,)), ((), ())), preferred_element_type=F32)  15.1 us
    all_to_all x2, starting transfers between devices, exchange(): return lax.all_to_all(x, axis, 0, 0, tiled=True)  12 us
    all_to_all x2, waiting for transfers between devices, exchange(): return lax.all_to_all(x, axis, 0, 0, tiled=True)  9.38 us
    unnamed x12, local copies, waits for them, and re-layouts  7.63 us
  transfers between devices with their start and end apart: 32, of which 9 were waited for; matrix products, arithmetic and copies ran while one was open for 8% of the time, Pallas kernels for 8%

profile of v11, /device:TPU:1, one launch (start us, length us, event | category | flops | bytes accessed | tf_op | source)
XLA Modules:
  0.0 332.7 jit_solution(15048204039020231333)
XLA Ops:
  7.2 6.8 %copy.30 = bf16[2048,8,128]{0,2,1:T(8,128)(2,1)} copy(bf16[2048,8,128]{2,1,0:T(8,128)(2,1)} %param.47) | data formatting | bytes 8388608 | tf_op args[7]
  21.0 2.7 collective-permute-start.14
  24.3 5.7 %fusion.15 = f32[8,2048]{1,0:T(8,128)S(1)} fusion(bf16[1,2048,2048]{2,1,0:T(8,128)(2,1)} %param.41, bf16[1,8,2048]{2,1,0:T(8,128)(2,1)S(1)} %copy-done.1), kind=kOutput, calls=%fused_computation.29 | convolution fusion | flops 67108864 | bytes 8486912 | tf_op jit(solution)/shard_map/dot_general | solution.py:14
  30.9 6.9 %all-to-all-start.12 = ((bf16[8,8,128]{2,1,0:T(8,128)(2,1)}), bf16[8,8,128]{2,1,0:T(8,128)(2,1)S(1)}, u32[]{:S(2)}, u32[]{:S(2)}) async-start(bf16[8,8,128]{2,1,0:T(8,128)(2,1)} %broadcast_in_dim.33), calls=%async_computation.12 | async-start | bytes 32768 | tf_op jit(solution)/shard_map/all_to_all | solution.py:22
  37.8 4.7 %all-to-all-done.12 = bf16[8,8,128]{2,1,0:T(8,128)(2,1)S(1)} async-done(((bf16[8,8,128]{2,1,0:T(8,128)(2,1)}), bf16[8,8,128]{2,1,0:T(8,128)(2,1)S(1)}, u32[]{:S(2)}, u32[]{:S(2)}) %all-to-all-start.12) | async-done | bytes 16416 | tf_op jit(solution)/shard_map/all_to_all | solution.py:22
  42.5 1.4 fusion.46
  43.9 13.9 %all_to_all.75 = f32[16,8,128]{2,1,0:T(8,128)S(1)} all-to-all(f32[16,8,128]{2,1,0:T(8,128)S(1)} %fusion.46), channel_id=1, replica_groups=mesh['row'=8,'col'=16] {'col'}, dimensions={0} | all-to-all | bytes 131072 | tf_op jit(solution)/shard_map/all_to_all | solution.py:22
  59.2 2.7 collective-permute-done.3
  63.4 15.6 %conditional.21 = (f32[128,128]{1,0:T(8,128)S(1)}) conditional(s32[]{:T(128)} %convert_element_type.191, f32[128,128]{1,0:T(8,128)S(1)} %bitcast.156, (bf16[16,128,128]{2,1,0:T(8,128)(2,1)S(1)}, f32[128,128]{1,0:T(8,128)S(1)}) %tuple.179), branch_computations={%region_0.1_spmd, %region_1.3_spmd} | conditional | flops 524288 | bytes 1835016 | solution.py:177
  63.4 15.5 %all_to_all.63 = bf16[16,128,128]{2,1,0:T(8,128)(2,1)S(1)} all-to-all(bf16[16,128,128]{2,1,0:T(8,128)(2,1)S(1)} %get-tuple-element.150), channel_id=1, replica_groups=mesh['row'=8,'col'=16] {'col'}, dimensions={0} | all-to-all | bytes 1048576 | tf_op jit(solution)/shard_map/cond/branch_1_fun/all_to_all | solution.py:22
  82.8 1.6 slice.68
  85.8 1.7 slice.69
  90.8 2.0 slice.70
  99.4 17.0 %all-gather.2.cloned.1.call-done.right_ref = bf16[2048,3072]{1,0:T(8,128)(2,1)} async-done(((bf16[128,3072]{1,0:T(8,128)(2,1)}), bf16[2048,3072]{1,0:T(8,128)(2,1)}) %all-gather.2.cloned.1.call-update) | async-done | bytes 12582928 | tf_op jit(solution)/shard_map/all_gather | solution.py:157
  116.4 17.2 %shard_map.95 = bf16[1024,2048]{1,0:T(8,128)(2,1)} custom-call(s32[3]{0:T(128)S(1)} %pad_add_fusion.at_ref, bf16[2048,3072]{1,0:T(8,128)(2,1)} %all-gather.2.cloned.1.call-done.right_ref, bf16[1024,2048]{1,0:T(8,128)(2,1)} %bitcast.155, bf16[768,1024]{1,0:T(8,128)(2,1)} %get-tuple-element.196.passed_low_ref, bf16[768,1024]{1,0:T(8,128)(2,1)} %get-tuple-element.197.passed_high_ref), custom_call_target="tpu_custom_call" | custom-call | tf_op jit(solution)/shard_map/pallas_call | solution.py:116
  133.6 26.7 %conditional.28 = (bf16[1024,2048]{1,0:T(8,128)(2,1)}) conditional(s32[]{:T(128)} %convert_element_type.205, bf16[1024,2048]{1,0:T(8,128)(2,1)} %shard_map.95, (pred[]{:T(512)}, bf16[1024,2048]{1,0:T(8,128)(2,1)}, s32[3]{0:T(128)S(1)}, bf16[2048,3072]{1,0:T(8,128)(2,1)}) %tuple.125), branch_computations={%region_22.23_spmd, %region_23.28_spmd} | conditional | flops 1 | bytes 25166012 | solution.py:288
  133.6 4.7 %collective-permute-start.1 = (bf16[1024,2048]{1,0:T(8,128)(2,1)}, bf16[1024,2048]{1,0:T(8,128)(2,1)}, u32[]{:S(2)}, u32[]{:S(2)}) collective-permute-start(bf16[1024,2048]{1,0:T(8,128)(2,1)} %get-tuple-element.183), channel_id=1, source_target_pairs={{16,0},{48,32},{80,64},{17,1},{49,33},{81,65},{18,2},{50,34},{82,6... | collective-permute-start | bytes 12582920 | tf_op jit(solution)/shard_map/cond/branch_1_fun/ppermute | solution.py:255
  138.3 5.2 %collective-permute-done.1 = bf16[1024,2048]{1,0:T(8,128)(2,1)} collective-permute-done((bf16[1024,2048]{1,0:T(8,128)(2,1)}, bf16[1024,2048]{1,0:T(8,128)(2,1)}, u32[]{:S(2)}, u32[]{:S(2)}) %collective-permute-start.1) | collective-permute-done | bytes 4194336 | tf_op jit(solution)/shard_map/cond/branch_1_fun/ppermute | solution.py:255
  143.5 10.7 %conditional.6 = (bf16[1024,1024]{1,0:T(8,128)(2,1)S(1)}) conditional(s32[]{:T(128)} %convert_element_type.134, (s32[3]{0:T(128)S(1)}, bf16[2048,3072]{1,0:T(8,128)(2,1)}, bf16[1024,2048]{1,0:T(8,128)(2,1)}) %tuple.99, (s32[3]{0:T(128)S(1)}, bf16[2048,3072]{1,0:T(8,128)(2,1)}, bf16[1024,2048]{1,0:T(8,128)(2,1)}) %tuple.100), branch_computations={%region_24.24_spmd, %region_25.25_spmd} | conditional | bytes 8 | solution.py:260
  143.5 10.6 %branch_0_fun.5 = bf16[1024,1024]{1,0:T(8,128)(2,1)S(1)} custom-call(s32[3]{0:T(128)S(1)} %get-tuple-element.171.at_ref, bf16[2048,3072]{1,0:T(8,128)(2,1)} %get-tuple-element.172.right_ref, bf16[1024,2048]{1,0:T(8,128)(2,1)} %get-tuple-element.173.left_ref), custom_call_target="tpu_custom_call" | custom-call | tf_op jit(solution)/shard_map/cond/branch_1_fun/cond/branch_0_fun/pallas_call | solution.py:116
  154.1 3.6 %collective-permute-start.2 = (bf16[1024,1024]{1,0:T(8,128)(2,1)S(1)}, bf16[1024,1024]{1,0:T(8,128)(2,1)}, u32[]{:S(2)}, u32[]{:S(2)}) collective-permute-start(bf16[1024,1024]{1,0:T(8,128)(2,1)S(1)} %get-tuple-element.226), channel_id=1, source_target_pairs={{16,0},{48,32},{80,64},{17,1},{49,33},{81,65},{18,2},{50,34},{82,6... | collective-permute-start | bytes 6291464 | tf_op jit(solution)/shard_map/cond/branch_1_fun/ppermute | solution.py:261
  157.7 2.6 collective-permute-done.2
  164.6 2.0 fusion.39
  170.9 2.5 fusion.42
  177.5 113.8 %collective-permute-done.25 = bf16[128,128]{1,0:T(8,128)(2,1)S(1)} collective-permute-done((bf16[128,128]{1,0:T(8,128)(2,1)S(1)}, bf16[128,128]{1,0:T(8,128)(2,1)S(1)}, u32[]{:S(2)}, u32[]{:S(2)}) %collective-permute-start.25) | collective-permute-done | bytes 32800 | tf_op jit(solution)/shard_map/ppermute | solution.py:327
  291.3 3.8 %collective-permute-done.26 = bf16[128,128]{1,0:T(8,128)(2,1)S(1)} collective-permute-done((bf16[128,128]{1,0:T(8,128)(2,1)S(1)}, bf16[128,128]{1,0:T(8,128)(2,1)S(1)}, u32[]{:S(2)}, u32[]{:S(2)}) %collective-permute-start.26) | collective-permute-done | bytes 32800 | tf_op jit(solution)/shard_map/ppermute | solution.py:328
  295.2 2.9 convolution_convert_fusion.2
  298.1 15.2 %conditional.34 = (f32[8,2048]{1,0:T(8,128)}, f32[8,2048]{1,0:T(8,128)S(1)}) conditional(s32[]{:T(128)} %convert_element_type.182, f32[128,128]{1,0:T(8,128)S(1)} %get-tuple-element.239, bf16[128,2048]{1,0:T(8,128)(2,1)S(1)} %convolution_convert_fusion.2), branch_computations={%region_40.41_spmd, %region_41.43_spmd} | conditional | flops 507904 | bytes 1769488
  298.1 13.6 %all_to_all.74 = bf16[16,8,2048]{2,1,0:T(8,128)(2,1)S(1)} all-to-all(bf16[16,8,2048]{2,1,0:T(8,128)(2,1)S(1)} %bitcast.162), channel_id=1, replica_groups=mesh['row'=8,'col'=16] {'col'}, dimensions={0} | all-to-all | bytes 1048576 | tf_op jit(solution)/shard_map/cond/branch_1_fun/all_to_all | solution.py:22
  313.3 2.0 fusion.52
  315.3 5.1 %all-to-all-start.14 = ((bf16[8,8,128]{2,1,0:T(8,128)(2,1)}), bf16[8,8,128]{2,1,0:T(8,128)(2,1)S(1)}, u32[]{:S(2)}, u32[]{:S(2)}) async-start(bf16[8,8,128]{2,1,0:T(8,128)(2,1)} %fusion.52), calls=%async_computation.14 | async-start | bytes 32768 | tf_op jit(solution)/shard_map/all_to_all | solution.py:22
  320.4 4.7 %all-to-all-done.14 = bf16[8,8,128]{2,1,0:T(8,128)(2,1)S(1)} async-done(((bf16[8,8,128]{2,1,0:T(8,128)(2,1)}), bf16[8,8,128]{2,1,0:T(8,128)(2,1)S(1)}, u32[]{:S(2)}, u32[]{:S(2)}) %all-to-all-start.14) | async-done | bytes 16416 | tf_op jit(solution)/shard_map/all_to_all | solution.py:22
  (134 shorter events, 40.2 us)
Async XLA Ops:
  7.2 109.3 %all-gather.2.cloned.1.call-start = ((), (), s32[]{:S(2)}) async-start(), calls=%async_computation.15 | async-start | bytes 13369344 | tf_op jit(solution)/shard_map/all_gather | solution.py:157
  15.1 3.7 %collective-permute-start.13 = (bf16[128,1024]{1,0:T(8,128)(2,1)S(1)}, bf16[128,1024]{1,0:T(8,128)(2,1)S(1)}, u32[]{:S(2)}, u32[]{:S(2)}) collective-permute-start(bf16[128,1024]{1,0:T(8,128)(2,1)S(1)} %broadcast_select_fusion), channel_id=1, source_target_pairs={{0,16},{32,48},{64,80},{112,96},{1,17},{33,49},{65,81},{113,97},{2... | collective-permute-start | bytes 786440 | tf_op jit(solution)/shard_map/ppermute | solution.py:154
  21.0 78.4 %collective-permute-start.14 = (bf16[1024,2048]{1,0:T(8,128)(2,1)}, bf16[1024,2048]{1,0:T(8,128)(2,1)}, u32[]{:S(2)}, u32[]{:S(2)}) collective-permute-start(bf16[1024,2048]{1,0:T(8,128)(2,1)} %bitcast.147), channel_id=1, source_target_pairs={{96,112},{97,113},{98,114},{99,115},{100,116},{101,117},{102,118},... | collective-permute-start | bytes 12582920 | tf_op jit(solution)/shard_map/ppermute | solution.py:202
  30.9 11.6 %all-to-all-start.12 = ((bf16[8,8,128]{2,1,0:T(8,128)(2,1)}), bf16[8,8,128]{2,1,0:T(8,128)(2,1)S(1)}, u32[]{:S(2)}, u32[]{:S(2)}) async-start(bf16[8,8,128]{2,1,0:T(8,128)(2,1)} %broadcast_in_dim.33), calls=%async_computation.12 | async-start | bytes 32768 | tf_op jit(solution)/shard_map/all_to_all | solution.py:22
  57.9 4.0 %collective-permute-start.3 = (bf16[128,128]{1,0:T(8,128)(2,1)S(1)}, bf16[128,128]{1,0:T(8,128)(2,1)S(1)}, u32[]{:S(2)}, u32[]{:S(2)}) collective-permute-start(bf16[128,128]{1,0:T(8,128)(2,1)S(1)} %bitcast_convert_fusion), channel_id=1, source_target_pairs={{0,16},{1,17},{2,18},{3,19},{4,20},{5,21},{6,22},{7,23},{8,24},{9,... | collective-permute-start | bytes 98312 | tf_op jit(solution)/shard_map/ppermute | solution.py:194
  79.1 2.6 collective-permute-start.4
  82.2 2.3 collective-permute-start.5
  85.1 2.4 collective-permute-start.6
  88.8 4.7 %collective-permute-start.8 = (bf16[128,640]{1,0:T(8,128)(2,1)}, bf16[128,640]{1,0:T(8,128)(2,1)}, u32[]{:S(2)}, u32[]{:S(2)}) collective-permute-start(bf16[128,640]{1,0:T(8,128)(2,1)} %pad_maximum_fusion.2), channel_id=1, source_target_pairs={{64,96},{65,97},{66,98},{67,99},{68,100},{69,101},{70,102},{71,103... | collective-permute-start | bytes 491528 | tf_op jit(solution)/shard_map/ppermute | solution.py:196
  90.1 4.7 %collective-permute-start.7 = (bf16[128,640]{1,0:T(8,128)(2,1)}, bf16[128,640]{1,0:T(8,128)(2,1)S(1)}, u32[]{:S(2)}, u32[]{:S(2)}) collective-permute-start(bf16[128,640]{1,0:T(8,128)(2,1)} %pad_maximum_fusion.2), channel_id=1, source_target_pairs={{64,80},{65,81},{66,82},{67,83},{68,84},{69,85},{70,86},{71,87},{7... | collective-permute-start | bytes 491528 | tf_op jit(solution)/shard_map/ppermute | solution.py:194
  92.8 4.2 %collective-permute-start.12 = (bf16[128,128]{1,0:T(8,128)(2,1)S(1)}, bf16[128,128]{1,0:T(8,128)(2,1)S(1)}, u32[]{:S(2)}, u32[]{:S(2)}) collective-permute-start(bf16[128,128]{1,0:T(8,128)(2,1)S(1)} %convert_element_type.198), channel_id=1, source_target_pairs={{96,112},{97,113},{98,114},{99,115},{100,116},{101,117},{102,118},... | collective-permute-start | bytes 98312 | tf_op jit(solution)/shard_map/ppermute | solution.py:203
  93.5 4.9 %collective-permute-start.10 = (bf16[128,640]{1,0:T(8,128)(2,1)}, bf16[128,640]{1,0:T(8,128)(2,1)}, u32[]{:S(2)}, u32[]{:S(2)}) collective-permute-start(bf16[128,640]{1,0:T(8,128)(2,1)} %collective-permute-done.8), channel_id=1, source_target_pairs={{96,112},{97,113},{98,114},{99,115},{100,116},{101,117},{102,118},... | collective-permute-start | bytes 491528 | tf_op jit(solution)/shard_map/ppermute | solution.py:206
  95.6 2.7 collective-permute-start.9
  96.3 2.1 collective-permute-start.11
  97.0 64.0 %collective-permute-start.16 = (bf16[128,128]{1,0:T(8,128)(2,1)S(1)}, bf16[128,128]{1,0:T(8,128)(2,1)S(1)}, u32[]{:S(2)}, u32[]{:S(2)}) collective-permute-start(bf16[128,128]{1,0:T(8,128)(2,1)S(1)} %convert_element_type.204), channel_id=1, source_target_pairs={{16,0},{48,32},{80,64},{17,1},{49,33},{81,65},{18,2},{50,34},{82,6... | collective-permute-start | bytes 98312 | tf_op jit(solution)/shard_map/ppermute | solution.py:281
  133.6 9.9 %collective-permute-start.1 = (bf16[1024,2048]{1,0:T(8,128)(2,1)}, bf16[1024,2048]{1,0:T(8,128)(2,1)}, u32[]{:S(2)}, u32[]{:S(2)}) collective-permute-start(bf16[1024,2048]{1,0:T(8,128)(2,1)} %get-tuple-element.183), channel_id=1, source_target_pairs={{16,0},{48,32},{80,64},{17,1},{49,33},{81,65},{18,2},{50,34},{82,6... | collective-permute-start | bytes 12582920 | tf_op jit(solution)/shard_map/cond/branch_1_fun/ppermute | solution.py:255
  154.1 6.2 %collective-permute-start.2 = (bf16[1024,1024]{1,0:T(8,128)(2,1)S(1)}, bf16[1024,1024]{1,0:T(8,128)(2,1)}, u32[]{:S(2)}, u32[]{:S(2)}) collective-permute-start(bf16[1024,1024]{1,0:T(8,128)(2,1)S(1)} %get-tuple-element.226), channel_id=1, source_target_pairs={{16,0},{48,32},{80,64},{17,1},{49,33},{81,65},{18,2},{50,34},{82,6... | collective-permute-start | bytes 6291464 | tf_op jit(solution)/shard_map/cond/branch_1_fun/ppermute | solution.py:261
  160.3 2.1 collective-permute-start.15
  161.0 3.5 %collective-permute-start.19 = (bf16[128,128]{1,0:T(8,128)(2,1)S(1)}, bf16[128,128]{1,0:T(8,128)(2,1)S(1)}, u32[]{:S(2)}, u32[]{:S(2)}) collective-permute-start(bf16[128,128]{1,0:T(8,128)(2,1)S(1)} %convert_element_type.207), channel_id=1, source_target_pairs={{112,80},{113,81},{114,82},{115,83},{116,84},{117,85},{118,86},{11... | collective-permute-start | bytes 98312 | tf_op jit(solution)/shard_map/ppermute | solution.py:297
  161.7 2.8 collective-permute-start.20
  162.5 2.1 collective-permute-start.17
  163.1 1.4 collective-permute-start.18
  163.8 4.3 %collective-permute-start.23 = (bf16[128,128]{1,0:T(8,128)(2,1)S(1)}, bf16[128,128]{1,0:T(8,128)(2,1)S(1)}, u32[]{:S(2)}, u32[]{:S(2)}) collective-permute-start(bf16[128,128]{1,0:T(8,128)(2,1)S(1)} %convert_element_type.208), channel_id=1, source_target_pairs={{96,112},{97,113},{98,114},{99,115},{100,116},{101,117},{102,118},... | collective-permute-start | bytes 98312 | tf_op jit(solution)/shard_map/ppermute | solution.py:310
  166.8 4.0 %collective-permute-start.21 = (bf16[128,128]{1,0:T(8,128)(2,1)S(1)}, bf16[128,128]{1,0:T(8,128)(2,1)S(1)}, u32[]{:S(2)}, u32[]{:S(2)}) collective-permute-start(bf16[128,128]{1,0:T(8,128)(2,1)S(1)} %convert_element_type.210), channel_id=1, source_target_pairs={{64,32},{80,48},{65,33},{81,49},{66,34},{82,50},{67,35},{83,51},{6... | collective-permute-start | bytes 98312 | tf_op jit(solution)/shard_map/ppermute | solution.py:327
  167.5 3.4 %collective-permute-start.22 = (bf16[128,128]{1,0:T(8,128)(2,1)S(1)}, bf16[128,128]{1,0:T(8,128)(2,1)S(1)}, u32[]{:S(2)}, u32[]{:S(2)}) collective-permute-start(bf16[128,128]{1,0:T(8,128)(2,1)S(1)} %convert_element_type.210), channel_id=1, source_target_pairs={{64,48},{80,32},{65,49},{81,33},{66,50},{82,34},{67,51},{83,35},{6... | collective-permute-start | bytes 98312 | tf_op jit(solution)/shard_map/ppermute | solution.py:328
  168.2 2.7 collective-permute-start.24
  168.9 126.2 %collective-permute-start.29 = (bf16[128,256]{1,0:T(8,128)(2,1)S(1)}, bf16[128,256]{1,0:T(8,128)(2,1)S(1)}, u32[]{:S(2)}, u32[]{:S(2)}) collective-permute-start(bf16[128,256]{1,0:T(8,128)(2,1)S(1)} %maximum_select_fusion.1), channel_id=1, source_target_pairs={{96,0},{112,16},{97,1},{113,17},{98,2},{114,18},{99,3},{115,19},{1... | collective-permute-start | bytes 196616 | tf_op jit(solution)/shard_map/ppermute | solution.py:317
  170.2 6.0 %collective-permute-start.27 = (bf16[128,128]{1,0:T(8,128)(2,1)S(1)}, bf16[128,128]{1,0:T(8,128)(2,1)S(1)}, u32[]{:S(2)}, u32[]{:S(2)}) collective-permute-start(bf16[128,128]{1,0:T(8,128)(2,1)S(1)} %convert_element_type.210), channel_id=1, source_target_pairs={{64,80},{80,64},{65,81},{81,65},{66,82},{82,66},{67,83},{83,67},{6... | collective-permute-start | bytes 98312 | tf_op jit(solution)/shard_map/ppermute | solution.py:332
  173.6 117.7 %collective-permute-start.25 = (bf16[128,128]{1,0:T(8,128)(2,1)S(1)}, bf16[128,128]{1,0:T(8,128)(2,1)S(1)}, u32[]{:S(2)}, u32[]{:S(2)}) collective-permute-start(bf16[128,128]{1,0:T(8,128)(2,1)S(1)} %convert_element_type.212), channel_id=1, source_target_pairs={{32,0},{48,16},{33,1},{49,17},{34,2},{50,18},{35,3},{51,19},{36,4}... | collective-permute-start | bytes 98312 | tf_op jit(solution)/shard_map/ppermute | solution.py:327
  174.9 120.2 %collective-permute-start.26 = (bf16[128,128]{1,0:T(8,128)(2,1)S(1)}, bf16[128,128]{1,0:T(8,128)(2,1)S(1)}, u32[]{:S(2)}, u32[]{:S(2)}) collective-permute-start(bf16[128,128]{1,0:T(8,128)(2,1)S(1)} %convert_element_type.212), channel_id=1, source_target_pairs={{32,16},{48,0},{33,17},{49,1},{34,18},{50,2},{35,19},{51,3},{36,20... | collective-permute-start | bytes 98312 | tf_op jit(solution)/shard_map/ppermute | solution.py:328
  176.2 118.9 %collective-permute-start.28 = (bf16[128,256]{1,0:T(8,128)(2,1)S(1)}, bf16[128,256]{1,0:T(8,128)(2,1)S(1)}, u32[]{:S(2)}, u32[]{:S(2)}) collective-permute-start(bf16[128,256]{1,0:T(8,128)(2,1)S(1)} %maximum_select_fusion.2), channel_id=1, source_target_pairs={{64,0},{80,16},{65,1},{81,17},{66,2},{82,18},{67,3},{83,19},{68,4}... | collective-permute-start | bytes 196616 | tf_op jit(solution)/shard_map/ppermute | solution.py:338
  315.3 9.8 %all-to-all-start.14 = ((bf16[8,8,128]{2,1,0:T(8,128)(2,1)}), bf16[8,8,128]{2,1,0:T(8,128)(2,1)S(1)}, u32[]{:S(2)}, u32[]{:S(2)}) async-start(bf16[8,8,128]{2,1,0:T(8,128)(2,1)} %fusion.52), calls=%async_computation.14 | async-start | bytes 32768 | tf_op jit(solution)/shard_map/all_to_all | solution.py:22
  (5 other events, 374.9 us)
Sparse Core Ops, SparseCore 0:
  21.1 95.3 all-gather.1

commit v12 on v10

--- a/solution.py
+++ b/solution.py
@@ -157,12 +157,17 @@
 
         return lax.cond(turn, reduce_columns, lambda run, tiles: run, run, tiles_of(partial))
 
-    def take_whole_turn(turn, run, sign, *operands):
-        def reduce_columns(run, x, weights):
-            total = jnp.sum(exchange(tiles_of(dot_nn(x, weights)), "col").astype(F32), axis=0)
-            return run - total if sign else total
-
-        return lax.cond(turn, reduce_columns, lambda run, *rest: run, run, *operands)
+    def reduce_product(x, weights):
+        return jnp.sum(exchange(tiles_of(dot_nn(x, weights)), "col").astype(F32), axis=0)
+
+    def take_whole_turn(turn, run, *operands):
+        return lax.cond(
+            turn,
+            lambda run, x, weights: reduce_product(x, weights),
+            lambda run, *rest: run,
+            run,
+            *operands,
+        )
 
     low = run.astype(BF)
     known = low
@@ -198,16 +203,27 @@
         return lax.ppermute(mine, "row", [(last - 1, last)]), mine
 
     def pass_nothing(whole, factor, partner):
-        nothing = jnp.zeros(((last - 1) * width, half), BF)
-        return nothing, nothing
+        shape = jax.ShapeDtypeStruct(((last - 1) * width, half), BF)
+        anywhere = pl.BlockSpec(memory_space=pl.ANY)
+        return pl.pallas_call(
+            lambda low_ref, high_ref: None,
+            out_shape=(shape, shape),
+            out_specs=(anywhere, anywhere),
+        )()
 
     passed_low, passed_high = lax.cond(
         row_at >= last - 1, pass_on, pass_nothing, whole, factor, partner
     )
-    known = jnp.concatenate([ahead, newest], axis=1)
     forward = low
-    run = take_whole_turn(
-        row_at == last - 1, run, -1, known, factor[: (last - 1) * width]
+    run = lax.cond(
+        row_at == last - 1,
+        lambda run, ahead, newest, factor: run
+        - reduce_product(jnp.concatenate([ahead, newest], axis=1), factor[: (last - 1) * width]),
+        lambda run, *rest: run,
+        run,
+        ahead,
+        newest,
+        factor,
     )
 
     first = jnp.where(row_at == last, 0, row_at // 2)
@@ -255,7 +271,7 @@
     )
 
     x = jnp.concatenate([-ahead_last, -newest_last, -partner_low, forward], axis=1)
-    run = take_whole_turn(row_at == last, run, 0, x, merged)
+    run = take_whole_turn(row_at == last, run, x, merged)
     low = run.astype(BF)
     seventh = low
     arrived = lax.ppermute(seventh, "row", [(last, last - 1)])
@@ -264,7 +280,6 @@
     run = take_whole_turn(
         row_at == last - 1,
         run,
-        0,
         jnp.concatenate([low, -arrived], axis=1),
         merged[(last - 1) * width :],
     )

time: 329 us -> 331 us (level)
    ppermute x2, waiting for transfers between devices: 110 us -> 114 us  [on_device(): straight = lax.ppermute(low, 'row', same)]
  transfers between devices with their start and end apart: 32 -> 32, of which waited for: 9 -> 9; matrix products, arithmetic and copies ran while one was open for 9% -> 8% of each run, Pallas kernels for 7% -> 7%
where the time goes in v12:
time: 331 us; the launch traced here: 329 us
  waiting for transfers between devices  156 us (47%)
  starting transfers between devices  46.8 us (14%)
  blocking collectives  43 us (13%)
  Pallas kernels  23.4 us (7%)
  matrix products  20.8 us (6%)
  local copies, waits for them, and re-layouts  16.8 us (5%)
  between operations  15.6 us (5%)
  other arithmetic  6.11 us (2%)
    ppermute x2, waiting for transfers between devices, on_device(): straight = lax.ppermute(low, 'row', same)  114 us
    all_to_all x3, blocking collectives, exchange(): return lax.all_to_all(x, axis, 0, 0, tiled=True)  43 us
    pallas_call x2, Pallas kernels, chunked(): pl.pallas_call(kernel, grid_spec=grid_spec, out_shape=jax.ShapeDtypeStruc...  23.4 us
    all_gather x1, waiting for transfers between devices, on_device(): whole = lax.all_gather(held, 'col', axis=0, tiled=True)  17 us
    dot_general x12, matrix products, dot_nn(): lax.dot_general(a, b, (((1,), (0,)), ((), ())), preferred_element_type=F32)  15.1 us
    all_to_all x2, starting transfers between devices, exchange(): return lax.all_to_all(x, axis, 0, 0, tiled=True)  12 us
    all_to_all x2, waiting for transfers between devices, exchange(): return lax.all_to_all(x, axis, 0, 0, tiled=True)  9.38 us
    unnamed x12, local copies, waits for them, and re-layouts  7.63 us
  transfers between devices with their start and end apart: 32, of which 9 were waited for; matrix products, arithmetic and copies ran while one was open for 8% of the time, Pallas kernels for 7%

profile of v12, /device:TPU:1, one launch (start us, length us, event | category | flops | bytes accessed | tf_op | source)
XLA Modules:
  0.0 329.2 jit_solution(7473981679398702430)
XLA Ops:
  7.2 6.8 %copy.30 = bf16[2048,8,128]{0,2,1:T(8,128)(2,1)} copy(bf16[2048,8,128]{2,1,0:T(8,128)(2,1)} %param.47) | data formatting | bytes 8388608 | tf_op args[7]
  21.0 2.7 collective-permute-start.14
  24.3 5.7 %fusion.15 = f32[8,2048]{1,0:T(8,128)S(1)} fusion(bf16[1,2048,2048]{2,1,0:T(8,128)(2,1)} %param.41, bf16[1,8,2048]{2,1,0:T(8,128)(2,1)S(1)} %copy-done.1), kind=kOutput, calls=%fused_computation.29 | convolution fusion | flops 67108864 | bytes 8486912 | tf_op jit(solution)/shard_map/dot_general | solution.py:14
  30.9 6.9 %all-to-all-start.12 = ((bf16[8,8,128]{2,1,0:T(8,128)(2,1)}), bf16[8,8,128]{2,1,0:T(8,128)(2,1)S(1)}, u32[]{:S(2)}, u32[]{:S(2)}) async-start(bf16[8,8,128]{2,1,0:T(8,128)(2,1)} %broadcast_in_dim.33), calls=%async_computation.12 | async-start | bytes 32768 | tf_op jit(solution)/shard_map/all_to_all | solution.py:22
  37.8 4.7 %all-to-all-done.12 = bf16[8,8,128]{2,1,0:T(8,128)(2,1)S(1)} async-done(((bf16[8,8,128]{2,1,0:T(8,128)(2,1)}), bf16[8,8,128]{2,1,0:T(8,128)(2,1)S(1)}, u32[]{:S(2)}, u32[]{:S(2)}) %all-to-all-start.12) | async-done | bytes 16416 | tf_op jit(solution)/shard_map/all_to_all | solution.py:22
  43.9 13.9 %all_to_all.75 = f32[16,8,128]{2,1,0:T(8,128)S(1)} all-to-all(f32[16,8,128]{2,1,0:T(8,128)S(1)} %fusion.46), channel_id=1, replica_groups=mesh['row'=8,'col'=16] {'col'}, dimensions={0} | all-to-all | bytes 131072 | tf_op jit(solution)/shard_map/all_to_all | solution.py:22
  59.2 2.7 collective-permute-done.3
  63.4 15.6 %conditional.21 = (f32[128,128]{1,0:T(8,128)S(1)}) conditional(s32[]{:T(128)} %convert_element_type.191, f32[128,128]{1,0:T(8,128)S(1)} %bitcast.156, (bf16[16,128,128]{2,1,0:T(8,128)(2,1)S(1)}, f32[128,128]{1,0:T(8,128)S(1)}) %tuple.179), branch_computations={%region_0.1_spmd, %region_1.3_spmd} | conditional | flops 524288 | bytes 1835016 | solution.py:158
  63.4 15.5 %all_to_all.63 = bf16[16,128,128]{2,1,0:T(8,128)(2,1)S(1)} all-to-all(bf16[16,128,128]{2,1,0:T(8,128)(2,1)S(1)} %get-tuple-element.150), channel_id=1, replica_groups=mesh['row'=8,'col'=16] {'col'}, dimensions={0} | all-to-all | bytes 1048576 | tf_op jit(solution)/shard_map/cond/branch_1_fun/all_to_all | solution.py:22
  82.8 1.6 slice.68
  85.8 1.7 slice.69
  90.8 2.0 slice.70
  99.4 17.0 %all-gather.2.cloned.1.call-done.right_ref = bf16[2048,3072]{1,0:T(8,128)(2,1)} async-done(((bf16[128,3072]{1,0:T(8,128)(2,1)}), bf16[2048,3072]{1,0:T(8,128)(2,1)}) %all-gather.2.cloned.1.call-update) | async-done | bytes 12582928 | tf_op jit(solution)/shard_map/all_gather | solution.py:138
  116.4 15.3 %shard_map.95 = bf16[1024,2048]{1,0:T(8,128)(2,1)} custom-call(s32[3]{0:T(128)S(1)} %pad_add_fusion.at_ref, bf16[2048,3072]{1,0:T(8,128)(2,1)} %all-gather.2.cloned.1.call-done.right_ref, bf16[1024,2048]{1,0:T(8,128)(2,1)} %bitcast.155, bf16[768,1024]{1,0:T(8,128)(2,1)} %get-tuple-element.196.passed_low_ref, bf16[768,1024]{1,0:T(8,128)(2,1)} %get-tuple-element.197.passed_high_ref), custom_call_target="tpu_custom_call" | custom-call | tf_op jit(solution)/shard_map/pallas_call | solution.py:97
  131.7 24.2 %conditional.28 = (bf16[1024,2048]{1,0:T(8,128)(2,1)}) conditional(s32[]{:T(128)} %convert_element_type.205, bf16[1024,2048]{1,0:T(8,128)(2,1)} %shard_map.95, (pred[]{:T(512)}, bf16[1024,2048]{1,0:T(8,128)(2,1)}, s32[3]{0:T(128)S(1)}, bf16[2048,3072]{1,0:T(8,128)(2,1)}) %tuple.125), branch_computations={%region_22.23_spmd, %region_23.28_spmd} | conditional | flops 1 | bytes 25166012 | solution.py:269
  131.7 4.7 %collective-permute-start.1 = (bf16[1024,2048]{1,0:T(8,128)(2,1)}, bf16[1024,2048]{1,0:T(8,128)(2,1)}, u32[]{:S(2)}, u32[]{:S(2)}) collective-permute-start(bf16[1024,2048]{1,0:T(8,128)(2,1)} %get-tuple-element.183), channel_id=1, source_target_pairs={{16,0},{48,32},{80,64},{17,1},{49,33},{81,65},{18,2},{50,34},{82,6... | collective-permute-start | bytes 12582920 | tf_op jit(solution)/shard_map/cond/branch_1_fun/ppermute | solution.py:236
  136.4 5.2 %collective-permute-done.1 = bf16[1024,2048]{1,0:T(8,128)(2,1)} collective-permute-done((bf16[1024,2048]{1,0:T(8,128)(2,1)}, bf16[1024,2048]{1,0:T(8,128)(2,1)}, u32[]{:S(2)}, u32[]{:S(2)}) %collective-permute-start.1) | collective-permute-done | bytes 4194336 | tf_op jit(solution)/shard_map/cond/branch_1_fun/ppermute | solution.py:236
  141.6 8.2 %conditional.6 = (bf16[1024,1024]{1,0:T(8,128)(2,1)S(1)}) conditional(s32[]{:T(128)} %convert_element_type.134, (s32[3]{0:T(128)S(1)}, bf16[2048,3072]{1,0:T(8,128)(2,1)}, bf16[1024,2048]{1,0:T(8,128)(2,1)}) %tuple.99, (s32[3]{0:T(128)S(1)}, bf16[2048,3072]{1,0:T(8,128)(2,1)}, bf16[1024,2048]{1,0:T(8,128)(2,1)}) %tuple.100), branch_computations={%region_24.24_spmd, %region_25.25_spmd} | conditional | bytes 8 | solution.py:241
  141.6 8.1 %branch_0_fun.5 = bf16[1024,1024]{1,0:T(8,128)(2,1)S(1)} custom-call(s32[3]{0:T(128)S(1)} %get-tuple-element.171.at_ref, bf16[2048,3072]{1,0:T(8,128)(2,1)} %get-tuple-element.172.right_ref, bf16[1024,2048]{1,0:T(8,128)(2,1)} %get-tuple-element.173.left_ref), custom_call_target="tpu_custom_call" | custom-call | tf_op jit(solution)/shard_map/cond/branch_1_fun/cond/branch_0_fun/pallas_call | solution.py:97
  149.7 3.6 %collective-permute-start.2 = (bf16[1024,1024]{1,0:T(8,128)(2,1)S(1)}, bf16[1024,1024]{1,0:T(8,128)(2,1)}, u32[]{:S(2)}, u32[]{:S(2)}) collective-permute-start(bf16[1024,1024]{1,0:T(8,128)(2,1)S(1)} %get-tuple-element.226), channel_id=1, source_target_pairs={{16,0},{48,32},{80,64},{17,1},{49,33},{81,65},{18,2},{50,34},{82,6... | collective-permute-start | bytes 6291464 | tf_op jit(solution)/shard_map/cond/branch_1_fun/ppermute | solution.py:242
  153.3 2.6 collective-permute-done.2
  160.2 2.0 fusion.39
  166.5 2.5 fusion.42
  171.8 1.5 collective-permute-start.28
  173.3 114.4 %collective-permute-done.25 = bf16[128,128]{1,0:T(8,128)(2,1)S(1)} collective-permute-done((bf16[128,128]{1,0:T(8,128)(2,1)S(1)}, bf16[128,128]{1,0:T(8,128)(2,1)S(1)}, u32[]{:S(2)}, u32[]{:S(2)}) %collective-permute-start.25) | collective-permute-done | bytes 32800 | tf_op jit(solution)/shard_map/ppermute | solution.py:308
  287.7 3.8 %collective-permute-done.26 = bf16[128,128]{1,0:T(8,128)(2,1)S(1)} collective-permute-done((bf16[128,128]{1,0:T(8,128)(2,1)S(1)}, bf16[128,128]{1,0:T(8,128)(2,1)S(1)}, u32[]{:S(2)}, u32[]{:S(2)}) %collective-permute-start.26) | collective-permute-done | bytes 32800 | tf_op jit(solution)/shard_map/ppermute | solution.py:309
  291.6 2.9 convolution_convert_fusion.2
  294.5 15.2 %conditional.34 = (f32[8,2048]{1,0:T(8,128)}, f32[8,2048]{1,0:T(8,128)S(1)}) conditional(s32[]{:T(128)} %convert_element_type.182, f32[128,128]{1,0:T(8,128)S(1)} %get-tuple-element.239, bf16[128,2048]{1,0:T(8,128)(2,1)S(1)} %convolution_convert_fusion.2), branch_computations={%region_40.41_spmd, %region_41.43_spmd} | conditional | flops 507904 | bytes 1769488
  294.6 13.6 %all_to_all.74 = bf16[16,8,2048]{2,1,0:T(8,128)(2,1)S(1)} all-to-all(bf16[16,8,2048]{2,1,0:T(8,128)(2,1)S(1)} %bitcast.162), channel_id=1, replica_groups=mesh['row'=8,'col'=16] {'col'}, dimensions={0} | all-to-all | bytes 1048576 | tf_op jit(solution)/shard_map/cond/branch_1_fun/all_to_all | solution.py:22
  309.7 2.0 fusion.52
  311.7 5.1 %all-to-all-start.14 = ((bf16[8,8,128]{2,1,0:T(8,128)(2,1)}), bf16[8,8,128]{2,1,0:T(8,128)(2,1)S(1)}, u32[]{:S(2)}, u32[]{:S(2)}) async-start(bf16[8,8,128]{2,1,0:T(8,128)(2,1)} %fusion.52), calls=%async_computation.14 | async-start | bytes 32768 | tf_op jit(solution)/shard_map/all_to_all | solution.py:22
  316.8 4.7 %all-to-all-done.14 = bf16[8,8,128]{2,1,0:T(8,128)(2,1)S(1)} async-done(((bf16[8,8,128]{2,1,0:T(8,128)(2,1)}), bf16[8,8,128]{2,1,0:T(8,128)(2,1)S(1)}, u32[]{:S(2)}, u32[]{:S(2)}) %all-to-all-start.14) | async-done | bytes 16416 | tf_op jit(solution)/shard_map/all_to_all | solution.py:22
  (134 shorter events, 40.3 us)
Async XLA Ops:
  7.2 109.3 %all-gather.2.cloned.1.call-start = ((), (), s32[]{:S(2)}) async-start(), calls=%async_computation.15 | async-start | bytes 13369344 | tf_op jit(solution)/shard_map/all_gather | solution.py:138
  15.1 3.7 %collective-permute-start.13 = (bf16[128,1024]{1,0:T(8,128)(2,1)S(1)}, bf16[128,1024]{1,0:T(8,128)(2,1)S(1)}, u32[]{:S(2)}, u32[]{:S(2)}) collective-permute-start(bf16[128,1024]{1,0:T(8,128)(2,1)S(1)} %broadcast_select_fusion), channel_id=1, source_target_pairs={{0,16},{32,48},{64,80},{112,96},{1,17},{33,49},{65,81},{113,97},{2... | collective-permute-start | bytes 786440 | tf_op jit(solution)/shard_map/ppermute | solution.py:135
  21.0 78.4 %collective-permute-start.14 = (bf16[1024,2048]{1,0:T(8,128)(2,1)}, bf16[1024,2048]{1,0:T(8,128)(2,1)}, u32[]{:S(2)}, u32[]{:S(2)}) collective-permute-start(bf16[1024,2048]{1,0:T(8,128)(2,1)} %bitcast.147), channel_id=1, source_target_pairs={{96,112},{97,113},{98,114},{99,115},{100,116},{101,117},{102,118},... | collective-permute-start | bytes 12582920 | tf_op jit(solution)/shard_map/ppermute | solution.py:183
  30.9 11.6 %all-to-all-start.12 = ((bf16[8,8,128]{2,1,0:T(8,128)(2,1)}), bf16[8,8,128]{2,1,0:T(8,128)(2,1)S(1)}, u32[]{:S(2)}, u32[]{:S(2)}) async-start(bf16[8,8,128]{2,1,0:T(8,128)(2,1)} %broadcast_in_dim.33), calls=%async_computation.12 | async-start | bytes 32768 | tf_op jit(solution)/shard_map/all_to_all | solution.py:22
  57.9 4.0 %collective-permute-start.3 = (bf16[128,128]{1,0:T(8,128)(2,1)S(1)}, bf16[128,128]{1,0:T(8,128)(2,1)S(1)}, u32[]{:S(2)}, u32[]{:S(2)}) collective-permute-start(bf16[128,128]{1,0:T(8,128)(2,1)S(1)} %bitcast_convert_fusion), channel_id=1, source_target_pairs={{0,16},{1,17},{2,18},{3,19},{4,20},{5,21},{6,22},{7,23},{8,24},{9,... | collective-permute-start | bytes 98312 | tf_op jit(solution)/shard_map/ppermute | solution.py:175
  79.1 2.6 collective-permute-start.4
  82.2 2.3 collective-permute-start.5
  85.1 2.4 collective-permute-start.6
  88.8 4.7 %collective-permute-start.8 = (bf16[128,640]{1,0:T(8,128)(2,1)}, bf16[128,640]{1,0:T(8,128)(2,1)}, u32[]{:S(2)}, u32[]{:S(2)}) collective-permute-start(bf16[128,640]{1,0:T(8,128)(2,1)} %pad_maximum_fusion.2), channel_id=1, source_target_pairs={{64,96},{65,97},{66,98},{67,99},{68,100},{69,101},{70,102},{71,103... | collective-permute-start | bytes 491528 | tf_op jit(solution)/shard_map/ppermute | solution.py:177
  90.1 4.7 %collective-permute-start.7 = (bf16[128,640]{1,0:T(8,128)(2,1)}, bf16[128,640]{1,0:T(8,128)(2,1)S(1)}, u32[]{:S(2)}, u32[]{:S(2)}) collective-permute-start(bf16[128,640]{1,0:T(8,128)(2,1)} %pad_maximum_fusion.2), channel_id=1, source_target_pairs={{64,80},{65,81},{66,82},{67,83},{68,84},{69,85},{70,86},{71,87},{7... | collective-permute-start | bytes 491528 | tf_op jit(solution)/shard_map/ppermute | solution.py:175
  92.8 4.2 %collective-permute-start.12 = (bf16[128,128]{1,0:T(8,128)(2,1)S(1)}, bf16[128,128]{1,0:T(8,128)(2,1)S(1)}, u32[]{:S(2)}, u32[]{:S(2)}) collective-permute-start(bf16[128,128]{1,0:T(8,128)(2,1)S(1)} %convert_element_type.198), channel_id=1, source_target_pairs={{96,112},{97,113},{98,114},{99,115},{100,116},{101,117},{102,118},... | collective-permute-start | bytes 98312 | tf_op jit(solution)/shard_map/ppermute | solution.py:184
  93.5 4.9 %collective-permute-start.10 = (bf16[128,640]{1,0:T(8,128)(2,1)}, bf16[128,640]{1,0:T(8,128)(2,1)}, u32[]{:S(2)}, u32[]{:S(2)}) collective-permute-start(bf16[128,640]{1,0:T(8,128)(2,1)} %collective-permute-done.8), channel_id=1, source_target_pairs={{96,112},{97,113},{98,114},{99,115},{100,116},{101,117},{102,118},... | collective-permute-start | bytes 491528 | tf_op jit(solution)/shard_map/ppermute | solution.py:187
  95.6 2.7 collective-permute-start.9
  96.3 2.1 collective-permute-start.11
  97.0 59.6 %collective-permute-start.16 = (bf16[128,128]{1,0:T(8,128)(2,1)S(1)}, bf16[128,128]{1,0:T(8,128)(2,1)S(1)}, u32[]{:S(2)}, u32[]{:S(2)}) collective-permute-start(bf16[128,128]{1,0:T(8,128)(2,1)S(1)} %convert_element_type.204), channel_id=1, source_target_pairs={{16,0},{48,32},{80,64},{17,1},{49,33},{81,65},{18,2},{50,34},{82,6... | collective-permute-start | bytes 98312 | tf_op jit(solution)/shard_map/ppermute | solution.py:262
  131.7 9.9 %collective-permute-start.1 = (bf16[1024,2048]{1,0:T(8,128)(2,1)}, bf16[1024,2048]{1,0:T(8,128)(2,1)}, u32[]{:S(2)}, u32[]{:S(2)}) collective-permute-start(bf16[1024,2048]{1,0:T(8,128)(2,1)} %get-tuple-element.183), channel_id=1, source_target_pairs={{16,0},{48,32},{80,64},{17,1},{49,33},{81,65},{18,2},{50,34},{82,6... | collective-permute-start | bytes 12582920 | tf_op jit(solution)/shard_map/cond/branch_1_fun/ppermute | solution.py:236
  149.7 6.2 %collective-permute-start.2 = (bf16[1024,1024]{1,0:T(8,128)(2,1)S(1)}, bf16[1024,1024]{1,0:T(8,128)(2,1)}, u32[]{:S(2)}, u32[]{:S(2)}) collective-permute-start(bf16[1024,1024]{1,0:T(8,128)(2,1)S(1)} %get-tuple-element.226), channel_id=1, source_target_pairs={{16,0},{48,32},{80,64},{17,1},{49,33},{81,65},{18,2},{50,34},{82,6... | collective-permute-start | bytes 6291464 | tf_op jit(solution)/shard_map/cond/branch_1_fun/ppermute | solution.py:242
  155.9 2.1 collective-permute-start.15
  156.6 3.5 %collective-permute-start.19 = (bf16[128,128]{1,0:T(8,128)(2,1)S(1)}, bf16[128,128]{1,0:T(8,128)(2,1)S(1)}, u32[]{:S(2)}, u32[]{:S(2)}) collective-permute-start(bf16[128,128]{1,0:T(8,128)(2,1)S(1)} %convert_element_type.207), channel_id=1, source_target_pairs={{112,80},{113,81},{114,82},{115,83},{116,84},{117,85},{118,86},{11... | collective-permute-start | bytes 98312 | tf_op jit(solution)/shard_map/ppermute | solution.py:278
  157.3 2.8 collective-permute-start.20
  158.1 2.1 collective-permute-start.17
  158.7 1.4 collective-permute-start.18
  159.4 4.3 %collective-permute-start.23 = (bf16[128,128]{1,0:T(8,128)(2,1)S(1)}, bf16[128,128]{1,0:T(8,128)(2,1)S(1)}, u32[]{:S(2)}, u32[]{:S(2)}) collective-permute-start(bf16[128,128]{1,0:T(8,128)(2,1)S(1)} %convert_element_type.208), channel_id=1, source_target_pairs={{96,112},{97,113},{98,114},{99,115},{100,116},{101,117},{102,118},... | collective-permute-start | bytes 98312 | tf_op jit(solution)/shard_map/ppermute | solution.py:291
  162.4 4.0 %collective-permute-start.21 = (bf16[128,128]{1,0:T(8,128)(2,1)S(1)}, bf16[128,128]{1,0:T(8,128)(2,1)S(1)}, u32[]{:S(2)}, u32[]{:S(2)}) collective-permute-start(bf16[128,128]{1,0:T(8,128)(2,1)S(1)} %convert_element_type.210), channel_id=1, source_target_pairs={{64,32},{80,48},{65,33},{81,49},{66,34},{82,50},{67,35},{83,51},{6... | collective-permute-start | bytes 98312 | tf_op jit(solution)/shard_map/ppermute | solution.py:308
  163.1 3.4 %collective-permute-start.22 = (bf16[128,128]{1,0:T(8,128)(2,1)S(1)}, bf16[128,128]{1,0:T(8,128)(2,1)S(1)}, u32[]{:S(2)}, u32[]{:S(2)}) collective-permute-start(bf16[128,128]{1,0:T(8,128)(2,1)S(1)} %convert_element_type.210), channel_id=1, source_target_pairs={{64,48},{80,32},{65,49},{81,33},{66,50},{82,34},{67,51},{83,35},{6... | collective-permute-start | bytes 98312 | tf_op jit(solution)/shard_map/ppermute | solution.py:309
  163.8 2.7 collective-permute-start.24
  164.5 127.1 %collective-permute-start.29 = (bf16[128,256]{1,0:T(8,128)(2,1)S(1)}, bf16[128,256]{1,0:T(8,128)(2,1)S(1)}, u32[]{:S(2)}, u32[]{:S(2)}) collective-permute-start(bf16[128,256]{1,0:T(8,128)(2,1)S(1)} %maximum_select_fusion.1), channel_id=1, source_target_pairs={{96,0},{112,16},{97,1},{113,17},{98,2},{114,18},{99,3},{115,19},{1... | collective-permute-start | bytes 196616 | tf_op jit(solution)/shard_map/ppermute | solution.py:298
  165.8 6.0 %collective-permute-start.27 = (bf16[128,128]{1,0:T(8,128)(2,1)S(1)}, bf16[128,128]{1,0:T(8,128)(2,1)S(1)}, u32[]{:S(2)}, u32[]{:S(2)}) collective-permute-start(bf16[128,128]{1,0:T(8,128)(2,1)S(1)} %convert_element_type.210), channel_id=1, source_target_pairs={{64,80},{80,64},{65,81},{81,65},{66,82},{82,66},{67,83},{83,67},{6... | collective-permute-start | bytes 98312 | tf_op jit(solution)/shard_map/ppermute | solution.py:313
  169.2 118.5 %collective-permute-start.25 = (bf16[128,128]{1,0:T(8,128)(2,1)S(1)}, bf16[128,128]{1,0:T(8,128)(2,1)S(1)}, u32[]{:S(2)}, u32[]{:S(2)}) collective-permute-start(bf16[128,128]{1,0:T(8,128)(2,1)S(1)} %convert_element_type.212), channel_id=1, source_target_pairs={{32,0},{48,16},{33,1},{49,17},{34,2},{50,18},{35,3},{51,19},{36,4}... | collective-permute-start | bytes 98312 | tf_op jit(solution)/shard_map/ppermute | solution.py:308
  170.5 121.0 %collective-permute-start.26 = (bf16[128,128]{1,0:T(8,128)(2,1)S(1)}, bf16[128,128]{1,0:T(8,128)(2,1)S(1)}, u32[]{:S(2)}, u32[]{:S(2)}) collective-permute-start(bf16[128,128]{1,0:T(8,128)(2,1)S(1)} %convert_element_type.212), channel_id=1, source_target_pairs={{32,16},{48,0},{33,17},{49,1},{34,18},{50,2},{35,19},{51,3},{36,20... | collective-permute-start | bytes 98312 | tf_op jit(solution)/shard_map/ppermute | solution.py:309
  171.8 119.7 %collective-permute-start.28 = (bf16[128,256]{1,0:T(8,128)(2,1)S(1)}, bf16[128,256]{1,0:T(8,128)(2,1)S(1)}, u32[]{:S(2)}, u32[]{:S(2)}) collective-permute-start(bf16[128,256]{1,0:T(8,128)(2,1)S(1)} %maximum_select_fusion.2), channel_id=1, source_target_pairs={{64,0},{80,16},{65,1},{81,17},{66,2},{82,18},{67,3},{83,19},{68,4}... | collective-permute-start | bytes 196616 | tf_op jit(solution)/shard_map/ppermute | solution.py:319
  311.7 9.8 %all-to-all-start.14 = ((bf16[8,8,128]{2,1,0:T(8,128)(2,1)}), bf16[8,8,128]{2,1,0:T(8,128)(2,1)S(1)}, u32[]{:S(2)}, u32[]{:S(2)}) async-start(bf16[8,8,128]{2,1,0:T(8,128)(2,1)} %fusion.52), calls=%async_computation.14 | async-start | bytes 32768 | tf_op jit(solution)/shard_map/all_to_all | solution.py:22
  (5 other events, 371.4 us)
Sparse Core Ops, SparseCore 0:
  21.1 95.3 all-gather.1
